TPU v7x, 32 devices: a whole 2x2x4 slice. The times are simulated.
32 devices in a mesh: dp: 4 (over y, x), feat: 8 (over z, core).
Axes of the slice: x: 2, y: 2, z: 4, core: 2. Of those that a mesh axis runs over, the one named last changes fastest.
Arguments:
- sketches: bfloat16 [4, 256, 65536], P('dp', None, 'feat'), may hold values from -24 to 24
Outputs:
- merged: bfloat16 [4, 256, 65536], P('dp', None, 'feat')
All inputs are finite; a program needn't handle non-finite values.
Results may differ from a plain program's by a relative error of at most 0.001.
The roundings to bfloat16 on the way count: a program that leaves them out, or rounds other values in their place, can miss the bound.
Values may be sent and summed in bfloat16 or wider, within the bound.
No kernel may reach another device: no remote copies, remote signals or barrier semaphores. Data moves between devices by JAX's collectives and lax.ppermute only.
A program may use at most 128 MiB of HBM per device.

v0:
```python
import functools

import jax
import jax.numpy as jnp
from jax import lax
from jax.experimental import pallas as pl
from jax.experimental.pallas import tpu as pltpu
from jax.sharding import PartitionSpec as P


LEVELS = 2
GROUP = 2**LEVELS
CORES = 2
F32, BF16 = jnp.float32, jnp.bfloat16
NT = (((1,), (1,)), ((), ()))
NN = (((1,), (0,)), ((), ()))
VMEM = pl.BlockSpec(memory_space=pltpu.VMEM)
SMEM = pl.BlockSpec(memory_space=pltpu.SMEM)
ANY = pl.BlockSpec(memory_space=pl.ANY)


def send(block, axis, shift):
    count = lax.axis_size(axis)
    return lax.ppermute(block, axis, [(i, i ^ shift) for i in range(count)])


def send_all(blocks, axis, shifts):
    return [send(b, axis, s) for b, s in zip(blocks, shifts)]


def dot(a, b, dims=NN):
    return lax.dot_general(a, b, dims, preferred_element_type=F32)


def shape(*dims, dtype=F32):
    return jax.ShapeDtypeStruct(dims, dtype)


def cost(flops, nbytes):
    return pl.CostEstimate(flops=int(flops), bytes_accessed=int(nbytes), transcendentals=0)


def halves(a):
    high = a.astype(BF16)
    return high, (a - high.astype(F32)).astype(BF16)


def product(a, b, dims=NN):
    (ah, al), (bh, bl) = a, b
    return dot(ah, bh, dims) + (dot(ah, bl, dims) + dot(al, bh, dims))


def eye_mask(n):
    return lax.broadcasted_iota(jnp.int32, (n, n), 0) == lax.broadcasted_iota(jnp.int32, (n, n), 1)


def invert(kernels, x_ref, limit):
    n = kernels[0].shape[0]
    mask = eye_mask(n)
    eye = jnp.where(mask, 1.0, 0.0)
    parts = [halves(k) for k in kernels]
    for j, k in enumerate(kernels):
        diag = jnp.where(mask, k, 0.0)
        row = 1.0 / jnp.sum(diag, axis=0, keepdims=True)
        col = 1.0 / jnp.sum(diag, axis=1, keepdims=True)
        scaled = jnp.where(mask, 0.0, k) * row
        spread = jnp.sum(scaled * (jnp.where(mask, 0.0, k) * col))
        bound = jnp.minimum(jnp.max(jnp.sum(jnp.abs(k), axis=1, keepdims=True)), limit)
        near = jnp.where(mask, row, -scaled * col)
        far = eye * (2.0 / (1.0 + bound))
        x_ref[j] = jnp.where(spread < 0.9, near, far)

    def step(state):
        count, _ = state
        worst = jnp.float32(0.0)
        for j, part in enumerate(parts):
            x = x_ref[j]
            xs = halves(x)
            rest = eye - product(part, xs)
            worst = jnp.maximum(worst, jnp.sum(rest * rest))
            x_ref[j] = x + product(xs, halves(rest))
        return count + 1, worst

    lax.while_loop(lambda s: (s[0] < 24) & (s[1] > 1e-6), step, (jnp.int32(0), jnp.float32(1.0)))


def resolvent(grams, x_ref, out_ref):
    n = grams[0][0].shape[0]
    mask = eye_mask(n)
    eye = jnp.where(mask, 1.0, 0.0)
    scaled = []
    for a, b, d in grams:
        average = jnp.sum(jnp.where(mask, a + d, 0.0)) / (2 * n)
        scaled.append((eye + a / average, b / average, eye + d / average))
    limit = 1.0 + 2 * n
    invert([d for _, _, d in scaled], x_ref, limit)
    ties, schurs = [], []
    for j, (a, b, d) in enumerate(scaled):
        bs = halves(b)
        tie = halves(product(bs, halves(x_ref[j])))
        ties.append(tie)
        schurs.append(a - product(tie, bs, NT))
    invert(schurs, x_ref, limit)
    for j, tie in enumerate(ties):
        x = x_ref[j]
        out_ref[j, :, :n] = x.astype(BF16)
        out_ref[j, :, n:] = (-product(halves(x), tie)).astype(BF16)


def own_gram_kernel(place, x_ref, keep_ref, give_ref, acc):
    step = pl.program_id(0)
    core = place[1]
    half = keep_ref.shape[0]

    @pl.when(step == 0)
    def _():
        acc[...] = jnp.zeros_like(acc)

    acc[...] += dot(x_ref[...], x_ref[...], NT)

    @pl.when(step == pl.num_programs(0) - 1)
    def _():
        keep_ref[...] = acc[pl.ds(pl.multiple_of(core * half, half), half), :]
        give_ref[...] = acc[pl.ds(pl.multiple_of((1 - core) * half, half), half), :]


def own_gram(place, x, tile=2048):
    rows, columns = x.shape
    half = shape(rows // CORES, rows)
    spec = pl.BlockSpec((rows // CORES, rows), lambda k, place: (0, 0))
    return pl.pallas_call(
        own_gram_kernel,
        out_shape=(half, half),
        grid_spec=pltpu.PrefetchScalarGridSpec(
            num_scalar_prefetch=1,
            grid=(columns // tile,),
            in_specs=[pl.BlockSpec((rows, tile), lambda k, place: (0, k))],
            out_specs=(spec, spec),
            scratch_shapes=[pltpu.VMEM((rows, rows), F32)],
        ),
        cost_estimate=cost(2 * rows * rows * columns, 2 * rows * columns),
        name="own_gram",
    )(place, x)


def near_gram_kernel(place, own, p1, out_ref, block):
    step = pl.program_id(0)
    for s, piece in enumerate((own, p1)):
        block[(place[0] ^ s) % 2] = piece[...]

    @pl.when(step == 0)
    def _():
        out_ref[...] = jnp.zeros_like(out_ref)

    out_ref[...] += dot(block[0], block[1], NT)


def near_gram(place, x, p1, tile=1024):
    rows, share = p1.shape
    steps = share // tile
    return pl.pallas_call(
        near_gram_kernel,
        out_shape=shape(rows, rows),
        grid_spec=pltpu.PrefetchScalarGridSpec(
            num_scalar_prefetch=1,
            grid=(steps,),
            in_specs=[
                pl.BlockSpec((rows, tile), lambda k, place: (0, place[0] * steps + k)),
                pl.BlockSpec((rows, tile), lambda k, place: (0, k)),
            ],
            out_specs=pl.BlockSpec((rows, rows), lambda k, place: (0, 0)),
            scratch_shapes=[pltpu.VMEM((2, rows, tile), BF16)],
        ),
        cost_estimate=cost(2 * rows * rows * share, 4 * rows * share),
        name="near_gram",
    )(place, x, p1)


def far_gram_kernel(place, near, p2, p3, keep_ref, give_ref, block, acc):
    step = pl.program_id(0)
    me, core = place[0], place[1]
    for s, piece in ((2, p2), (3, p3)):
        block[(me ^ s) % 2] = piece[...]

    @pl.when(step == 0)
    def _():
        acc[me // 2] = near[...]
        acc[1 - me // 2] = jnp.zeros_like(near)

    acc[1 - me // 2] += dot(block[0], block[1], NT)

    @pl.when(step == pl.num_programs(0) - 1)
    def _():
        part = keep_ref.shape[1]
        for s in range(GROUP):
            to = me ^ s
            pair, start = to // 2, (to % 2) * (CORES * part)
            keep_ref[s] = acc[pair, pl.ds(pl.multiple_of(start + core * part, part), part), :]
            give_ref[s] = acc[pair, pl.ds(pl.multiple_of(start + (1 - core) * part, part), part), :]


def far_gram(place, near, p2, p3, tile=1024):
    rows, share = p2.shape
    part = rows // (2 * CORES)
    out = shape(GROUP, part, rows)
    spec = pl.BlockSpec(out.shape, lambda k, place: (0, 0, 0))
    piece = pl.BlockSpec((rows, tile), lambda k, place: (0, k))
    return pl.pallas_call(
        far_gram_kernel,
        out_shape=(out, out),
        grid_spec=pltpu.PrefetchScalarGridSpec(
            num_scalar_prefetch=1,
            grid=(share // tile,),
            in_specs=[pl.BlockSpec((rows, rows), lambda k, place: (0, 0)), piece, piece],
            out_specs=(spec, spec),
            scratch_shapes=[pltpu.VMEM((2, rows, tile), BF16), pltpu.VMEM((GROUP // 2, rows, rows), F32)],
        ),
        cost_estimate=cost(2 * rows * rows * share, 4 * rows * share),
        name="far_gram",
    )(place, near, p2, p3)


def fold(mine, theirs):
    return [mine[s] + theirs[s] for s in range(mine.shape[0])]


def total(arrays):
    return functools.reduce(jnp.add, arrays)


def merge_rows(lower, upper, w):
    rows = lower.shape[0]
    update = dot(w[:, :rows], lower) + dot(w[:, rows:], upper)
    return (lower.astype(F32) - update).astype(BF16)


def first_kernel(tile, *refs):
    place, tails, crosses, (x, p1, p2, p3), refs = refs[0], refs[1:9], refs[9:17], refs[17:21], refs[21:]
    m_ref, e_ref, f_ref, keep_ref, give_ref, cross, diag, inverse, w, block, m, acc, load, save = refs
    ahead = e_ref.shape[2]
    me, core = place[0], place[1]
    rows, share = p1.shape
    loads = [pltpu.make_async_copy(x.at[:, pl.ds(pl.multiple_of(me * share, share), share)], block.at[me], load.at[0])]
    loads += [pltpu.make_async_copy(p, block.at[me ^ s], load.at[s]) for s, p in ((1, p1), (2, p2), (3, p3))]
    for copy in loads:
        copy.start()

    part, half = rows // (2 * CORES), rows // CORES
    for c in range(CORES):
        for s in range(GROUP):
            source, seat = me ^ s, core ^ c
            start = (source % 2) * (CORES * part) + seat * part
            cross[source // 2, pl.ds(pl.multiple_of(start, part), part), :] = crosses[c * GROUP + s][...]
            diag[source, pl.ds(pl.multiple_of(seat * half, half), half), :] = tails[c * GROUP + s][...]
    grams = [(diag[2 * j], cross[j], diag[2 * j + 1]) for j in range(GROUP // 2)]
    resolvent(grams, inverse, w)
    for copy in loads:
        copy.wait()

    acc[...] = jnp.zeros_like(acc)
    saves = []
    for k in range(share // tile):
        here = slice(k * tile, (k + 1) * tile)
        m0 = merge_rows(block[0, :, here], block[1, :, here], w[0])
        m1 = merge_rows(block[2, :, here], block[3, :, here], w[1])
        m[0, :, here] = m0
        m[1, :, here] = m1
        saves.append(pltpu.make_async_copy(m.at[:, :, here], m_ref.at[:, :, here], save.at[k]))
        saves[-1].start()
        acc[0] += dot(m0, m0, NT)
        acc[1] += dot(m0, m1, NT)
        acc[2] += dot(m1, m1, NT)
    for i, ref in enumerate((e_ref, f_ref)):
        source = m.at[:, :, i * ahead : (i + 1) * ahead]
        saves.append(pltpu.make_async_copy(source, ref, save.at[share // tile + i]))
        saves[-1].start()
    part = rows // (GROUP * CORES)
    for s in range(GROUP):
        to = me ^ s
        for b in range(3):
            here = pl.ds(b * part, part)
            keep_ref[s, here, :] = acc[b, pl.ds(pl.multiple_of((to * CORES + core) * part, part), part), :]
            give_ref[s, here, :] = acc[b, pl.ds(pl.multiple_of((to * CORES + 1 - core) * part, part), part), :]
    for copy in saves:
        copy.wait()


def first(place, diagonals, crosses, x, pieces, ahead, tile=512):
    rows, share = pieces[0].shape
    pairs = GROUP // 2
    out = shape(GROUP, 3 * rows // (GROUP * CORES), rows)
    return pl.pallas_call(
        functools.partial(first_kernel, tile),
        out_shape=tuple(shape(pairs, rows, n, dtype=BF16) for n in (share, ahead, ahead)) + (out, out),
        in_specs=[SMEM] + [VMEM] * (4 * GROUP) + [ANY] * 4,
        out_specs=(ANY, ANY, ANY, VMEM, VMEM),
        scratch_shapes=[
            pltpu.VMEM((pairs, rows, rows), F32),
            pltpu.VMEM((GROUP, rows, rows), F32),
            pltpu.VMEM((pairs, rows, rows), F32),
            pltpu.VMEM((pairs, rows, 2 * rows), BF16),
            pltpu.VMEM((GROUP, rows, share), BF16),
            pltpu.VMEM((pairs, rows, share), BF16),
            pltpu.VMEM((3, rows, rows), F32),
            pltpu.SemaphoreType.DMA((GROUP,)),
            pltpu.SemaphoreType.DMA((share // tile + 2,)),
        ],
        cost_estimate=cost(2 * pairs * rows**3 * 40 + 14 * rows * rows * share, 12 * rows * share),
        name="first",
    )(place, *diagonals, *crosses, x, *pieces)


def second_kernel(*refs):
    place, bundles, m_ref, refs = refs[0], refs[1:9], refs[9], refs[10:]
    a_ref, b_ref, e_ref, w_ref, gram, inverse, m, load = refs
    me, core = place[0], place[1]
    rows = m.shape[1]
    copy = pltpu.make_async_copy(m_ref, m, load)
    copy.start()
    part = rows // (GROUP * CORES)
    for c in range(CORES):
        for s in range(GROUP):
            seat = (me ^ s) * CORES + (core ^ c)
            for b in range(3):
                gram[b, pl.ds(pl.multiple_of(seat * part, part), part), :] = bundles[c * GROUP + s][b * part : (b + 1) * part]
    resolvent([(gram[0], gram[1], gram[2])], inverse, w_ref)
    copy.wait()
    start = 0
    for ref in (e_ref, a_ref, b_ref):
        here = slice(start, start + ref.shape[1])
        ref[...] = merge_rows(m[0, :, here], m[1, :, here], w_ref[0])
        start += ref.shape[1]


def second(place, bundles, m, ahead):
    _, rows, share = m.shape
    early, half = 2 * ahead, share // 2 - ahead
    return pl.pallas_call(
        second_kernel,
        out_shape=tuple(shape(rows, n, dtype=BF16) for n in (half, half, early)) + (shape(1, rows, 2 * rows, dtype=BF16),),
        in_specs=[SMEM] + [VMEM] * (2 * GROUP) + [ANY],
        out_specs=(VMEM,) * 4,
        scratch_shapes=[
            pltpu.VMEM((3, rows, rows), F32),
            pltpu.VMEM((1, rows, rows), F32),
            pltpu.VMEM(m.shape, BF16),
            pltpu.SemaphoreType.DMA,
        ],
        cost_estimate=cost(2 * rows**3 * 40 + 4 * rows * rows * share, 6 * rows * share),
        name="second",
    )(place, *bundles, m)


def late_kernel(share, place, w, a, b, e, *refs):
    early, (out, buffer, save) = refs[:-3], refs[-3:]
    me, ahead, half = place[0], e.shape[1] // 2, a.shape[1]
    saves = []

    def put(source, owner, column):
        target = out.at[:, pl.ds(pl.multiple_of(owner * share + column, 128), source.shape[1])]
        saves.append(pltpu.make_async_copy(source, target, save.at[len(saves)]))
        saves[-1].start()

    put(e, me, 0)
    put(a, me, 2 * ahead)
    put(b, me, 2 * ahead + half)
    for i, pair in enumerate(early):
        buffer[i] = merge_rows(pair[0], pair[1], w[0])
        put(buffer.at[i], me ^ (i % (GROUP - 1) + 1), i // (GROUP - 1) * ahead)
    for copy in saves:
        copy.wait()


def late(place, w, a, b, e, early, share):
    rows, ahead = e.shape[0], e.shape[1] // 2
    return pl.pallas_call(
        functools.partial(late_kernel, share),
        out_shape=shape(rows, GROUP * share, dtype=BF16),
        in_specs=[SMEM] + [VMEM] * (4 + len(early)),
        out_specs=ANY,
        scratch_shapes=[pltpu.VMEM((len(early), rows, ahead), BF16), pltpu.SemaphoreType.DMA((len(early) + 3,))],
        cost_estimate=cost(4 * rows * rows * ahead * len(early), 6 * rows * ahead * len(early)),
        name="late",
    )(place, w, a, b, e, *early)


def put_kernel(spots, share, place, *refs):
    blocks, out, save = refs[: len(spots)], refs[-2], refs[-1]
    saves = []
    for i, ((s, column), block) in enumerate(zip(spots, blocks)):
        start = pl.multiple_of((place[0] ^ s) * share + column, 128)
        saves.append(pltpu.make_async_copy(block, out.at[:, pl.ds(start, block.shape[1])], save.at[i]))
        saves[-1].start()
    for copy in saves:
        copy.wait()


def put(place, out, blocks, spots, share):
    size = sum(b.size for b in blocks)
    return pl.pallas_call(
        functools.partial(put_kernel, spots, share),
        out_shape=shape(*out.shape, dtype=out.dtype),
        in_specs=[SMEM] + [VMEM] * len(blocks) + [ANY],
        out_specs=ANY,
        scratch_shapes=[pltpu.SemaphoreType.DMA((len(blocks),))],
        input_output_aliases={1 + len(blocks): 0},
        cost_estimate=cost(0, 4 * size),
        name="put",
    )(place, *blocks, out)


PEERS = tuple(range(1, GROUP))


def over_chips(block):
    chips = lax.axis_size("feat") // CORES
    return total([block] + [send(block, "feat", CORES * s) for s in range(1, chips)])


def gather_group(bundle):
    mine = [bundle] + send_all([bundle] * len(PEERS), "dp", PEERS)
    return mine + [send(b, "feat", 1) for b in mine]


def run(sketches):
    x = sketches[0]
    rows, columns = x.shape
    share = columns // GROUP
    ahead = share // 8
    me = lax.axis_index("dp") % GROUP
    place = jnp.stack([me, lax.axis_index("feat") % CORES]).astype(jnp.int32)

    pieces, source = {}, x
    for s in (1, 3, 2):
        piece = lax.dynamic_slice(source, (0, (me ^ s) * share), (rows, share))
        source, piece = lax.optimization_barrier((source, piece))
        pieces[s] = send(piece, "dp", s)
    keep, give = own_gram(place, x)
    own = over_chips(total([keep, send(give, "feat", 1)]))
    near = near_gram(place, x, pieces[1])
    p2, p3, own, near = lax.optimization_barrier((pieces[2], pieces[3], own, near))

    keep, give = far_gram(place, near, p2, p3)
    parts = fold(keep, send(give, "feat", 1))
    parts, own = lax.optimization_barrier((parts, own))
    mine = total([parts[0]] + send_all(parts[1:], "dp", PEERS))
    diagonals = gather_group(own)
    crosses = gather_group(over_chips(mine))
    m, e, f, keep, give = first(place, diagonals, crosses, x, [pieces[1], p2, p3], ahead)

    parts = fold(keep, send(give, "feat", 1))
    parts, e = lax.optimization_barrier((parts, e))
    mine = total([parts[0]] + send_all(parts[1:], "dp", PEERS))
    early = send_all([e] * len(PEERS), "dp", PEERS)
    bundle = over_chips(mine)
    bundle, f = lax.optimization_barrier((bundle, f))
    bundles = gather_group(bundle)
    early += send_all([f] * len(PEERS), "dp", PEERS)
    a, b, e, w = second(place, bundles, m, ahead)

    ax, by = send(a, "dp", 1), send(b, "dp", 2)
    bx, ay = send(b, "dp", 1), send(a, "dp", 2)
    ad, bd = send(ax, "dp", 2), send(by, "dp", 1)
    left, right = 2 * ahead, ahead + share // 2
    out = late(place, w, a, b, e, early, share)
    out = put(place, out, [ax, by], ((1, left), (2, right)), share)
    out = put(place, out, [bx, ay], ((1, right), (2, left)), share)
    out = put(place, out, [ad, bd], ((3, left), (3, right)), share)
    return out[None]


def solution(mesh):
    spec = P("dp", None, "feat")
    return jax.shard_map(run, mesh=mesh, in_specs=(spec,), out_specs=spec, check_vma=False)
```

profile of v0, /device:TPU:0, one launch (start us, length us, event | category | flops | bytes accessed | tf_op | source)
XLA Modules:
  0.0 203.6 jit_solution(15009551329618605448)
XLA Ops:
  1.3 3.0 %collective-permute-start.6 = (bf16[256,2048]{1,0:T(8,128)(2,1)S(1)}, bf16[256,2048]{1,0:T(8,128)(2,1)}, u32[]{:S(2)}, u32[]{:S(2)}) collective-permute-start(bf16[256,2048]{1,0:T(8,128)(2,1)S(1)} %dynamic-slice_bitcast_fusion), channel_id=1, source_target_pairs={{0,8},{8,0},{16,24},{24,16},{1,9},{9,1},{17,25},{25,17},{2,10},{10... | collective-permute-start | bytes 3145736 | tf_op jit(solution)/shard_map/ppermute | solution.py:24
  4.3 2.3 %constant_dynamic-slice_fusion.1 = bf16[256,2048]{1,0:T(8,128)(2,1)} fusion(bf16[256,8192]{1,0:T(8,128)(2,1)} %bitcast.22, s32[]{:T(128)S(6)} %select_n.23), kind=kLoop, calls=%fused_computation.23 | loop fusion | bytes 2097156 | tf_op jit(solution)/shard_map/dynamic_slice | solution.py:435
  6.6 2.3 %constant_dynamic-slice_fusion = bf16[256,2048]{1,0:T(8,128)(2,1)} fusion(bf16[256,8192]{1,0:T(8,128)(2,1)} %bitcast.23, s32[]{:T(128)S(6)} %select_n.24), kind=kLoop, calls=%fused_computation.22 | loop fusion | bytes 2097156 | tf_op jit(solution)/shard_map/dynamic_slice | solution.py:435
  11.1 5.4 %own_gram.1 = (f32[128,256]{1,0:T(8,128)}, f32[128,256]{1,0:T(8,128)}) custom-call(s32[2]{0:T(128)} %pad_add_fusion.place.refs_0_, bf16[256,8192]{1,0:T(8,128)(2,1)} %bitcast.24), custom_call_target="tpu_custom_call" | custom-call | flops 1073741824 | bytes 4194304 | tf_op jit(solution)/shard_map/own_gram/pallas_call | solution.py:131
  19.0 2.1 %collective-permute-start.3 = (f32[128,256]{1,0:T(8,128)S(1)}, f32[128,256]{1,0:T(8,128)S(1)}, u32[]{:S(2)}, u32[]{:S(2)}) collective-permute-start(f32[128,256]{1,0:T(8,128)S(1)} %add.117), channel_id=1, source_target_pairs={{0,2},{1,3},{2,0},{3,1},{4,6},{5,7},{6,4},{7,5},{8,10},{9,11},{10,... | collective-permute-start | bytes 393224 | tf_op jit(solution)/shard_map/ppermute | solution.py:24
  21.1 2.6 %collective-permute-start.4 = (f32[128,256]{1,0:T(8,128)S(1)}, f32[128,256]{1,0:T(8,128)S(1)}, u32[]{:S(2)}, u32[]{:S(2)}) collective-permute-start(f32[128,256]{1,0:T(8,128)S(1)} %add.117), channel_id=1, source_target_pairs={{0,4},{1,5},{2,6},{3,7},{4,0},{5,1},{6,2},{7,3},{8,12},{9,13},{10,... | collective-permute-start | bytes 393224 | tf_op jit(solution)/shard_map/ppermute | solution.py:24
  23.7 3.4 %collective-permute-done.3 = f32[128,256]{1,0:T(8,128)S(1)} collective-permute-done((f32[128,256]{1,0:T(8,128)S(1)}, f32[128,256]{1,0:T(8,128)S(1)}, u32[]{:S(2)}, u32[]{:S(2)}) %collective-permute-start.3) | collective-permute-done | bytes 131104 | tf_op jit(solution)/shard_map/ppermute | solution.py:24
  27.1 3.2 %collective-permute-start.5 = (f32[128,256]{1,0:T(8,128)S(1)}, f32[128,256]{1,0:T(8,128)S(1)}, u32[]{:S(2)}, u32[]{:S(2)}) collective-permute-start(f32[128,256]{1,0:T(8,128)S(1)} %add.117), channel_id=1, source_target_pairs={{0,6},{1,7},{2,4},{3,5},{4,2},{5,3},{6,0},{7,1},{8,14},{9,15},{10,... | collective-permute-start | bytes 393224 | tf_op jit(solution)/shard_map/ppermute | solution.py:24
  30.2 3.6 %collective-permute-done.5 = f32[128,256]{1,0:T(8,128)S(1)} collective-permute-done((f32[128,256]{1,0:T(8,128)S(1)}, f32[128,256]{1,0:T(8,128)S(1)}, u32[]{:S(2)}, u32[]{:S(2)}) %collective-permute-start.5) | collective-permute-done | bytes 131104 | tf_op jit(solution)/shard_map/ppermute | solution.py:24
  33.9 3.4 %near_gram.1.near = f32[256,256]{1,0:T(8,128)} custom-call(s32[2]{0:T(128)} %pad_add_fusion.place.refs_0_, bf16[256,8192]{1,0:T(8,128)(2,1)} %bitcast.25, bf16[256,2048]{1,0:T(8,128)(2,1)} %collective-permute-done.6.p1.refs_18_), custom_call_target="tpu_custom_call" | custom-call | flops 268435456 | bytes 2097152 | tf_op jit(solution)/shard_map/near_gram/pallas_call | solution.py:161
  37.4 18.9 %collective-permute-done.p2.refs_19_ = bf16[256,2048]{1,0:T(8,128)(2,1)S(1)} collective-permute-done((bf16[256,2048]{1,0:T(8,128)(2,1)}, bf16[256,2048]{1,0:T(8,128)(2,1)S(1)}, u32[]{:S(2)}, u32[]{:S(2)}) %collective-permute-start) | collective-permute-done | bytes 1048608 | tf_op jit(solution)/shard_map/ppermute | solution.py:24
  58.2 3.7 %far_gram.1 = (f32[4,64,256]{2,1,0:T(8,128)}, f32[4,64,256]{2,1,0:T(8,128)}) custom-call(s32[2]{0:T(128)} %pad_add_fusion.place.refs_0_, f32[256,256]{1,0:T(8,128)} %near_gram.1.near, bf16[256,2048]{1,0:T(8,128)(2,1)} %copy-done, bf16[256,2048]{1,0:T(8,128)(2,1)} %copy-done.1), custom_call_target="tpu_custom_call" | custom-call | flops 268435456 | bytes 2097152 | tf_op jit(solution)/shard_map/far_gram/pallas_call | solution.py:208
  61.9 1.7 collective-permute-done.7
  65.0 1.7 collective-permute-start.16
  69.2 2.6 %collective-permute-done.17 = f32[64,256]{1,0:T(8,128)S(1)} collective-permute-done((f32[64,256]{1,0:T(8,128)S(1)}, f32[64,256]{1,0:T(8,128)S(1)}, u32[]{:S(2)}, u32[]{:S(2)}) %collective-permute-start.17) | collective-permute-done | bytes 65568 | tf_op jit(solution)/shard_map/ppermute | solution.py:24
  73.6 2.6 %collective-permute-start.19 = (f32[64,256]{1,0:T(8,128)S(1)}, f32[64,256]{1,0:T(8,128)S(1)}, u32[]{:S(2)}, u32[]{:S(2)}) collective-permute-start(f32[64,256]{1,0:T(8,128)S(1)} %add_add_fusion.4), channel_id=1, source_target_pairs={{0,4},{1,5},{2,6},{3,7},{4,0},{5,1},{6,2},{7,3},{8,12},{9,13},{10,... | collective-permute-start | bytes 196616 | tf_op jit(solution)/shard_map/ppermute | solution.py:24
  80.1 2.1 %collective-permute-done.20 = f32[64,256]{1,0:T(8,128)S(1)} collective-permute-done((f32[64,256]{1,0:T(8,128)S(1)}, f32[64,256]{1,0:T(8,128)S(1)}, u32[]{:S(2)}, u32[]{:S(2)}) %collective-permute-start.20) | collective-permute-done | bytes 65568 | tf_op jit(solution)/shard_map/ppermute | solution.py:24
  88.1 3.7 %collective-permute-done.23.refs_12_ = f32[64,256]{1,0:T(8,128)S(1)} collective-permute-done((f32[64,256]{1,0:T(8,128)S(1)}, f32[64,256]{1,0:T(8,128)S(1)}, u32[]{:S(2)}, u32[]{:S(2)}) %collective-permute-start.23) | collective-permute-done | bytes 65568 | tf_op jit(solution)/shard_map/ppermute | solution.py:24
  94.4 11.4 %first.1 = (bf16[2,256,2048]{2,1,0:T(8,128)(2,1)}, bf16[2,256,256]{2,1,0:T(8,128)(2,1)}, bf16[2,256,256]{2,1,0:T(8,128)(2,1)}, f32[4,96,256]{2,1,0:T(8,128)}, f32[4,96,256]{2,1,0:T(8,128)}) custom-call(s32[2]{0:T(128)} %pad_add_fusion.place.refs_0_, f32[128,256]{1,0:T(8,128)} %copy-done.12, f32[128,256]{1,0:T(8,128)} %copy-done.16, f32[128,256]{1,0:T(8,128)} %copy-done.17, ...), custom_call_target="tpu_custom_call" | custom-call | flops 4563402752 | bytes 6291456 | tf_op jit(solution)/shard_map/first/pallas_call | solution.py:292
  114.0 3.3 %collective-permute-done.30 = f32[96,256]{1,0:T(8,128)S(1)} collective-permute-done((f32[96,256]{1,0:T(8,128)S(1)}, f32[96,256]{1,0:T(8,128)S(1)}, u32[]{:S(2)}, u32[]{:S(2)}) %collective-permute-start.30) | collective-permute-done | bytes 98336 | tf_op jit(solution)/shard_map/ppermute | solution.py:24
  117.5 2.9 %collective-permute-start.33 = (f32[96,256]{1,0:T(8,128)S(1)}, f32[96,256]{1,0:T(8,128)S(1)}, u32[]{:S(2)}, u32[]{:S(2)}) collective-permute-start(f32[96,256]{1,0:T(8,128)S(1)} %add_add_fusion.2), channel_id=1, source_target_pairs={{0,4},{1,5},{2,6},{3,7},{4,0},{5,1},{6,2},{7,3},{8,12},{9,13},{10,... | collective-permute-start | bytes 294920 | tf_op jit(solution)/shard_map/ppermute | solution.py:24
  122.7 5.1 %collective-permute-done.33 = f32[96,256]{1,0:T(8,128)S(1)} collective-permute-done((f32[96,256]{1,0:T(8,128)S(1)}, f32[96,256]{1,0:T(8,128)S(1)}, u32[]{:S(2)}, u32[]{:S(2)}) %collective-permute-start.33) | collective-permute-done | bytes 98336 | tf_op jit(solution)/shard_map/ppermute | solution.py:24
  133.0 2.2 %collective-permute-done.37.refs_4_ = f32[96,256]{1,0:T(8,128)S(1)} collective-permute-done((f32[96,256]{1,0:T(8,128)S(1)}, f32[96,256]{1,0:T(8,128)S(1)}, u32[]{:S(2)}, u32[]{:S(2)}) %collective-permute-start.37) | collective-permute-done | bytes 98336 | tf_op jit(solution)/shard_map/ppermute | solution.py:24
  138.2 7.6 %second.1 = (bf16[256,768]{1,0:T(8,128)(2,1)}, bf16[256,768]{1,0:T(8,128)(2,1)}, bf16[256,512]{1,0:T(8,128)(2,1)}, bf16[1,256,512]{2,1,0:T(8,128)(2,1)}) custom-call(s32[2]{0:T(128)} %pad_add_fusion.place.refs_0_, f32[96,256]{1,0:T(8,128)} %copy-done.13, f32[96,256]{1,0:T(8,128)} %copy-done.23, f32[96,256]{1,0:T(8,128)} %copy-done.24, f32[96,256]{1,0:T(8,128)} %copy-done.25, ...), custom_call_target="tpu_custom_call" | custom-call | flops 1879048192 | bytes 3145728 | tf_op jit(solution)/shard_map/second/pallas_call | solution.py:338
  151.2 12.6 %collective-permute-done.50.refs_2_ = bf16[2,256,256]{2,1,0:T(8,128)(2,1)S(1)} collective-permute-done((bf16[2,256,256]{2,1,0:T(8,128)(2,1)S(1)}, bf16[2,256,256]{2,1,0:T(8,128)(2,1)S(1)}, u32[]{:S(2)}, u32[]{:S(2)}) %collective-permute-start.50) | collective-permute-done | bytes 262176 | tf_op jit(solution)/shard_map/ppermute | solution.py:24
  165.0 4.3 %collective-permute-done.51.refs_3_ = bf16[2,256,256]{2,1,0:T(8,128)(2,1)S(1)} collective-permute-done((bf16[2,256,256]{2,1,0:T(8,128)(2,1)}, bf16[2,256,256]{2,1,0:T(8,128)(2,1)S(1)}, u32[]{:S(2)}, u32[]{:S(2)}) %collective-permute-start.51) | collective-permute-done | bytes 262176 | tf_op jit(solution)/shard_map/ppermute | solution.py:24
  171.8 1.7 collective-permute-start.53
  173.5 17.6 %collective-permute-done.53.refs_5_ = bf16[2,256,256]{2,1,0:T(8,128)(2,1)} collective-permute-done((bf16[2,256,256]{2,1,0:T(8,128)(2,1)}, bf16[2,256,256]{2,1,0:T(8,128)(2,1)}, u32[]{:S(2)}, u32[]{:S(2)}) %collective-permute-start.53) | collective-permute-done | bytes 262176 | tf_op jit(solution)/shard_map/ppermute | solution.py:24
  191.1 3.1 %late.1.refs_2_ = bf16[256,8192]{1,0:T(8,128)(2,1)} custom-call(s32[2]{0:T(128)} %pad_add_fusion.place.refs_0_, bf16[1,256,512]{2,1,0:T(8,128)(2,1)} %get-tuple-element.69.w, bf16[256,768]{1,0:T(8,128)(2,1)} %get-tuple-element.67.a, bf16[256,768]{1,0:T(8,128)(2,1)} %get-tuple-element.68.b, bf16[256,512]{1,0:T(8,128)(2,1)} %get-tuple-element.70.e, ...), custom_call_target="tpu_custom_call" | custom-call | flops 402653184 | bytes 2359296 | tf_op jit(solution)/shard_map/late/pallas_call | solution.py:376
  194.3 2.0 put.3.refs_2_
  197.8 2.0 put.4.refs_2_
  201.4 2.0 put.5
  (171 shorter events, 56.7 us)
Async XLA Ops:
  1.3 32.6 %collective-permute-start.6 = (bf16[256,2048]{1,0:T(8,128)(2,1)S(1)}, bf16[256,2048]{1,0:T(8,128)(2,1)}, u32[]{:S(2)}, u32[]{:S(2)}) collective-permute-start(bf16[256,2048]{1,0:T(8,128)(2,1)S(1)} %dynamic-slice_bitcast_fusion), channel_id=1, source_target_pairs={{0,8},{8,0},{16,24},{24,16},{1,9},{9,1},{17,25},{25,17},{2,10},{10... | collective-permute-start | bytes 3145736 | tf_op jit(solution)/shard_map/ppermute | solution.py:24
  8.9 47.3 %collective-permute-start = (bf16[256,2048]{1,0:T(8,128)(2,1)}, bf16[256,2048]{1,0:T(8,128)(2,1)S(1)}, u32[]{:S(2)}, u32[]{:S(2)}) collective-permute-start(bf16[256,2048]{1,0:T(8,128)(2,1)} %constant_dynamic-slice_fusion), channel_id=1, source_target_pairs={{0,16},{8,24},{16,0},{24,8},{1,17},{9,25},{17,1},{25,9},{2,18},{10... | collective-permute-start | bytes 3145736 | tf_op jit(solution)/shard_map/ppermute | solution.py:24
  10.5 45.8 %collective-permute-start.1 = (bf16[256,2048]{1,0:T(8,128)(2,1)}, bf16[256,2048]{1,0:T(8,128)(2,1)S(1)}, u32[]{:S(2)}, u32[]{:S(2)}) collective-permute-start(bf16[256,2048]{1,0:T(8,128)(2,1)} %constant_dynamic-slice_fusion.1), channel_id=1, source_target_pairs={{0,24},{8,16},{16,8},{24,0},{1,25},{9,17},{17,9},{25,1},{2,26},{10... | collective-permute-start | bytes 3145736 | tf_op jit(solution)/shard_map/ppermute | solution.py:24
  19.0 8.1 %collective-permute-start.3 = (f32[128,256]{1,0:T(8,128)S(1)}, f32[128,256]{1,0:T(8,128)S(1)}, u32[]{:S(2)}, u32[]{:S(2)}) collective-permute-start(f32[128,256]{1,0:T(8,128)S(1)} %add.117), channel_id=1, source_target_pairs={{0,2},{1,3},{2,0},{3,1},{4,6},{5,7},{6,4},{7,5},{8,10},{9,11},{10,... | collective-permute-start | bytes 393224 | tf_op jit(solution)/shard_map/ppermute | solution.py:24
  21.1 9.2 %collective-permute-start.4 = (f32[128,256]{1,0:T(8,128)S(1)}, f32[128,256]{1,0:T(8,128)S(1)}, u32[]{:S(2)}, u32[]{:S(2)}) collective-permute-start(f32[128,256]{1,0:T(8,128)S(1)} %add.117), channel_id=1, source_target_pairs={{0,4},{1,5},{2,6},{3,7},{4,0},{5,1},{6,2},{7,3},{8,12},{9,13},{10,... | collective-permute-start | bytes 393224 | tf_op jit(solution)/shard_map/ppermute | solution.py:24
  27.1 6.8 %collective-permute-start.5 = (f32[128,256]{1,0:T(8,128)S(1)}, f32[128,256]{1,0:T(8,128)S(1)}, u32[]{:S(2)}, u32[]{:S(2)}) collective-permute-start(f32[128,256]{1,0:T(8,128)S(1)} %add.117), channel_id=1, source_target_pairs={{0,6},{1,7},{2,4},{3,5},{4,2},{5,3},{6,0},{7,1},{8,14},{9,15},{10,... | collective-permute-start | bytes 393224 | tf_op jit(solution)/shard_map/ppermute | solution.py:24
  71.9 6.5 %collective-permute-start.18 = (f32[64,256]{1,0:T(8,128)S(1)}, f32[64,256]{1,0:T(8,128)S(1)}, u32[]{:S(2)}, u32[]{:S(2)}) collective-permute-start(f32[64,256]{1,0:T(8,128)S(1)} %add_add_fusion.4), channel_id=1, source_target_pairs={{0,2},{1,3},{2,0},{3,1},{4,6},{5,7},{6,4},{7,5},{8,10},{9,11},{10,... | collective-permute-start | bytes 196616 | tf_op jit(solution)/shard_map/ppermute | solution.py:24
  73.6 6.6 %collective-permute-start.19 = (f32[64,256]{1,0:T(8,128)S(1)}, f32[64,256]{1,0:T(8,128)S(1)}, u32[]{:S(2)}, u32[]{:S(2)}) collective-permute-start(f32[64,256]{1,0:T(8,128)S(1)} %add_add_fusion.4), channel_id=1, source_target_pairs={{0,4},{1,5},{2,6},{3,7},{4,0},{5,1},{6,2},{7,3},{8,12},{9,13},{10,... | collective-permute-start | bytes 196616 | tf_op jit(solution)/shard_map/ppermute | solution.py:24
  76.1 6.1 %collective-permute-start.20 = (f32[64,256]{1,0:T(8,128)S(1)}, f32[64,256]{1,0:T(8,128)S(1)}, u32[]{:S(2)}, u32[]{:S(2)}) collective-permute-start(f32[64,256]{1,0:T(8,128)S(1)} %add_add_fusion.4), channel_id=1, source_target_pairs={{0,6},{1,7},{2,4},{3,5},{4,2},{5,3},{6,0},{7,1},{8,14},{9,15},{10,... | collective-permute-start | bytes 196616 | tf_op jit(solution)/shard_map/ppermute | solution.py:24
  76.4 7.4 %collective-permute-start.8 = (f32[128,256]{1,0:T(8,128)S(1)}, f32[128,256]{1,0:T(8,128)S(1)}, u32[]{:S(2)}, u32[]{:S(2)}) collective-permute-start(f32[128,256]{1,0:T(8,128)S(1)} %add_add_fusion.refs_1_), channel_id=1, source_target_pairs={{0,8},{8,0},{16,24},{24,16},{1,9},{9,1},{17,25},{25,17},{2,10},{10... | collective-permute-start | bytes 393224 | tf_op jit(solution)/shard_map/ppermute | solution.py:24
  77.8 6.5 %collective-permute-start.9 = (f32[128,256]{1,0:T(8,128)S(1)}, f32[128,256]{1,0:T(8,128)S(1)}, u32[]{:S(2)}, u32[]{:S(2)}) collective-permute-start(f32[128,256]{1,0:T(8,128)S(1)} %add_add_fusion.refs_1_), channel_id=1, source_target_pairs={{0,16},{8,24},{16,0},{24,8},{1,17},{9,25},{17,1},{25,9},{2,18},{10... | collective-permute-start | bytes 393224 | tf_op jit(solution)/shard_map/ppermute | solution.py:24
  78.4 6.7 %collective-permute-start.10 = (f32[128,256]{1,0:T(8,128)S(1)}, f32[128,256]{1,0:T(8,128)S(1)}, u32[]{:S(2)}, u32[]{:S(2)}) collective-permute-start(f32[128,256]{1,0:T(8,128)S(1)} %add_add_fusion.refs_1_), channel_id=1, source_target_pairs={{0,24},{8,16},{16,8},{24,0},{1,25},{9,17},{17,9},{25,1},{2,26},{10... | collective-permute-start | bytes 393224 | tf_op jit(solution)/shard_map/ppermute | solution.py:24
  84.3 7.9 %collective-permute-start.12 = (f32[128,256]{1,0:T(8,128)S(1)}, f32[128,256]{1,0:T(8,128)S(1)}, u32[]{:S(2)}, u32[]{:S(2)}) collective-permute-start(f32[128,256]{1,0:T(8,128)S(1)} %collective-permute-done.8.refs_2_), channel_id=1, source_target_pairs={{0,1},{1,0},{2,3},{3,2},{4,5},{5,4},{6,7},{7,6},{8,9},{9,8},{10,11... | collective-permute-start | bytes 393224 | tf_op jit(solution)/shard_map/ppermute | solution.py:24
  85.0 7.3 %collective-permute-start.13 = (f32[128,256]{1,0:T(8,128)S(1)}, f32[128,256]{1,0:T(8,128)S(1)}, u32[]{:S(2)}, u32[]{:S(2)}) collective-permute-start(f32[128,256]{1,0:T(8,128)S(1)} %collective-permute-done.9.refs_3_), channel_id=1, source_target_pairs={{0,1},{1,0},{2,3},{3,2},{4,5},{5,4},{6,7},{7,6},{8,9},{9,8},{10,11... | collective-permute-start | bytes 393224 | tf_op jit(solution)/shard_map/ppermute | solution.py:24
  85.0 7.3 %collective-permute-start.14 = (f32[128,256]{1,0:T(8,128)S(1)}, f32[128,256]{1,0:T(8,128)S(1)}, u32[]{:S(2)}, u32[]{:S(2)}) collective-permute-start(f32[128,256]{1,0:T(8,128)S(1)} %collective-permute-done.10.refs_4_), channel_id=1, source_target_pairs={{0,1},{1,0},{2,3},{3,2},{4,5},{5,4},{6,7},{7,6},{8,9},{9,8},{10,11... | collective-permute-start | bytes 393224 | tf_op jit(solution)/shard_map/ppermute | solution.py:24
  110.5 6.9 %collective-permute-start.30 = (f32[96,256]{1,0:T(8,128)S(1)}, f32[96,256]{1,0:T(8,128)S(1)}, u32[]{:S(2)}, u32[]{:S(2)}) collective-permute-start(f32[96,256]{1,0:T(8,128)S(1)} %get-tuple-element.62), channel_id=1, source_target_pairs={{0,16},{8,24},{16,0},{24,8},{1,17},{9,25},{17,1},{25,9},{2,18},{10... | collective-permute-start | bytes 294920 | tf_op jit(solution)/shard_map/ppermute | solution.py:24
  111.0 6.4 %collective-permute-start.31 = (f32[96,256]{1,0:T(8,128)S(1)}, f32[96,256]{1,0:T(8,128)S(1)}, u32[]{:S(2)}, u32[]{:S(2)}) collective-permute-start(f32[96,256]{1,0:T(8,128)S(1)} %get-tuple-element.63), channel_id=1, source_target_pairs={{0,24},{8,16},{16,8},{24,0},{1,25},{9,17},{17,9},{25,1},{2,26},{10... | collective-permute-start | bytes 294920 | tf_op jit(solution)/shard_map/ppermute | solution.py:24
  117.5 10.3 %collective-permute-start.33 = (f32[96,256]{1,0:T(8,128)S(1)}, f32[96,256]{1,0:T(8,128)S(1)}, u32[]{:S(2)}, u32[]{:S(2)}) collective-permute-start(f32[96,256]{1,0:T(8,128)S(1)} %add_add_fusion.2), channel_id=1, source_target_pairs={{0,4},{1,5},{2,6},{3,7},{4,0},{5,1},{6,2},{7,3},{8,12},{9,13},{10,... | collective-permute-start | bytes 294920 | tf_op jit(solution)/shard_map/ppermute | solution.py:24
  120.4 7.4 %collective-permute-start.34 = (f32[96,256]{1,0:T(8,128)S(1)}, f32[96,256]{1,0:T(8,128)S(1)}, u32[]{:S(2)}, u32[]{:S(2)}) collective-permute-start(f32[96,256]{1,0:T(8,128)S(1)} %add_add_fusion.2), channel_id=1, source_target_pairs={{0,6},{1,7},{2,4},{3,5},{4,2},{5,3},{6,0},{7,1},{8,14},{9,15},{10,... | collective-permute-start | bytes 294920 | tf_op jit(solution)/shard_map/ppermute | solution.py:24
  129.8 5.5 %collective-permute-start.37 = (f32[96,256]{1,0:T(8,128)S(1)}, f32[96,256]{1,0:T(8,128)S(1)}, u32[]{:S(2)}, u32[]{:S(2)}) collective-permute-start(f32[96,256]{1,0:T(8,128)S(1)} %add_add_fusion.1.refs_1_), channel_id=1, source_target_pairs={{0,24},{8,16},{16,8},{24,0},{1,25},{9,17},{17,9},{25,1},{2,26},{10... | collective-permute-start | bytes 294920 | tf_op jit(solution)/shard_map/ppermute | solution.py:24
  135.3 14.1 %collective-permute-start.48 = (bf16[2,256,256]{2,1,0:T(8,128)(2,1)}, bf16[2,256,256]{2,1,0:T(8,128)(2,1)S(1)}, u32[]{:S(2)}, u32[]{:S(2)}) collective-permute-start(bf16[2,256,256]{2,1,0:T(8,128)(2,1)} %get-tuple-element.71), channel_id=1, source_target_pairs={{0,8},{8,0},{16,24},{24,16},{1,9},{9,1},{17,25},{25,17},{2,10},{10... | collective-permute-start | bytes 786440 | tf_op jit(solution)/shard_map/ppermute | solution.py:24
  136.1 13.6 %collective-permute-start.49 = (bf16[2,256,256]{2,1,0:T(8,128)(2,1)}, bf16[2,256,256]{2,1,0:T(8,128)(2,1)S(1)}, u32[]{:S(2)}, u32[]{:S(2)}) collective-permute-start(bf16[2,256,256]{2,1,0:T(8,128)(2,1)} %get-tuple-element.71), channel_id=1, source_target_pairs={{0,16},{8,24},{16,0},{24,8},{1,17},{9,25},{17,1},{25,9},{2,18},{10... | collective-permute-start | bytes 786440 | tf_op jit(solution)/shard_map/ppermute | solution.py:24
  145.8 24.2 %collective-permute-start.42 = (bf16[256,768]{1,0:T(8,128)(2,1)}, bf16[256,768]{1,0:T(8,128)(2,1)S(1)}, u32[]{:S(2)}, u32[]{:S(2)}) collective-permute-start(bf16[256,768]{1,0:T(8,128)(2,1)} %get-tuple-element.67.a), channel_id=1, source_target_pairs={{0,8},{8,0},{16,24},{24,16},{1,9},{9,1},{17,25},{25,17},{2,10},{10... | collective-permute-start | bytes 1179656 | tf_op jit(solution)/shard_map/ppermute | solution.py:24
  146.2 25.1 %collective-permute-start.44 = (bf16[256,768]{1,0:T(8,128)(2,1)}, bf16[256,768]{1,0:T(8,128)(2,1)S(1)}, u32[]{:S(2)}, u32[]{:S(2)}) collective-permute-start(bf16[256,768]{1,0:T(8,128)(2,1)} %get-tuple-element.68.b), channel_id=1, source_target_pairs={{0,16},{8,24},{16,0},{24,8},{1,17},{9,25},{17,1},{25,9},{2,18},{10... | collective-permute-start | bytes 1179656 | tf_op jit(solution)/shard_map/ppermute | solution.py:24
  147.7 16.1 %collective-permute-start.50 = (bf16[2,256,256]{2,1,0:T(8,128)(2,1)S(1)}, bf16[2,256,256]{2,1,0:T(8,128)(2,1)S(1)}, u32[]{:S(2)}, u32[]{:S(2)}) collective-permute-start(bf16[2,256,256]{2,1,0:T(8,128)(2,1)S(1)} %copy-done.15), channel_id=1, source_target_pairs={{0,24},{8,16},{16,8},{24,0},{1,25},{9,17},{17,9},{25,1},{2,26},{10... | collective-permute-start | bytes 786440 | tf_op jit(solution)/shard_map/ppermute | solution.py:24
  149.4 20.0 %collective-permute-start.51 = (bf16[2,256,256]{2,1,0:T(8,128)(2,1)}, bf16[2,256,256]{2,1,0:T(8,128)(2,1)S(1)}, u32[]{:S(2)}, u32[]{:S(2)}) collective-permute-start(bf16[2,256,256]{2,1,0:T(8,128)(2,1)} %get-tuple-element.72), channel_id=1, source_target_pairs={{0,8},{8,0},{16,24},{24,16},{1,9},{9,1},{17,25},{25,17},{2,10},{10... | collective-permute-start | bytes 786440 | tf_op jit(solution)/shard_map/ppermute | solution.py:24
  149.7 22.0 %collective-permute-start.52 = (bf16[2,256,256]{2,1,0:T(8,128)(2,1)}, bf16[2,256,256]{2,1,0:T(8,128)(2,1)}, u32[]{:S(2)}, u32[]{:S(2)}) collective-permute-start(bf16[2,256,256]{2,1,0:T(8,128)(2,1)} %get-tuple-element.72), channel_id=1, source_target_pairs={{0,16},{8,24},{16,0},{24,8},{1,17},{9,25},{17,1},{25,9},{2,18},{10... | collective-permute-start | bytes 786440 | tf_op jit(solution)/shard_map/ppermute | solution.py:24
  163.8 32.5 %collective-permute-start.46 = (bf16[256,768]{1,0:T(8,128)(2,1)}, bf16[256,768]{1,0:T(8,128)(2,1)S(1)}, u32[]{:S(2)}, u32[]{:S(2)}) collective-permute-start(bf16[256,768]{1,0:T(8,128)(2,1)} %get-tuple-element.68.b), channel_id=1, source_target_pairs={{0,8},{8,0},{16,24},{24,16},{1,9},{9,1},{17,25},{25,17},{2,10},{10... | collective-permute-start | bytes 1179656 | tf_op jit(solution)/shard_map/ppermute | solution.py:24
  169.3 27.0 %collective-permute-start.47 = (bf16[256,768]{1,0:T(8,128)(2,1)}, bf16[256,768]{1,0:T(8,128)(2,1)S(1)}, u32[]{:S(2)}, u32[]{:S(2)}) collective-permute-start(bf16[256,768]{1,0:T(8,128)(2,1)} %get-tuple-element.67.a), channel_id=1, source_target_pairs={{0,16},{8,24},{16,0},{24,8},{1,17},{9,25},{17,1},{25,9},{2,18},{10... | collective-permute-start | bytes 1179656 | tf_op jit(solution)/shard_map/ppermute | solution.py:24
  170.0 29.8 %collective-permute-start.43 = (bf16[256,768]{1,0:T(8,128)(2,1)S(1)}, bf16[256,768]{1,0:T(8,128)(2,1)S(1)}, u32[]{:S(2)}, u32[]{:S(2)}) collective-permute-start(bf16[256,768]{1,0:T(8,128)(2,1)S(1)} %collective-permute-done.42.refs_0_), channel_id=1, source_target_pairs={{0,16},{8,24},{16,0},{24,8},{1,17},{9,25},{17,1},{25,9},{2,18},{10... | collective-permute-start | bytes 1179656 | tf_op jit(solution)/shard_map/ppermute | solution.py:24
  171.4 28.5 %collective-permute-start.45 = (bf16[256,768]{1,0:T(8,128)(2,1)S(1)}, bf16[256,768]{1,0:T(8,128)(2,1)S(1)}, u32[]{:S(2)}, u32[]{:S(2)}) collective-permute-start(bf16[256,768]{1,0:T(8,128)(2,1)S(1)} %collective-permute-done.44.refs_1_), channel_id=1, source_target_pairs={{0,8},{8,0},{16,24},{24,16},{1,9},{9,1},{17,25},{25,17},{2,10},{10... | collective-permute-start | bytes 1179656 | tf_op jit(solution)/shard_map/ppermute | solution.py:24
  171.8 19.3 %collective-permute-start.53 = (bf16[2,256,256]{2,1,0:T(8,128)(2,1)}, bf16[2,256,256]{2,1,0:T(8,128)(2,1)}, u32[]{:S(2)}, u32[]{:S(2)}) collective-permute-start(bf16[2,256,256]{2,1,0:T(8,128)(2,1)} %get-tuple-element.72), channel_id=1, source_target_pairs={{0,24},{8,16},{16,8},{24,0},{1,25},{9,17},{17,9},{25,1},{2,26},{10... | collective-permute-start | bytes 786440 | tf_op jit(solution)/shard_map/ppermute | solution.py:24
  (59 other events, 445.2 us)
where the time goes:
time: 204 us
  waiting for transfers between devices  92.5 us (45%)
  starting transfers between devices  53.6 us (26%)
  Pallas kernels  40.7 us (20%)
  local copies, waits for them, and re-layouts  12.4 us (6%)
  other arithmetic  3.74 us (2%)
    ppermute x54, waiting for transfers between devices, send(): return lax.ppermute(block, axis, [(i, i ^ shift) for i in range(count)])  92.5 us
    ppermute x54, starting transfers between devices, send(): return lax.ppermute(block, axis, [(i, i ^ shift) for i in range(count)])  53.6 us
    pallas_call x1, Pallas kernels, first(): pl.pallas_call(functools.partial(first_kernel, tile), out_shape=tuple((sh...  11.4 us
    pallas_call x1, Pallas kernels, second(): pl.pallas_call(second_kernel, out_shape=tuple((shape(rows, n, dtype=BF16)...  7.57 us
    unnamed x74, local copies, waits for them, and re-layouts  6.51 us
    pallas_call x3, Pallas kernels, put(): pl.pallas_call(functools.partial(put_kernel, spots, share), out_shape=sha...  6.06 us
    dynamic_slice x3, local copies, waits for them, and re-layouts, run(): piece = lax.dynamic_slice(source, (0, (me ^ s) * share), (rows, share))  5.9 us
    pallas_call x1, Pallas kernels, own_gram(): pl.pallas_call(own_gram_kernel, out_shape=(half, half), grid_spec=pltpu.P...  5.4 us
  transfers between devices with their start and end apart: 54, of which 27 were waited for; matrix products, arithmetic and copies ran while one was open for 3% of the time, Pallas kernels for 12%

commit v1 on v0

--- a/solution.py
+++ b/solution.py
@@ -17,6 +17,7 @@
 VMEM = pl.BlockSpec(memory_space=pltpu.VMEM)
 SMEM = pl.BlockSpec(memory_space=pltpu.SMEM)
 ANY = pl.BlockSpec(memory_space=pl.ANY)
+HBM = pl.BlockSpec(memory_space=pltpu.HBM)
 
 
 def send(block, axis, shift):
@@ -34,6 +35,9 @@
 
 def shape(*dims, dtype=F32):
     return jax.ShapeDtypeStruct(dims, dtype)
+
+
+WHOLE = pltpu.CompilerParams(vmem_limit_bytes=67_043_328)
 
 
 def cost(flops, nbytes):
@@ -78,7 +82,7 @@
             xs = halves(x)
             rest = eye - product(part, xs)
             worst = jnp.maximum(worst, jnp.sum(rest * rest))
-            x_ref[j] = x + product(xs, halves(rest))
+            x_ref[j] = x + dot(xs[0], rest.astype(BF16))
         return count + 1, worst
 
     lax.while_loop(lambda s: (s[0] < 24) & (s[1] > 1e-6), step, (jnp.int32(0), jnp.float32(1.0)))
@@ -143,79 +147,79 @@
     )(place, x)
 
 
-def near_gram_kernel(place, own, p1, out_ref, block):
-    step = pl.program_id(0)
-    for s, piece in enumerate((own, p1)):
-        block[(place[0] ^ s) % 2] = piece[...]
-
-    @pl.when(step == 0)
-    def _():
-        out_ref[...] = jnp.zeros_like(out_ref)
-
-    out_ref[...] += dot(block[0], block[1], NT)
-
-
-def near_gram(place, x, p1, tile=1024):
+def pair_gram(me, sources, block, load, chunk):
+    rows, share = block.shape[1:]
+    copies = []
+    for k in range(share // chunk):
+        here = slice(k * chunk, (k + 1) * chunk)
+        for i, (s, source) in enumerate(sources):
+            target = block.at[(me ^ s) % 2, :, here]
+            copies.append(pltpu.make_async_copy(source(k * chunk, chunk), target, load.at[2 * k + i]))
+            copies[-1].start()
+    value = jnp.zeros((rows, rows), F32)
+    for k in range(share // chunk):
+        copies[2 * k].wait()
+        copies[2 * k + 1].wait()
+        here = slice(k * chunk, (k + 1) * chunk)
+        value = value + dot(block[0, :, here], block[1, :, here], NT)
+    return value
+
+
+def near_gram_kernel(chunk, place, x, p1, out_ref, block, load):
+    me = place[0]
+    share = p1.shape[1]
+
+    def mine(column, size):
+        return x.at[:, pl.ds(pl.multiple_of(me * share + column, 128), size)]
+
+    def theirs(column, size):
+        return p1.at[:, column : column + size]
+
+    out_ref[...] = pair_gram(me, ((0, mine), (1, theirs)), block, load, chunk)
+
+
+def near_gram(place, x, p1, chunk=512):
     rows, share = p1.shape
-    steps = share // tile
-    return pl.pallas_call(
-        near_gram_kernel,
+    return pl.pallas_call(
+        functools.partial(near_gram_kernel, chunk),
         out_shape=shape(rows, rows),
-        grid_spec=pltpu.PrefetchScalarGridSpec(
-            num_scalar_prefetch=1,
-            grid=(steps,),
-            in_specs=[
-                pl.BlockSpec((rows, tile), lambda k, place: (0, place[0] * steps + k)),
-                pl.BlockSpec((rows, tile), lambda k, place: (0, k)),
-            ],
-            out_specs=pl.BlockSpec((rows, rows), lambda k, place: (0, 0)),
-            scratch_shapes=[pltpu.VMEM((2, rows, tile), BF16)],
-        ),
+        in_specs=[SMEM, HBM, HBM],
+        out_specs=VMEM,
+        scratch_shapes=[pltpu.VMEM((2, rows, share), BF16), pltpu.SemaphoreType.DMA((2 * share // chunk,))],
         cost_estimate=cost(2 * rows * rows * share, 4 * rows * share),
+        compiler_params=WHOLE,
         name="near_gram",
     )(place, x, p1)
 
 
-def far_gram_kernel(place, near, p2, p3, keep_ref, give_ref, block, acc):
-    step = pl.program_id(0)
+def far_gram_kernel(chunk, place, near, p2, p3, keep_ref, give_ref, block, acc, load):
     me, core = place[0], place[1]
-    for s, piece in ((2, p2), (3, p3)):
-        block[(me ^ s) % 2] = piece[...]
-
-    @pl.when(step == 0)
-    def _():
-        acc[me // 2] = near[...]
-        acc[1 - me // 2] = jnp.zeros_like(near)
-
-    acc[1 - me // 2] += dot(block[0], block[1], NT)
-
-    @pl.when(step == pl.num_programs(0) - 1)
-    def _():
-        part = keep_ref.shape[1]
-        for s in range(GROUP):
-            to = me ^ s
-            pair, start = to // 2, (to % 2) * (CORES * part)
-            keep_ref[s] = acc[pair, pl.ds(pl.multiple_of(start + core * part, part), part), :]
-            give_ref[s] = acc[pair, pl.ds(pl.multiple_of(start + (1 - core) * part, part), part), :]
-
-
-def far_gram(place, near, p2, p3, tile=1024):
+    sources = tuple((s, lambda column, size, p=p: p.at[:, column : column + size]) for s, p in ((2, p2), (3, p3)))
+    acc[me // 2] = near[...]
+    acc[1 - me // 2] = pair_gram(me, sources, block, load, chunk)
+    part = keep_ref.shape[1]
+    for s in range(GROUP):
+        to = me ^ s
+        pair, start = to // 2, (to % 2) * (CORES * part)
+        keep_ref[s] = acc[pair, pl.ds(pl.multiple_of(start + core * part, part), part), :]
+        give_ref[s] = acc[pair, pl.ds(pl.multiple_of(start + (1 - core) * part, part), part), :]
+
+
+def far_gram(place, near, p2, p3, chunk=512):
     rows, share = p2.shape
-    part = rows // (2 * CORES)
-    out = shape(GROUP, part, rows)
-    spec = pl.BlockSpec(out.shape, lambda k, place: (0, 0, 0))
-    piece = pl.BlockSpec((rows, tile), lambda k, place: (0, k))
-    return pl.pallas_call(
-        far_gram_kernel,
+    out = shape(GROUP, rows // (2 * CORES), rows)
+    return pl.pallas_call(
+        functools.partial(far_gram_kernel, chunk),
         out_shape=(out, out),
-        grid_spec=pltpu.PrefetchScalarGridSpec(
-            num_scalar_prefetch=1,
-            grid=(share // tile,),
-            in_specs=[pl.BlockSpec((rows, rows), lambda k, place: (0, 0)), piece, piece],
-            out_specs=(spec, spec),
-            scratch_shapes=[pltpu.VMEM((2, rows, tile), BF16), pltpu.VMEM((GROUP // 2, rows, rows), F32)],
-        ),
+        in_specs=[SMEM, VMEM, HBM, HBM],
+        out_specs=(VMEM, VMEM),
+        scratch_shapes=[
+            pltpu.VMEM((2, rows, share), BF16),
+            pltpu.VMEM((GROUP // 2, rows, rows), F32),
+            pltpu.SemaphoreType.DMA((2 * share // chunk,)),
+        ],
         cost_estimate=cost(2 * rows * rows * share, 4 * rows * share),
+        compiler_params=WHOLE,
         name="far_gram",
     )(place, near, p2, p3)
 
@@ -228,20 +232,22 @@
     return functools.reduce(jnp.add, arrays)
 
 
-def merge_rows(lower, upper, w):
-    rows = lower.shape[0]
-    update = dot(w[:, :rows], lower) + dot(w[:, rows:], upper)
-    return (lower.astype(F32) - update).astype(BF16)
+def merge_rows(stacked, w):
+    lower = stacked[: w.shape[0]]
+    return (lower.astype(F32) - dot(w, stacked)).astype(BF16)
 
 
 def first_kernel(tile, *refs):
     place, tails, crosses, (x, p1, p2, p3), refs = refs[0], refs[1:9], refs[9:17], refs[17:21], refs[21:]
     m_ref, e_ref, f_ref, keep_ref, give_ref, cross, diag, inverse, w, block, m, acc, load, save = refs
-    ahead = e_ref.shape[2]
+    ahead = e_ref.shape[1]
     me, core = place[0], place[1]
     rows, share = p1.shape
-    loads = [pltpu.make_async_copy(x.at[:, pl.ds(pl.multiple_of(me * share, share), share)], block.at[me], load.at[0])]
-    loads += [pltpu.make_async_copy(p, block.at[me ^ s], load.at[s]) for s, p in ((1, p1), (2, p2), (3, p3))]
+    sources = [x.at[:, pl.ds(pl.multiple_of(me * share, share), share)], p1, p2, p3]
+    loads = [
+        pltpu.make_async_copy(source, block.at[pl.ds(pl.multiple_of((me ^ s) * rows, rows), rows)], load.at[s])
+        for s, source in enumerate(sources)
+    ]
     for copy in loads:
         copy.start()
 
@@ -261,17 +267,17 @@
     saves = []
     for k in range(share // tile):
         here = slice(k * tile, (k + 1) * tile)
-        m0 = merge_rows(block[0, :, here], block[1, :, here], w[0])
-        m1 = merge_rows(block[2, :, here], block[3, :, here], w[1])
-        m[0, :, here] = m0
-        m[1, :, here] = m1
-        saves.append(pltpu.make_async_copy(m.at[:, :, here], m_ref.at[:, :, here], save.at[k]))
+        m0 = merge_rows(block[: 2 * rows, here], w[0])
+        m1 = merge_rows(block[2 * rows :, here], w[1])
+        m[:rows, here] = m0
+        m[rows:, here] = m1
+        saves.append(pltpu.make_async_copy(m.at[:, here], m_ref.at[:, here], save.at[k]))
         saves[-1].start()
         acc[0] += dot(m0, m0, NT)
         acc[1] += dot(m0, m1, NT)
         acc[2] += dot(m1, m1, NT)
     for i, ref in enumerate((e_ref, f_ref)):
-        source = m.at[:, :, i * ahead : (i + 1) * ahead]
+        source = m.at[:, i * ahead : (i + 1) * ahead]
         saves.append(pltpu.make_async_copy(source, ref, save.at[share // tile + i]))
         saves[-1].start()
     part = rows // (GROUP * CORES)
@@ -291,16 +297,16 @@
     out = shape(GROUP, 3 * rows // (GROUP * CORES), rows)
     return pl.pallas_call(
         functools.partial(first_kernel, tile),
-        out_shape=tuple(shape(pairs, rows, n, dtype=BF16) for n in (share, ahead, ahead)) + (out, out),
-        in_specs=[SMEM] + [VMEM] * (4 * GROUP) + [ANY] * 4,
+        out_shape=tuple(shape(pairs * rows, n, dtype=BF16) for n in (share, ahead, ahead)) + (out, out),
+        in_specs=[SMEM] + [VMEM] * (4 * GROUP) + [HBM] * 4,
         out_specs=(ANY, ANY, ANY, VMEM, VMEM),
         scratch_shapes=[
             pltpu.VMEM((pairs, rows, rows), F32),
             pltpu.VMEM((GROUP, rows, rows), F32),
             pltpu.VMEM((pairs, rows, rows), F32),
             pltpu.VMEM((pairs, rows, 2 * rows), BF16),
-            pltpu.VMEM((GROUP, rows, share), BF16),
-            pltpu.VMEM((pairs, rows, share), BF16),
+            pltpu.VMEM((GROUP * rows, share), BF16),
+            pltpu.VMEM((pairs * rows, share), BF16),
             pltpu.VMEM((3, rows, rows), F32),
             pltpu.SemaphoreType.DMA((GROUP,)),
             pltpu.SemaphoreType.DMA((share // tile + 2,)),
@@ -314,7 +320,7 @@
     place, bundles, m_ref, refs = refs[0], refs[1:9], refs[9], refs[10:]
     a_ref, b_ref, e_ref, w_ref, gram, inverse, m, load = refs
     me, core = place[0], place[1]
-    rows = m.shape[1]
+    rows = m.shape[0] // 2
     copy = pltpu.make_async_copy(m_ref, m, load)
     copy.start()
     part = rows // (GROUP * CORES)
@@ -328,12 +334,12 @@
     start = 0
     for ref in (e_ref, a_ref, b_ref):
         here = slice(start, start + ref.shape[1])
-        ref[...] = merge_rows(m[0, :, here], m[1, :, here], w_ref[0])
+        ref[...] = merge_rows(m[:, here], w_ref[0])
         start += ref.shape[1]
 
 
 def second(place, bundles, m, ahead):
-    _, rows, share = m.shape
+    rows, share = m.shape[0] // 2, m.shape[1]
     early, half = 2 * ahead, share // 2 - ahead
     return pl.pallas_call(
         second_kernel,
@@ -365,7 +371,7 @@
     put(a, me, 2 * ahead)
     put(b, me, 2 * ahead + half)
     for i, pair in enumerate(early):
-        buffer[i] = merge_rows(pair[0], pair[1], w[0])
+        buffer[i] = merge_rows(pair[...], w[0])
         put(buffer.at[i], me ^ (i % (GROUP - 1) + 1), i // (GROUP - 1) * ahead)
     for copy in saves:
         copy.wait()
@@ -377,7 +383,7 @@
         functools.partial(late_kernel, share),
         out_shape=shape(rows, GROUP * share, dtype=BF16),
         in_specs=[SMEM] + [VMEM] * (4 + len(early)),
-        out_specs=ANY,
+        out_specs=HBM,
         scratch_shapes=[pltpu.VMEM((len(early), rows, ahead), BF16), pltpu.SemaphoreType.DMA((len(early) + 3,))],
         cost_estimate=cost(4 * rows * rows * ahead * len(early), 6 * rows * ahead * len(early)),
         name="late",
@@ -385,12 +391,17 @@
 
 
 def put_kernel(spots, share, place, *refs):
-    blocks, out, save = refs[: len(spots)], refs[-2], refs[-1]
-    saves = []
-    for i, ((s, column), block) in enumerate(zip(spots, blocks)):
+    count = len(spots)
+    blocks, out, buffers, load, save = refs[:count], refs[count + 1], refs[count + 2 : -2], refs[-2], refs[-1]
+    loads, saves = [], []
+    for i, ((s, column), block, buffer) in enumerate(zip(spots, blocks, buffers)):
         start = pl.multiple_of((place[0] ^ s) * share + column, 128)
-        saves.append(pltpu.make_async_copy(block, out.at[:, pl.ds(start, block.shape[1])], save.at[i]))
-        saves[-1].start()
+        loads.append(pltpu.make_async_copy(block, buffer, load.at[i]))
+        loads[-1].start()
+        saves.append(pltpu.make_async_copy(buffer, out.at[:, pl.ds(start, block.shape[1])], save.at[i]))
+    for load_copy, save_copy in zip(loads, saves):
+        load_copy.wait()
+        save_copy.start()
     for copy in saves:
         copy.wait()
 
@@ -400,11 +411,12 @@
     return pl.pallas_call(
         functools.partial(put_kernel, spots, share),
         out_shape=shape(*out.shape, dtype=out.dtype),
-        in_specs=[SMEM] + [VMEM] * len(blocks) + [ANY],
-        out_specs=ANY,
-        scratch_shapes=[pltpu.SemaphoreType.DMA((len(blocks),))],
+        in_specs=[SMEM] + [HBM] * (len(blocks) + 1),
+        out_specs=HBM,
+        scratch_shapes=[pltpu.VMEM(b.shape, b.dtype) for b in blocks] + [pltpu.SemaphoreType.DMA((len(blocks),))] * 2,
         input_output_aliases={1 + len(blocks): 0},
         cost_estimate=cost(0, 4 * size),
+        compiler_params=WHOLE,
         name="put",
     )(place, *blocks, out)
 
@@ -431,7 +443,7 @@
     place = jnp.stack([me, lax.axis_index("feat") % CORES]).astype(jnp.int32)
 
     pieces, source = {}, x
-    for s in (1, 3, 2):
+    for s in PEERS:
         piece = lax.dynamic_slice(source, (0, (me ^ s) * share), (rows, share))
         source, piece = lax.optimization_barrier((source, piece))
         pieces[s] = send(piece, "dp", s)

time: 204 us -> 202 us (level)
  local copies, waits for them, and re-layouts: 12.4 us -> 8.12 us
    unnamed x74 -> x62, local copies, waits for them, and re-layouts: 6.51 us -> 2.19 us
  transfers between devices with their start and end apart: 54 -> 54, of which waited for: 27 -> 29; matrix products, arithmetic and copies ran while one was open for 3% -> 3% of each run, Pallas kernels for 12% -> 12%
where the time goes in v1:
time: 202 us; the launch traced here: 201 us
  waiting for transfers between devices  92.2 us (46%)
  starting transfers between devices  54.2 us (27%)
  Pallas kernels  42.1 us (21%)
  local copies, waits for them, and re-layouts  8.12 us (4%)
  other arithmetic  4.39 us (2%)
    ppermute x54, waiting for transfers between devices, send(): return lax.ppermute(block, axis, [(i, i ^ shift) for i in range(count)])  92.2 us
    ppermute x54, starting transfers between devices, send(): return lax.ppermute(block, axis, [(i, i ^ shift) for i in range(count)])  54.2 us
    pallas_call x1, Pallas kernels, first(): pl.pallas_call(functools.partial(first_kernel, tile), out_shape=tuple((sh...  11.6 us
    pallas_call x3, Pallas kernels, put(): pl.pallas_call(functools.partial(put_kernel, spots, share), out_shape=sha...  7.71 us
    pallas_call x1, Pallas kernels, second(): pl.pallas_call(second_kernel, out_shape=tuple((shape(rows, n, dtype=BF16)...  6.63 us
    dynamic_slice x3, local copies, waits for them, and re-layouts, run(): piece = lax.dynamic_slice(source, (0, (me ^ s) * share), (rows, share))  5.93 us
    pallas_call x1, Pallas kernels, own_gram(): pl.pallas_call(own_gram_kernel, out_shape=(half, half), grid_spec=pltpu.P...  5.4 us
    pallas_call x1, Pallas kernels, far_gram(): pl.pallas_call(functools.partial(far_gram_kernel, chunk), out_shape=(out,...  4.04 us
  transfers between devices with their start and end apart: 54, of which 29 were waited for; matrix products, arithmetic and copies ran while one was open for 3% of the time, Pallas kernels for 12%

profile of v1, /device:TPU:0, one launch (start us, length us, event | category | flops | bytes accessed | tf_op | source)
XLA Modules:
  0.0 201.5 jit_solution(11921644851087577137)
XLA Ops:
  1.3 3.0 %collective-permute-start.6 = (bf16[256,2048]{1,0:T(8,128)(2,1)S(1)}, bf16[256,2048]{1,0:T(8,128)(2,1)}, u32[]{:S(2)}, u32[]{:S(2)}) collective-permute-start(bf16[256,2048]{1,0:T(8,128)(2,1)S(1)} %dynamic-slice_bitcast_fusion), channel_id=1, source_target_pairs={{0,8},{8,0},{16,24},{24,16},{1,9},{9,1},{17,25},{25,17},{2,10},{10... | collective-permute-start | bytes 3145736 | tf_op jit(solution)/shard_map/ppermute | solution.py:25
  4.3 2.3 %constant_dynamic-slice_fusion.1 = bf16[256,2048]{1,0:T(8,128)(2,1)} fusion(bf16[256,8192]{1,0:T(8,128)(2,1)} %bitcast.22, s32[]{:T(128)S(6)} %select_n.23), kind=kLoop, calls=%fused_computation.23 | loop fusion | bytes 2097156 | tf_op jit(solution)/shard_map/dynamic_slice | solution.py:447
  6.6 2.3 %constant_dynamic-slice_fusion = bf16[256,2048]{1,0:T(8,128)(2,1)} fusion(bf16[256,8192]{1,0:T(8,128)(2,1)} %bitcast.23, s32[]{:T(128)S(6)} %select_n.24), kind=kLoop, calls=%fused_computation.22 | loop fusion | bytes 2097156 | tf_op jit(solution)/shard_map/dynamic_slice | solution.py:447
  11.1 5.4 %own_gram.1 = (f32[128,256]{1,0:T(8,128)}, f32[128,256]{1,0:T(8,128)}) custom-call(s32[2]{0:T(128)} %pad_add_fusion.place.refs_0_, bf16[256,8192]{1,0:T(8,128)(2,1)} %bitcast.24), custom_call_target="tpu_custom_call" | custom-call | flops 1073741824 | bytes 4194304 | tf_op jit(solution)/shard_map/own_gram/pallas_call | solution.py:135
  19.0 2.1 %collective-permute-start.3 = (f32[128,256]{1,0:T(8,128)S(1)}, f32[128,256]{1,0:T(8,128)S(1)}, u32[]{:S(2)}, u32[]{:S(2)}) collective-permute-start(f32[128,256]{1,0:T(8,128)S(1)} %add.117), channel_id=1, source_target_pairs={{0,2},{1,3},{2,0},{3,1},{4,6},{5,7},{6,4},{7,5},{8,10},{9,11},{10,... | collective-permute-start | bytes 393224 | tf_op jit(solution)/shard_map/ppermute | solution.py:25
  21.1 2.6 %collective-permute-start.4 = (f32[128,256]{1,0:T(8,128)S(1)}, f32[128,256]{1,0:T(8,128)S(1)}, u32[]{:S(2)}, u32[]{:S(2)}) collective-permute-start(f32[128,256]{1,0:T(8,128)S(1)} %add.117), channel_id=1, source_target_pairs={{0,4},{1,5},{2,6},{3,7},{4,0},{5,1},{6,2},{7,3},{8,12},{9,13},{10,... | collective-permute-start | bytes 393224 | tf_op jit(solution)/shard_map/ppermute | solution.py:25
  23.7 3.4 %collective-permute-done.3 = f32[128,256]{1,0:T(8,128)S(1)} collective-permute-done((f32[128,256]{1,0:T(8,128)S(1)}, f32[128,256]{1,0:T(8,128)S(1)}, u32[]{:S(2)}, u32[]{:S(2)}) %collective-permute-start.3) | collective-permute-done | bytes 131104 | tf_op jit(solution)/shard_map/ppermute | solution.py:25
  27.1 3.2 %collective-permute-start.5 = (f32[128,256]{1,0:T(8,128)S(1)}, f32[128,256]{1,0:T(8,128)S(1)}, u32[]{:S(2)}, u32[]{:S(2)}) collective-permute-start(f32[128,256]{1,0:T(8,128)S(1)} %add.117), channel_id=1, source_target_pairs={{0,6},{1,7},{2,4},{3,5},{4,2},{5,3},{6,0},{7,1},{8,14},{9,15},{10,... | collective-permute-start | bytes 393224 | tf_op jit(solution)/shard_map/ppermute | solution.py:25
  30.3 3.6 %collective-permute-done.5 = f32[128,256]{1,0:T(8,128)S(1)} collective-permute-done((f32[128,256]{1,0:T(8,128)S(1)}, f32[128,256]{1,0:T(8,128)S(1)}, u32[]{:S(2)}, u32[]{:S(2)}) %collective-permute-start.5) | collective-permute-done | bytes 131104 | tf_op jit(solution)/shard_map/ppermute | solution.py:25
  34.6 3.6 %near_gram.1.near = f32[256,256]{1,0:T(8,128)} custom-call(s32[2]{0:T(128)} %pad_add_fusion.place.refs_0_, bf16[256,8192]{1,0:T(8,128)(2,1)} %bitcast.25, bf16[256,2048]{1,0:T(8,128)(2,1)} %collective-permute-done.6.p1.refs_18_), custom_call_target="tpu_custom_call" | custom-call | flops 268435456 | bytes 2097152 | tf_op jit(solution)/shard_map/near_gram/pallas_call | solution.py:183
  38.2 13.2 %collective-permute-done.1.p3.refs_20_ = bf16[256,2048]{1,0:T(8,128)(2,1)} collective-permute-done((bf16[256,2048]{1,0:T(8,128)(2,1)}, bf16[256,2048]{1,0:T(8,128)(2,1)}, u32[]{:S(2)}, u32[]{:S(2)}) %collective-permute-start.1) | collective-permute-done | bytes 1048608 | tf_op jit(solution)/shard_map/ppermute | solution.py:25
  51.4 6.2 %collective-permute-done.p2.refs_19_ = bf16[256,2048]{1,0:T(8,128)(2,1)} collective-permute-done((bf16[256,2048]{1,0:T(8,128)(2,1)}, bf16[256,2048]{1,0:T(8,128)(2,1)}, u32[]{:S(2)}, u32[]{:S(2)}) %collective-permute-start) | collective-permute-done | bytes 1048608 | tf_op jit(solution)/shard_map/ppermute | solution.py:25
  57.6 4.0 %far_gram.1 = (f32[4,64,256]{2,1,0:T(8,128)}, f32[4,64,256]{2,1,0:T(8,128)}) custom-call(s32[2]{0:T(128)} %pad_add_fusion.place.refs_0_, f32[256,256]{1,0:T(8,128)} %near_gram.1.near, bf16[256,2048]{1,0:T(8,128)(2,1)} %collective-permute-done.p2.refs_19_, bf16[256,2048]{1,0:T(8,128)(2,1)} %collective-permute-done.1.p3.refs_20_), custom_call_target="tpu_custom_call" | custom-call | flops 268435456 | bytes 2097152 | tf_op jit(solution)/shard_map/far_gram/pallas_call | solution.py:211
  61.7 1.7 collective-permute-done.7
  68.8 2.2 %collective-permute-done.16 = f32[64,256]{1,0:T(8,128)S(1)} collective-permute-done((f32[64,256]{1,0:T(8,128)S(1)}, f32[64,256]{1,0:T(8,128)S(1)}, u32[]{:S(2)}, u32[]{:S(2)}) %collective-permute-start.16) | collective-permute-done | bytes 65568 | tf_op jit(solution)/shard_map/ppermute | solution.py:25
  73.3 2.6 %collective-permute-start.19 = (f32[64,256]{1,0:T(8,128)S(1)}, f32[64,256]{1,0:T(8,128)S(1)}, u32[]{:S(2)}, u32[]{:S(2)}) collective-permute-start(f32[64,256]{1,0:T(8,128)S(1)} %add_add_fusion.4), channel_id=1, source_target_pairs={{0,4},{1,5},{2,6},{3,7},{4,0},{5,1},{6,2},{7,3},{8,12},{9,13},{10,... | collective-permute-start | bytes 196616 | tf_op jit(solution)/shard_map/ppermute | solution.py:25
  79.9 2.1 %collective-permute-done.20 = f32[64,256]{1,0:T(8,128)S(1)} collective-permute-done((f32[64,256]{1,0:T(8,128)S(1)}, f32[64,256]{1,0:T(8,128)S(1)}, u32[]{:S(2)}, u32[]{:S(2)}) %collective-permute-start.20) | collective-permute-done | bytes 65568 | tf_op jit(solution)/shard_map/ppermute | solution.py:25
  87.8 3.7 %collective-permute-done.23.refs_12_ = f32[64,256]{1,0:T(8,128)S(1)} collective-permute-done((f32[64,256]{1,0:T(8,128)S(1)}, f32[64,256]{1,0:T(8,128)S(1)}, u32[]{:S(2)}, u32[]{:S(2)}) %collective-permute-start.23) | collective-permute-done | bytes 65568 | tf_op jit(solution)/shard_map/ppermute | solution.py:25
  94.2 11.6 %first.1 = (bf16[512,2048]{1,0:T(8,128)(2,1)}, bf16[512,256]{1,0:T(8,128)(2,1)}, bf16[512,256]{1,0:T(8,128)(2,1)}, f32[4,96,256]{2,1,0:T(8,128)}, f32[4,96,256]{2,1,0:T(8,128)}) custom-call(s32[2]{0:T(128)} %pad_add_fusion.place.refs_0_, f32[128,256]{1,0:T(8,128)} %add_add_fusion.refs_1_, f32[128,256]{1,0:T(8,128)} %copy-done.10, f32[128,256]{1,0:T(8,128)} %copy-done.11, ...), custom_call_target="tpu_custom_call" | custom-call | flops 4563402752 | bytes 6291456 | tf_op jit(solution)/shard_map/first/pallas_call | solution.py:298
  112.4 2.0 %collective-permute-done.29 = f32[96,256]{1,0:T(8,128)S(1)} collective-permute-done((f32[96,256]{1,0:T(8,128)S(1)}, f32[96,256]{1,0:T(8,128)S(1)}, u32[]{:S(2)}, u32[]{:S(2)}) %collective-permute-start.29) | collective-permute-done | bytes 98336 | tf_op jit(solution)/shard_map/ppermute | solution.py:25
  117.3 3.5 %collective-permute-start.33 = (f32[96,256]{1,0:T(8,128)S(1)}, f32[96,256]{1,0:T(8,128)S(1)}, u32[]{:S(2)}, u32[]{:S(2)}) collective-permute-start(f32[96,256]{1,0:T(8,128)S(1)} %add_add_fusion.2), channel_id=1, source_target_pairs={{0,4},{1,5},{2,6},{3,7},{4,0},{5,1},{6,2},{7,3},{8,12},{9,13},{10,... | collective-permute-start | bytes 294920 | tf_op jit(solution)/shard_map/ppermute | solution.py:25
  122.4 5.2 %collective-permute-done.33 = f32[96,256]{1,0:T(8,128)S(1)} collective-permute-done((f32[96,256]{1,0:T(8,128)S(1)}, f32[96,256]{1,0:T(8,128)S(1)}, u32[]{:S(2)}, u32[]{:S(2)}) %collective-permute-start.33) | collective-permute-done | bytes 98336 | tf_op jit(solution)/shard_map/ppermute | solution.py:25
  133.3 2.3 %collective-permute-done.37.refs_4_ = f32[96,256]{1,0:T(8,128)S(1)} collective-permute-done((f32[96,256]{1,0:T(8,128)S(1)}, f32[96,256]{1,0:T(8,128)S(1)}, u32[]{:S(2)}, u32[]{:S(2)}) %collective-permute-start.37) | collective-permute-done | bytes 98336 | tf_op jit(solution)/shard_map/ppermute | solution.py:25
  138.0 6.6 %second.1 = (bf16[256,768]{1,0:T(8,128)(2,1)}, bf16[256,768]{1,0:T(8,128)(2,1)}, bf16[256,512]{1,0:T(8,128)(2,1)}, bf16[1,256,512]{2,1,0:T(8,128)(2,1)}) custom-call(s32[2]{0:T(128)} %pad_add_fusion.place.refs_0_, f32[96,256]{1,0:T(8,128)} %copy-done.6, f32[96,256]{1,0:T(8,128)} %copy-done.17, f32[96,256]{1,0:T(8,128)} %copy-done.18, f32[96,256]{1,0:T(8,128)} %copy-done.19, ...), custom_call_target="tpu_custom_call" | custom-call | flops 1879048192 | bytes 3145728 | tf_op jit(solution)/shard_map/second/pallas_call | solution.py:344
  150.6 11.9 %collective-permute-done.50.refs_2_ = bf16[512,256]{1,0:T(8,128)(2,1)S(1)} collective-permute-done((bf16[512,256]{1,0:T(8,128)(2,1)S(1)}, bf16[512,256]{1,0:T(8,128)(2,1)S(1)}, u32[]{:S(2)}, u32[]{:S(2)}) %collective-permute-start.50) | collective-permute-done | bytes 262176 | tf_op jit(solution)/shard_map/ppermute | solution.py:25
  162.6 1.8 collective-permute-start.46
  164.4 3.8 %collective-permute-done.51.refs_3_ = bf16[512,256]{1,0:T(8,128)(2,1)S(1)} collective-permute-done((bf16[512,256]{1,0:T(8,128)(2,1)S(1)}, bf16[512,256]{1,0:T(8,128)(2,1)S(1)}, u32[]{:S(2)}, u32[]{:S(2)}) %collective-permute-start.51) | collective-permute-done | bytes 262176 | tf_op jit(solution)/shard_map/ppermute | solution.py:25
  172.2 17.6 %collective-permute-done.53.refs_5_ = bf16[512,256]{1,0:T(8,128)(2,1)S(1)} collective-permute-done((bf16[512,256]{1,0:T(8,128)(2,1)S(1)}, bf16[512,256]{1,0:T(8,128)(2,1)S(1)}, u32[]{:S(2)}, u32[]{:S(2)}) %collective-permute-start.53) | collective-permute-done | bytes 262176 | tf_op jit(solution)/shard_map/ppermute | solution.py:25
  190.6 3.1 %late.1.refs_2_ = bf16[256,8192]{1,0:T(8,128)(2,1)} custom-call(s32[2]{0:T(128)} %pad_add_fusion.place.refs_0_, bf16[1,256,512]{2,1,0:T(8,128)(2,1)} %get-tuple-element.69.w, bf16[256,768]{1,0:T(8,128)(2,1)} %get-tuple-element.67.a, bf16[256,768]{1,0:T(8,128)(2,1)} %get-tuple-element.68.b, bf16[256,512]{1,0:T(8,128)(2,1)} %get-tuple-element.70.e, ...), custom_call_target="tpu_custom_call" | custom-call | flops 402653184 | bytes 2359296 | tf_op jit(solution)/shard_map/late/pallas_call | solution.py:382
  193.7 2.6 %put.3.refs_2_ = bf16[256,8192]{1,0:T(8,128)(2,1)} custom-call(s32[2]{0:T(128)} %pad_add_fusion.place.refs_0_, bf16[256,768]{1,0:T(8,128)(2,1)} %collective-permute-done.42.refs_0_, bf16[256,768]{1,0:T(8,128)(2,1)} %collective-permute-done.44.refs_1_, bf16[256,8192]{1,0:T(8,128)(2,1)} %late.1.refs_2_), custom_call_target="tpu_custom_call", output_to_operand_aliasing={{}: (3, {})} | custom-call | bytes 1572864 | tf_op jit(solution)/shard_map/put/pallas_call | solution.py:411
  196.3 2.6 %put.4.refs_2_ = bf16[256,8192]{1,0:T(8,128)(2,1)} custom-call(s32[2]{0:T(128)} %pad_add_fusion.place.refs_0_, bf16[256,768]{1,0:T(8,128)(2,1)} %collective-permute-done.46.refs_0_, bf16[256,768]{1,0:T(8,128)(2,1)} %collective-permute-done.47.refs_1_, bf16[256,8192]{1,0:T(8,128)(2,1)} %put.3.refs_2_), custom_call_target="tpu_custom_call", output_to_operand_aliasing={{}: (3, {})} | custom-call | bytes 1572864 | tf_op jit(solution)/shard_map/put/pallas_call | solution.py:411
  198.9 2.6 %put.5 = bf16[256,8192]{1,0:T(8,128)(2,1)} custom-call(s32[2]{0:T(128)} %pad_add_fusion.place.refs_0_, bf16[256,768]{1,0:T(8,128)(2,1)} %collective-permute-done.43.refs_0_, bf16[256,768]{1,0:T(8,128)(2,1)} %collective-permute-done.45.refs_1_, bf16[256,8192]{1,0:T(8,128)(2,1)} %put.4.refs_2_), custom_call_target="tpu_custom_call", output_to_operand_aliasing={{}: (3, {})} | custom-call | bytes 1572864 | tf_op jit(solution)/shard_map/put/pallas_call | solution.py:411
  (159 shorter events, 56.6 us)
Async XLA Ops:
  1.3 33.3 %collective-permute-start.6 = (bf16[256,2048]{1,0:T(8,128)(2,1)S(1)}, bf16[256,2048]{1,0:T(8,128)(2,1)}, u32[]{:S(2)}, u32[]{:S(2)}) collective-permute-start(bf16[256,2048]{1,0:T(8,128)(2,1)S(1)} %dynamic-slice_bitcast_fusion), channel_id=1, source_target_pairs={{0,8},{8,0},{16,24},{24,16},{1,9},{9,1},{17,25},{25,17},{2,10},{10... | collective-permute-start | bytes 3145736 | tf_op jit(solution)/shard_map/ppermute | solution.py:25
  9.0 42.4 %collective-permute-start.1 = (bf16[256,2048]{1,0:T(8,128)(2,1)}, bf16[256,2048]{1,0:T(8,128)(2,1)}, u32[]{:S(2)}, u32[]{:S(2)}) collective-permute-start(bf16[256,2048]{1,0:T(8,128)(2,1)} %constant_dynamic-slice_fusion), channel_id=1, source_target_pairs={{0,24},{8,16},{16,8},{24,0},{1,25},{9,17},{17,9},{25,1},{2,26},{10... | collective-permute-start | bytes 3145736 | tf_op jit(solution)/shard_map/ppermute | solution.py:25
  10.5 47.1 %collective-permute-start = (bf16[256,2048]{1,0:T(8,128)(2,1)}, bf16[256,2048]{1,0:T(8,128)(2,1)}, u32[]{:S(2)}, u32[]{:S(2)}) collective-permute-start(bf16[256,2048]{1,0:T(8,128)(2,1)} %constant_dynamic-slice_fusion.1), channel_id=1, source_target_pairs={{0,16},{8,24},{16,0},{24,8},{1,17},{9,25},{17,1},{25,9},{2,18},{10... | collective-permute-start | bytes 3145736 | tf_op jit(solution)/shard_map/ppermute | solution.py:25
  19.0 8.1 %collective-permute-start.3 = (f32[128,256]{1,0:T(8,128)S(1)}, f32[128,256]{1,0:T(8,128)S(1)}, u32[]{:S(2)}, u32[]{:S(2)}) collective-permute-start(f32[128,256]{1,0:T(8,128)S(1)} %add.117), channel_id=1, source_target_pairs={{0,2},{1,3},{2,0},{3,1},{4,6},{5,7},{6,4},{7,5},{8,10},{9,11},{10,... | collective-permute-start | bytes 393224 | tf_op jit(solution)/shard_map/ppermute | solution.py:25
  21.1 9.2 %collective-permute-start.4 = (f32[128,256]{1,0:T(8,128)S(1)}, f32[128,256]{1,0:T(8,128)S(1)}, u32[]{:S(2)}, u32[]{:S(2)}) collective-permute-start(f32[128,256]{1,0:T(8,128)S(1)} %add.117), channel_id=1, source_target_pairs={{0,4},{1,5},{2,6},{3,7},{4,0},{5,1},{6,2},{7,3},{8,12},{9,13},{10,... | collective-permute-start | bytes 393224 | tf_op jit(solution)/shard_map/ppermute | solution.py:25
  27.1 6.8 %collective-permute-start.5 = (f32[128,256]{1,0:T(8,128)S(1)}, f32[128,256]{1,0:T(8,128)S(1)}, u32[]{:S(2)}, u32[]{:S(2)}) collective-permute-start(f32[128,256]{1,0:T(8,128)S(1)} %add.117), channel_id=1, source_target_pairs={{0,6},{1,7},{2,4},{3,5},{4,2},{5,3},{6,0},{7,1},{8,14},{9,15},{10,... | collective-permute-start | bytes 393224 | tf_op jit(solution)/shard_map/ppermute | solution.py:25
  71.7 6.5 %collective-permute-start.18 = (f32[64,256]{1,0:T(8,128)S(1)}, f32[64,256]{1,0:T(8,128)S(1)}, u32[]{:S(2)}, u32[]{:S(2)}) collective-permute-start(f32[64,256]{1,0:T(8,128)S(1)} %add_add_fusion.4), channel_id=1, source_target_pairs={{0,2},{1,3},{2,0},{3,1},{4,6},{5,7},{6,4},{7,5},{8,10},{9,11},{10,... | collective-permute-start | bytes 196616 | tf_op jit(solution)/shard_map/ppermute | solution.py:25
  73.3 6.6 %collective-permute-start.19 = (f32[64,256]{1,0:T(8,128)S(1)}, f32[64,256]{1,0:T(8,128)S(1)}, u32[]{:S(2)}, u32[]{:S(2)}) collective-permute-start(f32[64,256]{1,0:T(8,128)S(1)} %add_add_fusion.4), channel_id=1, source_target_pairs={{0,4},{1,5},{2,6},{3,7},{4,0},{5,1},{6,2},{7,3},{8,12},{9,13},{10,... | collective-permute-start | bytes 196616 | tf_op jit(solution)/shard_map/ppermute | solution.py:25
  75.9 6.1 %collective-permute-start.20 = (f32[64,256]{1,0:T(8,128)S(1)}, f32[64,256]{1,0:T(8,128)S(1)}, u32[]{:S(2)}, u32[]{:S(2)}) collective-permute-start(f32[64,256]{1,0:T(8,128)S(1)} %add_add_fusion.4), channel_id=1, source_target_pairs={{0,6},{1,7},{2,4},{3,5},{4,2},{5,3},{6,0},{7,1},{8,14},{9,15},{10,... | collective-permute-start | bytes 196616 | tf_op jit(solution)/shard_map/ppermute | solution.py:25
  76.1 6.5 %collective-permute-start.8 = (f32[128,256]{1,0:T(8,128)}, f32[128,256]{1,0:T(8,128)S(1)}, u32[]{:S(2)}, u32[]{:S(2)}) collective-permute-start(f32[128,256]{1,0:T(8,128)} %add_add_fusion.refs_1_), channel_id=1, source_target_pairs={{0,8},{8,0},{16,24},{24,16},{1,9},{9,1},{17,25},{25,17},{2,10},{10... | collective-permute-start | bytes 393224 | tf_op jit(solution)/shard_map/ppermute | solution.py:25
  76.6 7.5 %collective-permute-start.9 = (f32[128,256]{1,0:T(8,128)}, f32[128,256]{1,0:T(8,128)S(1)}, u32[]{:S(2)}, u32[]{:S(2)}) collective-permute-start(f32[128,256]{1,0:T(8,128)} %add_add_fusion.refs_1_), channel_id=1, source_target_pairs={{0,16},{8,24},{16,0},{24,8},{1,17},{9,25},{17,1},{25,9},{2,18},{10... | collective-permute-start | bytes 393224 | tf_op jit(solution)/shard_map/ppermute | solution.py:25
  78.2 6.3 %collective-permute-start.10 = (f32[128,256]{1,0:T(8,128)}, f32[128,256]{1,0:T(8,128)S(1)}, u32[]{:S(2)}, u32[]{:S(2)}) collective-permute-start(f32[128,256]{1,0:T(8,128)} %add_add_fusion.refs_1_), channel_id=1, source_target_pairs={{0,24},{8,16},{16,8},{24,0},{1,25},{9,17},{17,9},{25,1},{2,26},{10... | collective-permute-start | bytes 393224 | tf_op jit(solution)/shard_map/ppermute | solution.py:25
  84.1 7.9 %collective-permute-start.12 = (f32[128,256]{1,0:T(8,128)S(1)}, f32[128,256]{1,0:T(8,128)S(1)}, u32[]{:S(2)}, u32[]{:S(2)}) collective-permute-start(f32[128,256]{1,0:T(8,128)S(1)} %collective-permute-done.8.refs_2_), channel_id=1, source_target_pairs={{0,1},{1,0},{2,3},{3,2},{4,5},{5,4},{6,7},{7,6},{8,9},{9,8},{10,11... | collective-permute-start | bytes 393224 | tf_op jit(solution)/shard_map/ppermute | solution.py:25
  84.5 7.6 %collective-permute-start.13 = (f32[128,256]{1,0:T(8,128)S(1)}, f32[128,256]{1,0:T(8,128)S(1)}, u32[]{:S(2)}, u32[]{:S(2)}) collective-permute-start(f32[128,256]{1,0:T(8,128)S(1)} %collective-permute-done.9.refs_3_), channel_id=1, source_target_pairs={{0,1},{1,0},{2,3},{3,2},{4,5},{5,4},{6,7},{7,6},{8,9},{9,8},{10,11... | collective-permute-start | bytes 393224 | tf_op jit(solution)/shard_map/ppermute | solution.py:25
  84.7 7.5 %collective-permute-start.14 = (f32[128,256]{1,0:T(8,128)S(1)}, f32[128,256]{1,0:T(8,128)S(1)}, u32[]{:S(2)}, u32[]{:S(2)}) collective-permute-start(f32[128,256]{1,0:T(8,128)S(1)} %collective-permute-done.10.refs_4_), channel_id=1, source_target_pairs={{0,1},{1,0},{2,3},{3,2},{4,5},{5,4},{6,7},{7,6},{8,9},{9,8},{10,11... | collective-permute-start | bytes 393224 | tf_op jit(solution)/shard_map/ppermute | solution.py:25
  108.9 5.6 %collective-permute-start.29 = (f32[96,256]{1,0:T(8,128)S(1)}, f32[96,256]{1,0:T(8,128)S(1)}, u32[]{:S(2)}, u32[]{:S(2)}) collective-permute-start(f32[96,256]{1,0:T(8,128)S(1)} %get-tuple-element.61), channel_id=1, source_target_pairs={{0,8},{8,0},{16,24},{24,16},{1,9},{9,1},{17,25},{25,17},{2,10},{10... | collective-permute-start | bytes 294920 | tf_op jit(solution)/shard_map/ppermute | solution.py:25
  109.7 5.7 %collective-permute-start.30 = (f32[96,256]{1,0:T(8,128)S(1)}, f32[96,256]{1,0:T(8,128)S(1)}, u32[]{:S(2)}, u32[]{:S(2)}) collective-permute-start(f32[96,256]{1,0:T(8,128)S(1)} %get-tuple-element.62), channel_id=1, source_target_pairs={{0,16},{8,24},{16,0},{24,8},{1,17},{9,25},{17,1},{25,9},{2,18},{10... | collective-permute-start | bytes 294920 | tf_op jit(solution)/shard_map/ppermute | solution.py:25
  111.0 6.1 %collective-permute-start.31 = (f32[96,256]{1,0:T(8,128)S(1)}, f32[96,256]{1,0:T(8,128)S(1)}, u32[]{:S(2)}, u32[]{:S(2)}) collective-permute-start(f32[96,256]{1,0:T(8,128)S(1)} %get-tuple-element.63), channel_id=1, source_target_pairs={{0,24},{8,16},{16,8},{24,0},{1,25},{9,17},{17,9},{25,1},{2,26},{10... | collective-permute-start | bytes 294920 | tf_op jit(solution)/shard_map/ppermute | solution.py:25
  117.3 10.3 %collective-permute-start.33 = (f32[96,256]{1,0:T(8,128)S(1)}, f32[96,256]{1,0:T(8,128)S(1)}, u32[]{:S(2)}, u32[]{:S(2)}) collective-permute-start(f32[96,256]{1,0:T(8,128)S(1)} %add_add_fusion.2), channel_id=1, source_target_pairs={{0,4},{1,5},{2,6},{3,7},{4,0},{5,1},{6,2},{7,3},{8,12},{9,13},{10,... | collective-permute-start | bytes 294920 | tf_op jit(solution)/shard_map/ppermute | solution.py:25
  120.8 6.8 %collective-permute-start.34 = (f32[96,256]{1,0:T(8,128)S(1)}, f32[96,256]{1,0:T(8,128)S(1)}, u32[]{:S(2)}, u32[]{:S(2)}) collective-permute-start(f32[96,256]{1,0:T(8,128)S(1)} %add_add_fusion.2), channel_id=1, source_target_pairs={{0,6},{1,7},{2,4},{3,5},{4,2},{5,3},{6,0},{7,1},{8,14},{9,15},{10,... | collective-permute-start | bytes 294920 | tf_op jit(solution)/shard_map/ppermute | solution.py:25
  135.6 12.6 %collective-permute-start.48 = (bf16[512,256]{1,0:T(8,128)(2,1)}, bf16[512,256]{1,0:T(8,128)(2,1)S(1)}, u32[]{:S(2)}, u32[]{:S(2)}) collective-permute-start(bf16[512,256]{1,0:T(8,128)(2,1)} %get-tuple-element.71), channel_id=1, source_target_pairs={{0,8},{8,0},{16,24},{24,16},{1,9},{9,1},{17,25},{25,17},{2,10},{10... | collective-permute-start | bytes 786440 | tf_op jit(solution)/shard_map/ppermute | solution.py:25
  135.8 13.5 %collective-permute-start.49 = (bf16[512,256]{1,0:T(8,128)(2,1)}, bf16[512,256]{1,0:T(8,128)(2,1)S(1)}, u32[]{:S(2)}, u32[]{:S(2)}) collective-permute-start(bf16[512,256]{1,0:T(8,128)(2,1)} %get-tuple-element.71), channel_id=1, source_target_pairs={{0,16},{8,24},{16,0},{24,8},{1,17},{9,25},{17,1},{25,9},{2,18},{10... | collective-permute-start | bytes 786440 | tf_op jit(solution)/shard_map/ppermute | solution.py:25
  144.7 24.1 %collective-permute-start.42 = (bf16[256,768]{1,0:T(8,128)(2,1)}, bf16[256,768]{1,0:T(8,128)(2,1)}, u32[]{:S(2)}, u32[]{:S(2)}) collective-permute-start(bf16[256,768]{1,0:T(8,128)(2,1)} %get-tuple-element.67.a), channel_id=1, source_target_pairs={{0,8},{8,0},{16,24},{24,16},{1,9},{9,1},{17,25},{25,17},{2,10},{10... | collective-permute-start | bytes 1179656 | tf_op jit(solution)/shard_map/ppermute | solution.py:25
  145.7 24.5 %collective-permute-start.44 = (bf16[256,768]{1,0:T(8,128)(2,1)}, bf16[256,768]{1,0:T(8,128)(2,1)}, u32[]{:S(2)}, u32[]{:S(2)}) collective-permute-start(bf16[256,768]{1,0:T(8,128)(2,1)} %get-tuple-element.68.b), channel_id=1, source_target_pairs={{0,16},{8,24},{16,0},{24,8},{1,17},{9,25},{17,1},{25,9},{2,18},{10... | collective-permute-start | bytes 1179656 | tf_op jit(solution)/shard_map/ppermute | solution.py:25
  147.1 15.5 %collective-permute-start.50 = (bf16[512,256]{1,0:T(8,128)(2,1)S(1)}, bf16[512,256]{1,0:T(8,128)(2,1)S(1)}, u32[]{:S(2)}, u32[]{:S(2)}) collective-permute-start(bf16[512,256]{1,0:T(8,128)(2,1)S(1)} %copy-done.9), channel_id=1, source_target_pairs={{0,24},{8,16},{16,8},{24,0},{1,25},{9,17},{17,9},{25,1},{2,26},{10... | collective-permute-start | bytes 786440 | tf_op jit(solution)/shard_map/ppermute | solution.py:25
  148.2 20.0 %collective-permute-start.51 = (bf16[512,256]{1,0:T(8,128)(2,1)S(1)}, bf16[512,256]{1,0:T(8,128)(2,1)S(1)}, u32[]{:S(2)}, u32[]{:S(2)}) collective-permute-start(bf16[512,256]{1,0:T(8,128)(2,1)S(1)} %copy-done.8), channel_id=1, source_target_pairs={{0,8},{8,0},{16,24},{24,16},{1,9},{9,1},{17,25},{25,17},{2,10},{10... | collective-permute-start | bytes 786440 | tf_op jit(solution)/shard_map/ppermute | solution.py:25
  149.3 22.0 %collective-permute-start.52 = (bf16[512,256]{1,0:T(8,128)(2,1)S(1)}, bf16[512,256]{1,0:T(8,128)(2,1)S(1)}, u32[]{:S(2)}, u32[]{:S(2)}) collective-permute-start(bf16[512,256]{1,0:T(8,128)(2,1)S(1)} %copy-done.8), channel_id=1, source_target_pairs={{0,16},{8,24},{16,0},{24,8},{1,17},{9,25},{17,1},{25,9},{2,18},{10... | collective-permute-start | bytes 786440 | tf_op jit(solution)/shard_map/ppermute | solution.py:25
  162.6 33.7 %collective-permute-start.46 = (bf16[256,768]{1,0:T(8,128)(2,1)}, bf16[256,768]{1,0:T(8,128)(2,1)}, u32[]{:S(2)}, u32[]{:S(2)}) collective-permute-start(bf16[256,768]{1,0:T(8,128)(2,1)} %get-tuple-element.68.b), channel_id=1, source_target_pairs={{0,8},{8,0},{16,24},{24,16},{1,9},{9,1},{17,25},{25,17},{2,10},{10... | collective-permute-start | bytes 1179656 | tf_op jit(solution)/shard_map/ppermute | solution.py:25
  168.2 28.1 %collective-permute-start.47 = (bf16[256,768]{1,0:T(8,128)(2,1)}, bf16[256,768]{1,0:T(8,128)(2,1)}, u32[]{:S(2)}, u32[]{:S(2)}) collective-permute-start(bf16[256,768]{1,0:T(8,128)(2,1)} %get-tuple-element.67.a), channel_id=1, source_target_pairs={{0,16},{8,24},{16,0},{24,8},{1,17},{9,25},{17,1},{25,9},{2,18},{10... | collective-permute-start | bytes 1179656 | tf_op jit(solution)/shard_map/ppermute | solution.py:25
  168.7 30.1 %collective-permute-start.43 = (bf16[256,768]{1,0:T(8,128)(2,1)}, bf16[256,768]{1,0:T(8,128)(2,1)}, u32[]{:S(2)}, u32[]{:S(2)}) collective-permute-start(bf16[256,768]{1,0:T(8,128)(2,1)} %collective-permute-done.42.refs_0_), channel_id=1, source_target_pairs={{0,16},{8,24},{16,0},{24,8},{1,17},{9,25},{17,1},{25,9},{2,18},{10... | collective-permute-start | bytes 1179656 | tf_op jit(solution)/shard_map/ppermute | solution.py:25
  170.2 28.6 %collective-permute-start.45 = (bf16[256,768]{1,0:T(8,128)(2,1)}, bf16[256,768]{1,0:T(8,128)(2,1)}, u32[]{:S(2)}, u32[]{:S(2)}) collective-permute-start(bf16[256,768]{1,0:T(8,128)(2,1)} %collective-permute-done.44.refs_1_), channel_id=1, source_target_pairs={{0,8},{8,0},{16,24},{24,16},{1,9},{9,1},{17,25},{25,17},{2,10},{10... | collective-permute-start | bytes 1179656 | tf_op jit(solution)/shard_map/ppermute | solution.py:25
  171.2 18.6 %collective-permute-start.53 = (bf16[512,256]{1,0:T(8,128)(2,1)S(1)}, bf16[512,256]{1,0:T(8,128)(2,1)S(1)}, u32[]{:S(2)}, u32[]{:S(2)}) collective-permute-start(bf16[512,256]{1,0:T(8,128)(2,1)S(1)} %copy-done.8), channel_id=1, source_target_pairs={{0,24},{8,16},{16,8},{24,0},{1,25},{9,17},{17,9},{25,1},{2,26},{10... | collective-permute-start | bytes 786440 | tf_op jit(solution)/shard_map/ppermute | solution.py:25
  (53 other events, 405.1 us)

commit v2 on v1

--- a/solution.py
+++ b/solution.py
@@ -165,63 +165,90 @@
     return value
 
 
-def near_gram_kernel(chunk, place, x, p1, out_ref, block, load):
+SHARES_X, SHARES_Y = (0, 2, 3), (0, 1, 3)
+
+
+def near_gram_kernel(chunk, place, x, p1, out_ref, x_ref, y_ref, d_ref, block, pack, load, save):
     me = place[0]
-    share = p1.shape[1]
-
-    def mine(column, size):
-        return x.at[:, pl.ds(pl.multiple_of(me * share + column, 128), size)]
+    share, raw = p1.shape[1], d_ref.shape[1]
+
+    def mine(column, size, t=0):
+        return x.at[:, pl.ds(pl.multiple_of((me ^ t) * share + column, 128), size)]
 
     def theirs(column, size):
         return p1.at[:, column : column + size]
 
+    packs = [pltpu.make_async_copy(mine(0, raw, t), pack.at[t], save.at[t]) for t in range(GROUP)]
+    packs.append(pltpu.make_async_copy(theirs(0, raw), pack.at[GROUP], save.at[GROUP]))
+    for copy in packs:
+        copy.start()
     out_ref[...] = pair_gram(me, ((0, mine), (1, theirs)), block, load, chunk)
-
-
-def near_gram(place, x, p1, chunk=512):
+    for copy in packs:
+        copy.wait()
+    targets = [(t, x_ref.at[i]) for i, t in enumerate(SHARES_X)] + [(t, y_ref.at[i]) for i, t in enumerate(SHARES_Y)]
+    targets += [(GROUP, y_ref.at[GROUP - 1]), (0, d_ref)]
+    copies = [pltpu.make_async_copy(pack.at[t], target, save.at[i]) for i, (t, target) in enumerate(targets)]
+    for copy in copies:
+        copy.start()
+    for copy in copies:
+        copy.wait()
+
+
+def near_gram(place, x, p1, raw, chunk=512):
     rows, share = p1.shape
+    message = shape(GROUP, rows, raw, dtype=BF16)
     return pl.pallas_call(
         functools.partial(near_gram_kernel, chunk),
-        out_shape=shape(rows, rows),
+        out_shape=(shape(rows, rows), message, message, shape(rows, raw, dtype=BF16)),
         in_specs=[SMEM, HBM, HBM],
-        out_specs=VMEM,
-        scratch_shapes=[pltpu.VMEM((2, rows, share), BF16), pltpu.SemaphoreType.DMA((2 * share // chunk,))],
+        out_specs=(VMEM, HBM, HBM, HBM),
+        scratch_shapes=[
+            pltpu.VMEM((2, rows, share), BF16),
+            pltpu.VMEM((GROUP + 1, rows, raw), BF16),
+            pltpu.SemaphoreType.DMA((2 * share // chunk,)),
+            pltpu.SemaphoreType.DMA((2 * GROUP,)),
+        ],
         cost_estimate=cost(2 * rows * rows * share, 4 * rows * share),
         compiler_params=WHOLE,
         name="near_gram",
     )(place, x, p1)
 
 
-def far_gram_kernel(chunk, place, near, p2, p3, keep_ref, give_ref, block, acc, load):
+def far_gram_kernel(chunk, place, near, p2, p3, _, keep_ref, give_ref, x_ref, block, acc, load, save):
     me, core = place[0], place[1]
     sources = tuple((s, lambda column, size, p=p: p.at[:, column : column + size]) for s, p in ((2, p2), (3, p3)))
     acc[me // 2] = near[...]
     acc[1 - me // 2] = pair_gram(me, sources, block, load, chunk)
+    copy = pltpu.make_async_copy(block.at[(me ^ 2) % 2, :, : x_ref.shape[2]], x_ref.at[GROUP - 1], save)
+    copy.start()
     part = keep_ref.shape[1]
     for s in range(GROUP):
         to = me ^ s
         pair, start = to // 2, (to % 2) * (CORES * part)
         keep_ref[s] = acc[pair, pl.ds(pl.multiple_of(start + core * part, part), part), :]
         give_ref[s] = acc[pair, pl.ds(pl.multiple_of(start + (1 - core) * part, part), part), :]
-
-
-def far_gram(place, near, p2, p3, chunk=512):
+    copy.wait()
+
+
+def far_gram(place, near, p2, p3, message, chunk=512):
     rows, share = p2.shape
     out = shape(GROUP, rows // (2 * CORES), rows)
     return pl.pallas_call(
         functools.partial(far_gram_kernel, chunk),
-        out_shape=(out, out),
-        in_specs=[SMEM, VMEM, HBM, HBM],
-        out_specs=(VMEM, VMEM),
+        out_shape=(out, out, shape(*message.shape, dtype=BF16)),
+        in_specs=[SMEM, VMEM, HBM, HBM, HBM],
+        out_specs=(VMEM, VMEM, HBM),
         scratch_shapes=[
             pltpu.VMEM((2, rows, share), BF16),
             pltpu.VMEM((GROUP // 2, rows, rows), F32),
             pltpu.SemaphoreType.DMA((2 * share // chunk,)),
+            pltpu.SemaphoreType.DMA,
         ],
+        input_output_aliases={4: 2},
         cost_estimate=cost(2 * rows * rows * share, 4 * rows * share),
         compiler_params=WHOLE,
         name="far_gram",
-    )(place, near, p2, p3)
+    )(place, near, p2, p3, message)
 
 
 def fold(mine, theirs):
@@ -237,10 +264,9 @@
     return (lower.astype(F32) - dot(w, stacked)).astype(BF16)
 
 
-def first_kernel(tile, *refs):
+def first_kernel(raw, tile, *refs):
     place, tails, crosses, (x, p1, p2, p3), refs = refs[0], refs[1:9], refs[9:17], refs[17:21], refs[21:]
-    m_ref, e_ref, f_ref, keep_ref, give_ref, cross, diag, inverse, w, block, m, acc, load, save = refs
-    ahead = e_ref.shape[1]
+    m_ref, e_ref, f_ref, w, keep_ref, give_ref, cross, diag, inverse, block, m, acc, load, save = refs
     me, core = place[0], place[1]
     rows, share = p1.shape
     sources = [x.at[:, pl.ds(pl.multiple_of(me * share, share), share)], p1, p2, p3]
@@ -276,10 +302,12 @@
         acc[0] += dot(m0, m0, NT)
         acc[1] += dot(m0, m1, NT)
         acc[2] += dot(m1, m1, NT)
+    start = raw
     for i, ref in enumerate((e_ref, f_ref)):
-        source = m.at[:, i * ahead : (i + 1) * ahead]
+        source = m.at[:, start : start + ref.shape[1]]
         saves.append(pltpu.make_async_copy(source, ref, save.at[share // tile + i]))
         saves[-1].start()
+        start += ref.shape[1]
     part = rows // (GROUP * CORES)
     for s in range(GROUP):
         to = me ^ s
@@ -291,20 +319,19 @@
         copy.wait()
 
 
-def first(place, diagonals, crosses, x, pieces, ahead, tile=512):
+def first(place, diagonals, crosses, x, pieces, raw, ahead, tile=512):
     rows, share = pieces[0].shape
     pairs = GROUP // 2
     out = shape(GROUP, 3 * rows // (GROUP * CORES), rows)
     return pl.pallas_call(
-        functools.partial(first_kernel, tile),
-        out_shape=tuple(shape(pairs * rows, n, dtype=BF16) for n in (share, ahead, ahead)) + (out, out),
+        functools.partial(first_kernel, raw, tile),
+        out_shape=tuple(shape(pairs * rows, n, dtype=BF16) for n in (share, *ahead)) + (shape(pairs, rows, 2 * rows, dtype=BF16), out, out),
         in_specs=[SMEM] + [VMEM] * (4 * GROUP) + [HBM] * 4,
-        out_specs=(ANY, ANY, ANY, VMEM, VMEM),
+        out_specs=(ANY, ANY, ANY, VMEM, VMEM, VMEM),
         scratch_shapes=[
             pltpu.VMEM((pairs, rows, rows), F32),
             pltpu.VMEM((GROUP, rows, rows), F32),
             pltpu.VMEM((pairs, rows, rows), F32),
-            pltpu.VMEM((pairs, rows, 2 * rows), BF16),
             pltpu.VMEM((GROUP * rows, share), BF16),
             pltpu.VMEM((pairs * rows, share), BF16),
             pltpu.VMEM((3, rows, rows), F32),
@@ -338,9 +365,9 @@
         start += ref.shape[1]
 
 
-def second(place, bundles, m, ahead):
+def second(place, bundles, m, early):
     rows, share = m.shape[0] // 2, m.shape[1]
-    early, half = 2 * ahead, share // 2 - ahead
+    half = (share - early) // 2
     return pl.pallas_call(
         second_kernel,
         out_shape=tuple(shape(rows, n, dtype=BF16) for n in (half, half, early)) + (shape(1, rows, 2 * rows, dtype=BF16),),
@@ -357,9 +384,9 @@
     )(place, *bundles, m)
 
 
-def late_kernel(share, place, w, a, b, e, *refs):
+def late_kernel(share, raw, place, w, a, b, e, *refs):
     early, (out, buffer, save) = refs[:-3], refs[-3:]
-    me, ahead, half = place[0], e.shape[1] // 2, a.shape[1]
+    me, half = place[0], a.shape[1]
     saves = []
 
     def put(source, owner, column):
@@ -368,26 +395,78 @@
         saves[-1].start()
 
     put(e, me, 0)
-    put(a, me, 2 * ahead)
-    put(b, me, 2 * ahead + half)
+    put(a, me, e.shape[1])
+    put(b, me, e.shape[1] + half)
     for i, pair in enumerate(early):
-        buffer[i] = merge_rows(pair[...], w[0])
-        put(buffer.at[i], me ^ (i % (GROUP - 1) + 1), i // (GROUP - 1) * ahead)
+        s, size = i % (GROUP - 1), pair.shape[1]
+        column = raw if i < GROUP - 1 else raw + early[0].shape[1]
+        spot = buffer.at[s, :, column - raw : column - raw + size]
+        spot[...] = merge_rows(pair[...], w[0])
+        put(spot, me ^ (s + 1), column)
     for copy in saves:
         copy.wait()
 
 
-def late(place, w, a, b, e, early, share):
-    rows, ahead = e.shape[0], e.shape[1] // 2
-    return pl.pallas_call(
-        functools.partial(late_kernel, share),
+def late(place, w, a, b, e, early, raw, share):
+    rows, size = e.shape[0], e.shape[1] - raw
+    return pl.pallas_call(
+        functools.partial(late_kernel, share, raw),
         out_shape=shape(rows, GROUP * share, dtype=BF16),
         in_specs=[SMEM] + [VMEM] * (4 + len(early)),
         out_specs=HBM,
-        scratch_shapes=[pltpu.VMEM((len(early), rows, ahead), BF16), pltpu.SemaphoreType.DMA((len(early) + 3,))],
-        cost_estimate=cost(4 * rows * rows * ahead * len(early), 6 * rows * ahead * len(early)),
+        scratch_shapes=[pltpu.VMEM((GROUP - 1, rows, size), BF16), pltpu.SemaphoreType.DMA((len(early) + 3,))],
+        cost_estimate=cost(4 * rows * rows * size * (GROUP - 1), 6 * rows * size * (GROUP - 1)),
         name="late",
     )(place, w, a, b, e, *early)
+
+
+def raw_merge_kernel(share, place, w0, w1, x, xs, ys, d, _, out, block, pair, buffer, load, save):
+    me = place[0]
+    rows, raw = d.shape
+    saves = []
+    sources = {}
+    for v in range(1, GROUP):
+        mine = x.at[:, pl.ds(pl.multiple_of((me ^ v) * share, 128), raw)]
+        across = {1: xs.at[GROUP - 1], 2: ys.at[GROUP - 1], 3: d}[v]
+        sources[v] = (mine, xs.at[SHARES_X.index(v ^ 1)], ys.at[SHARES_Y.index(v ^ 2)], across)
+    loads = {}
+    for v, group in sources.items():
+        for s, source in enumerate(group):
+            target = block.at[v - 1, pl.ds(pl.multiple_of((me ^ s) * rows, rows), rows)]
+            loads[v, s] = pltpu.make_async_copy(source, target, load.at[(v - 1) * GROUP + s])
+            loads[v, s].start()
+    for v in sources:
+        for s in range(GROUP):
+            loads[v, s].wait()
+        for j in range(GROUP // 2):
+            pair[j * rows : (j + 1) * rows] = merge_rows(block[v - 1, 2 * j * rows : 2 * (j + 1) * rows], w0[j])
+        buffer[v - 1] = merge_rows(pair[...], w1[0])
+        target = out.at[:, pl.ds(pl.multiple_of((me ^ v) * share, 128), raw)]
+        saves.append(pltpu.make_async_copy(buffer.at[v - 1], target, save.at[v - 1]))
+        saves[-1].start()
+    for copy in saves:
+        copy.wait()
+
+
+def raw_merge(place, w0, w1, x, messages, out, share):
+    rows, raw = messages[2].shape
+    return pl.pallas_call(
+        functools.partial(raw_merge_kernel, share),
+        out_shape=shape(*out.shape, dtype=BF16),
+        in_specs=[SMEM, VMEM, VMEM] + [HBM] * 5,
+        out_specs=HBM,
+        scratch_shapes=[
+            pltpu.VMEM((GROUP - 1, GROUP * rows, raw), BF16),
+            pltpu.VMEM((2 * rows, raw), BF16),
+            pltpu.VMEM((GROUP - 1, rows, raw), BF16),
+            pltpu.SemaphoreType.DMA(((GROUP - 1) * GROUP,)),
+            pltpu.SemaphoreType.DMA((GROUP - 1,)),
+        ],
+        input_output_aliases={7: 0},
+        cost_estimate=cost(12 * rows * rows * raw * (GROUP - 1), 10 * rows * raw * (GROUP - 1)),
+        compiler_params=WHOLE,
+        name="raw_merge",
+    )(place, w0, w1, x, *messages, out)
 
 
 def put_kernel(spots, share, place, *refs):
@@ -438,7 +517,8 @@
     x = sketches[0]
     rows, columns = x.shape
     share = columns // GROUP
-    ahead = share // 8
+    raw, ahead = 3 * share // 16, (3 * share // 16, share // 8)
+    early = raw + sum(ahead)
     me = lax.axis_index("dp") % GROUP
     place = jnp.stack([me, lax.axis_index("feat") % CORES]).astype(jnp.int32)
 
@@ -449,34 +529,38 @@
         pieces[s] = send(piece, "dp", s)
     keep, give = own_gram(place, x)
     own = over_chips(total([keep, send(give, "feat", 1)]))
-    near = near_gram(place, x, pieces[1])
+    near, to_x, to_y, to_d = near_gram(place, x, pieces[1], raw)
     p2, p3, own, near = lax.optimization_barrier((pieces[2], pieces[3], own, near))
 
-    keep, give = far_gram(place, near, p2, p3)
+    keep, give, to_x = far_gram(place, near, p2, p3, to_x)
     parts = fold(keep, send(give, "feat", 1))
-    parts, own = lax.optimization_barrier((parts, own))
+    parts, own, to_d = lax.optimization_barrier((parts, own, to_d))
     mine = total([parts[0]] + send_all(parts[1:], "dp", PEERS))
     diagonals = gather_group(own)
-    crosses = gather_group(over_chips(mine))
-    m, e, f, keep, give = first(place, diagonals, crosses, x, [pieces[1], p2, p3], ahead)
+    from_d = send(to_d, "dp", 3)
+    bundle = over_chips(mine)
+    bundle, to_x, to_y = lax.optimization_barrier((bundle, to_x, to_y))
+    crosses = gather_group(bundle)
+    messages = [send(to_x, "dp", 1), send(to_y, "dp", 2), from_d]
+    m, e, f, w0, keep, give = first(place, diagonals, crosses, x, [pieces[1], p2, p3], raw, ahead)
 
     parts = fold(keep, send(give, "feat", 1))
     parts, e = lax.optimization_barrier((parts, e))
     mine = total([parts[0]] + send_all(parts[1:], "dp", PEERS))
-    early = send_all([e] * len(PEERS), "dp", PEERS)
+    pairs = send_all([e] * len(PEERS), "dp", PEERS)
     bundle = over_chips(mine)
     bundle, f = lax.optimization_barrier((bundle, f))
     bundles = gather_group(bundle)
-    early += send_all([f] * len(PEERS), "dp", PEERS)
-    a, b, e, w = second(place, bundles, m, ahead)
+    pairs += send_all([f] * len(PEERS), "dp", PEERS)
+    a, b, e, w1 = second(place, bundles, m, early)
 
     ax, by = send(a, "dp", 1), send(b, "dp", 2)
     bx, ay = send(b, "dp", 1), send(a, "dp", 2)
     ad, bd = send(ax, "dp", 2), send(by, "dp", 1)
-    left, right = 2 * ahead, ahead + share // 2
-    out = late(place, w, a, b, e, early, share)
-    out = put(place, out, [ax, by], ((1, left), (2, right)), share)
-    out = put(place, out, [bx, ay], ((1, right), (2, left)), share)
+    left, right = early, early + a.shape[1]
+    out = late(place, w1, a, b, e, pairs, raw, share)
+    out = raw_merge(place, w0, w1, x, messages, out, share)
+    out = put(place, out, [ax, by, bx, ay], ((1, left), (2, right), (1, right), (2, left)), share)
     out = put(place, out, [ad, bd], ((3, left), (3, right)), share)
     return out[None]
 

time: 202 us -> 213 us (1.054)
  Pallas kernels: 42.1 us -> 47.1 us
  waiting for transfers between devices: 92.2 us -> 96.1 us
  starting transfers between devices: 54.2 us -> 57.2 us
    pallas_call x3 -> x4, Pallas kernels: 18.3 us -> 25.3 us  [the longest x1 11.8 us: first(): pl.pallas_call(functools.partial(first_kernel, raw, tile), out_shape=tupl...]
    ppermute x54 -> x57, waiting for transfers between devices: 92.2 us -> 96.1 us  [send(): return lax.ppermute(block, axis, [(i, i ^ shift) for i in range(count)])]
    ppermute x54 -> x57, starting transfers between devices: 54.2 us -> 57.2 us  [send(): return lax.ppermute(block, axis, [(i, i ^ shift) for i in range(count)])]
    pallas_call x3 -> x2, Pallas kernels: 7.71 us -> 5.08 us  [put(): pl.pallas_call(functools.partial(put_kernel, spots, share), out_shape=sha...]
  transfers between devices with their start and end apart: 54 -> 57, of which waited for: 29 -> 31; matrix products, arithmetic and copies ran while one was open for 3% -> 3% of each run, Pallas kernels for 12% -> 13%
where the time goes in v2:
time: 213 us; the launch traced here: 212 us
  waiting for transfers between devices  96.1 us (45%)
  starting transfers between devices  57.2 us (27%)
  Pallas kernels  47.1 us (22%)
  local copies, waits for them, and re-layouts  6.84 us (3%)
  other arithmetic  4.34 us (2%)
    ppermute x57, waiting for transfers between devices, send(): return lax.ppermute(block, axis, [(i, i ^ shift) for i in range(count)])  96.1 us
    ppermute x57, starting transfers between devices, send(): return lax.ppermute(block, axis, [(i, i ^ shift) for i in range(count)])  57.2 us
    pallas_call x1, Pallas kernels, first(): pl.pallas_call(functools.partial(first_kernel, raw, tile), out_shape=tupl...  11.8 us
    pallas_call x1, Pallas kernels, second(): pl.pallas_call(second_kernel, out_shape=tuple((shape(rows, n, dtype=BF16)...  6.85 us
    dynamic_slice x3, local copies, waits for them, and re-layouts, run(): piece = lax.dynamic_slice(source, (0, (me ^ s) * share), (rows, share))  5.95 us
    pallas_call x1, Pallas kernels, own_gram(): pl.pallas_call(own_gram_kernel, out_shape=(half, half), grid_spec=pltpu.P...  5.4 us
    pallas_call x1, Pallas kernels, raw_merge(): pl.pallas_call(functools.partial(raw_merge_kernel, share), out_shape=shap...  5.17 us
    pallas_call x2, Pallas kernels, put(): pl.pallas_call(functools.partial(put_kernel, spots, share), out_shape=sha...  5.08 us
  transfers between devices with their start and end apart: 57, of which 31 were waited for; matrix products, arithmetic and copies ran while one was open for 3% of the time, Pallas kernels for 13%

profile of v2, /device:TPU:0, one launch (start us, length us, event | category | flops | bytes accessed | tf_op | source)
XLA Modules:
  0.0 212.1 jit_solution(7908152373983580939)
XLA Ops:
  1.3 3.0 %collective-permute-start.6 = (bf16[256,2048]{1,0:T(8,128)(2,1)S(1)}, bf16[256,2048]{1,0:T(8,128)(2,1)}, u32[]{:S(2)}, u32[]{:S(2)}) collective-permute-start(bf16[256,2048]{1,0:T(8,128)(2,1)S(1)} %dynamic-slice_bitcast_fusion), channel_id=1, source_target_pairs={{0,8},{8,0},{16,24},{24,16},{1,9},{9,1},{17,25},{25,17},{2,10},{10... | collective-permute-start | bytes 3145736 | tf_op jit(solution)/shard_map/ppermute | solution.py:25
  4.3 2.3 %constant_dynamic-slice_fusion.1 = bf16[256,2048]{1,0:T(8,128)(2,1)} fusion(bf16[256,8192]{1,0:T(8,128)(2,1)} %bitcast.22, s32[]{:T(128)S(6)} %select_n.23), kind=kLoop, calls=%fused_computation.23 | loop fusion | bytes 2097156 | tf_op jit(solution)/shard_map/dynamic_slice | solution.py:527
  6.6 2.4 %constant_dynamic-slice_fusion = bf16[256,2048]{1,0:T(8,128)(2,1)} fusion(bf16[256,8192]{1,0:T(8,128)(2,1)} %bitcast.23, s32[]{:T(128)S(6)} %select_n.24), kind=kLoop, calls=%fused_computation.22 | loop fusion | bytes 2097156 | tf_op jit(solution)/shard_map/dynamic_slice | solution.py:527
  11.1 5.4 %own_gram.1 = (f32[128,256]{1,0:T(8,128)}, f32[128,256]{1,0:T(8,128)}) custom-call(s32[2]{0:T(128)} %pad_add_fusion.place.refs_0_, bf16[256,8192]{1,0:T(8,128)(2,1)} %bitcast.24), custom_call_target="tpu_custom_call" | custom-call | flops 1073741824 | bytes 4194304 | tf_op jit(solution)/shard_map/own_gram/pallas_call | solution.py:135
  19.0 2.1 collective-permute-start.3
  21.1 2.6 %collective-permute-start.4 = (f32[128,256]{1,0:T(8,128)S(1)}, f32[128,256]{1,0:T(8,128)S(1)}, u32[]{:S(2)}, u32[]{:S(2)}) collective-permute-start(f32[128,256]{1,0:T(8,128)S(1)} %add.117), channel_id=1, source_target_pairs={{0,4},{1,5},{2,6},{3,7},{4,0},{5,1},{6,2},{7,3},{8,12},{9,13},{10,... | collective-permute-start | bytes 393224 | tf_op jit(solution)/shard_map/ppermute | solution.py:25
  23.7 3.4 %collective-permute-done.3 = f32[128,256]{1,0:T(8,128)S(1)} collective-permute-done((f32[128,256]{1,0:T(8,128)S(1)}, f32[128,256]{1,0:T(8,128)S(1)}, u32[]{:S(2)}, u32[]{:S(2)}) %collective-permute-start.3) | collective-permute-done | bytes 131104 | tf_op jit(solution)/shard_map/ppermute | solution.py:25
  27.1 3.2 %collective-permute-start.5 = (f32[128,256]{1,0:T(8,128)S(1)}, f32[128,256]{1,0:T(8,128)S(1)}, u32[]{:S(2)}, u32[]{:S(2)}) collective-permute-start(f32[128,256]{1,0:T(8,128)S(1)} %add.117), channel_id=1, source_target_pairs={{0,6},{1,7},{2,4},{3,5},{4,2},{5,3},{6,0},{7,1},{8,14},{9,15},{10,... | collective-permute-start | bytes 393224 | tf_op jit(solution)/shard_map/ppermute | solution.py:25
  30.2 3.6 %collective-permute-done.5 = f32[128,256]{1,0:T(8,128)S(1)} collective-permute-done((f32[128,256]{1,0:T(8,128)S(1)}, f32[128,256]{1,0:T(8,128)S(1)}, u32[]{:S(2)}, u32[]{:S(2)}) %collective-permute-start.5) | collective-permute-done | bytes 131104 | tf_op jit(solution)/shard_map/ppermute | solution.py:25
  34.5 5.0 %near_gram.1 = (f32[256,256]{1,0:T(8,128)}, bf16[4,256,384]{2,1,0:T(8,128)(2,1)}, bf16[4,256,384]{2,1,0:T(8,128)(2,1)}, bf16[256,384]{1,0:T(8,128)(2,1)}) custom-call(s32[2]{0:T(128)} %pad_add_fusion.place.refs_0_, bf16[256,8192]{1,0:T(8,128)(2,1)} %bitcast.25, bf16[256,2048]{1,0:T(8,128)(2,1)} %collective-permute-done.6.p1.refs_18_), custom_call_target="tpu_custom_call" | custom-call | flops 268435456 | bytes 2097152 | tf_op jit(solution)/shard_map/near_gram/pallas_call | solution.py:200
  39.5 11.9 %collective-permute-done.1.p3.refs_20_ = bf16[256,2048]{1,0:T(8,128)(2,1)} collective-permute-done((bf16[256,2048]{1,0:T(8,128)(2,1)}, bf16[256,2048]{1,0:T(8,128)(2,1)}, u32[]{:S(2)}, u32[]{:S(2)}) %collective-permute-start.1) | collective-permute-done | bytes 1048608 | tf_op jit(solution)/shard_map/ppermute | solution.py:25
  51.4 6.2 %collective-permute-done.p2.refs_19_ = bf16[256,2048]{1,0:T(8,128)(2,1)} collective-permute-done((bf16[256,2048]{1,0:T(8,128)(2,1)}, bf16[256,2048]{1,0:T(8,128)(2,1)}, u32[]{:S(2)}, u32[]{:S(2)}) %collective-permute-start) | collective-permute-done | bytes 1048608 | tf_op jit(solution)/shard_map/ppermute | solution.py:25
  57.6 4.4 %far_gram.1 = (f32[4,64,256]{2,1,0:T(8,128)}, f32[4,64,256]{2,1,0:T(8,128)}, bf16[4,256,384]{2,1,0:T(8,128)(2,1)}) custom-call(s32[2]{0:T(128)} %pad_add_fusion.place.refs_0_, f32[256,256]{1,0:T(8,128)} %get-tuple-element.57.near, bf16[256,2048]{1,0:T(8,128)(2,1)} %collective-permute-done.p2.refs_19_, ...), custom_call_target="tpu_custom_call", output_to_operand_aliasing={{2}: (4, {})} | custom-call | flops 268435456 | bytes 2097152 | tf_op jit(solution)/shard_map/far_gram/pallas_call | solution.py:236
  62.1 1.7 collective-permute-done.7
  69.1 2.2 %collective-permute-done.16 = f32[64,256]{1,0:T(8,128)S(1)} collective-permute-done((f32[64,256]{1,0:T(8,128)S(1)}, f32[64,256]{1,0:T(8,128)S(1)}, u32[]{:S(2)}, u32[]{:S(2)}) %collective-permute-start.16) | collective-permute-done | bytes 65568 | tf_op jit(solution)/shard_map/ppermute | solution.py:25
  72.0 1.6 collective-permute-start.18
  73.7 2.6 %collective-permute-start.19 = (f32[64,256]{1,0:T(8,128)S(1)}, f32[64,256]{1,0:T(8,128)S(1)}, u32[]{:S(2)}, u32[]{:S(2)}) collective-permute-start(f32[64,256]{1,0:T(8,128)S(1)} %add_add_fusion.4), channel_id=1, source_target_pairs={{0,4},{1,5},{2,6},{3,7},{4,0},{5,1},{6,2},{7,3},{8,12},{9,13},{10,... | collective-permute-start | bytes 196616 | tf_op jit(solution)/shard_map/ppermute | solution.py:25
  80.3 2.1 collective-permute-done.20
  88.2 3.7 %collective-permute-done.23.refs_12_ = f32[64,256]{1,0:T(8,128)S(1)} collective-permute-done((f32[64,256]{1,0:T(8,128)S(1)}, f32[64,256]{1,0:T(8,128)S(1)}, u32[]{:S(2)}, u32[]{:S(2)}) %collective-permute-start.23) | collective-permute-done | bytes 65568 | tf_op jit(solution)/shard_map/ppermute | solution.py:25
  94.5 11.8 %first.1 = (bf16[512,2048]{1,0:T(8,128)(2,1)}, bf16[512,384]{1,0:T(8,128)(2,1)}, bf16[512,256]{1,0:T(8,128)(2,1)}, bf16[2,256,512]{2,1,0:T(8,128)(2,1)}, f32[4,96,256]{2,1,0:T(8,128)}, /*index=5*/f32[4,96,256]{2,1,0:T(8,128)}) custom-call(s32[2]{0:T(128)} %pad_add_fusion.place.refs_0_, f32[128,256]{1,0:T(8,128)} %add_add_fusion.refs_1_, ...), custom_call_target="tpu_custom_call" | custom-call | flops 4563402752 | bytes 6291456 | tf_op jit(solution)/shard_map/first/pallas_call | solution.py:326
  115.5 2.8 %collective-permute-done.31 = f32[96,256]{1,0:T(8,128)S(1)} collective-permute-done((f32[96,256]{1,0:T(8,128)S(1)}, f32[96,256]{1,0:T(8,128)S(1)}, u32[]{:S(2)}, u32[]{:S(2)}) %collective-permute-start.31) | collective-permute-done | bytes 98336 | tf_op jit(solution)/shard_map/ppermute | solution.py:25
  118.4 3.3 %collective-permute-start.33 = (f32[96,256]{1,0:T(8,128)S(1)}, f32[96,256]{1,0:T(8,128)S(1)}, u32[]{:S(2)}, u32[]{:S(2)}) collective-permute-start(f32[96,256]{1,0:T(8,128)S(1)} %add_add_fusion.2), channel_id=1, source_target_pairs={{0,4},{1,5},{2,6},{3,7},{4,0},{5,1},{6,2},{7,3},{8,12},{9,13},{10,... | collective-permute-start | bytes 294920 | tf_op jit(solution)/shard_map/ppermute | solution.py:25
  124.1 3.1 %collective-permute-done.33 = f32[96,256]{1,0:T(8,128)S(1)} collective-permute-done((f32[96,256]{1,0:T(8,128)S(1)}, f32[96,256]{1,0:T(8,128)S(1)}, u32[]{:S(2)}, u32[]{:S(2)}) %collective-permute-start.33) | collective-permute-done | bytes 98336 | tf_op jit(solution)/shard_map/ppermute | solution.py:25
  131.8 7.5 %collective-permute-done.50.d = bf16[256,384]{1,0:T(8,128)(2,1)S(1)} collective-permute-done((bf16[256,384]{1,0:T(8,128)(2,1)S(1)}, bf16[256,384]{1,0:T(8,128)(2,1)S(1)}, u32[]{:S(2)}, u32[]{:S(2)}) %collective-permute-start.50) | collective-permute-done | bytes 196640 | tf_op jit(solution)/shard_map/ppermute | solution.py:25
  147.8 6.8 %second.1 = (bf16[256,512]{1,0:T(8,128)(2,1)}, bf16[256,512]{1,0:T(8,128)(2,1)}, bf16[256,1024]{1,0:T(8,128)(2,1)}, bf16[1,256,512]{2,1,0:T(8,128)(2,1)}) custom-call(s32[2]{0:T(128)} %pad_add_fusion.place.refs_0_, f32[96,256]{1,0:T(8,128)} %copy-done.8, f32[96,256]{1,0:T(8,128)} %copy-done.20, f32[96,256]{1,0:T(8,128)} %copy-done.21, f32[96,256]{1,0:T(8,128)} %copy-done.22, ...), custom_call_target="tpu_custom_call" | custom-call | flops 1879048192 | bytes 3145728 | tf_op jit(solution)/shard_map/second/pallas_call | solution.py:371
  155.6 7.9 %collective-permute-done.52.refs_1_ = bf16[512,384]{1,0:T(8,128)(2,1)S(1)} collective-permute-done((bf16[512,384]{1,0:T(8,128)(2,1)}, bf16[512,384]{1,0:T(8,128)(2,1)S(1)}, u32[]{:S(2)}, u32[]{:S(2)}) %collective-permute-start.52) | collective-permute-done | bytes 393248 | tf_op jit(solution)/shard_map/ppermute | solution.py:25
  168.8 22.8 %collective-permute-done.55.refs_4_ = bf16[512,256]{1,0:T(8,128)(2,1)S(1)} collective-permute-done((bf16[512,256]{1,0:T(8,128)(2,1)S(1)}, bf16[512,256]{1,0:T(8,128)(2,1)S(1)}, u32[]{:S(2)}, u32[]{:S(2)}) %collective-permute-start.55) | collective-permute-done | bytes 262176 | tf_op jit(solution)/shard_map/ppermute | solution.py:25
  194.5 2.9 %collective-permute-done.44.refs_1_ = bf16[256,512]{1,0:T(8,128)(2,1)} collective-permute-done((bf16[256,512]{1,0:T(8,128)(2,1)}, bf16[256,512]{1,0:T(8,128)(2,1)}, u32[]{:S(2)}, u32[]{:S(2)}) %collective-permute-start.44) | collective-permute-done | bytes 262176 | tf_op jit(solution)/shard_map/ppermute | solution.py:25
  198.2 3.4 %late.1._ = bf16[256,8192]{1,0:T(8,128)(2,1)} custom-call(s32[2]{0:T(128)} %pad_add_fusion.place.refs_0_, bf16[1,256,512]{2,1,0:T(8,128)(2,1)} %get-tuple-element.86.w.w1, bf16[256,512]{1,0:T(8,128)(2,1)} %get-tuple-element.83.a, bf16[256,512]{1,0:T(8,128)(2,1)} %get-tuple-element.84.b, bf16[256,1024]{1,0:T(8,128)(2,1)} %get-tuple-element.90.e, ...), custom_call_target="tpu_custom_call" | custom-call | flops 503316480 | bytes 2949120 | tf_op jit(solution)/shard_map/late/pallas_call | solution.py:412
  201.6 5.2 %raw_merge.1.refs_4_ = bf16[256,8192]{1,0:T(8,128)(2,1)} custom-call(s32[2]{0:T(128)} %pad_add_fusion.place.refs_0_, bf16[2,256,512]{2,1,0:T(8,128)(2,1)} %get-tuple-element.85.w0, bf16[1,256,512]{2,1,0:T(8,128)(2,1)} %get-tuple-element.86.w.w1, bf16[256,8192]{1,0:T(8,128)(2,1)} %bitcast.27, ...), custom_call_target="tpu_custom_call", output_to_operand_aliasing={{}: (7, {})} | custom-call | flops 905969664 | bytes 2949120 | tf_op jit(solution)/shard_map/raw_merge/pallas_call | solution.py:453
  206.8 2.6 %put.2.refs_2_ = bf16[256,8192]{1,0:T(8,128)(2,1)} custom-call(s32[2]{0:T(128)} %pad_add_fusion.place.refs_0_, bf16[256,512]{1,0:T(8,128)(2,1)} %collective-permute-done.42.refs_0_, bf16[256,512]{1,0:T(8,128)(2,1)} %collective-permute-done.44.refs_1_, bf16[256,512]{1,0:T(8,128)(2,1)} %collective-permute-done.46.refs_2_, ...), custom_call_target="tpu_custom_call", output_to_operand_aliasing={{}: (5, {})} | custom-call | bytes 2097152 | tf_op jit(solution)/shard_map/put/pallas_call | solution.py:490
  209.5 2.4 %put.3 = bf16[256,8192]{1,0:T(8,128)(2,1)} custom-call(s32[2]{0:T(128)} %pad_add_fusion.place.refs_0_, bf16[256,512]{1,0:T(8,128)(2,1)} %collective-permute-done.43.refs_0_, bf16[256,512]{1,0:T(8,128)(2,1)} %collective-permute-done.45.refs_1_, bf16[256,8192]{1,0:T(8,128)(2,1)} %put.2.refs_2_), custom_call_target="tpu_custom_call", output_to_operand_aliasing={{}: (3, {})} | custom-call | bytes 1048576 | tf_op jit(solution)/shard_map/put/pallas_call | solution.py:490
  (171 shorter events, 59.5 us)
Async XLA Ops:
  1.3 33.2 %collective-permute-start.6 = (bf16[256,2048]{1,0:T(8,128)(2,1)S(1)}, bf16[256,2048]{1,0:T(8,128)(2,1)}, u32[]{:S(2)}, u32[]{:S(2)}) collective-permute-start(bf16[256,2048]{1,0:T(8,128)(2,1)S(1)} %dynamic-slice_bitcast_fusion), channel_id=1, source_target_pairs={{0,8},{8,0},{16,24},{24,16},{1,9},{9,1},{17,25},{25,17},{2,10},{10... | collective-permute-start | bytes 3145736 | tf_op jit(solution)/shard_map/ppermute | solution.py:25
  9.0 42.4 %collective-permute-start.1 = (bf16[256,2048]{1,0:T(8,128)(2,1)}, bf16[256,2048]{1,0:T(8,128)(2,1)}, u32[]{:S(2)}, u32[]{:S(2)}) collective-permute-start(bf16[256,2048]{1,0:T(8,128)(2,1)} %constant_dynamic-slice_fusion), channel_id=1, source_target_pairs={{0,24},{8,16},{16,8},{24,0},{1,25},{9,17},{17,9},{25,1},{2,26},{10... | collective-permute-start | bytes 3145736 | tf_op jit(solution)/shard_map/ppermute | solution.py:25
  10.5 47.1 %collective-permute-start = (bf16[256,2048]{1,0:T(8,128)(2,1)}, bf16[256,2048]{1,0:T(8,128)(2,1)}, u32[]{:S(2)}, u32[]{:S(2)}) collective-permute-start(bf16[256,2048]{1,0:T(8,128)(2,1)} %constant_dynamic-slice_fusion.1), channel_id=1, source_target_pairs={{0,16},{8,24},{16,0},{24,8},{1,17},{9,25},{17,1},{25,9},{2,18},{10... | collective-permute-start | bytes 3145736 | tf_op jit(solution)/shard_map/ppermute | solution.py:25
  19.0 8.1 %collective-permute-start.3 = (f32[128,256]{1,0:T(8,128)S(1)}, f32[128,256]{1,0:T(8,128)S(1)}, u32[]{:S(2)}, u32[]{:S(2)}) collective-permute-start(f32[128,256]{1,0:T(8,128)S(1)} %add.117), channel_id=1, source_target_pairs={{0,2},{1,3},{2,0},{3,1},{4,6},{5,7},{6,4},{7,5},{8,10},{9,11},{10,... | collective-permute-start | bytes 393224 | tf_op jit(solution)/shard_map/ppermute | solution.py:25
  21.1 9.2 %collective-permute-start.4 = (f32[128,256]{1,0:T(8,128)S(1)}, f32[128,256]{1,0:T(8,128)S(1)}, u32[]{:S(2)}, u32[]{:S(2)}) collective-permute-start(f32[128,256]{1,0:T(8,128)S(1)} %add.117), channel_id=1, source_target_pairs={{0,4},{1,5},{2,6},{3,7},{4,0},{5,1},{6,2},{7,3},{8,12},{9,13},{10,... | collective-permute-start | bytes 393224 | tf_op jit(solution)/shard_map/ppermute | solution.py:25
  27.1 6.8 %collective-permute-start.5 = (f32[128,256]{1,0:T(8,128)S(1)}, f32[128,256]{1,0:T(8,128)S(1)}, u32[]{:S(2)}, u32[]{:S(2)}) collective-permute-start(f32[128,256]{1,0:T(8,128)S(1)} %add.117), channel_id=1, source_target_pairs={{0,6},{1,7},{2,4},{3,5},{4,2},{5,3},{6,0},{7,1},{8,14},{9,15},{10,... | collective-permute-start | bytes 393224 | tf_op jit(solution)/shard_map/ppermute | solution.py:25
  73.7 6.6 %collective-permute-start.19 = (f32[64,256]{1,0:T(8,128)S(1)}, f32[64,256]{1,0:T(8,128)S(1)}, u32[]{:S(2)}, u32[]{:S(2)}) collective-permute-start(f32[64,256]{1,0:T(8,128)S(1)} %add_add_fusion.4), channel_id=1, source_target_pairs={{0,4},{1,5},{2,6},{3,7},{4,0},{5,1},{6,2},{7,3},{8,12},{9,13},{10,... | collective-permute-start | bytes 196616 | tf_op jit(solution)/shard_map/ppermute | solution.py:25
  77.0 7.6 %collective-permute-start.9 = (f32[128,256]{1,0:T(8,128)}, f32[128,256]{1,0:T(8,128)S(1)}, u32[]{:S(2)}, u32[]{:S(2)}) collective-permute-start(f32[128,256]{1,0:T(8,128)} %add_add_fusion.refs_1_), channel_id=1, source_target_pairs={{0,16},{8,24},{16,0},{24,8},{1,17},{9,25},{17,1},{25,9},{2,18},{10... | collective-permute-start | bytes 393224 | tf_op jit(solution)/shard_map/ppermute | solution.py:25
  84.5 7.9 %collective-permute-start.12 = (f32[128,256]{1,0:T(8,128)S(1)}, f32[128,256]{1,0:T(8,128)S(1)}, u32[]{:S(2)}, u32[]{:S(2)}) collective-permute-start(f32[128,256]{1,0:T(8,128)S(1)} %collective-permute-done.8.refs_2_), channel_id=1, source_target_pairs={{0,1},{1,0},{2,3},{3,2},{4,5},{5,4},{6,7},{7,6},{8,9},{9,8},{10,11... | collective-permute-start | bytes 393224 | tf_op jit(solution)/shard_map/ppermute | solution.py:25
  84.8 7.7 %collective-permute-start.13 = (f32[128,256]{1,0:T(8,128)S(1)}, f32[128,256]{1,0:T(8,128)S(1)}, u32[]{:S(2)}, u32[]{:S(2)}) collective-permute-start(f32[128,256]{1,0:T(8,128)S(1)} %collective-permute-done.9.refs_3_), channel_id=1, source_target_pairs={{0,1},{1,0},{2,3},{3,2},{4,5},{5,4},{6,7},{7,6},{8,9},{9,8},{10,11... | collective-permute-start | bytes 393224 | tf_op jit(solution)/shard_map/ppermute | solution.py:25
  85.1 7.5 %collective-permute-start.14 = (f32[128,256]{1,0:T(8,128)S(1)}, f32[128,256]{1,0:T(8,128)S(1)}, u32[]{:S(2)}, u32[]{:S(2)}) collective-permute-start(f32[128,256]{1,0:T(8,128)S(1)} %collective-permute-done.10.refs_4_), channel_id=1, source_target_pairs={{0,1},{1,0},{2,3},{3,2},{4,5},{5,4},{6,7},{7,6},{8,9},{9,8},{10,11... | collective-permute-start | bytes 393224 | tf_op jit(solution)/shard_map/ppermute | solution.py:25
  111.6 6.7 %collective-permute-start.31 = (f32[96,256]{1,0:T(8,128)S(1)}, f32[96,256]{1,0:T(8,128)S(1)}, u32[]{:S(2)}, u32[]{:S(2)}) collective-permute-start(f32[96,256]{1,0:T(8,128)S(1)} %get-tuple-element.79), channel_id=1, source_target_pairs={{0,24},{8,16},{16,8},{24,0},{1,25},{9,17},{17,9},{25,1},{2,26},{10... | collective-permute-start | bytes 294920 | tf_op jit(solution)/shard_map/ppermute | solution.py:25
  113.0 28.1 %collective-permute-start.48 = (bf16[4,256,384]{2,1,0:T(8,128)(2,1)S(1)}, bf16[4,256,384]{2,1,0:T(8,128)(2,1)}, u32[]{:S(2)}, u32[]{:S(2)}) collective-permute-start(bf16[4,256,384]{2,1,0:T(8,128)(2,1)S(1)} %copy-done), channel_id=1, source_target_pairs={{0,8},{8,0},{16,24},{24,16},{1,9},{9,1},{17,25},{25,17},{2,10},{10... | collective-permute-start | bytes 2359304 | tf_op jit(solution)/shard_map/ppermute | solution.py:25
  118.4 8.8 %collective-permute-start.33 = (f32[96,256]{1,0:T(8,128)S(1)}, f32[96,256]{1,0:T(8,128)S(1)}, u32[]{:S(2)}, u32[]{:S(2)}) collective-permute-start(f32[96,256]{1,0:T(8,128)S(1)} %add_add_fusion.2), channel_id=1, source_target_pairs={{0,4},{1,5},{2,6},{3,7},{4,0},{5,1},{6,2},{7,3},{8,12},{9,13},{10,... | collective-permute-start | bytes 294920 | tf_op jit(solution)/shard_map/ppermute | solution.py:25
  121.7 6.5 %collective-permute-start.34 = (f32[96,256]{1,0:T(8,128)S(1)}, f32[96,256]{1,0:T(8,128)S(1)}, u32[]{:S(2)}, u32[]{:S(2)}) collective-permute-start(f32[96,256]{1,0:T(8,128)S(1)} %add_add_fusion.2), channel_id=1, source_target_pairs={{0,6},{1,7},{2,4},{3,5},{4,2},{5,3},{6,0},{7,1},{8,14},{9,15},{10,... | collective-permute-start | bytes 294920 | tf_op jit(solution)/shard_map/ppermute | solution.py:25
  122.8 16.6 %collective-permute-start.50 = (bf16[256,384]{1,0:T(8,128)(2,1)S(1)}, bf16[256,384]{1,0:T(8,128)(2,1)S(1)}, u32[]{:S(2)}, u32[]{:S(2)}) collective-permute-start(bf16[256,384]{1,0:T(8,128)(2,1)S(1)} %copy-done.12), channel_id=1, source_target_pairs={{0,24},{8,16},{16,8},{24,0},{1,25},{9,17},{17,9},{25,1},{2,26},{10... | collective-permute-start | bytes 589832 | tf_op jit(solution)/shard_map/ppermute | solution.py:25
  128.3 12.3 %collective-permute-start.35 = (f32[96,256]{1,0:T(8,128)S(1)}, f32[96,256]{1,0:T(8,128)S(1)}, u32[]{:S(2)}, u32[]{:S(2)}) collective-permute-start(f32[96,256]{1,0:T(8,128)S(1)} %add_add_fusion.1.refs_1_), channel_id=1, source_target_pairs={{0,8},{8,0},{16,24},{24,16},{1,9},{9,1},{17,25},{25,17},{2,10},{10... | collective-permute-start | bytes 294920 | tf_op jit(solution)/shard_map/ppermute | solution.py:25
  129.3 11.3 %collective-permute-start.36 = (f32[96,256]{1,0:T(8,128)S(1)}, f32[96,256]{1,0:T(8,128)S(1)}, u32[]{:S(2)}, u32[]{:S(2)}) collective-permute-start(f32[96,256]{1,0:T(8,128)S(1)} %add_add_fusion.1.refs_1_), channel_id=1, source_target_pairs={{0,16},{8,24},{16,0},{24,8},{1,17},{9,25},{17,1},{25,9},{2,18},{10... | collective-permute-start | bytes 294920 | tf_op jit(solution)/shard_map/ppermute | solution.py:25
  130.7 12.3 %collective-permute-start.37 = (f32[96,256]{1,0:T(8,128)S(1)}, f32[96,256]{1,0:T(8,128)S(1)}, u32[]{:S(2)}, u32[]{:S(2)}) collective-permute-start(f32[96,256]{1,0:T(8,128)S(1)} %add_add_fusion.1.refs_1_), channel_id=1, source_target_pairs={{0,24},{8,16},{16,8},{24,0},{1,25},{9,17},{17,9},{25,1},{2,26},{10... | collective-permute-start | bytes 294920 | tf_op jit(solution)/shard_map/ppermute | solution.py:25
  141.2 13.5 %collective-permute-start.51 = (bf16[512,384]{1,0:T(8,128)(2,1)}, bf16[512,384]{1,0:T(8,128)(2,1)S(1)}, u32[]{:S(2)}, u32[]{:S(2)}) collective-permute-start(bf16[512,384]{1,0:T(8,128)(2,1)} %get-tuple-element.91), channel_id=1, source_target_pairs={{0,8},{8,0},{16,24},{24,16},{1,9},{9,1},{17,25},{25,17},{2,10},{10... | collective-permute-start | bytes 1179656 | tf_op jit(solution)/shard_map/ppermute | solution.py:25
  142.9 20.6 %collective-permute-start.52 = (bf16[512,384]{1,0:T(8,128)(2,1)}, bf16[512,384]{1,0:T(8,128)(2,1)S(1)}, u32[]{:S(2)}, u32[]{:S(2)}) collective-permute-start(bf16[512,384]{1,0:T(8,128)(2,1)} %get-tuple-element.91), channel_id=1, source_target_pairs={{0,16},{8,24},{16,0},{24,8},{1,17},{9,25},{17,1},{25,9},{2,18},{10... | collective-permute-start | bytes 1179656 | tf_op jit(solution)/shard_map/ppermute | solution.py:25
  143.8 20.8 %collective-permute-start.53 = (bf16[512,384]{1,0:T(8,128)(2,1)}, bf16[512,384]{1,0:T(8,128)(2,1)S(1)}, u32[]{:S(2)}, u32[]{:S(2)}) collective-permute-start(bf16[512,384]{1,0:T(8,128)(2,1)} %get-tuple-element.91), channel_id=1, source_target_pairs={{0,24},{8,16},{16,8},{24,0},{1,25},{9,17},{17,9},{25,1},{2,26},{10... | collective-permute-start | bytes 1179656 | tf_op jit(solution)/shard_map/ppermute | solution.py:25
  145.3 56.4 %collective-permute-start.49 = (bf16[4,256,384]{2,1,0:T(8,128)(2,1)S(1)}, bf16[4,256,384]{2,1,0:T(8,128)(2,1)}, u32[]{:S(2)}, u32[]{:S(2)}) collective-permute-start(bf16[4,256,384]{2,1,0:T(8,128)(2,1)S(1)} %copy-done.10), channel_id=1, source_target_pairs={{0,16},{8,24},{16,0},{24,8},{1,17},{9,25},{17,1},{25,9},{2,18},{10... | collective-permute-start | bytes 2359304 | tf_op jit(solution)/shard_map/ppermute | solution.py:25
  146.5 20.9 %collective-permute-start.54 = (bf16[512,256]{1,0:T(8,128)(2,1)}, bf16[512,256]{1,0:T(8,128)(2,1)S(1)}, u32[]{:S(2)}, u32[]{:S(2)}) collective-permute-start(bf16[512,256]{1,0:T(8,128)(2,1)} %get-tuple-element.92), channel_id=1, source_target_pairs={{0,8},{8,0},{16,24},{24,16},{1,9},{9,1},{17,25},{25,17},{2,10},{10... | collective-permute-start | bytes 786440 | tf_op jit(solution)/shard_map/ppermute | solution.py:25
  154.7 37.0 %collective-permute-start.55 = (bf16[512,256]{1,0:T(8,128)(2,1)S(1)}, bf16[512,256]{1,0:T(8,128)(2,1)S(1)}, u32[]{:S(2)}, u32[]{:S(2)}) collective-permute-start(bf16[512,256]{1,0:T(8,128)(2,1)S(1)} %copy-done.11), channel_id=1, source_target_pairs={{0,16},{8,24},{16,0},{24,8},{1,17},{9,25},{17,1},{25,9},{2,18},{10... | collective-permute-start | bytes 786440 | tf_op jit(solution)/shard_map/ppermute | solution.py:25
  163.6 28.9 %collective-permute-start.56 = (bf16[512,256]{1,0:T(8,128)(2,1)S(1)}, bf16[512,256]{1,0:T(8,128)(2,1)S(1)}, u32[]{:S(2)}, u32[]{:S(2)}) collective-permute-start(bf16[512,256]{1,0:T(8,128)(2,1)S(1)} %copy-done.11), channel_id=1, source_target_pairs={{0,24},{8,16},{16,8},{24,0},{1,25},{9,17},{17,9},{25,1},{2,26},{10... | collective-permute-start | bytes 786440 | tf_op jit(solution)/shard_map/ppermute | solution.py:25
  164.6 28.7 %collective-permute-start.42 = (bf16[256,512]{1,0:T(8,128)(2,1)}, bf16[256,512]{1,0:T(8,128)(2,1)}, u32[]{:S(2)}, u32[]{:S(2)}) collective-permute-start(bf16[256,512]{1,0:T(8,128)(2,1)} %get-tuple-element.83.a), channel_id=1, source_target_pairs={{0,8},{8,0},{16,24},{24,16},{1,9},{9,1},{17,25},{25,17},{2,10},{10... | collective-permute-start | bytes 786440 | tf_op jit(solution)/shard_map/ppermute | solution.py:25
  167.4 29.9 %collective-permute-start.44 = (bf16[256,512]{1,0:T(8,128)(2,1)}, bf16[256,512]{1,0:T(8,128)(2,1)}, u32[]{:S(2)}, u32[]{:S(2)}) collective-permute-start(bf16[256,512]{1,0:T(8,128)(2,1)} %get-tuple-element.84.b), channel_id=1, source_target_pairs={{0,16},{8,24},{16,0},{24,8},{1,17},{9,25},{17,1},{25,9},{2,18},{10... | collective-permute-start | bytes 786440 | tf_op jit(solution)/shard_map/ppermute | solution.py:25
  191.7 15.2 %collective-permute-start.46 = (bf16[256,512]{1,0:T(8,128)(2,1)}, bf16[256,512]{1,0:T(8,128)(2,1)}, u32[]{:S(2)}, u32[]{:S(2)}) collective-permute-start(bf16[256,512]{1,0:T(8,128)(2,1)} %get-tuple-element.84.b), channel_id=1, source_target_pairs={{0,8},{8,0},{16,24},{24,16},{1,9},{9,1},{17,25},{25,17},{2,10},{10... | collective-permute-start | bytes 786440 | tf_op jit(solution)/shard_map/ppermute | solution.py:25
  192.5 14.3 %collective-permute-start.47 = (bf16[256,512]{1,0:T(8,128)(2,1)}, bf16[256,512]{1,0:T(8,128)(2,1)}, u32[]{:S(2)}, u32[]{:S(2)}) collective-permute-start(bf16[256,512]{1,0:T(8,128)(2,1)} %get-tuple-element.83.a), channel_id=1, source_target_pairs={{0,16},{8,24},{16,0},{24,8},{1,17},{9,25},{17,1},{25,9},{2,18},{10... | collective-permute-start | bytes 786440 | tf_op jit(solution)/shard_map/ppermute | solution.py:25
  193.3 16.2 %collective-permute-start.43 = (bf16[256,512]{1,0:T(8,128)(2,1)}, bf16[256,512]{1,0:T(8,128)(2,1)}, u32[]{:S(2)}, u32[]{:S(2)}) collective-permute-start(bf16[256,512]{1,0:T(8,128)(2,1)} %collective-permute-done.42.refs_0_), channel_id=1, source_target_pairs={{0,16},{8,24},{16,0},{24,8},{1,17},{9,25},{17,1},{25,9},{2,18},{10... | collective-permute-start | bytes 786440 | tf_op jit(solution)/shard_map/ppermute | solution.py:25
  197.4 12.1 %collective-permute-start.45 = (bf16[256,512]{1,0:T(8,128)(2,1)}, bf16[256,512]{1,0:T(8,128)(2,1)}, u32[]{:S(2)}, u32[]{:S(2)}) collective-permute-start(bf16[256,512]{1,0:T(8,128)(2,1)} %collective-permute-done.44.refs_1_), channel_id=1, source_target_pairs={{0,8},{8,0},{16,24},{24,16},{1,9},{9,1},{17,25},{25,17},{2,10},{10... | collective-permute-start | bytes 786440 | tf_op jit(solution)/shard_map/ppermute | solution.py:25
  (59 other events, 563.9 us)

commit v3 on v2

--- a/solution.py
+++ b/solution.py
@@ -214,20 +214,26 @@
     )(place, x, p1)
 
 
-def far_gram_kernel(chunk, place, near, p2, p3, _, keep_ref, give_ref, x_ref, block, acc, load, save):
+def far_gram_kernel(chunk, place, near, p2, p3, _, keep_out, give_out, x_ref, block, acc, keep_ref, give_ref, load, save):
     me, core = place[0], place[1]
+    first_load = pltpu.make_async_copy(near, acc.at[me // 2], save.at[3])
+    first_load.start()
     sources = tuple((s, lambda column, size, p=p: p.at[:, column : column + size]) for s, p in ((2, p2), (3, p3)))
-    acc[me // 2] = near[...]
     acc[1 - me // 2] = pair_gram(me, sources, block, load, chunk)
-    copy = pltpu.make_async_copy(block.at[(me ^ 2) % 2, :, : x_ref.shape[2]], x_ref.at[GROUP - 1], save)
-    copy.start()
+    copies = [pltpu.make_async_copy(block.at[(me ^ 2) % 2, :, : x_ref.shape[2]], x_ref.at[GROUP - 1], save.at[0])]
+    copies[0].start()
+    first_load.wait()
     part = keep_ref.shape[1]
     for s in range(GROUP):
         to = me ^ s
         pair, start = to // 2, (to % 2) * (CORES * part)
         keep_ref[s] = acc[pair, pl.ds(pl.multiple_of(start + core * part, part), part), :]
         give_ref[s] = acc[pair, pl.ds(pl.multiple_of(start + (1 - core) * part, part), part), :]
-    copy.wait()
+    for i, (source, target) in enumerate(((give_ref, give_out), (keep_ref, keep_out))):
+        copies.append(pltpu.make_async_copy(source, target, save.at[1 + i]))
+        copies[-1].start()
+    for copy in copies:
+        copy.wait()
 
 
 def far_gram(place, near, p2, p3, message, chunk=512):
@@ -236,13 +242,15 @@
     return pl.pallas_call(
         functools.partial(far_gram_kernel, chunk),
         out_shape=(out, out, shape(*message.shape, dtype=BF16)),
-        in_specs=[SMEM, VMEM, HBM, HBM, HBM],
-        out_specs=(VMEM, VMEM, HBM),
+        in_specs=[SMEM, HBM, HBM, HBM, HBM],
+        out_specs=(HBM, HBM, HBM),
         scratch_shapes=[
             pltpu.VMEM((2, rows, share), BF16),
             pltpu.VMEM((GROUP // 2, rows, rows), F32),
+            pltpu.VMEM(out.shape, F32),
+            pltpu.VMEM(out.shape, F32),
             pltpu.SemaphoreType.DMA((2 * share // chunk,)),
-            pltpu.SemaphoreType.DMA,
+            pltpu.SemaphoreType.DMA((4,)),
         ],
         input_output_aliases={4: 2},
         cost_estimate=cost(2 * rows * rows * share, 4 * rows * share),
@@ -266,7 +274,7 @@
 
 def first_kernel(raw, tile, *refs):
     place, tails, crosses, (x, p1, p2, p3), refs = refs[0], refs[1:9], refs[9:17], refs[17:21], refs[21:]
-    m_ref, e_ref, f_ref, w, keep_ref, give_ref, cross, diag, inverse, block, m, acc, load, save = refs
+    m_ref, e_ref, f_ref, w, keep_out, give_out, cross, diag, inverse, block, m, acc, keep_ref, give_ref, load, save = refs
     me, core = place[0], place[1]
     rows, share = p1.shape
     sources = [x.at[:, pl.ds(pl.multiple_of(me * share, share), share)], p1, p2, p3]
@@ -308,13 +316,20 @@
         saves.append(pltpu.make_async_copy(source, ref, save.at[share // tile + i]))
         saves[-1].start()
         start += ref.shape[1]
+    lower = lax.broadcasted_iota(jnp.int32, (rows, rows), 0) >= lax.broadcasted_iota(jnp.int32, (rows, rows), 1)
+    row = jnp.sum(jnp.where(eye_mask(rows), acc[2], 0.0), axis=0, keepdims=True)
+    acc[2] = jnp.where(lower, acc[0], acc[2])
     part = rows // (GROUP * CORES)
     for s in range(GROUP):
         to = me ^ s
-        for b in range(3):
-            here = pl.ds(b * part, part)
-            keep_ref[s, here, :] = acc[b, pl.ds(pl.multiple_of((to * CORES + core) * part, part), part), :]
-            give_ref[s, here, :] = acc[b, pl.ds(pl.multiple_of((to * CORES + 1 - core) * part, part), part), :]
+        for ref, seat in ((give_ref, to * CORES + 1 - core), (keep_ref, to * CORES + core)):
+            here = pl.ds(pl.multiple_of(seat * part, part), part)
+            ref[s, :part] = acc[1, here, :]
+            ref[s, part : 2 * part] = acc[2, here, :]
+            ref[s, 2 * part :] = jnp.broadcast_to(row, (8, rows))
+    for i, (source, target) in enumerate(((give_ref, give_out), (keep_ref, keep_out))):
+        saves.append(pltpu.make_async_copy(source, target, save.at[share // tile + 2 + i]))
+        saves[-1].start()
     for copy in saves:
         copy.wait()
 
@@ -322,12 +337,12 @@
 def first(place, diagonals, crosses, x, pieces, raw, ahead, tile=512):
     rows, share = pieces[0].shape
     pairs = GROUP // 2
-    out = shape(GROUP, 3 * rows // (GROUP * CORES), rows)
+    out = shape(GROUP, 2 * rows // (GROUP * CORES) + 8, rows)
     return pl.pallas_call(
         functools.partial(first_kernel, raw, tile),
         out_shape=tuple(shape(pairs * rows, n, dtype=BF16) for n in (share, *ahead)) + (shape(pairs, rows, 2 * rows, dtype=BF16), out, out),
         in_specs=[SMEM] + [VMEM] * (4 * GROUP) + [HBM] * 4,
-        out_specs=(ANY, ANY, ANY, VMEM, VMEM, VMEM),
+        out_specs=(ANY, ANY, ANY, VMEM, ANY, ANY),
         scratch_shapes=[
             pltpu.VMEM((pairs, rows, rows), F32),
             pltpu.VMEM((GROUP, rows, rows), F32),
@@ -335,8 +350,10 @@
             pltpu.VMEM((GROUP * rows, share), BF16),
             pltpu.VMEM((pairs * rows, share), BF16),
             pltpu.VMEM((3, rows, rows), F32),
+            pltpu.VMEM(out.shape, F32),
+            pltpu.VMEM(out.shape, F32),
             pltpu.SemaphoreType.DMA((GROUP,)),
-            pltpu.SemaphoreType.DMA((share // tile + 2,)),
+            pltpu.SemaphoreType.DMA((share // tile + 4,)),
         ],
         cost_estimate=cost(2 * pairs * rows**3 * 40 + 14 * rows * rows * share, 12 * rows * share),
         name="first",
@@ -354,9 +371,14 @@
     for c in range(CORES):
         for s in range(GROUP):
             seat = (me ^ s) * CORES + (core ^ c)
-            for b in range(3):
+            for b in range(2):
                 gram[b, pl.ds(pl.multiple_of(seat * part, part), part), :] = bundles[c * GROUP + s][b * part : (b + 1) * part]
-    resolvent([(gram[0], gram[1], gram[2])], inverse, w_ref)
+    packed = gram[1]
+    turned = packed.T
+    lower = lax.broadcasted_iota(jnp.int32, (rows, rows), 0) >= lax.broadcasted_iota(jnp.int32, (rows, rows), 1)
+    diagonal = jnp.broadcast_to(bundles[0][2 * part : 2 * part + 1], (rows, rows))
+    upper_gram = jnp.where(eye_mask(rows), diagonal, jnp.where(lower, turned, packed))
+    resolvent([(jnp.where(lower, packed, turned), gram[0], upper_gram)], inverse, w_ref)
     copy.wait()
     start = 0
     for ref in (e_ref, a_ref, b_ref):
@@ -374,7 +396,7 @@
         in_specs=[SMEM] + [VMEM] * (2 * GROUP) + [ANY],
         out_specs=(VMEM,) * 4,
         scratch_shapes=[
-            pltpu.VMEM((3, rows, rows), F32),
+            pltpu.VMEM((2, rows, rows), F32),
             pltpu.VMEM((1, rows, rows), F32),
             pltpu.VMEM(m.shape, BF16),
             pltpu.SemaphoreType.DMA,
@@ -522,11 +544,12 @@
     me = lax.axis_index("dp") % GROUP
     place = jnp.stack([me, lax.axis_index("feat") % CORES]).astype(jnp.int32)
 
-    pieces, source = {}, x
+    cuts, source = {}, x
     for s in PEERS:
-        piece = lax.dynamic_slice(source, (0, (me ^ s) * share), (rows, share))
-        source, piece = lax.optimization_barrier((source, piece))
-        pieces[s] = send(piece, "dp", s)
+        cuts[s] = lax.dynamic_slice(source, (0, (me ^ s) * share), (rows, share))
+        if s == 2:
+            source, cuts = lax.optimization_barrier((source, cuts))
+    pieces = {s: send(cut, "dp", s) for s, cut in cuts.items()}
     keep, give = own_gram(place, x)
     own = over_chips(total([keep, send(give, "feat", 1)]))
     near, to_x, to_y, to_d = near_gram(place, x, pieces[1], raw)
@@ -561,7 +584,8 @@
     out = late(place, w1, a, b, e, pairs, raw, share)
     out = raw_merge(place, w0, w1, x, messages, out, share)
     out = put(place, out, [ax, by, bx, ay], ((1, left), (2, right), (1, right), (2, left)), share)
-    out = put(place, out, [ad, bd], ((3, left), (3, right)), share)
+    for block, column in ((ad, left), (bd, right)):
+        out = lax.dynamic_update_slice(out, block, (0, (me ^ 3) * share + column))
     return out[None]
 
 

time: 213 us -> 209 us (0.981)
  Pallas kernels: 47.1 us -> 44 us
  local copies, waits for them, and re-layouts: 6.84 us -> 9.32 us
  waiting for transfers between devices: 96.1 us -> 93.9 us
    dynamic_update_slice x0 -> x2, local copies, waits for them, and re-layouts: none -> 3.34 us  [run(): out = lax.dynamic_update_slice(out, block, (0, (me ^ 3) * share + column))]
    pallas_call x2 -> x1, Pallas kernels: 5.08 us -> 2.65 us  [put(): pl.pallas_call(functools.partial(put_kernel, spots, share), out_shape=sha...]
    ppermute x57, waiting for transfers between devices: 96.1 us -> 93.9 us  [send(): return lax.ppermute(block, axis, [(i, i ^ shift) for i in range(count)])]
    dynamic_slice x3 -> x2, local copies, waits for them, and re-layouts: 5.95 us -> 5.08 us  [run(): cuts[s] = lax.dynamic_slice(source, (0, (me ^ s) * share), (rows, share))]
  transfers between devices with their start and end apart: 57 -> 57, of which waited for: 31 -> 31; matrix products, arithmetic and copies ran while one was open for 3% -> 3% of each run, Pallas kernels for 13% -> 14%
where the time goes in v3:
time: 209 us
  waiting for transfers between devices  93.9 us (45%)
  starting transfers between devices  56.6 us (27%)
  Pallas kernels  44 us (21%)
  local copies, waits for them, and re-layouts  9.32 us (4%)
  other arithmetic  4.41 us (2%)
    ppermute x57, waiting for transfers between devices, send(): return lax.ppermute(block, axis, [(i, i ^ shift) for i in range(count)])  93.9 us
    ppermute x57, starting transfers between devices, send(): return lax.ppermute(block, axis, [(i, i ^ shift) for i in range(count)])  56.6 us
    pallas_call x1, Pallas kernels, first(): pl.pallas_call(functools.partial(first_kernel, raw, tile), out_shape=tupl...  11.8 us
    pallas_call x1, Pallas kernels, second(): pl.pallas_call(second_kernel, out_shape=tuple((shape(rows, n, dtype=BF16)...  6.91 us
    pallas_call x1, Pallas kernels, own_gram(): pl.pallas_call(own_gram_kernel, out_shape=(half, half), grid_spec=pltpu.P...  5.39 us
    pallas_call x1, Pallas kernels, raw_merge(): pl.pallas_call(functools.partial(raw_merge_kernel, share), out_shape=shap...  5.16 us
    dynamic_slice x2, local copies, waits for them, and re-layouts, run(): cuts[s] = lax.dynamic_slice(source, (0, (me ^ s) * share), (rows, share))  5.08 us
    pallas_call x1, Pallas kernels, near_gram(): pl.pallas_call(functools.partial(near_gram_kernel, chunk), out_shape=(sha...  5 us
  transfers between devices with their start and end apart: 57, of which 31 were waited for; matrix products, arithmetic and copies ran while one was open for 3% of the time, Pallas kernels for 14%

profile of v3, /device:TPU:0, one launch (start us, length us, event | category | flops | bytes accessed | tf_op | source)
XLA Modules:
  0.0 208.7 jit_solution(4940505959688690899)
XLA Ops:
  0.0 2.7 %dynamic-slice_bitcast_fusion = (bf16[256,2048]{1,0:T(8,128)(2,1)}, bf16[256,2048]{1,0:T(8,128)(2,1)S(1)}) fusion(bf16[1,256,8192]{2,1,0:T(8,128)(2,1)} %param.1, s32[]{:T(128)S(6)} %select_n.29, s32[]{:T(128)S(6)} %select_n.28), kind=kLoop, calls=%fused_computation | loop fusion | bytes 4194312 | tf_op jit(solution)/shard_map/dynamic_slice | solution.py:549
  2.7 3.0 %collective-permute-start.6 = (bf16[256,2048]{1,0:T(8,128)(2,1)S(1)}, bf16[256,2048]{1,0:T(8,128)(2,1)}, u32[]{:S(2)}, u32[]{:S(2)}) collective-permute-start(bf16[256,2048]{1,0:T(8,128)(2,1)S(1)} %get-tuple-element.51), channel_id=1, source_target_pairs={{0,8},{8,0},{16,24},{24,16},{1,9},{9,1},{17,25},{25,17},{2,10},{10... | collective-permute-start | bytes 3145736 | tf_op jit(solution)/shard_map/ppermute | solution.py:25
  5.7 2.4 %constant_dynamic-slice_fusion = bf16[256,2048]{1,0:T(8,128)(2,1)} fusion(bf16[256,8192]{1,0:T(8,128)(2,1)} %bitcast.28, s32[]{:T(128)S(6)} %select_n.30), kind=kLoop, calls=%fused_computation.25 | loop fusion | bytes 2097156 | tf_op jit(solution)/shard_map/dynamic_slice | solution.py:549
  10.2 5.4 %own_gram.1 = (f32[128,256]{1,0:T(8,128)}, f32[128,256]{1,0:T(8,128)}) custom-call(s32[2]{0:T(128)} %pad_add_fusion.place.refs_0_, bf16[256,8192]{1,0:T(8,128)(2,1)} %bitcast.29), custom_call_target="tpu_custom_call" | custom-call | flops 1073741824 | bytes 4194304 | tf_op jit(solution)/shard_map/own_gram/pallas_call | solution.py:135
  18.1 2.1 %collective-permute-start.3 = (f32[128,256]{1,0:T(8,128)S(1)}, f32[128,256]{1,0:T(8,128)S(1)}, u32[]{:S(2)}, u32[]{:S(2)}) collective-permute-start(f32[128,256]{1,0:T(8,128)S(1)} %add.133), channel_id=1, source_target_pairs={{0,2},{1,3},{2,0},{3,1},{4,6},{5,7},{6,4},{7,5},{8,10},{9,11},{10,... | collective-permute-start | bytes 393224 | tf_op jit(solution)/shard_map/ppermute | solution.py:25
  20.2 2.6 %collective-permute-start.4 = (f32[128,256]{1,0:T(8,128)S(1)}, f32[128,256]{1,0:T(8,128)S(1)}, u32[]{:S(2)}, u32[]{:S(2)}) collective-permute-start(f32[128,256]{1,0:T(8,128)S(1)} %add.133), channel_id=1, source_target_pairs={{0,4},{1,5},{2,6},{3,7},{4,0},{5,1},{6,2},{7,3},{8,12},{9,13},{10,... | collective-permute-start | bytes 393224 | tf_op jit(solution)/shard_map/ppermute | solution.py:25
  22.8 3.4 %collective-permute-done.3 = f32[128,256]{1,0:T(8,128)S(1)} collective-permute-done((f32[128,256]{1,0:T(8,128)S(1)}, f32[128,256]{1,0:T(8,128)S(1)}, u32[]{:S(2)}, u32[]{:S(2)}) %collective-permute-start.3) | collective-permute-done | bytes 131104 | tf_op jit(solution)/shard_map/ppermute | solution.py:25
  26.2 3.1 %collective-permute-start.5 = (f32[128,256]{1,0:T(8,128)S(1)}, f32[128,256]{1,0:T(8,128)S(1)}, u32[]{:S(2)}, u32[]{:S(2)}) collective-permute-start(f32[128,256]{1,0:T(8,128)S(1)} %add.133), channel_id=1, source_target_pairs={{0,6},{1,7},{2,4},{3,5},{4,2},{5,3},{6,0},{7,1},{8,14},{9,15},{10,... | collective-permute-start | bytes 393224 | tf_op jit(solution)/shard_map/ppermute | solution.py:25
  29.4 3.7 %collective-permute-done.5 = f32[128,256]{1,0:T(8,128)S(1)} collective-permute-done((f32[128,256]{1,0:T(8,128)S(1)}, f32[128,256]{1,0:T(8,128)S(1)}, u32[]{:S(2)}, u32[]{:S(2)}) %collective-permute-start.5) | collective-permute-done | bytes 131104 | tf_op jit(solution)/shard_map/ppermute | solution.py:25
  33.8 5.0 %near_gram.1 = (f32[256,256]{1,0:T(8,128)}, bf16[4,256,384]{2,1,0:T(8,128)(2,1)}, bf16[4,256,384]{2,1,0:T(8,128)(2,1)}, bf16[256,384]{1,0:T(8,128)(2,1)}) custom-call(s32[2]{0:T(128)} %pad_add_fusion.place.refs_0_, bf16[256,8192]{1,0:T(8,128)(2,1)} %bitcast.30, bf16[256,2048]{1,0:T(8,128)(2,1)} %collective-permute-done.6.p1.refs_18_), custom_call_target="tpu_custom_call" | custom-call | flops 268435456 | bytes 2097152 | tf_op jit(solution)/shard_map/near_gram/pallas_call | solution.py:200
  38.8 13.9 %collective-permute-done.1.p3.refs_20_ = bf16[256,2048]{1,0:T(8,128)(2,1)} collective-permute-done((bf16[256,2048]{1,0:T(8,128)(2,1)}, bf16[256,2048]{1,0:T(8,128)(2,1)}, u32[]{:S(2)}, u32[]{:S(2)}) %collective-permute-start.1) | collective-permute-done | bytes 1048608 | tf_op jit(solution)/shard_map/ppermute | solution.py:25
  52.7 3.9 %collective-permute-done.p2.refs_19_ = bf16[256,2048]{1,0:T(8,128)(2,1)} collective-permute-done((bf16[256,2048]{1,0:T(8,128)(2,1)}, bf16[256,2048]{1,0:T(8,128)(2,1)}, u32[]{:S(2)}, u32[]{:S(2)}) %collective-permute-start) | collective-permute-done | bytes 1048608 | tf_op jit(solution)/shard_map/ppermute | solution.py:25
  56.7 3.8 %far_gram.1 = (f32[4,64,256]{2,1,0:T(8,128)}, f32[4,64,256]{2,1,0:T(8,128)}, bf16[4,256,384]{2,1,0:T(8,128)(2,1)}) custom-call(s32[2]{0:T(128)} %pad_add_fusion.place.refs_0_, f32[256,256]{1,0:T(8,128)} %get-tuple-element.53.near, bf16[256,2048]{1,0:T(8,128)(2,1)} %collective-permute-done.p2.refs_19_, ...), custom_call_target="tpu_custom_call", output_to_operand_aliasing={{2}: (4, {})} | custom-call | flops 268435456 | bytes 2097152 | tf_op jit(solution)/shard_map/far_gram/pallas_call | solution.py:242
  60.5 1.7 collective-permute-done.7
  67.5 2.2 %collective-permute-done.16 = f32[64,256]{1,0:T(8,128)S(1)} collective-permute-done((f32[64,256]{1,0:T(8,128)S(1)}, f32[64,256]{1,0:T(8,128)S(1)}, u32[]{:S(2)}, u32[]{:S(2)}) %collective-permute-start.16) | collective-permute-done | bytes 65568 | tf_op jit(solution)/shard_map/ppermute | solution.py:25
  72.1 2.6 %collective-permute-start.19 = (f32[64,256]{1,0:T(8,128)S(1)}, f32[64,256]{1,0:T(8,128)S(1)}, u32[]{:S(2)}, u32[]{:S(2)}) collective-permute-start(f32[64,256]{1,0:T(8,128)S(1)} %add_add_fusion.4), channel_id=1, source_target_pairs={{0,4},{1,5},{2,6},{3,7},{4,0},{5,1},{6,2},{7,3},{8,12},{9,13},{10,... | collective-permute-start | bytes 196616 | tf_op jit(solution)/shard_map/ppermute | solution.py:25
  78.7 2.1 collective-permute-done.20
  86.7 3.7 %collective-permute-done.23.refs_12_ = f32[64,256]{1,0:T(8,128)S(1)} collective-permute-done((f32[64,256]{1,0:T(8,128)S(1)}, f32[64,256]{1,0:T(8,128)S(1)}, u32[]{:S(2)}, u32[]{:S(2)}) %collective-permute-start.23) | collective-permute-done | bytes 65568 | tf_op jit(solution)/shard_map/ppermute | solution.py:25
  93.0 11.8 %first.1 = (bf16[512,2048]{1,0:T(8,128)(2,1)}, bf16[512,384]{1,0:T(8,128)(2,1)}, bf16[512,256]{1,0:T(8,128)(2,1)}, bf16[2,256,512]{2,1,0:T(8,128)(2,1)}, f32[4,72,256]{2,1,0:T(8,128)}, /*index=5*/f32[4,72,256]{2,1,0:T(8,128)}) custom-call(s32[2]{0:T(128)} %pad_add_fusion.place.refs_0_, f32[128,256]{1,0:T(8,128)} %add_add_fusion.refs_1_, ...), custom_call_target="tpu_custom_call" | custom-call | flops 4563402752 | bytes 6291456 | tf_op jit(solution)/shard_map/first/pallas_call | solution.py:341
  112.8 3.0 %collective-permute-done.31 = f32[72,256]{1,0:T(8,128)S(1)} collective-permute-done((f32[72,256]{1,0:T(8,128)S(1)}, f32[72,256]{1,0:T(8,128)S(1)}, u32[]{:S(2)}, u32[]{:S(2)}) %collective-permute-start.31) | collective-permute-done | bytes 73760 | tf_op jit(solution)/shard_map/ppermute | solution.py:25
  115.9 3.5 %collective-permute-start.33 = (f32[72,256]{1,0:T(8,128)S(1)}, f32[72,256]{1,0:T(8,128)S(1)}, u32[]{:S(2)}, u32[]{:S(2)}) collective-permute-start(f32[72,256]{1,0:T(8,128)S(1)} %add_add_fusion.2), channel_id=1, source_target_pairs={{0,4},{1,5},{2,6},{3,7},{4,0},{5,1},{6,2},{7,3},{8,12},{9,13},{10,... | collective-permute-start | bytes 221192 | tf_op jit(solution)/shard_map/ppermute | solution.py:25
  123.3 2.2 %collective-permute-done.34 = f32[72,256]{1,0:T(8,128)S(1)} collective-permute-done((f32[72,256]{1,0:T(8,128)S(1)}, f32[72,256]{1,0:T(8,128)S(1)}, u32[]{:S(2)}, u32[]{:S(2)}) %collective-permute-start.34) | collective-permute-done | bytes 73760 | tf_op jit(solution)/shard_map/ppermute | solution.py:25
  127.1 2.0 collective-permute-start.37
  129.2 7.7 %collective-permute-done.48.d = bf16[256,384]{1,0:T(8,128)(2,1)S(1)} collective-permute-done((bf16[256,384]{1,0:T(8,128)(2,1)S(1)}, bf16[256,384]{1,0:T(8,128)(2,1)S(1)}, u32[]{:S(2)}, u32[]{:S(2)}) %collective-permute-start.48) | collective-permute-done | bytes 196640 | tf_op jit(solution)/shard_map/ppermute | solution.py:25
  141.0 1.9 collective-permute-start.51
  144.6 6.9 %second.1 = (bf16[256,512]{1,0:T(8,128)(2,1)}, bf16[256,512]{1,0:T(8,128)(2,1)}, bf16[256,1024]{1,0:T(8,128)(2,1)}, bf16[1,256,512]{2,1,0:T(8,128)(2,1)}) custom-call(s32[2]{0:T(128)} %pad_add_fusion.place.refs_0_, f32[72,256]{1,0:T(8,128)} %copy-done.8, f32[72,256]{1,0:T(8,128)} %copy-done.20, f32[72,256]{1,0:T(8,128)} %copy-done.21, f32[72,256]{1,0:T(8,128)} %copy-done.22, ...), custom_call_target="tpu_custom_call" | custom-call | flops 1879048192 | bytes 3145728 | tf_op jit(solution)/shard_map/second/pallas_call | solution.py:393
  153.2 8.0 %collective-permute-done.50.refs_1_ = bf16[512,384]{1,0:T(8,128)(2,1)S(1)} collective-permute-done((bf16[512,384]{1,0:T(8,128)(2,1)}, bf16[512,384]{1,0:T(8,128)(2,1)S(1)}, u32[]{:S(2)}, u32[]{:S(2)}) %collective-permute-start.50) | collective-permute-done | bytes 393248 | tf_op jit(solution)/shard_map/ppermute | solution.py:25
  163.1 2.6 %collective-permute-done.52.refs_3_ = bf16[512,256]{1,0:T(8,128)(2,1)S(1)} collective-permute-done((bf16[512,256]{1,0:T(8,128)(2,1)}, bf16[512,256]{1,0:T(8,128)(2,1)S(1)}, u32[]{:S(2)}, u32[]{:S(2)}) %collective-permute-start.52) | collective-permute-done | bytes 262176 | tf_op jit(solution)/shard_map/ppermute | solution.py:25
  166.2 23.0 %collective-permute-done.53.refs_4_ = bf16[512,256]{1,0:T(8,128)(2,1)S(1)} collective-permute-done((bf16[512,256]{1,0:T(8,128)(2,1)S(1)}, bf16[512,256]{1,0:T(8,128)(2,1)S(1)}, u32[]{:S(2)}, u32[]{:S(2)}) %collective-permute-start.53) | collective-permute-done | bytes 262176 | tf_op jit(solution)/shard_map/ppermute | solution.py:25
  192.2 3.4 %late.1._ = bf16[256,8192]{1,0:T(8,128)(2,1)} custom-call(s32[2]{0:T(128)} %pad_add_fusion.place.refs_0_, bf16[1,256,512]{2,1,0:T(8,128)(2,1)} %get-tuple-element.82.w.w1, bf16[256,512]{1,0:T(8,128)(2,1)} %get-tuple-element.79.a, bf16[256,512]{1,0:T(8,128)(2,1)} %get-tuple-element.80.b, bf16[256,1024]{1,0:T(8,128)(2,1)} %get-tuple-element.86.e, ...), custom_call_target="tpu_custom_call" | custom-call | flops 503316480 | bytes 2949120 | tf_op jit(solution)/shard_map/late/pallas_call | solution.py:434
  196.8 5.2 %raw_merge.1.refs_4_ = bf16[256,8192]{1,0:T(8,128)(2,1)} custom-call(s32[2]{0:T(128)} %pad_add_fusion.place.refs_0_, bf16[2,256,512]{2,1,0:T(8,128)(2,1)} %get-tuple-element.81.w0, bf16[1,256,512]{2,1,0:T(8,128)(2,1)} %get-tuple-element.82.w.w1, bf16[256,8192]{1,0:T(8,128)(2,1)} %bitcast.32, ...), custom_call_target="tpu_custom_call", output_to_operand_aliasing={{}: (7, {})} | custom-call | flops 905969664 | bytes 2949120 | tf_op jit(solution)/shard_map/raw_merge/pallas_call | solution.py:475
  202.0 2.6 %put.1 = bf16[256,8192]{1,0:T(8,128)(2,1)} custom-call(s32[2]{0:T(128)} %pad_add_fusion.place.refs_0_, bf16[256,512]{1,0:T(8,128)(2,1)} %collective-permute-done.42.refs_0_, bf16[256,512]{1,0:T(8,128)(2,1)} %collective-permute-done.43.refs_1_, bf16[256,512]{1,0:T(8,128)(2,1)} %collective-permute-done.44.refs_2_, ...), custom_call_target="tpu_custom_call", output_to_operand_aliasing={{}: (5, {})} | custom-call | bytes 2097152 | tf_op jit(solution)/shard_map/put/pallas_call | solution.py:512
  (171 shorter events, 57.4 us)
Async XLA Ops:
  2.7 31.1 %collective-permute-start.6 = (bf16[256,2048]{1,0:T(8,128)(2,1)S(1)}, bf16[256,2048]{1,0:T(8,128)(2,1)}, u32[]{:S(2)}, u32[]{:S(2)}) collective-permute-start(bf16[256,2048]{1,0:T(8,128)(2,1)S(1)} %get-tuple-element.51), channel_id=1, source_target_pairs={{0,8},{8,0},{16,24},{24,16},{1,9},{9,1},{17,25},{25,17},{2,10},{10... | collective-permute-start | bytes 3145736 | tf_op jit(solution)/shard_map/ppermute | solution.py:25
  8.0 44.7 %collective-permute-start.1 = (bf16[256,2048]{1,0:T(8,128)(2,1)}, bf16[256,2048]{1,0:T(8,128)(2,1)}, u32[]{:S(2)}, u32[]{:S(2)}) collective-permute-start(bf16[256,2048]{1,0:T(8,128)(2,1)} %constant_dynamic-slice_fusion), channel_id=1, source_target_pairs={{0,24},{8,16},{16,8},{24,0},{1,25},{9,17},{17,9},{25,1},{2,26},{10... | collective-permute-start | bytes 3145736 | tf_op jit(solution)/shard_map/ppermute | solution.py:25
  9.5 47.1 %collective-permute-start = (bf16[256,2048]{1,0:T(8,128)(2,1)}, bf16[256,2048]{1,0:T(8,128)(2,1)}, u32[]{:S(2)}, u32[]{:S(2)}) collective-permute-start(bf16[256,2048]{1,0:T(8,128)(2,1)} %get-tuple-element.47), channel_id=1, source_target_pairs={{0,16},{8,24},{16,0},{24,8},{1,17},{9,25},{17,1},{25,9},{2,18},{10... | collective-permute-start | bytes 3145736 | tf_op jit(solution)/shard_map/ppermute | solution.py:25
  18.1 8.1 %collective-permute-start.3 = (f32[128,256]{1,0:T(8,128)S(1)}, f32[128,256]{1,0:T(8,128)S(1)}, u32[]{:S(2)}, u32[]{:S(2)}) collective-permute-start(f32[128,256]{1,0:T(8,128)S(1)} %add.133), channel_id=1, source_target_pairs={{0,2},{1,3},{2,0},{3,1},{4,6},{5,7},{6,4},{7,5},{8,10},{9,11},{10,... | collective-permute-start | bytes 393224 | tf_op jit(solution)/shard_map/ppermute | solution.py:25
  20.2 9.1 %collective-permute-start.4 = (f32[128,256]{1,0:T(8,128)S(1)}, f32[128,256]{1,0:T(8,128)S(1)}, u32[]{:S(2)}, u32[]{:S(2)}) collective-permute-start(f32[128,256]{1,0:T(8,128)S(1)} %add.133), channel_id=1, source_target_pairs={{0,4},{1,5},{2,6},{3,7},{4,0},{5,1},{6,2},{7,3},{8,12},{9,13},{10,... | collective-permute-start | bytes 393224 | tf_op jit(solution)/shard_map/ppermute | solution.py:25
  26.2 6.9 %collective-permute-start.5 = (f32[128,256]{1,0:T(8,128)S(1)}, f32[128,256]{1,0:T(8,128)S(1)}, u32[]{:S(2)}, u32[]{:S(2)}) collective-permute-start(f32[128,256]{1,0:T(8,128)S(1)} %add.133), channel_id=1, source_target_pairs={{0,6},{1,7},{2,4},{3,5},{4,2},{5,3},{6,0},{7,1},{8,14},{9,15},{10,... | collective-permute-start | bytes 393224 | tf_op jit(solution)/shard_map/ppermute | solution.py:25
  70.5 6.5 %collective-permute-start.18 = (f32[64,256]{1,0:T(8,128)S(1)}, f32[64,256]{1,0:T(8,128)S(1)}, u32[]{:S(2)}, u32[]{:S(2)}) collective-permute-start(f32[64,256]{1,0:T(8,128)S(1)} %add_add_fusion.4), channel_id=1, source_target_pairs={{0,2},{1,3},{2,0},{3,1},{4,6},{5,7},{6,4},{7,5},{8,10},{9,11},{10,... | collective-permute-start | bytes 196616 | tf_op jit(solution)/shard_map/ppermute | solution.py:25
  72.1 6.6 %collective-permute-start.19 = (f32[64,256]{1,0:T(8,128)S(1)}, f32[64,256]{1,0:T(8,128)S(1)}, u32[]{:S(2)}, u32[]{:S(2)}) collective-permute-start(f32[64,256]{1,0:T(8,128)S(1)} %add_add_fusion.4), channel_id=1, source_target_pairs={{0,4},{1,5},{2,6},{3,7},{4,0},{5,1},{6,2},{7,3},{8,12},{9,13},{10,... | collective-permute-start | bytes 196616 | tf_op jit(solution)/shard_map/ppermute | solution.py:25
  74.9 6.5 %collective-permute-start.8 = (f32[128,256]{1,0:T(8,128)}, f32[128,256]{1,0:T(8,128)S(1)}, u32[]{:S(2)}, u32[]{:S(2)}) collective-permute-start(f32[128,256]{1,0:T(8,128)} %add_add_fusion.refs_1_), channel_id=1, source_target_pairs={{0,8},{8,0},{16,24},{24,16},{1,9},{9,1},{17,25},{25,17},{2,10},{10... | collective-permute-start | bytes 393224 | tf_op jit(solution)/shard_map/ppermute | solution.py:25
  75.4 7.6 %collective-permute-start.9 = (f32[128,256]{1,0:T(8,128)}, f32[128,256]{1,0:T(8,128)S(1)}, u32[]{:S(2)}, u32[]{:S(2)}) collective-permute-start(f32[128,256]{1,0:T(8,128)} %add_add_fusion.refs_1_), channel_id=1, source_target_pairs={{0,16},{8,24},{16,0},{24,8},{1,17},{9,25},{17,1},{25,9},{2,18},{10... | collective-permute-start | bytes 393224 | tf_op jit(solution)/shard_map/ppermute | solution.py:25
  83.0 7.9 %collective-permute-start.12 = (f32[128,256]{1,0:T(8,128)S(1)}, f32[128,256]{1,0:T(8,128)S(1)}, u32[]{:S(2)}, u32[]{:S(2)}) collective-permute-start(f32[128,256]{1,0:T(8,128)S(1)} %collective-permute-done.8.refs_2_), channel_id=1, source_target_pairs={{0,1},{1,0},{2,3},{3,2},{4,5},{5,4},{6,7},{7,6},{8,9},{9,8},{10,11... | collective-permute-start | bytes 393224 | tf_op jit(solution)/shard_map/ppermute | solution.py:25
  83.2 7.7 %collective-permute-start.13 = (f32[128,256]{1,0:T(8,128)S(1)}, f32[128,256]{1,0:T(8,128)S(1)}, u32[]{:S(2)}, u32[]{:S(2)}) collective-permute-start(f32[128,256]{1,0:T(8,128)S(1)} %collective-permute-done.9.refs_3_), channel_id=1, source_target_pairs={{0,1},{1,0},{2,3},{3,2},{4,5},{5,4},{6,7},{7,6},{8,9},{9,8},{10,11... | collective-permute-start | bytes 393224 | tf_op jit(solution)/shard_map/ppermute | solution.py:25
  83.5 7.5 %collective-permute-start.14 = (f32[128,256]{1,0:T(8,128)S(1)}, f32[128,256]{1,0:T(8,128)S(1)}, u32[]{:S(2)}, u32[]{:S(2)}) collective-permute-start(f32[128,256]{1,0:T(8,128)S(1)} %collective-permute-done.10.refs_4_), channel_id=1, source_target_pairs={{0,1},{1,0},{2,3},{3,2},{4,5},{5,4},{6,7},{7,6},{8,9},{9,8},{10,11... | collective-permute-start | bytes 393224 | tf_op jit(solution)/shard_map/ppermute | solution.py:25
  111.3 32.2 %collective-permute-start.46 = (bf16[4,256,384]{2,1,0:T(8,128)(2,1)S(1)}, bf16[4,256,384]{2,1,0:T(8,128)(2,1)}, u32[]{:S(2)}, u32[]{:S(2)}) collective-permute-start(bf16[4,256,384]{2,1,0:T(8,128)(2,1)S(1)} %copy-done), channel_id=1, source_target_pairs={{0,8},{8,0},{16,24},{24,16},{1,9},{9,1},{17,25},{25,17},{2,10},{10... | collective-permute-start | bytes 2359304 | tf_op jit(solution)/shard_map/ppermute | solution.py:25
  115.9 7.4 %collective-permute-start.33 = (f32[72,256]{1,0:T(8,128)S(1)}, f32[72,256]{1,0:T(8,128)S(1)}, u32[]{:S(2)}, u32[]{:S(2)}) collective-permute-start(f32[72,256]{1,0:T(8,128)S(1)} %add_add_fusion.2), channel_id=1, source_target_pairs={{0,4},{1,5},{2,6},{3,7},{4,0},{5,1},{6,2},{7,3},{8,12},{9,13},{10,... | collective-permute-start | bytes 221192 | tf_op jit(solution)/shard_map/ppermute | solution.py:25
  120.3 16.6 %collective-permute-start.48 = (bf16[256,384]{1,0:T(8,128)(2,1)S(1)}, bf16[256,384]{1,0:T(8,128)(2,1)S(1)}, u32[]{:S(2)}, u32[]{:S(2)}) collective-permute-start(bf16[256,384]{1,0:T(8,128)(2,1)S(1)} %copy-done.12), channel_id=1, source_target_pairs={{0,24},{8,16},{16,8},{24,0},{1,25},{9,17},{17,9},{25,1},{2,26},{10... | collective-permute-start | bytes 589832 | tf_op jit(solution)/shard_map/ppermute | solution.py:25
  125.6 12.0 %collective-permute-start.35 = (f32[72,256]{1,0:T(8,128)S(1)}, f32[72,256]{1,0:T(8,128)S(1)}, u32[]{:S(2)}, u32[]{:S(2)}) collective-permute-start(f32[72,256]{1,0:T(8,128)S(1)} %add_add_fusion.1.refs_1_), channel_id=1, source_target_pairs={{0,8},{8,0},{16,24},{24,16},{1,9},{9,1},{17,25},{25,17},{2,10},{10... | collective-permute-start | bytes 221192 | tf_op jit(solution)/shard_map/ppermute | solution.py:25
  126.2 11.4 %collective-permute-start.36 = (f32[72,256]{1,0:T(8,128)S(1)}, f32[72,256]{1,0:T(8,128)S(1)}, u32[]{:S(2)}, u32[]{:S(2)}) collective-permute-start(f32[72,256]{1,0:T(8,128)S(1)} %add_add_fusion.1.refs_1_), channel_id=1, source_target_pairs={{0,16},{8,24},{16,0},{24,8},{1,17},{9,25},{17,1},{25,9},{2,18},{10... | collective-permute-start | bytes 221192 | tf_op jit(solution)/shard_map/ppermute | solution.py:25
  127.1 12.2 %collective-permute-start.37 = (f32[72,256]{1,0:T(8,128)S(1)}, f32[72,256]{1,0:T(8,128)S(1)}, u32[]{:S(2)}, u32[]{:S(2)}) collective-permute-start(f32[72,256]{1,0:T(8,128)S(1)} %add_add_fusion.1.refs_1_), channel_id=1, source_target_pairs={{0,24},{8,16},{16,8},{24,0},{1,25},{9,17},{17,9},{25,1},{2,26},{10... | collective-permute-start | bytes 221192 | tf_op jit(solution)/shard_map/ppermute | solution.py:25
  139.3 12.3 %collective-permute-start.49 = (bf16[512,384]{1,0:T(8,128)(2,1)}, bf16[512,384]{1,0:T(8,128)(2,1)S(1)}, u32[]{:S(2)}, u32[]{:S(2)}) collective-permute-start(bf16[512,384]{1,0:T(8,128)(2,1)} %get-tuple-element.87), channel_id=1, source_target_pairs={{0,8},{8,0},{16,24},{24,16},{1,9},{9,1},{17,25},{25,17},{2,10},{10... | collective-permute-start | bytes 1179656 | tf_op jit(solution)/shard_map/ppermute | solution.py:25
  140.5 20.6 %collective-permute-start.50 = (bf16[512,384]{1,0:T(8,128)(2,1)}, bf16[512,384]{1,0:T(8,128)(2,1)S(1)}, u32[]{:S(2)}, u32[]{:S(2)}) collective-permute-start(bf16[512,384]{1,0:T(8,128)(2,1)} %get-tuple-element.87), channel_id=1, source_target_pairs={{0,16},{8,24},{16,0},{24,8},{1,17},{9,25},{17,1},{25,9},{2,18},{10... | collective-permute-start | bytes 1179656 | tf_op jit(solution)/shard_map/ppermute | solution.py:25
  141.0 21.0 %collective-permute-start.51 = (bf16[512,384]{1,0:T(8,128)(2,1)}, bf16[512,384]{1,0:T(8,128)(2,1)S(1)}, u32[]{:S(2)}, u32[]{:S(2)}) collective-permute-start(bf16[512,384]{1,0:T(8,128)(2,1)} %get-tuple-element.87), channel_id=1, source_target_pairs={{0,24},{8,16},{16,8},{24,0},{1,25},{9,17},{17,9},{25,1},{2,26},{10... | collective-permute-start | bytes 1179656 | tf_op jit(solution)/shard_map/ppermute | solution.py:25
  142.9 53.9 %collective-permute-start.47 = (bf16[4,256,384]{2,1,0:T(8,128)(2,1)S(1)}, bf16[4,256,384]{2,1,0:T(8,128)(2,1)}, u32[]{:S(2)}, u32[]{:S(2)}) collective-permute-start(bf16[4,256,384]{2,1,0:T(8,128)(2,1)S(1)} %copy-done.10), channel_id=1, source_target_pairs={{0,16},{8,24},{16,0},{24,8},{1,17},{9,25},{17,1},{25,9},{2,18},{10... | collective-permute-start | bytes 2359304 | tf_op jit(solution)/shard_map/ppermute | solution.py:25
  143.5 22.2 %collective-permute-start.52 = (bf16[512,256]{1,0:T(8,128)(2,1)}, bf16[512,256]{1,0:T(8,128)(2,1)S(1)}, u32[]{:S(2)}, u32[]{:S(2)}) collective-permute-start(bf16[512,256]{1,0:T(8,128)(2,1)} %get-tuple-element.88), channel_id=1, source_target_pairs={{0,8},{8,0},{16,24},{24,16},{1,9},{9,1},{17,25},{25,17},{2,10},{10... | collective-permute-start | bytes 786440 | tf_op jit(solution)/shard_map/ppermute | solution.py:25
  151.6 37.6 %collective-permute-start.53 = (bf16[512,256]{1,0:T(8,128)(2,1)S(1)}, bf16[512,256]{1,0:T(8,128)(2,1)S(1)}, u32[]{:S(2)}, u32[]{:S(2)}) collective-permute-start(bf16[512,256]{1,0:T(8,128)(2,1)S(1)} %copy-done.11), channel_id=1, source_target_pairs={{0,16},{8,24},{16,0},{24,8},{1,17},{9,25},{17,1},{25,9},{2,18},{10... | collective-permute-start | bytes 786440 | tf_op jit(solution)/shard_map/ppermute | solution.py:25
  161.1 29.0 %collective-permute-start.54 = (bf16[512,256]{1,0:T(8,128)(2,1)S(1)}, bf16[512,256]{1,0:T(8,128)(2,1)S(1)}, u32[]{:S(2)}, u32[]{:S(2)}) collective-permute-start(bf16[512,256]{1,0:T(8,128)(2,1)S(1)} %copy-done.11), channel_id=1, source_target_pairs={{0,24},{8,16},{16,8},{24,0},{1,25},{9,17},{17,9},{25,1},{2,26},{10... | collective-permute-start | bytes 786440 | tf_op jit(solution)/shard_map/ppermute | solution.py:25
  162.0 28.7 %collective-permute-start.42 = (bf16[256,512]{1,0:T(8,128)(2,1)}, bf16[256,512]{1,0:T(8,128)(2,1)}, u32[]{:S(2)}, u32[]{:S(2)}) collective-permute-start(bf16[256,512]{1,0:T(8,128)(2,1)} %get-tuple-element.79.a), channel_id=1, source_target_pairs={{0,8},{8,0},{16,24},{24,16},{1,9},{9,1},{17,25},{25,17},{2,10},{10... | collective-permute-start | bytes 786440 | tf_op jit(solution)/shard_map/ppermute | solution.py:25
  165.7 29.9 %collective-permute-start.43 = (bf16[256,512]{1,0:T(8,128)(2,1)}, bf16[256,512]{1,0:T(8,128)(2,1)}, u32[]{:S(2)}, u32[]{:S(2)}) collective-permute-start(bf16[256,512]{1,0:T(8,128)(2,1)} %get-tuple-element.80.b), channel_id=1, source_target_pairs={{0,16},{8,24},{16,0},{24,8},{1,17},{9,25},{17,1},{25,9},{2,18},{10... | collective-permute-start | bytes 786440 | tf_op jit(solution)/shard_map/ppermute | solution.py:25
  189.2 12.7 %collective-permute-start.44 = (bf16[256,512]{1,0:T(8,128)(2,1)}, bf16[256,512]{1,0:T(8,128)(2,1)}, u32[]{:S(2)}, u32[]{:S(2)}) collective-permute-start(bf16[256,512]{1,0:T(8,128)(2,1)} %get-tuple-element.80.b), channel_id=1, source_target_pairs={{0,8},{8,0},{16,24},{24,16},{1,9},{9,1},{17,25},{25,17},{2,10},{10... | collective-permute-start | bytes 786440 | tf_op jit(solution)/shard_map/ppermute | solution.py:25
  190.1 11.8 %collective-permute-start.45 = (bf16[256,512]{1,0:T(8,128)(2,1)}, bf16[256,512]{1,0:T(8,128)(2,1)}, u32[]{:S(2)}, u32[]{:S(2)}) collective-permute-start(bf16[256,512]{1,0:T(8,128)(2,1)} %get-tuple-element.79.a), channel_id=1, source_target_pairs={{0,16},{8,24},{16,0},{24,8},{1,17},{9,25},{17,1},{25,9},{2,18},{10... | collective-permute-start | bytes 786440 | tf_op jit(solution)/shard_map/ppermute | solution.py:25
  190.7 14.7 %collective-permute-start.55 = (bf16[256,512]{1,0:T(8,128)(2,1)}, bf16[256,512]{1,0:T(8,128)(2,1)}, u32[]{:S(2)}, u32[]{:S(2)}) collective-permute-start(bf16[256,512]{1,0:T(8,128)(2,1)} %collective-permute-done.42.refs_0_), channel_id=1, source_target_pairs={{0,16},{8,24},{16,0},{24,8},{1,17},{9,25},{17,1},{25,9},{2,18},{10... | collective-permute-start | bytes 786440 | tf_op jit(solution)/shard_map/ppermute | solution.py:25
  195.6 11.4 %collective-permute-start.56 = (bf16[256,512]{1,0:T(8,128)(2,1)}, bf16[256,512]{1,0:T(8,128)(2,1)}, u32[]{:S(2)}, u32[]{:S(2)}) collective-permute-start(bf16[256,512]{1,0:T(8,128)(2,1)} %collective-permute-done.43.refs_1_), channel_id=1, source_target_pairs={{0,8},{8,0},{16,24},{24,16},{1,9},{9,1},{17,25},{25,17},{2,10},{10... | collective-permute-start | bytes 786440 | tf_op jit(solution)/shard_map/ppermute | solution.py:25
  (59 other events, 538.9 us)

commit v4 on v3

--- a/solution.py
+++ b/solution.py
@@ -11,6 +11,7 @@
 LEVELS = 2
 GROUP = 2**LEVELS
 CORES = 2
+PEERS = tuple(range(1, GROUP))
 F32, BF16 = jnp.float32, jnp.bfloat16
 NT = (((1,), (1,)), ((), ()))
 NN = (((1,), (0,)), ((), ()))
@@ -69,13 +70,12 @@
         col = 1.0 / jnp.sum(diag, axis=1, keepdims=True)
         scaled = jnp.where(mask, 0.0, k) * row
         spread = jnp.sum(scaled * (jnp.where(mask, 0.0, k) * col))
-        bound = jnp.minimum(jnp.max(jnp.sum(jnp.abs(k), axis=1, keepdims=True)), limit)
+        bound = jnp.minimum(jnp.max(jnp.sum(jnp.abs(k), axis=0, keepdims=True)), limit)
         near = jnp.where(mask, row, -scaled * col)
         far = eye * (2.0 / (1.0 + bound))
         x_ref[j] = jnp.where(spread < 0.9, near, far)
 
-    def step(state):
-        count, _ = state
+    def step():
         worst = jnp.float32(0.0)
         for j, part in enumerate(parts):
             x = x_ref[j]
@@ -83,9 +83,10 @@
             rest = eye - product(part, xs)
             worst = jnp.maximum(worst, jnp.sum(rest * rest))
             x_ref[j] = x + dot(xs[0], rest.astype(BF16))
-        return count + 1, worst
-
-    lax.while_loop(lambda s: (s[0] < 24) & (s[1] > 1e-6), step, (jnp.int32(0), jnp.float32(1.0)))
+        return worst
+
+    step()
+    lax.while_loop(lambda s: (s[0] < 24) & (s[1] > 1e-6), lambda s: (s[0] + 1, step()), (jnp.int32(2), step()))
 
 
 def resolvent(grams, x_ref, out_ref):
@@ -274,7 +275,7 @@
 
 def first_kernel(raw, tile, *refs):
     place, tails, crosses, (x, p1, p2, p3), refs = refs[0], refs[1:9], refs[9:17], refs[17:21], refs[21:]
-    m_ref, e_ref, f_ref, w, keep_out, give_out, cross, diag, inverse, block, m, acc, keep_ref, give_ref, load, save = refs
+    m_ref, e_ref, f_ref, w_out, keep_out, give_out, cross, diag, inverse, block, m, acc, keep_ref, give_ref, w, load, save = refs
     me, core = place[0], place[1]
     rows, share = p1.shape
     sources = [x.at[:, pl.ds(pl.multiple_of(me * share, share), share)], p1, p2, p3]
@@ -298,7 +299,8 @@
         copy.wait()
 
     acc[...] = jnp.zeros_like(acc)
-    saves = []
+    saves = [pltpu.make_async_copy(w, w_out, save.at[share // tile + 4])]
+    saves[0].start()
     for k in range(share // tile):
         here = slice(k * tile, (k + 1) * tile)
         m0 = merge_rows(block[: 2 * rows, here], w[0])
@@ -342,7 +344,7 @@
         functools.partial(first_kernel, raw, tile),
         out_shape=tuple(shape(pairs * rows, n, dtype=BF16) for n in (share, *ahead)) + (shape(pairs, rows, 2 * rows, dtype=BF16), out, out),
         in_specs=[SMEM] + [VMEM] * (4 * GROUP) + [HBM] * 4,
-        out_specs=(ANY, ANY, ANY, VMEM, ANY, ANY),
+        out_specs=(ANY,) * 6,
         scratch_shapes=[
             pltpu.VMEM((pairs, rows, rows), F32),
             pltpu.VMEM((GROUP, rows, rows), F32),
@@ -352,8 +354,9 @@
             pltpu.VMEM((3, rows, rows), F32),
             pltpu.VMEM(out.shape, F32),
             pltpu.VMEM(out.shape, F32),
+            pltpu.VMEM((pairs, rows, 2 * rows), BF16),
             pltpu.SemaphoreType.DMA((GROUP,)),
-            pltpu.SemaphoreType.DMA((share // tile + 4,)),
+            pltpu.SemaphoreType.DMA((share // tile + 5,)),
         ],
         cost_estimate=cost(2 * pairs * rows**3 * 40 + 14 * rows * rows * share, 12 * rows * share),
         name="first",
@@ -362,7 +365,7 @@
 
 def second_kernel(*refs):
     place, bundles, m_ref, refs = refs[0], refs[1:9], refs[9], refs[10:]
-    a_ref, b_ref, e_ref, w_ref, gram, inverse, m, load = refs
+    a_ref, b_ref, e_ref, w_out, gram, inverse, m, w_ref, merged, load, save = refs
     me, core = place[0], place[1]
     rows = m.shape[0] // 2
     copy = pltpu.make_async_copy(m_ref, m, load)
@@ -380,11 +383,17 @@
     upper_gram = jnp.where(eye_mask(rows), diagonal, jnp.where(lower, turned, packed))
     resolvent([(jnp.where(lower, packed, turned), gram[0], upper_gram)], inverse, w_ref)
     copy.wait()
-    start = 0
-    for ref in (e_ref, a_ref, b_ref):
+    saves = []
+    early, half = e_ref.shape[1], a_ref.shape[1]
+    for i, (ref, start) in enumerate(((a_ref, early), (b_ref, early + half), (e_ref, 0))):
         here = slice(start, start + ref.shape[1])
-        ref[...] = merge_rows(m[:, here], w_ref[0])
-        start += ref.shape[1]
+        merged[:, here] = merge_rows(m[:, here], w_ref[0])
+        saves.append(pltpu.make_async_copy(merged.at[:, here], ref, save.at[i]))
+        saves[-1].start()
+    saves.append(pltpu.make_async_copy(w_ref, w_out, save.at[3]))
+    saves[-1].start()
+    for save_copy in saves:
+        save_copy.wait()
 
 
 def second(place, bundles, m, early):
@@ -394,101 +403,100 @@
         second_kernel,
         out_shape=tuple(shape(rows, n, dtype=BF16) for n in (half, half, early)) + (shape(1, rows, 2 * rows, dtype=BF16),),
         in_specs=[SMEM] + [VMEM] * (2 * GROUP) + [ANY],
-        out_specs=(VMEM,) * 4,
+        out_specs=(ANY,) * 4,
         scratch_shapes=[
             pltpu.VMEM((2, rows, rows), F32),
             pltpu.VMEM((1, rows, rows), F32),
             pltpu.VMEM(m.shape, BF16),
+            pltpu.VMEM((1, rows, 2 * rows), BF16),
+            pltpu.VMEM((rows, share), BF16),
             pltpu.SemaphoreType.DMA,
+            pltpu.SemaphoreType.DMA((4,)),
         ],
         cost_estimate=cost(2 * rows**3 * 40 + 4 * rows * rows * share, 6 * rows * share),
         name="second",
     )(place, *bundles, m)
 
 
-def late_kernel(share, raw, place, w, a, b, e, *refs):
-    early, (out, buffer, save) = refs[:-3], refs[-3:]
-    me, half = place[0], a.shape[1]
-    saves = []
-
-    def put(source, owner, column):
-        target = out.at[:, pl.ds(pl.multiple_of(owner * share + column, 128), source.shape[1])]
-        saves.append(pltpu.make_async_copy(source, target, save.at[len(saves)]))
-        saves[-1].start()
-
-    put(e, me, 0)
-    put(a, me, e.shape[1])
-    put(b, me, e.shape[1] + half)
-    for i, pair in enumerate(early):
-        s, size = i % (GROUP - 1), pair.shape[1]
-        column = raw if i < GROUP - 1 else raw + early[0].shape[1]
-        spot = buffer.at[s, :, column - raw : column - raw + size]
-        spot[...] = merge_rows(pair[...], w[0])
-        put(spot, me ^ (s + 1), column)
-    for copy in saves:
-        copy.wait()
-
-
-def late(place, w, a, b, e, early, raw, share):
-    rows, size = e.shape[0], e.shape[1] - raw
-    return pl.pallas_call(
-        functools.partial(late_kernel, share, raw),
-        out_shape=shape(rows, GROUP * share, dtype=BF16),
-        in_specs=[SMEM] + [VMEM] * (4 + len(early)),
-        out_specs=HBM,
-        scratch_shapes=[pltpu.VMEM((GROUP - 1, rows, size), BF16), pltpu.SemaphoreType.DMA((len(early) + 3,))],
-        cost_estimate=cost(4 * rows * rows * size * (GROUP - 1), 6 * rows * size * (GROUP - 1)),
-        name="late",
-    )(place, w, a, b, e, *early)
-
-
-def raw_merge_kernel(share, place, w0, w1, x, xs, ys, d, _, out, block, pair, buffer, load, save):
+def raw_first_kernel(share, place, w, x, xs, ys, d, out, block, pair, load, save):
     me = place[0]
     rows, raw = d.shape
-    saves = []
-    sources = {}
-    for v in range(1, GROUP):
+    saves, loads, sources = [], {}, {}
+    for v in PEERS:
         mine = x.at[:, pl.ds(pl.multiple_of((me ^ v) * share, 128), raw)]
         across = {1: xs.at[GROUP - 1], 2: ys.at[GROUP - 1], 3: d}[v]
         sources[v] = (mine, xs.at[SHARES_X.index(v ^ 1)], ys.at[SHARES_Y.index(v ^ 2)], across)
-    loads = {}
     for v, group in sources.items():
         for s, source in enumerate(group):
             target = block.at[v - 1, pl.ds(pl.multiple_of((me ^ s) * rows, rows), rows)]
             loads[v, s] = pltpu.make_async_copy(source, target, load.at[(v - 1) * GROUP + s])
             loads[v, s].start()
-    for v in sources:
+    for v in PEERS:
         for s in range(GROUP):
             loads[v, s].wait()
         for j in range(GROUP // 2):
-            pair[j * rows : (j + 1) * rows] = merge_rows(block[v - 1, 2 * j * rows : 2 * (j + 1) * rows], w0[j])
-        buffer[v - 1] = merge_rows(pair[...], w1[0])
-        target = out.at[:, pl.ds(pl.multiple_of((me ^ v) * share, 128), raw)]
-        saves.append(pltpu.make_async_copy(buffer.at[v - 1], target, save.at[v - 1]))
+            pair[v - 1, j * rows : (j + 1) * rows] = merge_rows(block[v - 1, 2 * j * rows : 2 * (j + 1) * rows], w[j])
+        saves.append(pltpu.make_async_copy(pair.at[v - 1], out.at[v - 1], save.at[v - 1]))
         saves[-1].start()
     for copy in saves:
         copy.wait()
 
 
-def raw_merge(place, w0, w1, x, messages, out, share):
+def raw_first(place, w, x, messages, share):
     rows, raw = messages[2].shape
-    return pl.pallas_call(
-        functools.partial(raw_merge_kernel, share),
-        out_shape=shape(*out.shape, dtype=BF16),
-        in_specs=[SMEM, VMEM, VMEM] + [HBM] * 5,
+    pairs = (GROUP - 1, 2 * rows, raw)
+    return pl.pallas_call(
+        functools.partial(raw_first_kernel, share),
+        out_shape=shape(*pairs, dtype=BF16),
+        in_specs=[SMEM, VMEM] + [HBM] * 4,
         out_specs=HBM,
         scratch_shapes=[
             pltpu.VMEM((GROUP - 1, GROUP * rows, raw), BF16),
-            pltpu.VMEM((2 * rows, raw), BF16),
-            pltpu.VMEM((GROUP - 1, rows, raw), BF16),
+            pltpu.VMEM(pairs, BF16),
             pltpu.SemaphoreType.DMA(((GROUP - 1) * GROUP,)),
             pltpu.SemaphoreType.DMA((GROUP - 1,)),
         ],
-        input_output_aliases={7: 0},
-        cost_estimate=cost(12 * rows * rows * raw * (GROUP - 1), 10 * rows * raw * (GROUP - 1)),
+        cost_estimate=cost(8 * rows * rows * raw * (GROUP - 1), 12 * rows * raw * (GROUP - 1)),
         compiler_params=WHOLE,
-        name="raw_merge",
-    )(place, w0, w1, x, *messages, out)
+        name="raw_first",
+    )(place, w, x, *messages)
+
+
+def late_kernel(share, raw, place, w, a, b, e, raws, *refs):
+    early, (out, buffer, save) = refs[:-3], refs[-3:]
+    me, half = place[0], a.shape[1]
+    saves = []
+
+    def put(source, owner, column):
+        target = out.at[:, pl.ds(pl.multiple_of(owner * share + column, 128), source.shape[1])]
+        saves.append(pltpu.make_async_copy(source, target, save.at[len(saves)]))
+        saves[-1].start()
+
+    put(e, me, 0)
+    put(a, me, e.shape[1])
+    put(b, me, e.shape[1] + half)
+    work = [(raws.at[s - 1], s, 0) for s in PEERS]
+    work += [(pair, s, raw) for pair, s in zip(early, PEERS)]
+    work += [(pair, s, raw + early[0].shape[1]) for pair, s in zip(early[len(PEERS) :], PEERS)]
+    for pair, s, column in work:
+        spot = buffer.at[s - 1, :, column : column + pair.shape[1]]
+        spot[...] = merge_rows(pair[...], w[0])
+        put(spot, me ^ s, column)
+    for copy in saves:
+        copy.wait()
+
+
+def late(place, w, a, b, e, raws, early, share):
+    rows, size = e.shape
+    return pl.pallas_call(
+        functools.partial(late_kernel, share, raws.shape[2]),
+        out_shape=shape(rows, GROUP * share, dtype=BF16),
+        in_specs=[SMEM] + [VMEM] * (5 + len(early)),
+        out_specs=HBM,
+        scratch_shapes=[pltpu.VMEM((GROUP - 1, rows, size), BF16), pltpu.SemaphoreType.DMA((len(early) + GROUP + 2,))],
+        cost_estimate=cost(4 * rows * rows * size * (GROUP - 1), 6 * rows * size * (GROUP - 1)),
+        name="late",
+    )(place, w, a, b, e, raws, *early)
 
 
 def put_kernel(spots, share, place, *refs):
@@ -522,9 +530,6 @@
     )(place, *blocks, out)
 
 
-PEERS = tuple(range(1, GROUP))
-
-
 def over_chips(block):
     chips = lax.axis_size("feat") // CORES
     return total([block] + [send(block, "feat", CORES * s) for s in range(1, chips)])
@@ -571,6 +576,7 @@
     parts, e = lax.optimization_barrier((parts, e))
     mine = total([parts[0]] + send_all(parts[1:], "dp", PEERS))
     pairs = send_all([e] * len(PEERS), "dp", PEERS)
+    raws = raw_first(place, w0, x, messages, share)
     bundle = over_chips(mine)
     bundle, f = lax.optimization_barrier((bundle, f))
     bundles = gather_group(bundle)
@@ -581,11 +587,9 @@
     bx, ay = send(b, "dp", 1), send(a, "dp", 2)
     ad, bd = send(ax, "dp", 2), send(by, "dp", 1)
     left, right = early, early + a.shape[1]
-    out = late(place, w1, a, b, e, pairs, raw, share)
-    out = raw_merge(place, w0, w1, x, messages, out, share)
+    out = late(place, w1, a, b, e, raws, pairs, share)
     out = put(place, out, [ax, by, bx, ay], ((1, left), (2, right), (1, right), (2, left)), share)
-    for block, column in ((ad, left), (bd, right)):
-        out = lax.dynamic_update_slice(out, block, (0, (me ^ 3) * share + column))
+    out = put(place, out, [ad, bd], ((3, left), (3, right)), share)
     return out[None]
 
 

time: 209 us -> 197 us (0.943)
  waiting for transfers between devices: 93.9 us -> 82.3 us
  local copies, waits for them, and re-layouts: 9.32 us -> 6.04 us
    ppermute x57, waiting for transfers between devices: 93.9 us -> 82.3 us  [send(): return lax.ppermute(block, axis, [(i, i ^ shift) for i in range(count)])]
    dynamic_update_slice x2 -> x0, local copies, waits for them, and re-layouts: 3.34 us -> none  [run(): out = lax.dynamic_update_slice(out, block, (0, (me ^ 3) * share + column))]
    pallas_call x1 -> x2, Pallas kernels: 2.65 us -> 5.08 us  [put(): pl.pallas_call(functools.partial(put_kernel, spots, share), out_shape=sha...]
  transfers between devices with their start and end apart: 57 -> 57, of which waited for: 31 -> 34; matrix products, arithmetic and copies ran while one was open for 3% -> 2% of each run, Pallas kernels for 14% -> 15%
where the time goes in v4:
time: 197 us
  waiting for transfers between devices  82.3 us (42%)
  starting transfers between devices  58.1 us (29%)
  Pallas kernels  45.3 us (23%)
  local copies, waits for them, and re-layouts  6.04 us (3%)
  other arithmetic  4.33 us (2%)
    ppermute x57, waiting for transfers between devices, send(): return lax.ppermute(block, axis, [(i, i ^ shift) for i in range(count)])  82.3 us
    ppermute x57, starting transfers between devices, send(): return lax.ppermute(block, axis, [(i, i ^ shift) for i in range(count)])  58.1 us
    pallas_call x1, Pallas kernels, first(): pl.pallas_call(functools.partial(first_kernel, raw, tile), out_shape=tupl...  10.6 us
    pallas_call x1, Pallas kernels, second(): pl.pallas_call(second_kernel, out_shape=tuple((shape(rows, n, dtype=BF16)...  6.92 us
    pallas_call x1, Pallas kernels, own_gram(): pl.pallas_call(own_gram_kernel, out_shape=(half, half), grid_spec=pltpu.P...  5.37 us
    pallas_call x2, Pallas kernels, put(): pl.pallas_call(functools.partial(put_kernel, spots, share), out_shape=sha...  5.08 us
    dynamic_slice x2, local copies, waits for them, and re-layouts, run(): cuts[s] = lax.dynamic_slice(source, (0, (me ^ s) * share), (rows, share))  4.98 us
    pallas_call x1, Pallas kernels, near_gram(): pl.pallas_call(functools.partial(near_gram_kernel, chunk), out_shape=(sha...  4.93 us
  transfers between devices with their start and end apart: 57, of which 34 were waited for; matrix products, arithmetic and copies ran while one was open for 2% of the time, Pallas kernels for 15%

profile of v4, /device:TPU:0, one launch (start us, length us, event | category | flops | bytes accessed | tf_op | source)
XLA Modules:
  0.0 196.6 jit_solution(12377325037889294602)
XLA Ops:
  0.0 2.7 %dynamic-slice_bitcast_fusion = (bf16[256,2048]{1,0:T(8,128)(2,1)}, bf16[256,2048]{1,0:T(8,128)(2,1)S(1)}) fusion(bf16[1,256,8192]{2,1,0:T(8,128)(2,1)} %param.1, s32[]{:T(128)S(6)} %select_n.23, s32[]{:T(128)S(6)} %select_n.22), kind=kLoop, calls=%fused_computation | loop fusion | bytes 4194312 | tf_op jit(solution)/shard_map/dynamic_slice | solution.py:554
  2.7 3.0 %collective-permute-start.6 = (bf16[256,2048]{1,0:T(8,128)(2,1)S(1)}, bf16[256,2048]{1,0:T(8,128)(2,1)}, u32[]{:S(2)}, u32[]{:S(2)}) collective-permute-start(bf16[256,2048]{1,0:T(8,128)(2,1)S(1)} %get-tuple-element.51), channel_id=1, source_target_pairs={{0,8},{8,0},{16,24},{24,16},{1,9},{9,1},{17,25},{25,17},{2,10},{10... | collective-permute-start | bytes 3145736 | tf_op jit(solution)/shard_map/ppermute | solution.py:26
  5.7 2.3 %constant_dynamic-slice_fusion = bf16[256,2048]{1,0:T(8,128)(2,1)} fusion(bf16[256,8192]{1,0:T(8,128)(2,1)} %bitcast.24, s32[]{:T(128)S(6)} %select_n.24), kind=kLoop, calls=%fused_computation.23 | loop fusion | bytes 2097156 | tf_op jit(solution)/shard_map/dynamic_slice | solution.py:554
  10.1 5.4 %own_gram.1 = (f32[128,256]{1,0:T(8,128)}, f32[128,256]{1,0:T(8,128)}) custom-call(s32[2]{0:T(128)} %pad_add_fusion.place.refs_0_, bf16[256,8192]{1,0:T(8,128)(2,1)} %bitcast.25), custom_call_target="tpu_custom_call" | custom-call | flops 1073741824 | bytes 4194304 | tf_op jit(solution)/shard_map/own_gram/pallas_call | solution.py:136
  18.0 4.1 %collective-permute-start.5 = (f32[128,256]{1,0:T(8,128)S(1)}, f32[128,256]{1,0:T(8,128)S(1)}, u32[]{:S(2)}, u32[]{:S(2)}) collective-permute-start(f32[128,256]{1,0:T(8,128)S(1)} %add.117), channel_id=1, source_target_pairs={{0,6},{1,7},{2,4},{3,5},{4,2},{5,3},{6,0},{7,1},{8,14},{9,15},{10,... | collective-permute-start | bytes 393224 | tf_op jit(solution)/shard_map/ppermute | solution.py:26
  22.1 4.4 %collective-permute-done.5 = f32[128,256]{1,0:T(8,128)S(1)} collective-permute-done((f32[128,256]{1,0:T(8,128)S(1)}, f32[128,256]{1,0:T(8,128)S(1)}, u32[]{:S(2)}, u32[]{:S(2)}) %collective-permute-start.5) | collective-permute-done | bytes 131104 | tf_op jit(solution)/shard_map/ppermute | solution.py:26
  26.6 5.5 %collective-permute-start.3 = (f32[128,256]{1,0:T(8,128)S(1)}, f32[128,256]{1,0:T(8,128)S(1)}, u32[]{:S(2)}, u32[]{:S(2)}) collective-permute-start(f32[128,256]{1,0:T(8,128)S(1)} %add.117), channel_id=1, source_target_pairs={{0,2},{1,3},{2,0},{3,1},{4,6},{5,7},{6,4},{7,5},{8,10},{9,11},{10,... | collective-permute-start | bytes 393224 | tf_op jit(solution)/shard_map/ppermute | solution.py:26
  33.6 2.7 %collective-permute-done.3 = f32[128,256]{1,0:T(8,128)S(1)} collective-permute-done((f32[128,256]{1,0:T(8,128)S(1)}, f32[128,256]{1,0:T(8,128)S(1)}, u32[]{:S(2)}, u32[]{:S(2)}) %collective-permute-start.3) | collective-permute-done | bytes 131104 | tf_op jit(solution)/shard_map/ppermute | solution.py:26
  37.0 4.9 %near_gram.1 = (f32[256,256]{1,0:T(8,128)}, bf16[4,256,384]{2,1,0:T(8,128)(2,1)}, bf16[4,256,384]{2,1,0:T(8,128)(2,1)}, bf16[256,384]{1,0:T(8,128)(2,1)}) custom-call(s32[2]{0:T(128)} %pad_add_fusion.place.refs_0_, bf16[256,8192]{1,0:T(8,128)(2,1)} %bitcast.26, bf16[256,2048]{1,0:T(8,128)(2,1)} %collective-permute-done.6.p1.refs_18_), custom_call_target="tpu_custom_call" | custom-call | flops 268435456 | bytes 2097152 | tf_op jit(solution)/shard_map/near_gram/pallas_call | solution.py:201
  41.9 10.8 %collective-permute-done.1.p3.refs_20_ = bf16[256,2048]{1,0:T(8,128)(2,1)} collective-permute-done((bf16[256,2048]{1,0:T(8,128)(2,1)}, bf16[256,2048]{1,0:T(8,128)(2,1)}, u32[]{:S(2)}, u32[]{:S(2)}) %collective-permute-start.1) | collective-permute-done | bytes 1048608 | tf_op jit(solution)/shard_map/ppermute | solution.py:26
  52.7 3.9 %collective-permute-done.p2.refs_19_ = bf16[256,2048]{1,0:T(8,128)(2,1)} collective-permute-done((bf16[256,2048]{1,0:T(8,128)(2,1)}, bf16[256,2048]{1,0:T(8,128)(2,1)}, u32[]{:S(2)}, u32[]{:S(2)}) %collective-permute-start) | collective-permute-done | bytes 1048608 | tf_op jit(solution)/shard_map/ppermute | solution.py:26
  56.6 3.8 %far_gram.1 = (f32[4,64,256]{2,1,0:T(8,128)}, f32[4,64,256]{2,1,0:T(8,128)}, bf16[4,256,384]{2,1,0:T(8,128)(2,1)}) custom-call(s32[2]{0:T(128)} %pad_add_fusion.place.refs_0_, f32[256,256]{1,0:T(8,128)} %get-tuple-element.53.near, bf16[256,2048]{1,0:T(8,128)(2,1)} %collective-permute-done.p2.refs_19_, ...), custom_call_target="tpu_custom_call", output_to_operand_aliasing={{2}: (4, {})} | custom-call | flops 268435456 | bytes 2097152 | tf_op jit(solution)/shard_map/far_gram/pallas_call | solution.py:243
  67.5 2.2 %collective-permute-done.16 = f32[64,256]{1,0:T(8,128)S(1)} collective-permute-done((f32[64,256]{1,0:T(8,128)S(1)}, f32[64,256]{1,0:T(8,128)S(1)}, u32[]{:S(2)}, u32[]{:S(2)}) %collective-permute-start.16) | collective-permute-done | bytes 65568 | tf_op jit(solution)/shard_map/ppermute | solution.py:26
  70.4 3.7 %collective-permute-start.20 = (f32[64,256]{1,0:T(8,128)S(1)}, f32[64,256]{1,0:T(8,128)S(1)}, u32[]{:S(2)}, u32[]{:S(2)}) collective-permute-start(f32[64,256]{1,0:T(8,128)S(1)} %add_add_fusion.4), channel_id=1, source_target_pairs={{0,6},{1,7},{2,4},{3,5},{4,2},{5,3},{6,0},{7,1},{8,14},{9,15},{10,... | collective-permute-start | bytes 196616 | tf_op jit(solution)/shard_map/ppermute | solution.py:26
  79.9 2.5 %collective-permute-start.23 = (f32[64,256]{1,0:T(8,128)S(1)}, f32[64,256]{1,0:T(8,128)S(1)}, u32[]{:S(2)}, u32[]{:S(2)}) collective-permute-start(f32[64,256]{1,0:T(8,128)S(1)} %add_add_fusion.3.refs_9_), channel_id=1, source_target_pairs={{0,24},{8,16},{16,8},{24,0},{1,25},{9,17},{17,9},{25,1},{2,26},{10... | collective-permute-start | bytes 196616 | tf_op jit(solution)/shard_map/ppermute | solution.py:26
  82.6 2.8 %collective-permute-done.9.refs_3_ = f32[128,256]{1,0:T(8,128)S(1)} collective-permute-done((f32[128,256]{1,0:T(8,128)}, f32[128,256]{1,0:T(8,128)S(1)}, u32[]{:S(2)}, u32[]{:S(2)}) %collective-permute-start.9) | collective-permute-done | bytes 131104 | tf_op jit(solution)/shard_map/ppermute | solution.py:26
  87.3 2.9 %collective-permute-done.22.refs_11_ = f32[64,256]{1,0:T(8,128)S(1)} collective-permute-done((f32[64,256]{1,0:T(8,128)S(1)}, f32[64,256]{1,0:T(8,128)S(1)}, u32[]{:S(2)}, u32[]{:S(2)}) %collective-permute-start.22) | collective-permute-done | bytes 65568 | tf_op jit(solution)/shard_map/ppermute | solution.py:26
  93.4 10.6 %first.1 = (bf16[512,2048]{1,0:T(8,128)(2,1)}, bf16[512,384]{1,0:T(8,128)(2,1)}, bf16[512,256]{1,0:T(8,128)(2,1)}, bf16[2,256,512]{2,1,0:T(8,128)(2,1)}, f32[4,72,256]{2,1,0:T(8,128)}, /*index=5*/f32[4,72,256]{2,1,0:T(8,128)}) custom-call(s32[2]{0:T(128)} %pad_add_fusion.place.refs_0_, f32[128,256]{1,0:T(8,128)} %add_add_fusion.refs_1_, ...), custom_call_target="tpu_custom_call" | custom-call | flops 4563402752 | bytes 6291456 | tf_op jit(solution)/shard_map/first/pallas_call | solution.py:343
  108.6 1.9 collective-permute-start.31
  113.8 3.8 %collective-permute-start.34 = (f32[72,256]{1,0:T(8,128)S(1)}, f32[72,256]{1,0:T(8,128)S(1)}, u32[]{:S(2)}, u32[]{:S(2)}) collective-permute-start(f32[72,256]{1,0:T(8,128)S(1)} %add_add_fusion.2), channel_id=1, source_target_pairs={{0,6},{1,7},{2,4},{3,5},{4,2},{5,3},{6,0},{7,1},{8,14},{9,15},{10,... | collective-permute-start | bytes 221192 | tf_op jit(solution)/shard_map/ppermute | solution.py:26
  124.6 17.0 %collective-permute-done.50.d = bf16[256,384]{1,0:T(8,128)(2,1)} collective-permute-done((bf16[256,384]{1,0:T(8,128)(2,1)S(1)}, bf16[256,384]{1,0:T(8,128)(2,1)}, u32[]{:S(2)}, u32[]{:S(2)}) %collective-permute-start.50) | collective-permute-done | bytes 196640 | tf_op jit(solution)/shard_map/ppermute | solution.py:26
  144.1 1.9 collective-permute-done.36.refs_3_
  152.1 6.9 %second.1 = (bf16[256,512]{1,0:T(8,128)(2,1)}, bf16[256,512]{1,0:T(8,128)(2,1)}, bf16[256,1024]{1,0:T(8,128)(2,1)}, bf16[1,256,512]{2,1,0:T(8,128)(2,1)}) custom-call(s32[2]{0:T(128)} %pad_add_fusion.place.refs_0_, f32[72,256]{1,0:T(8,128)} %copy-done.1, f32[72,256]{1,0:T(8,128)} %copy-done.15, f32[72,256]{1,0:T(8,128)} %copy-done.14, f32[72,256]{1,0:T(8,128)} %copy-done.13, ...), custom_call_target="tpu_custom_call" | custom-call | flops 1879048192 | bytes 3145728 | tf_op jit(solution)/shard_map/second/pallas_call | solution.py:402
  159.1 1.9 collective-permute-start.56
  162.6 4.7 %collective-permute-done.52.refs_1_ = bf16[512,384]{1,0:T(8,128)(2,1)} collective-permute-done((bf16[512,384]{1,0:T(8,128)(2,1)}, bf16[512,384]{1,0:T(8,128)(2,1)}, u32[]{:S(2)}, u32[]{:S(2)}) %collective-permute-start.52) | collective-permute-done | bytes 393248 | tf_op jit(solution)/shard_map/ppermute | solution.py:26
  168.8 4.2 %collective-permute-done.56.refs_5_ = bf16[512,256]{1,0:T(8,128)(2,1)} collective-permute-done((bf16[512,256]{1,0:T(8,128)(2,1)}, bf16[512,256]{1,0:T(8,128)(2,1)}, u32[]{:S(2)}, u32[]{:S(2)}) %collective-permute-start.56) | collective-permute-done | bytes 262176 | tf_op jit(solution)/shard_map/ppermute | solution.py:26
  173.7 2.9 %collective-permute-done.55.refs_4_ = bf16[512,256]{1,0:T(8,128)(2,1)} collective-permute-done((bf16[512,256]{1,0:T(8,128)(2,1)}, bf16[512,256]{1,0:T(8,128)(2,1)}, u32[]{:S(2)}, u32[]{:S(2)}) %collective-permute-start.55) | collective-permute-done | bytes 262176 | tf_op jit(solution)/shard_map/ppermute | solution.py:26
  179.1 3.1 %collective-permute-done.44.refs_1_ = bf16[256,512]{1,0:T(8,128)(2,1)} collective-permute-done((bf16[256,512]{1,0:T(8,128)(2,1)}, bf16[256,512]{1,0:T(8,128)(2,1)}, u32[]{:S(2)}, u32[]{:S(2)}) %collective-permute-start.44) | collective-permute-done | bytes 262176 | tf_op jit(solution)/shard_map/ppermute | solution.py:26
  182.6 4.5 %raw_first.1.raws = bf16[3,512,384]{2,1,0:T(8,128)(2,1)} custom-call(s32[2]{0:T(128)} %pad_add_fusion.place.refs_0_, bf16[2,256,512]{2,1,0:T(8,128)(2,1)} %get-tuple-element.83.w, bf16[256,8192]{1,0:T(8,128)(2,1)} %bitcast.28, bf16[4,256,384]{2,1,0:T(8,128)(2,1)} %collective-permute-done.48.xs, bf16[4,256,384]{2,1,0:T(8,128)(2,1)} %collective-permute-done.49.ys, ...), custom_call_target="tpu_custom_call" | custom-call | flops 603979776 | bytes 3538944 | tf_op jit(solution)/shard_map/raw_first/pallas_call | solution.py:448
  187.1 4.2 %late.1.refs_4_ = bf16[256,8192]{1,0:T(8,128)(2,1)} custom-call(s32[2]{0:T(128)} %pad_add_fusion.place.refs_0_, bf16[1,256,512]{2,1,0:T(8,128)(2,1)} %get-tuple-element.81.w, bf16[256,512]{1,0:T(8,128)(2,1)} %get-tuple-element.79.a, bf16[256,512]{1,0:T(8,128)(2,1)} %get-tuple-element.80.b, bf16[256,1024]{1,0:T(8,128)(2,1)} %get-tuple-element.82.e, ...), custom_call_target="tpu_custom_call" | custom-call | flops 805306368 | bytes 4718592 | tf_op jit(solution)/shard_map/late/pallas_call | solution.py:491
  191.4 2.6 %put.2.refs_2_ = bf16[256,8192]{1,0:T(8,128)(2,1)} custom-call(s32[2]{0:T(128)} %pad_add_fusion.place.refs_0_, bf16[256,512]{1,0:T(8,128)(2,1)} %collective-permute-done.42.refs_0_, bf16[256,512]{1,0:T(8,128)(2,1)} %collective-permute-done.44.refs_1_, bf16[256,512]{1,0:T(8,128)(2,1)} %collective-permute-done.46.refs_2_, ...), custom_call_target="tpu_custom_call", output_to_operand_aliasing={{}: (5, {})} | custom-call | bytes 2097152 | tf_op jit(solution)/shard_map/put/pallas_call | solution.py:520
  194.0 2.4 %put.3 = bf16[256,8192]{1,0:T(8,128)(2,1)} custom-call(s32[2]{0:T(128)} %pad_add_fusion.place.refs_0_, bf16[256,512]{1,0:T(8,128)(2,1)} %collective-permute-done.43.refs_0_, bf16[256,512]{1,0:T(8,128)(2,1)} %collective-permute-done.45.refs_1_, bf16[256,8192]{1,0:T(8,128)(2,1)} %put.2.refs_2_), custom_call_target="tpu_custom_call", output_to_operand_aliasing={{}: (3, {})} | custom-call | bytes 1048576 | tf_op jit(solution)/shard_map/put/pallas_call | solution.py:520
  (154 shorter events, 55.8 us)
Async XLA Ops:
  2.7 34.3 %collective-permute-start.6 = (bf16[256,2048]{1,0:T(8,128)(2,1)S(1)}, bf16[256,2048]{1,0:T(8,128)(2,1)}, u32[]{:S(2)}, u32[]{:S(2)}) collective-permute-start(bf16[256,2048]{1,0:T(8,128)(2,1)S(1)} %get-tuple-element.51), channel_id=1, source_target_pairs={{0,8},{8,0},{16,24},{24,16},{1,9},{9,1},{17,25},{25,17},{2,10},{10... | collective-permute-start | bytes 3145736 | tf_op jit(solution)/shard_map/ppermute | solution.py:26
  8.0 44.8 %collective-permute-start.1 = (bf16[256,2048]{1,0:T(8,128)(2,1)}, bf16[256,2048]{1,0:T(8,128)(2,1)}, u32[]{:S(2)}, u32[]{:S(2)}) collective-permute-start(bf16[256,2048]{1,0:T(8,128)(2,1)} %constant_dynamic-slice_fusion), channel_id=1, source_target_pairs={{0,24},{8,16},{16,8},{24,0},{1,25},{9,17},{17,9},{25,1},{2,26},{10... | collective-permute-start | bytes 3145736 | tf_op jit(solution)/shard_map/ppermute | solution.py:26
  9.4 47.1 %collective-permute-start = (bf16[256,2048]{1,0:T(8,128)(2,1)}, bf16[256,2048]{1,0:T(8,128)(2,1)}, u32[]{:S(2)}, u32[]{:S(2)}) collective-permute-start(bf16[256,2048]{1,0:T(8,128)(2,1)} %get-tuple-element.47), channel_id=1, source_target_pairs={{0,16},{8,24},{16,0},{24,8},{1,17},{9,25},{17,1},{25,9},{2,18},{10... | collective-permute-start | bytes 3145736 | tf_op jit(solution)/shard_map/ppermute | solution.py:26
  18.0 8.6 %collective-permute-start.5 = (f32[128,256]{1,0:T(8,128)S(1)}, f32[128,256]{1,0:T(8,128)S(1)}, u32[]{:S(2)}, u32[]{:S(2)}) collective-permute-start(f32[128,256]{1,0:T(8,128)S(1)} %add.117), channel_id=1, source_target_pairs={{0,6},{1,7},{2,4},{3,5},{4,2},{5,3},{6,0},{7,1},{8,14},{9,15},{10,... | collective-permute-start | bytes 393224 | tf_op jit(solution)/shard_map/ppermute | solution.py:26
  22.1 11.5 %collective-permute-start.4 = (f32[128,256]{1,0:T(8,128)S(1)}, f32[128,256]{1,0:T(8,128)S(1)}, u32[]{:S(2)}, u32[]{:S(2)}) collective-permute-start(f32[128,256]{1,0:T(8,128)S(1)} %add.117), channel_id=1, source_target_pairs={{0,4},{1,5},{2,6},{3,7},{4,0},{5,1},{6,2},{7,3},{8,12},{9,13},{10,... | collective-permute-start | bytes 393224 | tf_op jit(solution)/shard_map/ppermute | solution.py:26
  26.6 9.7 %collective-permute-start.3 = (f32[128,256]{1,0:T(8,128)S(1)}, f32[128,256]{1,0:T(8,128)S(1)}, u32[]{:S(2)}, u32[]{:S(2)}) collective-permute-start(f32[128,256]{1,0:T(8,128)S(1)} %add.117), channel_id=1, source_target_pairs={{0,2},{1,3},{2,0},{3,1},{4,6},{5,7},{6,4},{7,5},{8,10},{9,11},{10,... | collective-permute-start | bytes 393224 | tf_op jit(solution)/shard_map/ppermute | solution.py:26
  70.4 6.1 %collective-permute-start.20 = (f32[64,256]{1,0:T(8,128)S(1)}, f32[64,256]{1,0:T(8,128)S(1)}, u32[]{:S(2)}, u32[]{:S(2)}) collective-permute-start(f32[64,256]{1,0:T(8,128)S(1)} %add_add_fusion.4), channel_id=1, source_target_pairs={{0,6},{1,7},{2,4},{3,5},{4,2},{5,3},{6,0},{7,1},{8,14},{9,15},{10,... | collective-permute-start | bytes 196616 | tf_op jit(solution)/shard_map/ppermute | solution.py:26
  74.8 7.6 %collective-permute-start.10 = (f32[128,256]{1,0:T(8,128)}, f32[128,256]{1,0:T(8,128)S(1)}, u32[]{:S(2)}, u32[]{:S(2)}) collective-permute-start(f32[128,256]{1,0:T(8,128)} %add_add_fusion.refs_1_), channel_id=1, source_target_pairs={{0,24},{8,16},{16,8},{24,0},{1,25},{9,17},{17,9},{25,1},{2,26},{10... | collective-permute-start | bytes 393224 | tf_op jit(solution)/shard_map/ppermute | solution.py:26
  76.5 8.9 %collective-permute-start.9 = (f32[128,256]{1,0:T(8,128)}, f32[128,256]{1,0:T(8,128)S(1)}, u32[]{:S(2)}, u32[]{:S(2)}) collective-permute-start(f32[128,256]{1,0:T(8,128)} %add_add_fusion.refs_1_), channel_id=1, source_target_pairs={{0,16},{8,24},{16,0},{24,8},{1,17},{9,25},{17,1},{25,9},{2,18},{10... | collective-permute-start | bytes 393224 | tf_op jit(solution)/shard_map/ppermute | solution.py:26
  79.2 6.3 %collective-permute-start.8 = (f32[128,256]{1,0:T(8,128)}, f32[128,256]{1,0:T(8,128)S(1)}, u32[]{:S(2)}, u32[]{:S(2)}) collective-permute-start(f32[128,256]{1,0:T(8,128)} %add_add_fusion.refs_1_), channel_id=1, source_target_pairs={{0,8},{8,0},{16,24},{24,16},{1,9},{9,1},{17,25},{25,17},{2,10},{10... | collective-permute-start | bytes 393224 | tf_op jit(solution)/shard_map/ppermute | solution.py:26
  79.8 6.1 %collective-permute-start.24 = (f32[64,256]{1,0:T(8,128)S(1)}, f32[64,256]{1,0:T(8,128)S(1)}, u32[]{:S(2)}, u32[]{:S(2)}) collective-permute-start(f32[64,256]{1,0:T(8,128)S(1)} %add_add_fusion.3.refs_9_), channel_id=1, source_target_pairs={{0,1},{1,0},{2,3},{3,2},{4,5},{5,4},{6,7},{7,6},{8,9},{9,8},{10,11... | collective-permute-start | bytes 196616 | tf_op jit(solution)/shard_map/ppermute | solution.py:26
  79.9 6.8 %collective-permute-start.23 = (f32[64,256]{1,0:T(8,128)S(1)}, f32[64,256]{1,0:T(8,128)S(1)}, u32[]{:S(2)}, u32[]{:S(2)}) collective-permute-start(f32[64,256]{1,0:T(8,128)S(1)} %add_add_fusion.3.refs_9_), channel_id=1, source_target_pairs={{0,24},{8,16},{16,8},{24,0},{1,25},{9,17},{17,9},{25,1},{2,26},{10... | collective-permute-start | bytes 196616 | tf_op jit(solution)/shard_map/ppermute | solution.py:26
  82.4 8.5 %collective-permute-start.14 = (f32[128,256]{1,0:T(8,128)S(1)}, f32[128,256]{1,0:T(8,128)S(1)}, u32[]{:S(2)}, u32[]{:S(2)}) collective-permute-start(f32[128,256]{1,0:T(8,128)S(1)} %collective-permute-done.10.refs_4_), channel_id=1, source_target_pairs={{0,1},{1,0},{2,3},{3,2},{4,5},{5,4},{6,7},{7,6},{8,9},{9,8},{10,11... | collective-permute-start | bytes 393224 | tf_op jit(solution)/shard_map/ppermute | solution.py:26
  85.4 6.1 %collective-permute-start.13 = (f32[128,256]{1,0:T(8,128)S(1)}, f32[128,256]{1,0:T(8,128)S(1)}, u32[]{:S(2)}, u32[]{:S(2)}) collective-permute-start(f32[128,256]{1,0:T(8,128)S(1)} %collective-permute-done.9.refs_3_), channel_id=1, source_target_pairs={{0,1},{1,0},{2,3},{3,2},{4,5},{5,4},{6,7},{7,6},{8,9},{9,8},{10,11... | collective-permute-start | bytes 393224 | tf_op jit(solution)/shard_map/ppermute | solution.py:26
  113.8 6.9 %collective-permute-start.34 = (f32[72,256]{1,0:T(8,128)S(1)}, f32[72,256]{1,0:T(8,128)S(1)}, u32[]{:S(2)}, u32[]{:S(2)}) collective-permute-start(f32[72,256]{1,0:T(8,128)S(1)} %add_add_fusion.2), channel_id=1, source_target_pairs={{0,6},{1,7},{2,4},{3,5},{4,2},{5,3},{6,0},{7,1},{8,14},{9,15},{10,... | collective-permute-start | bytes 221192 | tf_op jit(solution)/shard_map/ppermute | solution.py:26
  118.3 40.8 %collective-permute-start.48 = (bf16[4,256,384]{2,1,0:T(8,128)(2,1)S(1)}, bf16[4,256,384]{2,1,0:T(8,128)(2,1)}, u32[]{:S(2)}, u32[]{:S(2)}) collective-permute-start(bf16[4,256,384]{2,1,0:T(8,128)(2,1)S(1)} %copy-done), channel_id=1, source_target_pairs={{0,8},{8,0},{16,24},{24,16},{1,9},{9,1},{17,25},{25,17},{2,10},{10... | collective-permute-start | bytes 2359304 | tf_op jit(solution)/shard_map/ppermute | solution.py:26
  120.0 41.0 %collective-permute-start.49 = (bf16[4,256,384]{2,1,0:T(8,128)(2,1)S(1)}, bf16[4,256,384]{2,1,0:T(8,128)(2,1)}, u32[]{:S(2)}, u32[]{:S(2)}) collective-permute-start(bf16[4,256,384]{2,1,0:T(8,128)(2,1)S(1)} %copy-done.3), channel_id=1, source_target_pairs={{0,16},{8,24},{16,0},{24,8},{1,17},{9,25},{17,1},{25,9},{2,18},{10... | collective-permute-start | bytes 2359304 | tf_op jit(solution)/shard_map/ppermute | solution.py:26
  120.8 20.9 %collective-permute-start.50 = (bf16[256,384]{1,0:T(8,128)(2,1)S(1)}, bf16[256,384]{1,0:T(8,128)(2,1)}, u32[]{:S(2)}, u32[]{:S(2)}) collective-permute-start(bf16[256,384]{1,0:T(8,128)(2,1)S(1)} %copy-done.4), channel_id=1, source_target_pairs={{0,24},{8,16},{16,8},{24,0},{1,25},{9,17},{17,9},{25,1},{2,26},{10... | collective-permute-start | bytes 589832 | tf_op jit(solution)/shard_map/ppermute | solution.py:26
  123.1 19.3 %collective-permute-start.38 = (f32[72,256]{1,0:T(8,128)S(1)}, f32[72,256]{1,0:T(8,128)S(1)}, u32[]{:S(2)}, u32[]{:S(2)}) collective-permute-start(f32[72,256]{1,0:T(8,128)S(1)} %add_add_fusion.1.refs_1_), channel_id=1, source_target_pairs={{0,1},{1,0},{2,3},{3,2},{4,5},{5,4},{6,7},{7,6},{8,9},{9,8},{10,11... | collective-permute-start | bytes 221192 | tf_op jit(solution)/shard_map/ppermute | solution.py:26
  123.2 20.9 %collective-permute-start.37 = (f32[72,256]{1,0:T(8,128)S(1)}, f32[72,256]{1,0:T(8,128)S(1)}, u32[]{:S(2)}, u32[]{:S(2)}) collective-permute-start(f32[72,256]{1,0:T(8,128)S(1)} %add_add_fusion.1.refs_1_), channel_id=1, source_target_pairs={{0,24},{8,16},{16,8},{24,0},{1,25},{9,17},{17,9},{25,1},{2,26},{10... | collective-permute-start | bytes 221192 | tf_op jit(solution)/shard_map/ppermute | solution.py:26
  146.0 15.8 %collective-permute-start.53 = (bf16[512,384]{1,0:T(8,128)(2,1)}, bf16[512,384]{1,0:T(8,128)(2,1)}, u32[]{:S(2)}, u32[]{:S(2)}) collective-permute-start(bf16[512,384]{1,0:T(8,128)(2,1)} %get-tuple-element.87), channel_id=1, source_target_pairs={{0,24},{8,16},{16,8},{24,0},{1,25},{9,17},{17,9},{25,1},{2,26},{10... | collective-permute-start | bytes 1179656 | tf_op jit(solution)/shard_map/ppermute | solution.py:26
  147.9 19.4 %collective-permute-start.52 = (bf16[512,384]{1,0:T(8,128)(2,1)}, bf16[512,384]{1,0:T(8,128)(2,1)}, u32[]{:S(2)}, u32[]{:S(2)}) collective-permute-start(bf16[512,384]{1,0:T(8,128)(2,1)} %get-tuple-element.87), channel_id=1, source_target_pairs={{0,16},{8,24},{16,0},{24,8},{1,17},{9,25},{17,1},{25,9},{2,18},{10... | collective-permute-start | bytes 1179656 | tf_op jit(solution)/shard_map/ppermute | solution.py:26
  151.2 16.9 %collective-permute-start.51 = (bf16[512,384]{1,0:T(8,128)(2,1)}, bf16[512,384]{1,0:T(8,128)(2,1)}, u32[]{:S(2)}, u32[]{:S(2)}) collective-permute-start(bf16[512,384]{1,0:T(8,128)(2,1)} %get-tuple-element.87), channel_id=1, source_target_pairs={{0,8},{8,0},{16,24},{24,16},{1,9},{9,1},{17,25},{25,17},{2,10},{10... | collective-permute-start | bytes 1179656 | tf_op jit(solution)/shard_map/ppermute | solution.py:26
  159.1 13.9 %collective-permute-start.56 = (bf16[512,256]{1,0:T(8,128)(2,1)}, bf16[512,256]{1,0:T(8,128)(2,1)}, u32[]{:S(2)}, u32[]{:S(2)}) collective-permute-start(bf16[512,256]{1,0:T(8,128)(2,1)} %get-tuple-element.88), channel_id=1, source_target_pairs={{0,24},{8,16},{16,8},{24,0},{1,25},{9,17},{17,9},{25,1},{2,26},{10... | collective-permute-start | bytes 786440 | tf_op jit(solution)/shard_map/ppermute | solution.py:26
  161.0 15.6 %collective-permute-start.55 = (bf16[512,256]{1,0:T(8,128)(2,1)}, bf16[512,256]{1,0:T(8,128)(2,1)}, u32[]{:S(2)}, u32[]{:S(2)}) collective-permute-start(bf16[512,256]{1,0:T(8,128)(2,1)} %get-tuple-element.88), channel_id=1, source_target_pairs={{0,16},{8,24},{16,0},{24,8},{1,17},{9,25},{17,1},{25,9},{2,18},{10... | collective-permute-start | bytes 786440 | tf_op jit(solution)/shard_map/ppermute | solution.py:26
  161.8 16.1 %collective-permute-start.42 = (bf16[256,512]{1,0:T(8,128)(2,1)}, bf16[256,512]{1,0:T(8,128)(2,1)}, u32[]{:S(2)}, u32[]{:S(2)}) collective-permute-start(bf16[256,512]{1,0:T(8,128)(2,1)} %get-tuple-element.79.a), channel_id=1, source_target_pairs={{0,8},{8,0},{16,24},{24,16},{1,9},{9,1},{17,25},{25,17},{2,10},{10... | collective-permute-start | bytes 786440 | tf_op jit(solution)/shard_map/ppermute | solution.py:26
  167.3 14.9 %collective-permute-start.44 = (bf16[256,512]{1,0:T(8,128)(2,1)}, bf16[256,512]{1,0:T(8,128)(2,1)}, u32[]{:S(2)}, u32[]{:S(2)}) collective-permute-start(bf16[256,512]{1,0:T(8,128)(2,1)} %get-tuple-element.80.b), channel_id=1, source_target_pairs={{0,16},{8,24},{16,0},{24,8},{1,17},{9,25},{17,1},{25,9},{2,18},{10... | collective-permute-start | bytes 786440 | tf_op jit(solution)/shard_map/ppermute | solution.py:26
  168.1 19.0 %collective-permute-start.54 = (bf16[512,256]{1,0:T(8,128)(2,1)}, bf16[512,256]{1,0:T(8,128)(2,1)}, u32[]{:S(2)}, u32[]{:S(2)}) collective-permute-start(bf16[512,256]{1,0:T(8,128)(2,1)} %get-tuple-element.88), channel_id=1, source_target_pairs={{0,8},{8,0},{16,24},{24,16},{1,9},{9,1},{17,25},{25,17},{2,10},{10... | collective-permute-start | bytes 786440 | tf_op jit(solution)/shard_map/ppermute | solution.py:26
  173.0 18.4 %collective-permute-start.47 = (bf16[256,512]{1,0:T(8,128)(2,1)}, bf16[256,512]{1,0:T(8,128)(2,1)}, u32[]{:S(2)}, u32[]{:S(2)}) collective-permute-start(bf16[256,512]{1,0:T(8,128)(2,1)} %get-tuple-element.79.a), channel_id=1, source_target_pairs={{0,16},{8,24},{16,0},{24,8},{1,17},{9,25},{17,1},{25,9},{2,18},{10... | collective-permute-start | bytes 786440 | tf_op jit(solution)/shard_map/ppermute | solution.py:26
  176.6 14.7 %collective-permute-start.46 = (bf16[256,512]{1,0:T(8,128)(2,1)}, bf16[256,512]{1,0:T(8,128)(2,1)}, u32[]{:S(2)}, u32[]{:S(2)}) collective-permute-start(bf16[256,512]{1,0:T(8,128)(2,1)} %get-tuple-element.80.b), channel_id=1, source_target_pairs={{0,8},{8,0},{16,24},{24,16},{1,9},{9,1},{17,25},{25,17},{2,10},{10... | collective-permute-start | bytes 786440 | tf_op jit(solution)/shard_map/ppermute | solution.py:26
  177.9 16.1 %collective-permute-start.43 = (bf16[256,512]{1,0:T(8,128)(2,1)}, bf16[256,512]{1,0:T(8,128)(2,1)}, u32[]{:S(2)}, u32[]{:S(2)}) collective-permute-start(bf16[256,512]{1,0:T(8,128)(2,1)} %collective-permute-done.42.refs_0_), channel_id=1, source_target_pairs={{0,16},{8,24},{16,0},{24,8},{1,17},{9,25},{17,1},{25,9},{2,18},{10... | collective-permute-start | bytes 786440 | tf_op jit(solution)/shard_map/ppermute | solution.py:26
  182.3 11.8 %collective-permute-start.45 = (bf16[256,512]{1,0:T(8,128)(2,1)}, bf16[256,512]{1,0:T(8,128)(2,1)}, u32[]{:S(2)}, u32[]{:S(2)}) collective-permute-start(bf16[256,512]{1,0:T(8,128)(2,1)} %collective-permute-done.44.refs_1_), channel_id=1, source_target_pairs={{0,8},{8,0},{16,24},{24,16},{1,9},{9,1},{17,25},{25,17},{2,10},{10... | collective-permute-start | bytes 786440 | tf_op jit(solution)/shard_map/ppermute | solution.py:26
  (51 other events, 349.7 us)

commit v5 on v4

--- a/solution.py
+++ b/solution.py
@@ -573,14 +573,12 @@
     m, e, f, w0, keep, give = first(place, diagonals, crosses, x, [pieces[1], p2, p3], raw, ahead)
 
     parts = fold(keep, send(give, "feat", 1))
-    parts, e = lax.optimization_barrier((parts, e))
+    parts, e, f = lax.optimization_barrier((parts, e, f))
     mine = total([parts[0]] + send_all(parts[1:], "dp", PEERS))
-    pairs = send_all([e] * len(PEERS), "dp", PEERS)
+    pairs_a, pairs_b = [[send(block, "dp", s) for s in (1, 2)] for block in (e, f)]
     raws = raw_first(place, w0, x, messages, share)
-    bundle = over_chips(mine)
-    bundle, f = lax.optimization_barrier((bundle, f))
-    bundles = gather_group(bundle)
-    pairs += send_all([f] * len(PEERS), "dp", PEERS)
+    bundles = gather_group(over_chips(mine))
+    pairs = pairs_a + [send(pairs_a[0], "dp", 2)] + pairs_b + [send(pairs_b[1], "dp", 1)]
     a, b, e, w1 = second(place, bundles, m, early)
 
     ax, by = send(a, "dp", 1), send(b, "dp", 2)

time: 197 us -> 196 us (level)
  no operation moved by 1% of the time
where the time goes in v5:
time: 196 us; the launch traced here: 195 us
  waiting for transfers between devices  80.6 us (41%)
  starting transfers between devices  58.3 us (30%)
  Pallas kernels  45.4 us (23%)
  local copies, waits for them, and re-layouts  6.14 us (3%)
  other arithmetic  4.27 us (2%)
    ppermute x57, waiting for transfers between devices, send(): return lax.ppermute(block, axis, [(i, i ^ shift) for i in range(count)])  80.6 us
    ppermute x57, starting transfers between devices, send(): return lax.ppermute(block, axis, [(i, i ^ shift) for i in range(count)])  58.3 us
    pallas_call x1, Pallas kernels, first(): pl.pallas_call(functools.partial(first_kernel, raw, tile), out_shape=tupl...  10.6 us
    pallas_call x1, Pallas kernels, second(): pl.pallas_call(second_kernel, out_shape=tuple((shape(rows, n, dtype=BF16)...  6.92 us
    pallas_call x1, Pallas kernels, own_gram(): pl.pallas_call(own_gram_kernel, out_shape=(half, half), grid_spec=pltpu.P...  5.39 us
    pallas_call x2, Pallas kernels, put(): pl.pallas_call(functools.partial(put_kernel, spots, share), out_shape=sha...  5.08 us
    dynamic_slice x2, local copies, waits for them, and re-layouts, run(): cuts[s] = lax.dynamic_slice(source, (0, (me ^ s) * share), (rows, share))  5.04 us
    pallas_call x1, Pallas kernels, near_gram(): pl.pallas_call(functools.partial(near_gram_kernel, chunk), out_shape=(sha...  4.96 us
  transfers between devices with their start and end apart: 57, of which 34 were waited for; matrix products, arithmetic and copies ran while one was open for 2% of the time, Pallas kernels for 15%

profile of v5, /device:TPU:0, one launch (start us, length us, event | category | flops | bytes accessed | tf_op | source)
XLA Modules:
  0.0 195.2 jit_solution(5999065092827501538)
XLA Ops:
  0.0 2.7 %dynamic-slice_bitcast_fusion = (bf16[256,2048]{1,0:T(8,128)(2,1)}, bf16[256,2048]{1,0:T(8,128)(2,1)S(1)}) fusion(bf16[1,256,8192]{2,1,0:T(8,128)(2,1)} %param.1, s32[]{:T(128)S(6)} %select_n.23, s32[]{:T(128)S(6)} %select_n.22), kind=kLoop, calls=%fused_computation | loop fusion | bytes 4194312 | tf_op jit(solution)/shard_map/dynamic_slice | solution.py:554
  2.7 3.0 %collective-permute-start.6 = (bf16[256,2048]{1,0:T(8,128)(2,1)S(1)}, bf16[256,2048]{1,0:T(8,128)(2,1)}, u32[]{:S(2)}, u32[]{:S(2)}) collective-permute-start(bf16[256,2048]{1,0:T(8,128)(2,1)S(1)} %get-tuple-element.50), channel_id=1, source_target_pairs={{0,8},{8,0},{16,24},{24,16},{1,9},{9,1},{17,25},{25,17},{2,10},{10... | collective-permute-start | bytes 3145736 | tf_op jit(solution)/shard_map/ppermute | solution.py:26
  5.7 2.3 %constant_dynamic-slice_fusion = bf16[256,2048]{1,0:T(8,128)(2,1)} fusion(bf16[256,8192]{1,0:T(8,128)(2,1)} %bitcast.24, s32[]{:T(128)S(6)} %select_n.24), kind=kLoop, calls=%fused_computation.23 | loop fusion | bytes 2097156 | tf_op jit(solution)/shard_map/dynamic_slice | solution.py:554
  10.1 5.4 %own_gram.1 = (f32[128,256]{1,0:T(8,128)}, f32[128,256]{1,0:T(8,128)}) custom-call(s32[2]{0:T(128)} %pad_add_fusion.place.refs_0_, bf16[256,8192]{1,0:T(8,128)(2,1)} %bitcast.25), custom_call_target="tpu_custom_call" | custom-call | flops 1073741824 | bytes 4194304 | tf_op jit(solution)/shard_map/own_gram/pallas_call | solution.py:136
  18.0 4.1 %collective-permute-start.5 = (f32[128,256]{1,0:T(8,128)S(1)}, f32[128,256]{1,0:T(8,128)S(1)}, u32[]{:S(2)}, u32[]{:S(2)}) collective-permute-start(f32[128,256]{1,0:T(8,128)S(1)} %add.117), channel_id=1, source_target_pairs={{0,6},{1,7},{2,4},{3,5},{4,2},{5,3},{6,0},{7,1},{8,14},{9,15},{10,... | collective-permute-start | bytes 393224 | tf_op jit(solution)/shard_map/ppermute | solution.py:26
  22.1 4.4 %collective-permute-done.5 = f32[128,256]{1,0:T(8,128)S(1)} collective-permute-done((f32[128,256]{1,0:T(8,128)S(1)}, f32[128,256]{1,0:T(8,128)S(1)}, u32[]{:S(2)}, u32[]{:S(2)}) %collective-permute-start.5) | collective-permute-done | bytes 131104 | tf_op jit(solution)/shard_map/ppermute | solution.py:26
  26.6 5.5 %collective-permute-start.3 = (f32[128,256]{1,0:T(8,128)S(1)}, f32[128,256]{1,0:T(8,128)S(1)}, u32[]{:S(2)}, u32[]{:S(2)}) collective-permute-start(f32[128,256]{1,0:T(8,128)S(1)} %add.117), channel_id=1, source_target_pairs={{0,2},{1,3},{2,0},{3,1},{4,6},{5,7},{6,4},{7,5},{8,10},{9,11},{10,... | collective-permute-start | bytes 393224 | tf_op jit(solution)/shard_map/ppermute | solution.py:26
  33.6 2.7 %collective-permute-done.3 = f32[128,256]{1,0:T(8,128)S(1)} collective-permute-done((f32[128,256]{1,0:T(8,128)S(1)}, f32[128,256]{1,0:T(8,128)S(1)}, u32[]{:S(2)}, u32[]{:S(2)}) %collective-permute-start.3) | collective-permute-done | bytes 131104 | tf_op jit(solution)/shard_map/ppermute | solution.py:26
  37.0 5.0 %near_gram.1 = (f32[256,256]{1,0:T(8,128)}, bf16[4,256,384]{2,1,0:T(8,128)(2,1)}, bf16[4,256,384]{2,1,0:T(8,128)(2,1)}, bf16[256,384]{1,0:T(8,128)(2,1)}) custom-call(s32[2]{0:T(128)} %pad_add_fusion.place.refs_0_, bf16[256,8192]{1,0:T(8,128)(2,1)} %bitcast.26, bf16[256,2048]{1,0:T(8,128)(2,1)} %collective-permute-done.6.p1.refs_18_), custom_call_target="tpu_custom_call" | custom-call | flops 268435456 | bytes 2097152 | tf_op jit(solution)/shard_map/near_gram/pallas_call | solution.py:201
  42.0 10.7 %collective-permute-done.1.p3.refs_20_ = bf16[256,2048]{1,0:T(8,128)(2,1)} collective-permute-done((bf16[256,2048]{1,0:T(8,128)(2,1)}, bf16[256,2048]{1,0:T(8,128)(2,1)}, u32[]{:S(2)}, u32[]{:S(2)}) %collective-permute-start.1) | collective-permute-done | bytes 1048608 | tf_op jit(solution)/shard_map/ppermute | solution.py:26
  52.7 3.9 %collective-permute-done.p2.refs_19_ = bf16[256,2048]{1,0:T(8,128)(2,1)} collective-permute-done((bf16[256,2048]{1,0:T(8,128)(2,1)}, bf16[256,2048]{1,0:T(8,128)(2,1)}, u32[]{:S(2)}, u32[]{:S(2)}) %collective-permute-start) | collective-permute-done | bytes 1048608 | tf_op jit(solution)/shard_map/ppermute | solution.py:26
  56.6 3.8 %far_gram.1 = (f32[4,64,256]{2,1,0:T(8,128)}, f32[4,64,256]{2,1,0:T(8,128)}, bf16[4,256,384]{2,1,0:T(8,128)(2,1)}) custom-call(s32[2]{0:T(128)} %pad_add_fusion.place.refs_0_, f32[256,256]{1,0:T(8,128)} %get-tuple-element.52.near, bf16[256,2048]{1,0:T(8,128)(2,1)} %collective-permute-done.p2.refs_19_, ...), custom_call_target="tpu_custom_call", output_to_operand_aliasing={{2}: (4, {})} | custom-call | flops 268435456 | bytes 2097152 | tf_op jit(solution)/shard_map/far_gram/pallas_call | solution.py:243
  60.5 1.7 collective-permute-done.7
  67.5 2.2 %collective-permute-done.16 = f32[64,256]{1,0:T(8,128)S(1)} collective-permute-done((f32[64,256]{1,0:T(8,128)S(1)}, f32[64,256]{1,0:T(8,128)S(1)}, u32[]{:S(2)}, u32[]{:S(2)}) %collective-permute-start.16) | collective-permute-done | bytes 65568 | tf_op jit(solution)/shard_map/ppermute | solution.py:26
  70.4 3.7 %collective-permute-start.20 = (f32[64,256]{1,0:T(8,128)S(1)}, f32[64,256]{1,0:T(8,128)S(1)}, u32[]{:S(2)}, u32[]{:S(2)}) collective-permute-start(f32[64,256]{1,0:T(8,128)S(1)} %add_add_fusion.4), channel_id=1, source_target_pairs={{0,6},{1,7},{2,4},{3,5},{4,2},{5,3},{6,0},{7,1},{8,14},{9,15},{10,... | collective-permute-start | bytes 196616 | tf_op jit(solution)/shard_map/ppermute | solution.py:26
  80.0 2.5 %collective-permute-start.23 = (f32[64,256]{1,0:T(8,128)S(1)}, f32[64,256]{1,0:T(8,128)S(1)}, u32[]{:S(2)}, u32[]{:S(2)}) collective-permute-start(f32[64,256]{1,0:T(8,128)S(1)} %add_add_fusion.3.refs_9_), channel_id=1, source_target_pairs={{0,24},{8,16},{16,8},{24,0},{1,25},{9,17},{17,9},{25,1},{2,26},{10... | collective-permute-start | bytes 196616 | tf_op jit(solution)/shard_map/ppermute | solution.py:26
  82.6 2.8 %collective-permute-done.9.refs_3_ = f32[128,256]{1,0:T(8,128)S(1)} collective-permute-done((f32[128,256]{1,0:T(8,128)}, f32[128,256]{1,0:T(8,128)S(1)}, u32[]{:S(2)}, u32[]{:S(2)}) %collective-permute-start.9) | collective-permute-done | bytes 131104 | tf_op jit(solution)/shard_map/ppermute | solution.py:26
  87.3 2.9 %collective-permute-done.22.refs_11_ = f32[64,256]{1,0:T(8,128)S(1)} collective-permute-done((f32[64,256]{1,0:T(8,128)S(1)}, f32[64,256]{1,0:T(8,128)S(1)}, u32[]{:S(2)}, u32[]{:S(2)}) %collective-permute-start.22) | collective-permute-done | bytes 65568 | tf_op jit(solution)/shard_map/ppermute | solution.py:26
  93.5 10.6 %first.1 = (bf16[512,2048]{1,0:T(8,128)(2,1)}, bf16[512,384]{1,0:T(8,128)(2,1)}, bf16[512,256]{1,0:T(8,128)(2,1)}, bf16[2,256,512]{2,1,0:T(8,128)(2,1)}, f32[4,72,256]{2,1,0:T(8,128)}, /*index=5*/f32[4,72,256]{2,1,0:T(8,128)}) custom-call(s32[2]{0:T(128)} %pad_add_fusion.place.refs_0_, f32[128,256]{1,0:T(8,128)} %add_add_fusion.refs_1_, ...), custom_call_target="tpu_custom_call" | custom-call | flops 4563402752 | bytes 6291456 | tf_op jit(solution)/shard_map/first/pallas_call | solution.py:343
  108.7 1.9 collective-permute-start.31
  114.0 3.8 %collective-permute-start.34 = (f32[72,256]{1,0:T(8,128)S(1)}, f32[72,256]{1,0:T(8,128)S(1)}, u32[]{:S(2)}, u32[]{:S(2)}) collective-permute-start(f32[72,256]{1,0:T(8,128)S(1)} %add_add_fusion.2), channel_id=1, source_target_pairs={{0,6},{1,7},{2,4},{3,5},{4,2},{5,3},{6,0},{7,1},{8,14},{9,15},{10,... | collective-permute-start | bytes 221192 | tf_op jit(solution)/shard_map/ppermute | solution.py:26
  124.4 16.4 %collective-permute-done.50.d = bf16[256,384]{1,0:T(8,128)(2,1)S(1)} collective-permute-done((bf16[256,384]{1,0:T(8,128)(2,1)S(1)}, bf16[256,384]{1,0:T(8,128)(2,1)S(1)}, u32[]{:S(2)}, u32[]{:S(2)}) %collective-permute-start.50) | collective-permute-done | bytes 196640 | tf_op jit(solution)/shard_map/ppermute | solution.py:26
  143.2 2.9 %collective-permute-done.37.refs_4_ = f32[72,256]{1,0:T(8,128)S(1)} collective-permute-done((f32[72,256]{1,0:T(8,128)S(1)}, f32[72,256]{1,0:T(8,128)S(1)}, u32[]{:S(2)}, u32[]{:S(2)}) %collective-permute-start.37) | collective-permute-done | bytes 73760 | tf_op jit(solution)/shard_map/ppermute | solution.py:26
  147.3 2.6 %collective-permute-done.36.refs_3_ = f32[72,256]{1,0:T(8,128)S(1)} collective-permute-done((f32[72,256]{1,0:T(8,128)S(1)}, f32[72,256]{1,0:T(8,128)S(1)}, u32[]{:S(2)}, u32[]{:S(2)}) %collective-permute-start.36) | collective-permute-done | bytes 73760 | tf_op jit(solution)/shard_map/ppermute | solution.py:26
  156.1 6.9 %second.1 = (bf16[256,512]{1,0:T(8,128)(2,1)}, bf16[256,512]{1,0:T(8,128)(2,1)}, bf16[256,1024]{1,0:T(8,128)(2,1)}, bf16[1,256,512]{2,1,0:T(8,128)(2,1)}) custom-call(s32[2]{0:T(128)} %pad_add_fusion.place.refs_0_, f32[72,256]{1,0:T(8,128)} %copy-done.5, f32[72,256]{1,0:T(8,128)} %copy-done.19, f32[72,256]{1,0:T(8,128)} %copy-done.18, f32[72,256]{1,0:T(8,128)} %copy-done.17, ...), custom_call_target="tpu_custom_call" | custom-call | flops 1879048192 | bytes 3145728 | tf_op jit(solution)/shard_map/second/pallas_call | solution.py:402
  166.5 1.7 collective-permute-start.53
  168.5 4.8 %collective-permute-done.56.refs_5_ = bf16[512,256]{1,0:T(8,128)(2,1)S(1)} collective-permute-done((bf16[512,256]{1,0:T(8,128)(2,1)S(1)}, bf16[512,256]{1,0:T(8,128)(2,1)S(1)}, u32[]{:S(2)}, u32[]{:S(2)}) %collective-permute-start.56) | collective-permute-done | bytes 262176 | tf_op jit(solution)/shard_map/ppermute | solution.py:26
  174.3 4.8 %collective-permute-done.42.refs_0_ = bf16[256,512]{1,0:T(8,128)(2,1)} collective-permute-done((bf16[256,512]{1,0:T(8,128)(2,1)}, bf16[256,512]{1,0:T(8,128)(2,1)}, u32[]{:S(2)}, u32[]{:S(2)}) %collective-permute-start.42) | collective-permute-done | bytes 262176 | tf_op jit(solution)/shard_map/ppermute | solution.py:26
  181.0 4.5 %raw_first.1.raws = bf16[3,512,384]{2,1,0:T(8,128)(2,1)} custom-call(s32[2]{0:T(128)} %pad_add_fusion.place.refs_0_, bf16[2,256,512]{2,1,0:T(8,128)(2,1)} %get-tuple-element.81.w, bf16[256,8192]{1,0:T(8,128)(2,1)} %bitcast.28, bf16[4,256,384]{2,1,0:T(8,128)(2,1)} %collective-permute-done.48.xs, bf16[4,256,384]{2,1,0:T(8,128)(2,1)} %collective-permute-done.49.ys, ...), custom_call_target="tpu_custom_call" | custom-call | flops 603979776 | bytes 3538944 | tf_op jit(solution)/shard_map/raw_first/pallas_call | solution.py:448
  185.5 4.2 %late.1.refs_4_ = bf16[256,8192]{1,0:T(8,128)(2,1)} custom-call(s32[2]{0:T(128)} %pad_add_fusion.place.refs_0_, bf16[1,256,512]{2,1,0:T(8,128)(2,1)} %get-tuple-element.79.w, bf16[256,512]{1,0:T(8,128)(2,1)} %get-tuple-element.77.a, bf16[256,512]{1,0:T(8,128)(2,1)} %get-tuple-element.78.b, bf16[256,1024]{1,0:T(8,128)(2,1)} %get-tuple-element.80.e, ...), custom_call_target="tpu_custom_call" | custom-call | flops 805306368 | bytes 4718592 | tf_op jit(solution)/shard_map/late/pallas_call | solution.py:491
  189.8 2.6 %put.2.refs_2_ = bf16[256,8192]{1,0:T(8,128)(2,1)} custom-call(s32[2]{0:T(128)} %pad_add_fusion.place.refs_0_, bf16[256,512]{1,0:T(8,128)(2,1)} %collective-permute-done.42.refs_0_, bf16[256,512]{1,0:T(8,128)(2,1)} %collective-permute-done.44.refs_1_, bf16[256,512]{1,0:T(8,128)(2,1)} %collective-permute-done.46.refs_2_, ...), custom_call_target="tpu_custom_call", output_to_operand_aliasing={{}: (5, {})} | custom-call | bytes 2097152 | tf_op jit(solution)/shard_map/put/pallas_call | solution.py:520
  192.6 2.4 %put.3 = bf16[256,8192]{1,0:T(8,128)(2,1)} custom-call(s32[2]{0:T(128)} %pad_add_fusion.place.refs_0_, bf16[256,512]{1,0:T(8,128)(2,1)} %collective-permute-done.43.refs_0_, bf16[256,512]{1,0:T(8,128)(2,1)} %collective-permute-done.45.refs_1_, bf16[256,8192]{1,0:T(8,128)(2,1)} %put.2.refs_2_), custom_call_target="tpu_custom_call", output_to_operand_aliasing={{}: (3, {})} | custom-call | bytes 1048576 | tf_op jit(solution)/shard_map/put/pallas_call | solution.py:520
  (162 shorter events, 55.2 us)
Async XLA Ops:
  2.7 34.3 %collective-permute-start.6 = (bf16[256,2048]{1,0:T(8,128)(2,1)S(1)}, bf16[256,2048]{1,0:T(8,128)(2,1)}, u32[]{:S(2)}, u32[]{:S(2)}) collective-permute-start(bf16[256,2048]{1,0:T(8,128)(2,1)S(1)} %get-tuple-element.50), channel_id=1, source_target_pairs={{0,8},{8,0},{16,24},{24,16},{1,9},{9,1},{17,25},{25,17},{2,10},{10... | collective-permute-start | bytes 3145736 | tf_op jit(solution)/shard_map/ppermute | solution.py:26
  8.0 44.7 %collective-permute-start.1 = (bf16[256,2048]{1,0:T(8,128)(2,1)}, bf16[256,2048]{1,0:T(8,128)(2,1)}, u32[]{:S(2)}, u32[]{:S(2)}) collective-permute-start(bf16[256,2048]{1,0:T(8,128)(2,1)} %constant_dynamic-slice_fusion), channel_id=1, source_target_pairs={{0,24},{8,16},{16,8},{24,0},{1,25},{9,17},{17,9},{25,1},{2,26},{10... | collective-permute-start | bytes 3145736 | tf_op jit(solution)/shard_map/ppermute | solution.py:26
  9.5 47.1 %collective-permute-start = (bf16[256,2048]{1,0:T(8,128)(2,1)}, bf16[256,2048]{1,0:T(8,128)(2,1)}, u32[]{:S(2)}, u32[]{:S(2)}) collective-permute-start(bf16[256,2048]{1,0:T(8,128)(2,1)} %get-tuple-element.46), channel_id=1, source_target_pairs={{0,16},{8,24},{16,0},{24,8},{1,17},{9,25},{17,1},{25,9},{2,18},{10... | collective-permute-start | bytes 3145736 | tf_op jit(solution)/shard_map/ppermute | solution.py:26
  18.0 8.6 %collective-permute-start.5 = (f32[128,256]{1,0:T(8,128)S(1)}, f32[128,256]{1,0:T(8,128)S(1)}, u32[]{:S(2)}, u32[]{:S(2)}) collective-permute-start(f32[128,256]{1,0:T(8,128)S(1)} %add.117), channel_id=1, source_target_pairs={{0,6},{1,7},{2,4},{3,5},{4,2},{5,3},{6,0},{7,1},{8,14},{9,15},{10,... | collective-permute-start | bytes 393224 | tf_op jit(solution)/shard_map/ppermute | solution.py:26
  22.1 11.5 %collective-permute-start.4 = (f32[128,256]{1,0:T(8,128)S(1)}, f32[128,256]{1,0:T(8,128)S(1)}, u32[]{:S(2)}, u32[]{:S(2)}) collective-permute-start(f32[128,256]{1,0:T(8,128)S(1)} %add.117), channel_id=1, source_target_pairs={{0,4},{1,5},{2,6},{3,7},{4,0},{5,1},{6,2},{7,3},{8,12},{9,13},{10,... | collective-permute-start | bytes 393224 | tf_op jit(solution)/shard_map/ppermute | solution.py:26
  26.6 9.7 %collective-permute-start.3 = (f32[128,256]{1,0:T(8,128)S(1)}, f32[128,256]{1,0:T(8,128)S(1)}, u32[]{:S(2)}, u32[]{:S(2)}) collective-permute-start(f32[128,256]{1,0:T(8,128)S(1)} %add.117), channel_id=1, source_target_pairs={{0,2},{1,3},{2,0},{3,1},{4,6},{5,7},{6,4},{7,5},{8,10},{9,11},{10,... | collective-permute-start | bytes 393224 | tf_op jit(solution)/shard_map/ppermute | solution.py:26
  70.4 6.1 %collective-permute-start.20 = (f32[64,256]{1,0:T(8,128)S(1)}, f32[64,256]{1,0:T(8,128)S(1)}, u32[]{:S(2)}, u32[]{:S(2)}) collective-permute-start(f32[64,256]{1,0:T(8,128)S(1)} %add_add_fusion.4), channel_id=1, source_target_pairs={{0,6},{1,7},{2,4},{3,5},{4,2},{5,3},{6,0},{7,1},{8,14},{9,15},{10,... | collective-permute-start | bytes 196616 | tf_op jit(solution)/shard_map/ppermute | solution.py:26
  74.9 7.6 %collective-permute-start.10 = (f32[128,256]{1,0:T(8,128)}, f32[128,256]{1,0:T(8,128)S(1)}, u32[]{:S(2)}, u32[]{:S(2)}) collective-permute-start(f32[128,256]{1,0:T(8,128)} %add_add_fusion.refs_1_), channel_id=1, source_target_pairs={{0,24},{8,16},{16,8},{24,0},{1,25},{9,17},{17,9},{25,1},{2,26},{10... | collective-permute-start | bytes 393224 | tf_op jit(solution)/shard_map/ppermute | solution.py:26
  76.6 8.9 %collective-permute-start.9 = (f32[128,256]{1,0:T(8,128)}, f32[128,256]{1,0:T(8,128)S(1)}, u32[]{:S(2)}, u32[]{:S(2)}) collective-permute-start(f32[128,256]{1,0:T(8,128)} %add_add_fusion.refs_1_), channel_id=1, source_target_pairs={{0,16},{8,24},{16,0},{24,8},{1,17},{9,25},{17,1},{25,9},{2,18},{10... | collective-permute-start | bytes 393224 | tf_op jit(solution)/shard_map/ppermute | solution.py:26
  79.3 6.3 %collective-permute-start.8 = (f32[128,256]{1,0:T(8,128)}, f32[128,256]{1,0:T(8,128)S(1)}, u32[]{:S(2)}, u32[]{:S(2)}) collective-permute-start(f32[128,256]{1,0:T(8,128)} %add_add_fusion.refs_1_), channel_id=1, source_target_pairs={{0,8},{8,0},{16,24},{24,16},{1,9},{9,1},{17,25},{25,17},{2,10},{10... | collective-permute-start | bytes 393224 | tf_op jit(solution)/shard_map/ppermute | solution.py:26
  80.0 6.8 %collective-permute-start.23 = (f32[64,256]{1,0:T(8,128)S(1)}, f32[64,256]{1,0:T(8,128)S(1)}, u32[]{:S(2)}, u32[]{:S(2)}) collective-permute-start(f32[64,256]{1,0:T(8,128)S(1)} %add_add_fusion.3.refs_9_), channel_id=1, source_target_pairs={{0,24},{8,16},{16,8},{24,0},{1,25},{9,17},{17,9},{25,1},{2,26},{10... | collective-permute-start | bytes 196616 | tf_op jit(solution)/shard_map/ppermute | solution.py:26
  82.5 8.5 %collective-permute-start.14 = (f32[128,256]{1,0:T(8,128)S(1)}, f32[128,256]{1,0:T(8,128)S(1)}, u32[]{:S(2)}, u32[]{:S(2)}) collective-permute-start(f32[128,256]{1,0:T(8,128)S(1)} %collective-permute-done.10.refs_4_), channel_id=1, source_target_pairs={{0,1},{1,0},{2,3},{3,2},{4,5},{5,4},{6,7},{7,6},{8,9},{9,8},{10,11... | collective-permute-start | bytes 393224 | tf_op jit(solution)/shard_map/ppermute | solution.py:26
  85.4 6.1 %collective-permute-start.13 = (f32[128,256]{1,0:T(8,128)S(1)}, f32[128,256]{1,0:T(8,128)S(1)}, u32[]{:S(2)}, u32[]{:S(2)}) collective-permute-start(f32[128,256]{1,0:T(8,128)S(1)} %collective-permute-done.9.refs_3_), channel_id=1, source_target_pairs={{0,1},{1,0},{2,3},{3,2},{4,5},{5,4},{6,7},{7,6},{8,9},{9,8},{10,11... | collective-permute-start | bytes 393224 | tf_op jit(solution)/shard_map/ppermute | solution.py:26
  114.0 6.9 %collective-permute-start.34 = (f32[72,256]{1,0:T(8,128)S(1)}, f32[72,256]{1,0:T(8,128)S(1)}, u32[]{:S(2)}, u32[]{:S(2)}) collective-permute-start(f32[72,256]{1,0:T(8,128)S(1)} %add_add_fusion.2), channel_id=1, source_target_pairs={{0,6},{1,7},{2,4},{3,5},{4,2},{5,3},{6,0},{7,1},{8,14},{9,15},{10,... | collective-permute-start | bytes 221192 | tf_op jit(solution)/shard_map/ppermute | solution.py:26
  117.8 6.5 %collective-permute-start.32 = (f32[72,256]{1,0:T(8,128)S(1)}, f32[72,256]{1,0:T(8,128)S(1)}, u32[]{:S(2)}, u32[]{:S(2)}) collective-permute-start(f32[72,256]{1,0:T(8,128)S(1)} %add_add_fusion.2), channel_id=1, source_target_pairs={{0,2},{1,3},{2,0},{3,1},{4,6},{5,7},{6,4},{7,5},{8,10},{9,11},{10,... | collective-permute-start | bytes 221192 | tf_op jit(solution)/shard_map/ppermute | solution.py:26
  118.4 46.6 %collective-permute-start.48 = (bf16[4,256,384]{2,1,0:T(8,128)(2,1)S(1)}, bf16[4,256,384]{2,1,0:T(8,128)(2,1)}, u32[]{:S(2)}, u32[]{:S(2)}) collective-permute-start(bf16[4,256,384]{2,1,0:T(8,128)(2,1)S(1)} %copy-done), channel_id=1, source_target_pairs={{0,8},{8,0},{16,24},{24,16},{1,9},{9,1},{17,25},{25,17},{2,10},{10... | collective-permute-start | bytes 2359304 | tf_op jit(solution)/shard_map/ppermute | solution.py:26
  120.1 46.1 %collective-permute-start.49 = (bf16[4,256,384]{2,1,0:T(8,128)(2,1)S(1)}, bf16[4,256,384]{2,1,0:T(8,128)(2,1)}, u32[]{:S(2)}, u32[]{:S(2)}) collective-permute-start(bf16[4,256,384]{2,1,0:T(8,128)(2,1)S(1)} %copy-done.7), channel_id=1, source_target_pairs={{0,16},{8,24},{16,0},{24,8},{1,17},{9,25},{17,1},{25,9},{2,18},{10... | collective-permute-start | bytes 2359304 | tf_op jit(solution)/shard_map/ppermute | solution.py:26
  120.9 19.9 %collective-permute-start.50 = (bf16[256,384]{1,0:T(8,128)(2,1)S(1)}, bf16[256,384]{1,0:T(8,128)(2,1)S(1)}, u32[]{:S(2)}, u32[]{:S(2)}) collective-permute-start(bf16[256,384]{1,0:T(8,128)(2,1)S(1)} %copy-done.8), channel_id=1, source_target_pairs={{0,24},{8,16},{16,8},{24,0},{1,25},{9,17},{17,9},{25,1},{2,26},{10... | collective-permute-start | bytes 589832 | tf_op jit(solution)/shard_map/ppermute | solution.py:26
  123.1 28.2 %collective-permute-start.55 = (bf16[512,256]{1,0:T(8,128)(2,1)}, bf16[512,256]{1,0:T(8,128)(2,1)S(1)}, u32[]{:S(2)}, u32[]{:S(2)}) collective-permute-start(bf16[512,256]{1,0:T(8,128)(2,1)} %get-tuple-element.86), channel_id=1, source_target_pairs={{0,16},{8,24},{16,0},{24,8},{1,17},{9,25},{17,1},{25,9},{2,18},{10... | collective-permute-start | bytes 786440 | tf_op jit(solution)/shard_map/ppermute | solution.py:26
  124.3 18.1 %collective-permute-start.38 = (f32[72,256]{1,0:T(8,128)S(1)}, f32[72,256]{1,0:T(8,128)S(1)}, u32[]{:S(2)}, u32[]{:S(2)}) collective-permute-start(f32[72,256]{1,0:T(8,128)S(1)} %add_add_fusion.1.refs_1_), channel_id=1, source_target_pairs={{0,1},{1,0},{2,3},{3,2},{4,5},{5,4},{6,7},{7,6},{8,9},{9,8},{10,11... | collective-permute-start | bytes 221192 | tf_op jit(solution)/shard_map/ppermute | solution.py:26
  142.4 7.4 %collective-permute-start.36 = (f32[72,256]{1,0:T(8,128)S(1)}, f32[72,256]{1,0:T(8,128)S(1)}, u32[]{:S(2)}, u32[]{:S(2)}) collective-permute-start(f32[72,256]{1,0:T(8,128)S(1)} %add_add_fusion.1.refs_1_), channel_id=1, source_target_pairs={{0,16},{8,24},{16,0},{24,8},{1,17},{9,25},{17,1},{25,9},{2,18},{10... | collective-permute-start | bytes 221192 | tf_op jit(solution)/shard_map/ppermute | solution.py:26
  149.9 16.6 %collective-permute-start.51 = (bf16[512,384]{1,0:T(8,128)(2,1)}, bf16[512,384]{1,0:T(8,128)(2,1)}, u32[]{:S(2)}, u32[]{:S(2)}) collective-permute-start(bf16[512,384]{1,0:T(8,128)(2,1)} %get-tuple-element.85), channel_id=1, source_target_pairs={{0,8},{8,0},{16,24},{24,16},{1,9},{9,1},{17,25},{25,17},{2,10},{10... | collective-permute-start | bytes 1179656 | tf_op jit(solution)/shard_map/ppermute | solution.py:26
  152.6 11.5 %collective-permute-start.54 = (bf16[512,256]{1,0:T(8,128)(2,1)}, bf16[512,256]{1,0:T(8,128)(2,1)S(1)}, u32[]{:S(2)}, u32[]{:S(2)}) collective-permute-start(bf16[512,256]{1,0:T(8,128)(2,1)} %get-tuple-element.86), channel_id=1, source_target_pairs={{0,8},{8,0},{16,24},{24,16},{1,9},{9,1},{17,25},{25,17},{2,10},{10... | collective-permute-start | bytes 786440 | tf_op jit(solution)/shard_map/ppermute | solution.py:26
  155.0 13.3 %collective-permute-start.52 = (bf16[512,384]{1,0:T(8,128)(2,1)}, bf16[512,384]{1,0:T(8,128)(2,1)}, u32[]{:S(2)}, u32[]{:S(2)}) collective-permute-start(bf16[512,384]{1,0:T(8,128)(2,1)} %get-tuple-element.85), channel_id=1, source_target_pairs={{0,16},{8,24},{16,0},{24,8},{1,17},{9,25},{17,1},{25,9},{2,18},{10... | collective-permute-start | bytes 1179656 | tf_op jit(solution)/shard_map/ppermute | solution.py:26
  164.1 9.2 %collective-permute-start.56 = (bf16[512,256]{1,0:T(8,128)(2,1)S(1)}, bf16[512,256]{1,0:T(8,128)(2,1)S(1)}, u32[]{:S(2)}, u32[]{:S(2)}) collective-permute-start(bf16[512,256]{1,0:T(8,128)(2,1)S(1)} %collective-permute-done.55.refs_4_), channel_id=1, source_target_pairs={{0,8},{8,0},{16,24},{24,16},{1,9},{9,1},{17,25},{25,17},{2,10},{10... | collective-permute-start | bytes 786440 | tf_op jit(solution)/shard_map/ppermute | solution.py:26
  165.1 14.0 %collective-permute-start.42 = (bf16[256,512]{1,0:T(8,128)(2,1)}, bf16[256,512]{1,0:T(8,128)(2,1)}, u32[]{:S(2)}, u32[]{:S(2)}) collective-permute-start(bf16[256,512]{1,0:T(8,128)(2,1)} %get-tuple-element.77.a), channel_id=1, source_target_pairs={{0,8},{8,0},{16,24},{24,16},{1,9},{9,1},{17,25},{25,17},{2,10},{10... | collective-permute-start | bytes 786440 | tf_op jit(solution)/shard_map/ppermute | solution.py:26
  166.2 13.2 %collective-permute-start.44 = (bf16[256,512]{1,0:T(8,128)(2,1)}, bf16[256,512]{1,0:T(8,128)(2,1)}, u32[]{:S(2)}, u32[]{:S(2)}) collective-permute-start(bf16[256,512]{1,0:T(8,128)(2,1)} %get-tuple-element.78.b), channel_id=1, source_target_pairs={{0,16},{8,24},{16,0},{24,8},{1,17},{9,25},{17,1},{25,9},{2,18},{10... | collective-permute-start | bytes 786440 | tf_op jit(solution)/shard_map/ppermute | solution.py:26
  166.5 19.1 %collective-permute-start.53 = (bf16[512,384]{1,0:T(8,128)(2,1)}, bf16[512,384]{1,0:T(8,128)(2,1)}, u32[]{:S(2)}, u32[]{:S(2)}) collective-permute-start(bf16[512,384]{1,0:T(8,128)(2,1)} %collective-permute-done.51.refs_0_), channel_id=1, source_target_pairs={{0,16},{8,24},{16,0},{24,8},{1,17},{9,25},{17,1},{25,9},{2,18},{10... | collective-permute-start | bytes 1179656 | tf_op jit(solution)/shard_map/ppermute | solution.py:26
  168.2 21.5 %collective-permute-start.47 = (bf16[256,512]{1,0:T(8,128)(2,1)}, bf16[256,512]{1,0:T(8,128)(2,1)}, u32[]{:S(2)}, u32[]{:S(2)}) collective-permute-start(bf16[256,512]{1,0:T(8,128)(2,1)} %get-tuple-element.77.a), channel_id=1, source_target_pairs={{0,16},{8,24},{16,0},{24,8},{1,17},{9,25},{17,1},{25,9},{2,18},{10... | collective-permute-start | bytes 786440 | tf_op jit(solution)/shard_map/ppermute | solution.py:26
  173.3 16.4 %collective-permute-start.46 = (bf16[256,512]{1,0:T(8,128)(2,1)}, bf16[256,512]{1,0:T(8,128)(2,1)}, u32[]{:S(2)}, u32[]{:S(2)}) collective-permute-start(bf16[256,512]{1,0:T(8,128)(2,1)} %get-tuple-element.78.b), channel_id=1, source_target_pairs={{0,8},{8,0},{16,24},{24,16},{1,9},{9,1},{17,25},{25,17},{2,10},{10... | collective-permute-start | bytes 786440 | tf_op jit(solution)/shard_map/ppermute | solution.py:26
  179.0 13.6 %collective-permute-start.43 = (bf16[256,512]{1,0:T(8,128)(2,1)}, bf16[256,512]{1,0:T(8,128)(2,1)}, u32[]{:S(2)}, u32[]{:S(2)}) collective-permute-start(bf16[256,512]{1,0:T(8,128)(2,1)} %collective-permute-done.42.refs_0_), channel_id=1, source_target_pairs={{0,16},{8,24},{16,0},{24,8},{1,17},{9,25},{17,1},{25,9},{2,18},{10... | collective-permute-start | bytes 786440 | tf_op jit(solution)/shard_map/ppermute | solution.py:26
  179.3 13.3 %collective-permute-start.45 = (bf16[256,512]{1,0:T(8,128)(2,1)}, bf16[256,512]{1,0:T(8,128)(2,1)}, u32[]{:S(2)}, u32[]{:S(2)}) collective-permute-start(bf16[256,512]{1,0:T(8,128)(2,1)} %collective-permute-done.44.refs_1_), channel_id=1, source_target_pairs={{0,8},{8,0},{16,24},{24,16},{1,9},{9,1},{17,25},{25,17},{2,10},{10... | collective-permute-start | bytes 786440 | tf_op jit(solution)/shard_map/ppermute | solution.py:26
  (55 other events, 393.9 us)

commit v6 on v5

--- a/solution.py
+++ b/solution.py
@@ -365,10 +365,10 @@
 
 def second_kernel(*refs):
     place, bundles, m_ref, refs = refs[0], refs[1:9], refs[9], refs[10:]
-    a_ref, b_ref, e_ref, w_out, gram, inverse, m, w_ref, merged, load, save = refs
+    a_ref, b_ref, w_out, gram, inverse, m, w_ref, merged, load, save = refs
     me, core = place[0], place[1]
     rows = m.shape[0] // 2
-    copy = pltpu.make_async_copy(m_ref, m, load)
+    copy = pltpu.make_async_copy(m_ref.at[:, m_ref.shape[1] - m.shape[1] :], m, load)
     copy.start()
     part = rows // (GROUP * CORES)
     for c in range(CORES):
@@ -383,15 +383,14 @@
     upper_gram = jnp.where(eye_mask(rows), diagonal, jnp.where(lower, turned, packed))
     resolvent([(jnp.where(lower, packed, turned), gram[0], upper_gram)], inverse, w_ref)
     copy.wait()
-    saves = []
-    early, half = e_ref.shape[1], a_ref.shape[1]
-    for i, (ref, start) in enumerate(((a_ref, early), (b_ref, early + half), (e_ref, 0))):
-        here = slice(start, start + ref.shape[1])
+    saves = [pltpu.make_async_copy(w_ref, w_out, save.at[2])]
+    saves[0].start()
+    half = a_ref.shape[1]
+    for i, ref in enumerate((a_ref, b_ref)):
+        here = slice(i * half, (i + 1) * half)
         merged[:, here] = merge_rows(m[:, here], w_ref[0])
         saves.append(pltpu.make_async_copy(merged.at[:, here], ref, save.at[i]))
         saves[-1].start()
-    saves.append(pltpu.make_async_copy(w_ref, w_out, save.at[3]))
-    saves[-1].start()
     for save_copy in saves:
         save_copy.wait()
 
@@ -401,70 +400,77 @@
     half = (share - early) // 2
     return pl.pallas_call(
         second_kernel,
-        out_shape=tuple(shape(rows, n, dtype=BF16) for n in (half, half, early)) + (shape(1, rows, 2 * rows, dtype=BF16),),
+        out_shape=(shape(rows, half, dtype=BF16),) * 2 + (shape(1, rows, 2 * rows, dtype=BF16),),
         in_specs=[SMEM] + [VMEM] * (2 * GROUP) + [ANY],
-        out_specs=(ANY,) * 4,
+        out_specs=(ANY,) * 3,
         scratch_shapes=[
             pltpu.VMEM((2, rows, rows), F32),
             pltpu.VMEM((1, rows, rows), F32),
-            pltpu.VMEM(m.shape, BF16),
+            pltpu.VMEM((2 * rows, 2 * half), BF16),
             pltpu.VMEM((1, rows, 2 * rows), BF16),
-            pltpu.VMEM((rows, share), BF16),
+            pltpu.VMEM((rows, 2 * half), BF16),
             pltpu.SemaphoreType.DMA,
-            pltpu.SemaphoreType.DMA((4,)),
+            pltpu.SemaphoreType.DMA((3,)),
         ],
-        cost_estimate=cost(2 * rows**3 * 40 + 4 * rows * rows * share, 6 * rows * share),
+        cost_estimate=cost(2 * rows**3 * 40 + 8 * rows * rows * half, 6 * rows * share),
         name="second",
     )(place, *bundles, m)
 
 
-def raw_first_kernel(share, place, w, x, xs, ys, d, out, block, pair, load, save):
+def raw_merge_kernel(share, place, w0, w1, x, xs, ys, d, _, out, block, pair, buffer, load, save):
     me = place[0]
     rows, raw = d.shape
-    saves, loads, sources = [], {}, {}
+    saves = []
+    sources = {}
     for v in PEERS:
         mine = x.at[:, pl.ds(pl.multiple_of((me ^ v) * share, 128), raw)]
         across = {1: xs.at[GROUP - 1], 2: ys.at[GROUP - 1], 3: d}[v]
         sources[v] = (mine, xs.at[SHARES_X.index(v ^ 1)], ys.at[SHARES_Y.index(v ^ 2)], across)
+    loads = {}
     for v, group in sources.items():
         for s, source in enumerate(group):
             target = block.at[v - 1, pl.ds(pl.multiple_of((me ^ s) * rows, rows), rows)]
             loads[v, s] = pltpu.make_async_copy(source, target, load.at[(v - 1) * GROUP + s])
             loads[v, s].start()
-    for v in PEERS:
+    for v in sources:
         for s in range(GROUP):
             loads[v, s].wait()
         for j in range(GROUP // 2):
-            pair[v - 1, j * rows : (j + 1) * rows] = merge_rows(block[v - 1, 2 * j * rows : 2 * (j + 1) * rows], w[j])
-        saves.append(pltpu.make_async_copy(pair.at[v - 1], out.at[v - 1], save.at[v - 1]))
+            pair[j * rows : (j + 1) * rows] = merge_rows(block[v - 1, 2 * j * rows : 2 * (j + 1) * rows], w0[j])
+        buffer[v - 1] = merge_rows(pair[...], w1[0])
+        target = out.at[:, pl.ds(pl.multiple_of((me ^ v) * share, 128), raw)]
+        saves.append(pltpu.make_async_copy(buffer.at[v - 1], target, save.at[v - 1]))
         saves[-1].start()
     for copy in saves:
         copy.wait()
 
 
-def raw_first(place, w, x, messages, share):
+def raw_merge(place, w0, w1, x, messages, out, share):
     rows, raw = messages[2].shape
-    pairs = (GROUP - 1, 2 * rows, raw)
-    return pl.pallas_call(
-        functools.partial(raw_first_kernel, share),
-        out_shape=shape(*pairs, dtype=BF16),
-        in_specs=[SMEM, VMEM] + [HBM] * 4,
+    return pl.pallas_call(
+        functools.partial(raw_merge_kernel, share),
+        out_shape=shape(*out.shape, dtype=BF16),
+        in_specs=[SMEM, VMEM, VMEM] + [HBM] * 5,
         out_specs=HBM,
         scratch_shapes=[
             pltpu.VMEM((GROUP - 1, GROUP * rows, raw), BF16),
-            pltpu.VMEM(pairs, BF16),
+            pltpu.VMEM((2 * rows, raw), BF16),
+            pltpu.VMEM((GROUP - 1, rows, raw), BF16),
             pltpu.SemaphoreType.DMA(((GROUP - 1) * GROUP,)),
             pltpu.SemaphoreType.DMA((GROUP - 1,)),
         ],
-        cost_estimate=cost(8 * rows * rows * raw * (GROUP - 1), 12 * rows * raw * (GROUP - 1)),
+        input_output_aliases={7: 0},
+        cost_estimate=cost(12 * rows * rows * raw * (GROUP - 1), 10 * rows * raw * (GROUP - 1)),
         compiler_params=WHOLE,
-        name="raw_first",
-    )(place, w, x, *messages)
-
-
-def late_kernel(share, raw, place, w, a, b, e, raws, *refs):
-    early, (out, buffer, save) = refs[:-3], refs[-3:]
-    me, half = place[0], a.shape[1]
+        name="raw_merge",
+    )(place, w0, w1, x, *messages, out)
+
+
+def late_kernel(share, raw, place, w, a, b, m, *refs):
+    early, (out, mine, own, buffer, load, save) = refs[:-6], refs[-6:]
+    me, size, half = place[0], mine.shape[1], a.shape[1]
+    copy = pltpu.make_async_copy(m.at[:, :size], mine, load)
+    copy.start()
     saves = []
 
     def put(source, owner, column):
@@ -472,31 +478,38 @@
         saves.append(pltpu.make_async_copy(source, target, save.at[len(saves)]))
         saves[-1].start()
 
-    put(e, me, 0)
-    put(a, me, e.shape[1])
-    put(b, me, e.shape[1] + half)
-    work = [(raws.at[s - 1], s, 0) for s in PEERS]
-    work += [(pair, s, raw) for pair, s in zip(early, PEERS)]
+    put(a, me, size)
+    put(b, me, size + half)
+    work = [(pair, s, raw) for pair, s in zip(early, PEERS)]
     work += [(pair, s, raw + early[0].shape[1]) for pair, s in zip(early[len(PEERS) :], PEERS)]
     for pair, s, column in work:
-        spot = buffer.at[s - 1, :, column : column + pair.shape[1]]
+        spot = buffer.at[s - 1, :, column - raw : column - raw + pair.shape[1]]
         spot[...] = merge_rows(pair[...], w[0])
         put(spot, me ^ s, column)
+    copy.wait()
+    own[...] = merge_rows(mine[...], w[0])
+    put(own, me, 0)
     for copy in saves:
         copy.wait()
 
 
-def late(place, w, a, b, e, raws, early, share):
-    rows, size = e.shape
-    return pl.pallas_call(
-        functools.partial(late_kernel, share, raws.shape[2]),
+def late(place, w, a, b, m, pairs, raw, share):
+    rows, size = a.shape[0], share - 2 * a.shape[1]
+    return pl.pallas_call(
+        functools.partial(late_kernel, share, raw),
         out_shape=shape(rows, GROUP * share, dtype=BF16),
-        in_specs=[SMEM] + [VMEM] * (5 + len(early)),
+        in_specs=[SMEM] + [VMEM] * 3 + [HBM] + [VMEM] * len(pairs),
         out_specs=HBM,
-        scratch_shapes=[pltpu.VMEM((GROUP - 1, rows, size), BF16), pltpu.SemaphoreType.DMA((len(early) + GROUP + 2,))],
-        cost_estimate=cost(4 * rows * rows * size * (GROUP - 1), 6 * rows * size * (GROUP - 1)),
+        scratch_shapes=[
+            pltpu.VMEM((2 * rows, size), BF16),
+            pltpu.VMEM((rows, size), BF16),
+            pltpu.VMEM((GROUP - 1, rows, size - raw), BF16),
+            pltpu.SemaphoreType.DMA,
+            pltpu.SemaphoreType.DMA((len(pairs) + 3,)),
+        ],
+        cost_estimate=cost(4 * rows * rows * size * GROUP, 6 * rows * size * GROUP),
         name="late",
-    )(place, w, a, b, e, raws, *early)
+    )(place, w, a, b, m, *pairs)
 
 
 def put_kernel(spots, share, place, *refs):
@@ -576,16 +589,16 @@
     parts, e, f = lax.optimization_barrier((parts, e, f))
     mine = total([parts[0]] + send_all(parts[1:], "dp", PEERS))
     pairs_a, pairs_b = [[send(block, "dp", s) for s in (1, 2)] for block in (e, f)]
-    raws = raw_first(place, w0, x, messages, share)
     bundles = gather_group(over_chips(mine))
     pairs = pairs_a + [send(pairs_a[0], "dp", 2)] + pairs_b + [send(pairs_b[1], "dp", 1)]
-    a, b, e, w1 = second(place, bundles, m, early)
+    a, b, w1 = second(place, bundles, m, early)
 
     ax, by = send(a, "dp", 1), send(b, "dp", 2)
     bx, ay = send(b, "dp", 1), send(a, "dp", 2)
     ad, bd = send(ax, "dp", 2), send(by, "dp", 1)
     left, right = early, early + a.shape[1]
-    out = late(place, w1, a, b, e, raws, pairs, share)
+    out = late(place, w1, a, b, m, pairs, raw, share)
+    out = raw_merge(place, w0, w1, x, messages, out, share)
     out = put(place, out, [ax, by, bx, ay], ((1, left), (2, right), (1, right), (2, left)), share)
     out = put(place, out, [ad, bd], ((3, left), (3, right)), share)
     return out[None]

time: 196 us -> 215 us (1.097)
  waiting for transfers between devices: 80.6 us -> 98.2 us
    ppermute x57, waiting for transfers between devices: 80.6 us -> 98.2 us  [send(): return lax.ppermute(block, axis, [(i, i ^ shift) for i in range(count)])]
  transfers between devices with their start and end apart: 57 -> 57, of which waited for: 34 -> 30; matrix products, arithmetic and copies ran while one was open for 2% -> 2% of each run, Pallas kernels for 15% -> 14%
where the time goes in v6:
time: 215 us
  waiting for transfers between devices  98.2 us (46%)
  starting transfers between devices  58.3 us (27%)
  Pallas kernels  46.5 us (22%)
  local copies, waits for them, and re-layouts  6.81 us (3%)
  other arithmetic  4.34 us (2%)
    ppermute x57, waiting for transfers between devices, send(): return lax.ppermute(block, axis, [(i, i ^ shift) for i in range(count)])  98.2 us
    ppermute x57, starting transfers between devices, send(): return lax.ppermute(block, axis, [(i, i ^ shift) for i in range(count)])  58.3 us
    pallas_call x1, Pallas kernels, first(): pl.pallas_call(functools.partial(first_kernel, raw, tile), out_shape=tupl...  10.6 us
    pallas_call x1, Pallas kernels, second(): pl.pallas_call(second_kernel, out_shape=(shape(rows, half, dtype=BF16),)...  6.43 us
    pallas_call x1, Pallas kernels, own_gram(): pl.pallas_call(own_gram_kernel, out_shape=(half, half), grid_spec=pltpu.P...  5.39 us
    pallas_call x1, Pallas kernels, raw_merge(): pl.pallas_call(functools.partial(raw_merge_kernel, share), out_shape=shap...  5.16 us
    pallas_call x1, Pallas kernels, late(): pl.pallas_call(functools.partial(late_kernel, share, raw), out_shape=shap...  5.12 us
    pallas_call x2, Pallas kernels, put(): pl.pallas_call(functools.partial(put_kernel, spots, share), out_shape=sha...  5.08 us
  transfers between devices with their start and end apart: 57, of which 30 were waited for; matrix products, arithmetic and copies ran while one was open for 2% of the time, Pallas kernels for 14%

profile of v6, /device:TPU:0, one launch (start us, length us, event | category | flops | bytes accessed | tf_op | source)
XLA Modules:
  0.0 214.6 jit_solution(311031813168138918)
XLA Ops:
  0.0 2.7 %dynamic-slice_bitcast_fusion = (bf16[256,2048]{1,0:T(8,128)(2,1)}, bf16[256,2048]{1,0:T(8,128)(2,1)S(1)}) fusion(bf16[1,256,8192]{2,1,0:T(8,128)(2,1)} %param.1, s32[]{:T(128)S(6)} %select_n.23, s32[]{:T(128)S(6)} %select_n.22), kind=kLoop, calls=%fused_computation | loop fusion | bytes 4194312 | tf_op jit(solution)/shard_map/dynamic_slice | solution.py:567
  2.7 3.0 %collective-permute-start.6 = (bf16[256,2048]{1,0:T(8,128)(2,1)S(1)}, bf16[256,2048]{1,0:T(8,128)(2,1)}, u32[]{:S(2)}, u32[]{:S(2)}) collective-permute-start(bf16[256,2048]{1,0:T(8,128)(2,1)S(1)} %get-tuple-element.49), channel_id=1, source_target_pairs={{0,8},{8,0},{16,24},{24,16},{1,9},{9,1},{17,25},{25,17},{2,10},{10... | collective-permute-start | bytes 3145736 | tf_op jit(solution)/shard_map/ppermute | solution.py:26
  5.7 2.3 %constant_dynamic-slice_fusion = bf16[256,2048]{1,0:T(8,128)(2,1)} fusion(bf16[256,8192]{1,0:T(8,128)(2,1)} %bitcast.24, s32[]{:T(128)S(6)} %select_n.24), kind=kLoop, calls=%fused_computation.23 | loop fusion | bytes 2097156 | tf_op jit(solution)/shard_map/dynamic_slice | solution.py:567
  10.2 5.4 %own_gram.1 = (f32[128,256]{1,0:T(8,128)}, f32[128,256]{1,0:T(8,128)}) custom-call(s32[2]{0:T(128)} %pad_add_fusion.place.refs_0_, bf16[256,8192]{1,0:T(8,128)(2,1)} %bitcast.25), custom_call_target="tpu_custom_call" | custom-call | flops 1073741824 | bytes 4194304 | tf_op jit(solution)/shard_map/own_gram/pallas_call | solution.py:136
  18.0 2.1 collective-permute-start.3
  20.2 2.6 %collective-permute-start.4 = (f32[128,256]{1,0:T(8,128)S(1)}, f32[128,256]{1,0:T(8,128)S(1)}, u32[]{:S(2)}, u32[]{:S(2)}) collective-permute-start(f32[128,256]{1,0:T(8,128)S(1)} %add.117), channel_id=1, source_target_pairs={{0,4},{1,5},{2,6},{3,7},{4,0},{5,1},{6,2},{7,3},{8,12},{9,13},{10,... | collective-permute-start | bytes 393224 | tf_op jit(solution)/shard_map/ppermute | solution.py:26
  22.7 3.4 %collective-permute-done.3 = f32[128,256]{1,0:T(8,128)S(1)} collective-permute-done((f32[128,256]{1,0:T(8,128)S(1)}, f32[128,256]{1,0:T(8,128)S(1)}, u32[]{:S(2)}, u32[]{:S(2)}) %collective-permute-start.3) | collective-permute-done | bytes 131104 | tf_op jit(solution)/shard_map/ppermute | solution.py:26
  26.1 3.2 %collective-permute-start.5 = (f32[128,256]{1,0:T(8,128)S(1)}, f32[128,256]{1,0:T(8,128)S(1)}, u32[]{:S(2)}, u32[]{:S(2)}) collective-permute-start(f32[128,256]{1,0:T(8,128)S(1)} %add.117), channel_id=1, source_target_pairs={{0,6},{1,7},{2,4},{3,5},{4,2},{5,3},{6,0},{7,1},{8,14},{9,15},{10,... | collective-permute-start | bytes 393224 | tf_op jit(solution)/shard_map/ppermute | solution.py:26
  29.3 3.6 %collective-permute-done.5 = f32[128,256]{1,0:T(8,128)S(1)} collective-permute-done((f32[128,256]{1,0:T(8,128)S(1)}, f32[128,256]{1,0:T(8,128)S(1)}, u32[]{:S(2)}, u32[]{:S(2)}) %collective-permute-start.5) | collective-permute-done | bytes 131104 | tf_op jit(solution)/shard_map/ppermute | solution.py:26
  33.6 4.9 %near_gram.1 = (f32[256,256]{1,0:T(8,128)}, bf16[4,256,384]{2,1,0:T(8,128)(2,1)}, bf16[4,256,384]{2,1,0:T(8,128)(2,1)}, bf16[256,384]{1,0:T(8,128)(2,1)}) custom-call(s32[2]{0:T(128)} %pad_add_fusion.place.refs_0_, bf16[256,8192]{1,0:T(8,128)(2,1)} %bitcast.26, bf16[256,2048]{1,0:T(8,128)(2,1)} %collective-permute-done.6.p1.refs_18_), custom_call_target="tpu_custom_call" | custom-call | flops 268435456 | bytes 2097152 | tf_op jit(solution)/shard_map/near_gram/pallas_call | solution.py:201
  38.5 14.2 %collective-permute-done.1.p3.refs_20_ = bf16[256,2048]{1,0:T(8,128)(2,1)} collective-permute-done((bf16[256,2048]{1,0:T(8,128)(2,1)}, bf16[256,2048]{1,0:T(8,128)(2,1)}, u32[]{:S(2)}, u32[]{:S(2)}) %collective-permute-start.1) | collective-permute-done | bytes 1048608 | tf_op jit(solution)/shard_map/ppermute | solution.py:26
  52.7 3.9 %collective-permute-done.p2.refs_19_ = bf16[256,2048]{1,0:T(8,128)(2,1)} collective-permute-done((bf16[256,2048]{1,0:T(8,128)(2,1)}, bf16[256,2048]{1,0:T(8,128)(2,1)}, u32[]{:S(2)}, u32[]{:S(2)}) %collective-permute-start) | collective-permute-done | bytes 1048608 | tf_op jit(solution)/shard_map/ppermute | solution.py:26
  56.6 3.8 %far_gram.1 = (f32[4,64,256]{2,1,0:T(8,128)}, f32[4,64,256]{2,1,0:T(8,128)}, bf16[4,256,384]{2,1,0:T(8,128)(2,1)}) custom-call(s32[2]{0:T(128)} %pad_add_fusion.place.refs_0_, f32[256,256]{1,0:T(8,128)} %get-tuple-element.51.near, bf16[256,2048]{1,0:T(8,128)(2,1)} %collective-permute-done.p2.refs_19_, ...), custom_call_target="tpu_custom_call", output_to_operand_aliasing={{2}: (4, {})} | custom-call | flops 268435456 | bytes 2097152 | tf_op jit(solution)/shard_map/far_gram/pallas_call | solution.py:243
  67.5 2.2 %collective-permute-done.16 = f32[64,256]{1,0:T(8,128)S(1)} collective-permute-done((f32[64,256]{1,0:T(8,128)S(1)}, f32[64,256]{1,0:T(8,128)S(1)}, u32[]{:S(2)}, u32[]{:S(2)}) %collective-permute-start.16) | collective-permute-done | bytes 65568 | tf_op jit(solution)/shard_map/ppermute | solution.py:26
  72.0 2.6 %collective-permute-start.19 = (f32[64,256]{1,0:T(8,128)S(1)}, f32[64,256]{1,0:T(8,128)S(1)}, u32[]{:S(2)}, u32[]{:S(2)}) collective-permute-start(f32[64,256]{1,0:T(8,128)S(1)} %add_add_fusion.4), channel_id=1, source_target_pairs={{0,4},{1,5},{2,6},{3,7},{4,0},{5,1},{6,2},{7,3},{8,12},{9,13},{10,... | collective-permute-start | bytes 196616 | tf_op jit(solution)/shard_map/ppermute | solution.py:26
  78.6 2.1 collective-permute-done.20
  86.6 3.7 %collective-permute-done.23.refs_12_ = f32[64,256]{1,0:T(8,128)S(1)} collective-permute-done((f32[64,256]{1,0:T(8,128)S(1)}, f32[64,256]{1,0:T(8,128)S(1)}, u32[]{:S(2)}, u32[]{:S(2)}) %collective-permute-start.23) | collective-permute-done | bytes 65568 | tf_op jit(solution)/shard_map/ppermute | solution.py:26
  92.9 10.6 %first.1 = (bf16[512,2048]{1,0:T(8,128)(2,1)}, bf16[512,384]{1,0:T(8,128)(2,1)}, bf16[512,256]{1,0:T(8,128)(2,1)}, bf16[2,256,512]{2,1,0:T(8,128)(2,1)}, f32[4,72,256]{2,1,0:T(8,128)}, /*index=5*/f32[4,72,256]{2,1,0:T(8,128)}) custom-call(s32[2]{0:T(128)} %pad_add_fusion.place.refs_0_, f32[128,256]{1,0:T(8,128)} %add_add_fusion.refs_1_, ...), custom_call_target="tpu_custom_call" | custom-call | flops 4563402752 | bytes 6291456 | tf_op jit(solution)/shard_map/first/pallas_call | solution.py:343
  111.6 2.2 %collective-permute-done.31 = f32[72,256]{1,0:T(8,128)S(1)} collective-permute-done((f32[72,256]{1,0:T(8,128)S(1)}, f32[72,256]{1,0:T(8,128)S(1)}, u32[]{:S(2)}, u32[]{:S(2)}) %collective-permute-start.31) | collective-permute-done | bytes 73760 | tf_op jit(solution)/shard_map/ppermute | solution.py:26
  113.9 3.5 %collective-permute-start.33 = (f32[72,256]{1,0:T(8,128)S(1)}, f32[72,256]{1,0:T(8,128)S(1)}, u32[]{:S(2)}, u32[]{:S(2)}) collective-permute-start(f32[72,256]{1,0:T(8,128)S(1)} %add_add_fusion.2), channel_id=1, source_target_pairs={{0,4},{1,5},{2,6},{3,7},{4,0},{5,1},{6,2},{7,3},{8,12},{9,13},{10,... | collective-permute-start | bytes 221192 | tf_op jit(solution)/shard_map/ppermute | solution.py:26
  121.8 1.8 collective-permute-done.34
  128.4 16.2 %collective-permute-done.35.refs_2_ = f32[72,256]{1,0:T(8,128)S(1)} collective-permute-done((f32[72,256]{1,0:T(8,128)S(1)}, f32[72,256]{1,0:T(8,128)S(1)}, u32[]{:S(2)}, u32[]{:S(2)}) %collective-permute-start.35) | collective-permute-done | bytes 73760 | tf_op jit(solution)/shard_map/ppermute | solution.py:26
  144.6 2.2 %collective-permute-start.37 = (f32[72,256]{1,0:T(8,128)S(1)}, f32[72,256]{1,0:T(8,128)S(1)}, u32[]{:S(2)}, u32[]{:S(2)}) collective-permute-start(f32[72,256]{1,0:T(8,128)S(1)} %add_add_fusion.1.refs_1_), channel_id=1, source_target_pairs={{0,24},{8,16},{16,8},{24,0},{1,25},{9,17},{17,9},{25,1},{2,26},{10... | collective-permute-start | bytes 221192 | tf_op jit(solution)/shard_map/ppermute | solution.py:26
  146.9 5.5 %collective-permute-done.37.refs_4_ = f32[72,256]{1,0:T(8,128)S(1)} collective-permute-done((f32[72,256]{1,0:T(8,128)S(1)}, f32[72,256]{1,0:T(8,128)S(1)}, u32[]{:S(2)}, u32[]{:S(2)}) %collective-permute-start.37) | collective-permute-done | bytes 73760 | tf_op jit(solution)/shard_map/ppermute | solution.py:26
  158.5 6.4 %second.1 = (bf16[256,512]{1,0:T(8,128)(2,1)}, bf16[256,512]{1,0:T(8,128)(2,1)}, bf16[1,256,512]{2,1,0:T(8,128)(2,1)}) custom-call(s32[2]{0:T(128)} %pad_add_fusion.place.refs_0_, f32[72,256]{1,0:T(8,128)} %copy-done.9, f32[72,256]{1,0:T(8,128)} %copy-done.19, f32[72,256]{1,0:T(8,128)} %copy-done.20, f32[72,256]{1,0:T(8,128)} %copy-done.21, ...), custom_call_target="tpu_custom_call" | custom-call | flops 1610612736 | bytes 3145728 | tf_op jit(solution)/shard_map/second/pallas_call | solution.py:401
  168.2 6.2 %collective-permute-done.56.refs_5_ = bf16[512,256]{1,0:T(8,128)(2,1)S(1)} collective-permute-done((bf16[512,256]{1,0:T(8,128)(2,1)}, bf16[512,256]{1,0:T(8,128)(2,1)S(1)}, u32[]{:S(2)}, u32[]{:S(2)}) %collective-permute-start.56) | collective-permute-done | bytes 262176 | tf_op jit(solution)/shard_map/ppermute | solution.py:26
  175.6 4.5 %collective-permute-done.42.refs_0_ = bf16[256,512]{1,0:T(8,128)(2,1)} collective-permute-done((bf16[256,512]{1,0:T(8,128)(2,1)}, bf16[256,512]{1,0:T(8,128)(2,1)}, u32[]{:S(2)}, u32[]{:S(2)}) %collective-permute-start.42) | collective-permute-done | bytes 262176 | tf_op jit(solution)/shard_map/ppermute | solution.py:26
  181.3 14.8 %collective-permute-done.44.refs_1_ = bf16[256,512]{1,0:T(8,128)(2,1)} collective-permute-done((bf16[256,512]{1,0:T(8,128)(2,1)}, bf16[256,512]{1,0:T(8,128)(2,1)}, u32[]{:S(2)}, u32[]{:S(2)}) %collective-permute-start.44) | collective-permute-done | bytes 262176 | tf_op jit(solution)/shard_map/ppermute | solution.py:26
  198.1 5.1 %late.1._ = bf16[256,8192]{1,0:T(8,128)(2,1)} custom-call(s32[2]{0:T(128)} %pad_add_fusion.place.refs_0_, bf16[1,256,512]{2,1,0:T(8,128)(2,1)} %get-tuple-element.79.w.w1, bf16[256,512]{1,0:T(8,128)(2,1)} %get-tuple-element.76.a, bf16[256,512]{1,0:T(8,128)(2,1)} %get-tuple-element.77.b, bf16[512,2048]{1,0:T(8,128)(2,1)} %get-tuple-element.75.refs_9_.m, ...), custom_call_target="tpu_custom_call" | custom-call | flops 1073741824 | bytes 6291456 | tf_op jit(solution)/shard_map/late/pallas_call | solution.py:498
  204.2 5.2 %raw_merge.1.refs_4_ = bf16[256,8192]{1,0:T(8,128)(2,1)} custom-call(s32[2]{0:T(128)} %pad_add_fusion.place.refs_0_, bf16[2,256,512]{2,1,0:T(8,128)(2,1)} %get-tuple-element.78.w0, bf16[1,256,512]{2,1,0:T(8,128)(2,1)} %get-tuple-element.79.w.w1, bf16[256,8192]{1,0:T(8,128)(2,1)} %bitcast.28, ...), custom_call_target="tpu_custom_call", output_to_operand_aliasing={{}: (7, {})} | custom-call | flops 905969664 | bytes 2949120 | tf_op jit(solution)/shard_map/raw_merge/pallas_call | solution.py:450
  209.4 2.6 %put.2.refs_2_ = bf16[256,8192]{1,0:T(8,128)(2,1)} custom-call(s32[2]{0:T(128)} %pad_add_fusion.place.refs_0_, bf16[256,512]{1,0:T(8,128)(2,1)} %collective-permute-done.42.refs_0_, bf16[256,512]{1,0:T(8,128)(2,1)} %collective-permute-done.44.refs_1_, bf16[256,512]{1,0:T(8,128)(2,1)} %collective-permute-done.46.refs_2_, ...), custom_call_target="tpu_custom_call", output_to_operand_aliasing={{}: (5, {})} | custom-call | bytes 2097152 | tf_op jit(solution)/shard_map/put/pallas_call | solution.py:533
  212.0 2.4 %put.3 = bf16[256,8192]{1,0:T(8,128)(2,1)} custom-call(s32[2]{0:T(128)} %pad_add_fusion.place.refs_0_, bf16[256,512]{1,0:T(8,128)(2,1)} %collective-permute-done.43.refs_0_, bf16[256,512]{1,0:T(8,128)(2,1)} %collective-permute-done.45.refs_1_, bf16[256,8192]{1,0:T(8,128)(2,1)} %put.2.refs_2_), custom_call_target="tpu_custom_call", output_to_operand_aliasing={{}: (3, {})} | custom-call | bytes 1048576 | tf_op jit(solution)/shard_map/put/pallas_call | solution.py:533
  (166 shorter events, 59.2 us)
Async XLA Ops:
  2.7 30.9 %collective-permute-start.6 = (bf16[256,2048]{1,0:T(8,128)(2,1)S(1)}, bf16[256,2048]{1,0:T(8,128)(2,1)}, u32[]{:S(2)}, u32[]{:S(2)}) collective-permute-start(bf16[256,2048]{1,0:T(8,128)(2,1)S(1)} %get-tuple-element.49), channel_id=1, source_target_pairs={{0,8},{8,0},{16,24},{24,16},{1,9},{9,1},{17,25},{25,17},{2,10},{10... | collective-permute-start | bytes 3145736 | tf_op jit(solution)/shard_map/ppermute | solution.py:26
  8.0 44.7 %collective-permute-start.1 = (bf16[256,2048]{1,0:T(8,128)(2,1)}, bf16[256,2048]{1,0:T(8,128)(2,1)}, u32[]{:S(2)}, u32[]{:S(2)}) collective-permute-start(bf16[256,2048]{1,0:T(8,128)(2,1)} %constant_dynamic-slice_fusion), channel_id=1, source_target_pairs={{0,24},{8,16},{16,8},{24,0},{1,25},{9,17},{17,9},{25,1},{2,26},{10... | collective-permute-start | bytes 3145736 | tf_op jit(solution)/shard_map/ppermute | solution.py:26
  9.5 47.1 %collective-permute-start = (bf16[256,2048]{1,0:T(8,128)(2,1)}, bf16[256,2048]{1,0:T(8,128)(2,1)}, u32[]{:S(2)}, u32[]{:S(2)}) collective-permute-start(bf16[256,2048]{1,0:T(8,128)(2,1)} %get-tuple-element.45), channel_id=1, source_target_pairs={{0,16},{8,24},{16,0},{24,8},{1,17},{9,25},{17,1},{25,9},{2,18},{10... | collective-permute-start | bytes 3145736 | tf_op jit(solution)/shard_map/ppermute | solution.py:26
  18.0 8.1 %collective-permute-start.3 = (f32[128,256]{1,0:T(8,128)S(1)}, f32[128,256]{1,0:T(8,128)S(1)}, u32[]{:S(2)}, u32[]{:S(2)}) collective-permute-start(f32[128,256]{1,0:T(8,128)S(1)} %add.117), channel_id=1, source_target_pairs={{0,2},{1,3},{2,0},{3,1},{4,6},{5,7},{6,4},{7,5},{8,10},{9,11},{10,... | collective-permute-start | bytes 393224 | tf_op jit(solution)/shard_map/ppermute | solution.py:26
  20.2 9.2 %collective-permute-start.4 = (f32[128,256]{1,0:T(8,128)S(1)}, f32[128,256]{1,0:T(8,128)S(1)}, u32[]{:S(2)}, u32[]{:S(2)}) collective-permute-start(f32[128,256]{1,0:T(8,128)S(1)} %add.117), channel_id=1, source_target_pairs={{0,4},{1,5},{2,6},{3,7},{4,0},{5,1},{6,2},{7,3},{8,12},{9,13},{10,... | collective-permute-start | bytes 393224 | tf_op jit(solution)/shard_map/ppermute | solution.py:26
  26.1 6.8 %collective-permute-start.5 = (f32[128,256]{1,0:T(8,128)S(1)}, f32[128,256]{1,0:T(8,128)S(1)}, u32[]{:S(2)}, u32[]{:S(2)}) collective-permute-start(f32[128,256]{1,0:T(8,128)S(1)} %add.117), channel_id=1, source_target_pairs={{0,6},{1,7},{2,4},{3,5},{4,2},{5,3},{6,0},{7,1},{8,14},{9,15},{10,... | collective-permute-start | bytes 393224 | tf_op jit(solution)/shard_map/ppermute | solution.py:26
  70.4 6.5 %collective-permute-start.18 = (f32[64,256]{1,0:T(8,128)S(1)}, f32[64,256]{1,0:T(8,128)S(1)}, u32[]{:S(2)}, u32[]{:S(2)}) collective-permute-start(f32[64,256]{1,0:T(8,128)S(1)} %add_add_fusion.4), channel_id=1, source_target_pairs={{0,2},{1,3},{2,0},{3,1},{4,6},{5,7},{6,4},{7,5},{8,10},{9,11},{10,... | collective-permute-start | bytes 196616 | tf_op jit(solution)/shard_map/ppermute | solution.py:26
  72.0 6.6 %collective-permute-start.19 = (f32[64,256]{1,0:T(8,128)S(1)}, f32[64,256]{1,0:T(8,128)S(1)}, u32[]{:S(2)}, u32[]{:S(2)}) collective-permute-start(f32[64,256]{1,0:T(8,128)S(1)} %add_add_fusion.4), channel_id=1, source_target_pairs={{0,4},{1,5},{2,6},{3,7},{4,0},{5,1},{6,2},{7,3},{8,12},{9,13},{10,... | collective-permute-start | bytes 196616 | tf_op jit(solution)/shard_map/ppermute | solution.py:26
  75.3 7.6 %collective-permute-start.9 = (f32[128,256]{1,0:T(8,128)}, f32[128,256]{1,0:T(8,128)S(1)}, u32[]{:S(2)}, u32[]{:S(2)}) collective-permute-start(f32[128,256]{1,0:T(8,128)} %add_add_fusion.refs_1_), channel_id=1, source_target_pairs={{0,16},{8,24},{16,0},{24,8},{1,17},{9,25},{17,1},{25,9},{2,18},{10... | collective-permute-start | bytes 393224 | tf_op jit(solution)/shard_map/ppermute | solution.py:26
  82.9 7.9 %collective-permute-start.12 = (f32[128,256]{1,0:T(8,128)S(1)}, f32[128,256]{1,0:T(8,128)S(1)}, u32[]{:S(2)}, u32[]{:S(2)}) collective-permute-start(f32[128,256]{1,0:T(8,128)S(1)} %collective-permute-done.8.refs_2_), channel_id=1, source_target_pairs={{0,1},{1,0},{2,3},{3,2},{4,5},{5,4},{6,7},{7,6},{8,9},{9,8},{10,11... | collective-permute-start | bytes 393224 | tf_op jit(solution)/shard_map/ppermute | solution.py:26
  83.2 7.7 %collective-permute-start.13 = (f32[128,256]{1,0:T(8,128)S(1)}, f32[128,256]{1,0:T(8,128)S(1)}, u32[]{:S(2)}, u32[]{:S(2)}) collective-permute-start(f32[128,256]{1,0:T(8,128)S(1)} %collective-permute-done.9.refs_3_), channel_id=1, source_target_pairs={{0,1},{1,0},{2,3},{3,2},{4,5},{5,4},{6,7},{7,6},{8,9},{9,8},{10,11... | collective-permute-start | bytes 393224 | tf_op jit(solution)/shard_map/ppermute | solution.py:26
  83.4 7.5 %collective-permute-start.14 = (f32[128,256]{1,0:T(8,128)S(1)}, f32[128,256]{1,0:T(8,128)S(1)}, u32[]{:S(2)}, u32[]{:S(2)}) collective-permute-start(f32[128,256]{1,0:T(8,128)S(1)} %collective-permute-done.10.refs_4_), channel_id=1, source_target_pairs={{0,1},{1,0},{2,3},{3,2},{4,5},{5,4},{6,7},{7,6},{8,9},{9,8},{10,11... | collective-permute-start | bytes 393224 | tf_op jit(solution)/shard_map/ppermute | solution.py:26
  113.8 6.6 %collective-permute-start.32 = (f32[72,256]{1,0:T(8,128)S(1)}, f32[72,256]{1,0:T(8,128)S(1)}, u32[]{:S(2)}, u32[]{:S(2)}) collective-permute-start(f32[72,256]{1,0:T(8,128)S(1)} %add_add_fusion.2), channel_id=1, source_target_pairs={{0,2},{1,3},{2,0},{3,1},{4,6},{5,7},{6,4},{7,5},{8,10},{9,11},{10,... | collective-permute-start | bytes 221192 | tf_op jit(solution)/shard_map/ppermute | solution.py:26
  113.9 7.9 %collective-permute-start.33 = (f32[72,256]{1,0:T(8,128)S(1)}, f32[72,256]{1,0:T(8,128)S(1)}, u32[]{:S(2)}, u32[]{:S(2)}) collective-permute-start(f32[72,256]{1,0:T(8,128)S(1)} %add_add_fusion.2), channel_id=1, source_target_pairs={{0,4},{1,5},{2,6},{3,7},{4,0},{5,1},{6,2},{7,3},{8,12},{9,13},{10,... | collective-permute-start | bytes 221192 | tf_op jit(solution)/shard_map/ppermute | solution.py:26
  118.3 8.7 %collective-permute-start.50 = (bf16[256,384]{1,0:T(8,128)(2,1)S(1)}, bf16[256,384]{1,0:T(8,128)(2,1)S(1)}, u32[]{:S(2)}, u32[]{:S(2)}) collective-permute-start(bf16[256,384]{1,0:T(8,128)(2,1)S(1)} %copy-done.11), channel_id=1, source_target_pairs={{0,24},{8,16},{16,8},{24,0},{1,25},{9,17},{17,9},{25,1},{2,26},{10... | collective-permute-start | bytes 589832 | tf_op jit(solution)/shard_map/ppermute | solution.py:26
  119.9 46.3 %collective-permute-start.48 = (bf16[4,256,384]{2,1,0:T(8,128)(2,1)S(1)}, bf16[4,256,384]{2,1,0:T(8,128)(2,1)S(1)}, u32[]{:S(2)}, u32[]{:S(2)}) collective-permute-start(bf16[4,256,384]{2,1,0:T(8,128)(2,1)S(1)} %copy-done.2), channel_id=1, source_target_pairs={{0,8},{8,0},{16,24},{24,16},{1,9},{9,1},{17,25},{25,17},{2,10},{10... | collective-permute-start | bytes 2359304 | tf_op jit(solution)/shard_map/ppermute | solution.py:26
  120.4 32.4 %collective-permute-start.55 = (bf16[512,256]{1,0:T(8,128)(2,1)}, bf16[512,256]{1,0:T(8,128)(2,1)S(1)}, u32[]{:S(2)}, u32[]{:S(2)}) collective-permute-start(bf16[512,256]{1,0:T(8,128)(2,1)} %get-tuple-element.84), channel_id=1, source_target_pairs={{0,16},{8,24},{16,0},{24,8},{1,17},{9,25},{17,1},{25,9},{2,18},{10... | collective-permute-start | bytes 786440 | tf_op jit(solution)/shard_map/ppermute | solution.py:26
  123.6 21.0 %collective-permute-start.35 = (f32[72,256]{1,0:T(8,128)S(1)}, f32[72,256]{1,0:T(8,128)S(1)}, u32[]{:S(2)}, u32[]{:S(2)}) collective-permute-start(f32[72,256]{1,0:T(8,128)S(1)} %add_add_fusion.1.refs_1_), channel_id=1, source_target_pairs={{0,8},{8,0},{16,24},{24,16},{1,9},{9,1},{17,25},{25,17},{2,10},{10... | collective-permute-start | bytes 221192 | tf_op jit(solution)/shard_map/ppermute | solution.py:26
  124.1 22.7 %collective-permute-start.36 = (f32[72,256]{1,0:T(8,128)S(1)}, f32[72,256]{1,0:T(8,128)S(1)}, u32[]{:S(2)}, u32[]{:S(2)}) collective-permute-start(f32[72,256]{1,0:T(8,128)S(1)} %add_add_fusion.1.refs_1_), channel_id=1, source_target_pairs={{0,16},{8,24},{16,0},{24,8},{1,17},{9,25},{17,1},{25,9},{2,18},{10... | collective-permute-start | bytes 221192 | tf_op jit(solution)/shard_map/ppermute | solution.py:26
  126.9 30.6 %collective-permute-start.51 = (bf16[512,384]{1,0:T(8,128)(2,1)}, bf16[512,384]{1,0:T(8,128)(2,1)S(1)}, u32[]{:S(2)}, u32[]{:S(2)}) collective-permute-start(bf16[512,384]{1,0:T(8,128)(2,1)} %get-tuple-element.83), channel_id=1, source_target_pairs={{0,8},{8,0},{16,24},{24,16},{1,9},{9,1},{17,25},{25,17},{2,10},{10... | collective-permute-start | bytes 1179656 | tf_op jit(solution)/shard_map/ppermute | solution.py:26
  144.6 7.7 %collective-permute-start.37 = (f32[72,256]{1,0:T(8,128)S(1)}, f32[72,256]{1,0:T(8,128)S(1)}, u32[]{:S(2)}, u32[]{:S(2)}) collective-permute-start(f32[72,256]{1,0:T(8,128)S(1)} %add_add_fusion.1.refs_1_), channel_id=1, source_target_pairs={{0,24},{8,16},{16,8},{24,0},{1,25},{9,17},{17,9},{25,1},{2,26},{10... | collective-permute-start | bytes 221192 | tf_op jit(solution)/shard_map/ppermute | solution.py:26
  152.9 14.2 %collective-permute-start.52 = (bf16[512,384]{1,0:T(8,128)(2,1)}, bf16[512,384]{1,0:T(8,128)(2,1)S(1)}, u32[]{:S(2)}, u32[]{:S(2)}) collective-permute-start(bf16[512,384]{1,0:T(8,128)(2,1)} %get-tuple-element.83), channel_id=1, source_target_pairs={{0,16},{8,24},{16,0},{24,8},{1,17},{9,25},{17,1},{25,9},{2,18},{10... | collective-permute-start | bytes 1179656 | tf_op jit(solution)/shard_map/ppermute | solution.py:26
  153.8 49.5 %collective-permute-start.49 = (bf16[4,256,384]{2,1,0:T(8,128)(2,1)}, bf16[4,256,384]{2,1,0:T(8,128)(2,1)S(1)}, u32[]{:S(2)}, u32[]{:S(2)}) collective-permute-start(bf16[4,256,384]{2,1,0:T(8,128)(2,1)} %get-tuple-element.81), channel_id=1, source_target_pairs={{0,16},{8,24},{16,0},{24,8},{1,17},{9,25},{17,1},{25,9},{2,18},{10... | collective-permute-start | bytes 2359304 | tf_op jit(solution)/shard_map/ppermute | solution.py:26
  156.2 8.8 %collective-permute-start.54 = (bf16[512,256]{1,0:T(8,128)(2,1)}, bf16[512,256]{1,0:T(8,128)(2,1)}, u32[]{:S(2)}, u32[]{:S(2)}) collective-permute-start(bf16[512,256]{1,0:T(8,128)(2,1)} %get-tuple-element.84), channel_id=1, source_target_pairs={{0,8},{8,0},{16,24},{24,16},{1,9},{9,1},{17,25},{25,17},{2,10},{10... | collective-permute-start | bytes 786440 | tf_op jit(solution)/shard_map/ppermute | solution.py:26
  157.5 39.2 %collective-permute-start.53 = (bf16[512,384]{1,0:T(8,128)(2,1)S(1)}, bf16[512,384]{1,0:T(8,128)(2,1)S(1)}, u32[]{:S(2)}, u32[]{:S(2)}) collective-permute-start(bf16[512,384]{1,0:T(8,128)(2,1)S(1)} %collective-permute-done.51.refs_0_), channel_id=1, source_target_pairs={{0,16},{8,24},{16,0},{24,8},{1,17},{9,25},{17,1},{25,9},{2,18},{10... | collective-permute-start | bytes 1179656 | tf_op jit(solution)/shard_map/ppermute | solution.py:26
  165.0 9.5 %collective-permute-start.56 = (bf16[512,256]{1,0:T(8,128)(2,1)}, bf16[512,256]{1,0:T(8,128)(2,1)S(1)}, u32[]{:S(2)}, u32[]{:S(2)}) collective-permute-start(bf16[512,256]{1,0:T(8,128)(2,1)} %copy-done.6), channel_id=1, source_target_pairs={{0,8},{8,0},{16,24},{24,16},{1,9},{9,1},{17,25},{25,17},{2,10},{10... | collective-permute-start | bytes 786440 | tf_op jit(solution)/shard_map/ppermute | solution.py:26
  166.2 13.9 %collective-permute-start.42 = (bf16[256,512]{1,0:T(8,128)(2,1)}, bf16[256,512]{1,0:T(8,128)(2,1)}, u32[]{:S(2)}, u32[]{:S(2)}) collective-permute-start(bf16[256,512]{1,0:T(8,128)(2,1)} %get-tuple-element.76.a), channel_id=1, source_target_pairs={{0,8},{8,0},{16,24},{24,16},{1,9},{9,1},{17,25},{25,17},{2,10},{10... | collective-permute-start | bytes 786440 | tf_op jit(solution)/shard_map/ppermute | solution.py:26
  167.1 29.0 %collective-permute-start.44 = (bf16[256,512]{1,0:T(8,128)(2,1)}, bf16[256,512]{1,0:T(8,128)(2,1)}, u32[]{:S(2)}, u32[]{:S(2)}) collective-permute-start(bf16[256,512]{1,0:T(8,128)(2,1)} %get-tuple-element.77.b), channel_id=1, source_target_pairs={{0,16},{8,24},{16,0},{24,8},{1,17},{9,25},{17,1},{25,9},{2,18},{10... | collective-permute-start | bytes 786440 | tf_op jit(solution)/shard_map/ppermute | solution.py:26
  174.4 34.9 %collective-permute-start.46 = (bf16[256,512]{1,0:T(8,128)(2,1)}, bf16[256,512]{1,0:T(8,128)(2,1)}, u32[]{:S(2)}, u32[]{:S(2)}) collective-permute-start(bf16[256,512]{1,0:T(8,128)(2,1)} %get-tuple-element.77.b), channel_id=1, source_target_pairs={{0,8},{8,0},{16,24},{24,16},{1,9},{9,1},{17,25},{25,17},{2,10},{10... | collective-permute-start | bytes 786440 | tf_op jit(solution)/shard_map/ppermute | solution.py:26
  180.2 29.2 %collective-permute-start.47 = (bf16[256,512]{1,0:T(8,128)(2,1)}, bf16[256,512]{1,0:T(8,128)(2,1)}, u32[]{:S(2)}, u32[]{:S(2)}) collective-permute-start(bf16[256,512]{1,0:T(8,128)(2,1)} %get-tuple-element.76.a), channel_id=1, source_target_pairs={{0,16},{8,24},{16,0},{24,8},{1,17},{9,25},{17,1},{25,9},{2,18},{10... | collective-permute-start | bytes 786440 | tf_op jit(solution)/shard_map/ppermute | solution.py:26
  196.1 15.9 %collective-permute-start.43 = (bf16[256,512]{1,0:T(8,128)(2,1)}, bf16[256,512]{1,0:T(8,128)(2,1)}, u32[]{:S(2)}, u32[]{:S(2)}) collective-permute-start(bf16[256,512]{1,0:T(8,128)(2,1)} %collective-permute-done.42.refs_0_), channel_id=1, source_target_pairs={{0,16},{8,24},{16,0},{24,8},{1,17},{9,25},{17,1},{25,9},{2,18},{10... | collective-permute-start | bytes 786440 | tf_op jit(solution)/shard_map/ppermute | solution.py:26
  196.8 15.3 %collective-permute-start.45 = (bf16[256,512]{1,0:T(8,128)(2,1)}, bf16[256,512]{1,0:T(8,128)(2,1)}, u32[]{:S(2)}, u32[]{:S(2)}) collective-permute-start(bf16[256,512]{1,0:T(8,128)(2,1)} %collective-permute-done.44.refs_1_), channel_id=1, source_target_pairs={{0,8},{8,0},{16,24},{24,16},{1,9},{9,1},{17,25},{25,17},{2,10},{10... | collective-permute-start | bytes 786440 | tf_op jit(solution)/shard_map/ppermute | solution.py:26
  (57 other events, 491.9 us)

commit v7 on v6

--- a/solution.py
+++ b/solution.py
@@ -89,22 +89,20 @@
     lax.while_loop(lambda s: (s[0] < 24) & (s[1] > 1e-6), lambda s: (s[0] + 1, step()), (jnp.int32(2), step()))
 
 
-def resolvent(grams, x_ref, out_ref):
+def resolvent(grams, x_ref, out_ref, ready=lambda: None):
     n = grams[0][0].shape[0]
     mask = eye_mask(n)
     eye = jnp.where(mask, 1.0, 0.0)
-    scaled = []
-    for a, b, d in grams:
-        average = jnp.sum(jnp.where(mask, a + d, 0.0)) / (2 * n)
-        scaled.append((eye + a / average, b / average, eye + d / average))
+    scales = [(2 * n) / jnp.sum(jnp.where(mask, a + d, 0.0)) for a, _, d in grams]
     limit = 1.0 + 2 * n
-    invert([d for _, _, d in scaled], x_ref, limit)
+    invert([eye + d * scale for (_, _, d), scale in zip(grams, scales)], x_ref, limit)
+    ready()
     ties, schurs = [], []
-    for j, (a, b, d) in enumerate(scaled):
-        bs = halves(b)
+    for j, ((a, b, _), scale) in enumerate(zip(grams, scales)):
+        bs = halves(b[...] * scale)
         tie = halves(product(bs, halves(x_ref[j])))
         ties.append(tie)
-        schurs.append(a - product(tie, bs, NT))
+        schurs.append(eye + a * scale - product(tie, bs, NT))
     invert(schurs, x_ref, limit)
     for j, tie in enumerate(ties):
         x = x_ref[j]
@@ -283,18 +281,27 @@
         pltpu.make_async_copy(source, block.at[pl.ds(pl.multiple_of((me ^ s) * rows, rows), rows)], load.at[s])
         for s, source in enumerate(sources)
     ]
-    for copy in loads:
-        copy.start()
-
     part, half = rows // (2 * CORES), rows // CORES
+    squares, places = [], []
     for c in range(CORES):
         for s in range(GROUP):
-            source, seat = me ^ s, core ^ c
+            source, seat, i = me ^ s, core ^ c, c * GROUP + s
             start = (source % 2) * (CORES * part) + seat * part
-            cross[source // 2, pl.ds(pl.multiple_of(start, part), part), :] = crosses[c * GROUP + s][...]
-            diag[source, pl.ds(pl.multiple_of(seat * half, half), half), :] = tails[c * GROUP + s][...]
-    grams = [(diag[2 * j], cross[j], diag[2 * j + 1]) for j in range(GROUP // 2)]
-    resolvent(grams, inverse, w)
+            target = cross.at[source // 2, pl.ds(pl.multiple_of(start, part), part)]
+            places.append(pltpu.make_async_copy(crosses[i], target, load.at[GROUP + i]))
+            target = diag.at[source, pl.ds(pl.multiple_of(seat * half, half), half)]
+            squares.append(pltpu.make_async_copy(tails[i], target, load.at[3 * GROUP + i]))
+    for copy in squares + places + loads:
+        copy.start()
+    for copy in squares:
+        copy.wait()
+
+    def ready():
+        for copy in places:
+            copy.wait()
+
+    grams = [(diag[2 * j], cross.at[j], diag[2 * j + 1]) for j in range(GROUP // 2)]
+    resolvent(grams, inverse, w, ready)
     for copy in loads:
         copy.wait()
 
@@ -343,7 +350,7 @@
     return pl.pallas_call(
         functools.partial(first_kernel, raw, tile),
         out_shape=tuple(shape(pairs * rows, n, dtype=BF16) for n in (share, *ahead)) + (shape(pairs, rows, 2 * rows, dtype=BF16), out, out),
-        in_specs=[SMEM] + [VMEM] * (4 * GROUP) + [HBM] * 4,
+        in_specs=[SMEM] + [HBM] * (4 * GROUP + 4),
         out_specs=(ANY,) * 6,
         scratch_shapes=[
             pltpu.VMEM((pairs, rows, rows), F32),
@@ -355,10 +362,11 @@
             pltpu.VMEM(out.shape, F32),
             pltpu.VMEM(out.shape, F32),
             pltpu.VMEM((pairs, rows, 2 * rows), BF16),
-            pltpu.SemaphoreType.DMA((GROUP,)),
+            pltpu.SemaphoreType.DMA((5 * GROUP,)),
             pltpu.SemaphoreType.DMA((share // tile + 5,)),
         ],
         cost_estimate=cost(2 * pairs * rows**3 * 40 + 14 * rows * rows * share, 12 * rows * share),
+        compiler_params=WHOLE,
         name="first",
     )(place, *diagonals, *crosses, x, *pieces)
 
@@ -381,7 +389,7 @@
     lower = lax.broadcasted_iota(jnp.int32, (rows, rows), 0) >= lax.broadcasted_iota(jnp.int32, (rows, rows), 1)
     diagonal = jnp.broadcast_to(bundles[0][2 * part : 2 * part + 1], (rows, rows))
     upper_gram = jnp.where(eye_mask(rows), diagonal, jnp.where(lower, turned, packed))
-    resolvent([(jnp.where(lower, packed, turned), gram[0], upper_gram)], inverse, w_ref)
+    resolvent([(jnp.where(lower, packed, turned), gram.at[0], upper_gram)], inverse, w_ref)
     copy.wait()
     saves = [pltpu.make_async_copy(w_ref, w_out, save.at[2])]
     saves[0].start()

time: 215 us -> 216 us (level)
  transfers between devices with their start and end apart: 57 -> 57, of which waited for: 30 -> 29; matrix products, arithmetic and copies ran while one was open for 2% -> 2% of each run, Pallas kernels for 14% -> 14%
where the time goes in v7:
time: 216 us; the launch traced here: 215 us
  waiting for transfers between devices  97.3 us (45%)
  starting transfers between devices  58.2 us (27%)
  Pallas kernels  47.1 us (22%)
  local copies, waits for them, and re-layouts  7.56 us (4%)
  other arithmetic  4.3 us (2%)
    ppermute x57, waiting for transfers between devices, send(): return lax.ppermute(block, axis, [(i, i ^ shift) for i in range(count)])  97.3 us
    ppermute x57, starting transfers between devices, send(): return lax.ppermute(block, axis, [(i, i ^ shift) for i in range(count)])  58.2 us
    pallas_call x1, Pallas kernels, first(): pl.pallas_call(functools.partial(first_kernel, raw, tile), out_shape=tupl...  11.2 us
    pallas_call x1, Pallas kernels, second(): pl.pallas_call(second_kernel, out_shape=(shape(rows, half, dtype=BF16),)...  6.46 us
    pallas_call x1, Pallas kernels, own_gram(): pl.pallas_call(own_gram_kernel, out_shape=(half, half), grid_spec=pltpu.P...  5.39 us
    pallas_call x1, Pallas kernels, raw_merge(): pl.pallas_call(functools.partial(raw_merge_kernel, share), out_shape=shap...  5.16 us
    pallas_call x1, Pallas kernels, late(): pl.pallas_call(functools.partial(late_kernel, share, raw), out_shape=shap...  5.12 us
    pallas_call x2, Pallas kernels, put(): pl.pallas_call(functools.partial(put_kernel, spots, share), out_shape=sha...  5.08 us
  transfers between devices with their start and end apart: 57, of which 29 were waited for; matrix products, arithmetic and copies ran while one was open for 2% of the time, Pallas kernels for 14%

profile of v7, /device:TPU:0, one launch (start us, length us, event | category | flops | bytes accessed | tf_op | source)
XLA Modules:
  0.0 215.0 jit_solution(12977685506733574387)
XLA Ops:
  0.0 2.7 %dynamic-slice_bitcast_fusion = (bf16[256,2048]{1,0:T(8,128)(2,1)}, bf16[256,2048]{1,0:T(8,128)(2,1)S(1)}) fusion(bf16[1,256,8192]{2,1,0:T(8,128)(2,1)} %param.1, s32[]{:T(128)S(6)} %select_n.23, s32[]{:T(128)S(6)} %select_n.22), kind=kLoop, calls=%fused_computation | loop fusion | bytes 4194312 | tf_op jit(solution)/shard_map/dynamic_slice | solution.py:575
  2.7 3.0 %collective-permute-start.6 = (bf16[256,2048]{1,0:T(8,128)(2,1)S(1)}, bf16[256,2048]{1,0:T(8,128)(2,1)}, u32[]{:S(2)}, u32[]{:S(2)}) collective-permute-start(bf16[256,2048]{1,0:T(8,128)(2,1)S(1)} %get-tuple-element.49), channel_id=1, source_target_pairs={{0,8},{8,0},{16,24},{24,16},{1,9},{9,1},{17,25},{25,17},{2,10},{10... | collective-permute-start | bytes 3145736 | tf_op jit(solution)/shard_map/ppermute | solution.py:26
  5.7 2.3 %constant_dynamic-slice_fusion = bf16[256,2048]{1,0:T(8,128)(2,1)} fusion(bf16[256,8192]{1,0:T(8,128)(2,1)} %bitcast.24, s32[]{:T(128)S(6)} %select_n.24), kind=kLoop, calls=%fused_computation.23 | loop fusion | bytes 2097156 | tf_op jit(solution)/shard_map/dynamic_slice | solution.py:575
  10.1 5.4 %own_gram.1 = (f32[128,256]{1,0:T(8,128)}, f32[128,256]{1,0:T(8,128)}) custom-call(s32[2]{0:T(128)} %pad_add_fusion.place.refs_0_, bf16[256,8192]{1,0:T(8,128)(2,1)} %bitcast.25), custom_call_target="tpu_custom_call" | custom-call | flops 1073741824 | bytes 4194304 | tf_op jit(solution)/shard_map/own_gram/pallas_call | solution.py:134
  18.0 2.1 collective-permute-start.3
  20.1 2.6 %collective-permute-start.4 = (f32[128,256]{1,0:T(8,128)S(1)}, f32[128,256]{1,0:T(8,128)S(1)}, u32[]{:S(2)}, u32[]{:S(2)}) collective-permute-start(f32[128,256]{1,0:T(8,128)S(1)} %add.117), channel_id=1, source_target_pairs={{0,4},{1,5},{2,6},{3,7},{4,0},{5,1},{6,2},{7,3},{8,12},{9,13},{10,... | collective-permute-start | bytes 393224 | tf_op jit(solution)/shard_map/ppermute | solution.py:26
  22.7 3.4 %collective-permute-done.3 = f32[128,256]{1,0:T(8,128)S(1)} collective-permute-done((f32[128,256]{1,0:T(8,128)S(1)}, f32[128,256]{1,0:T(8,128)S(1)}, u32[]{:S(2)}, u32[]{:S(2)}) %collective-permute-start.3) | collective-permute-done | bytes 131104 | tf_op jit(solution)/shard_map/ppermute | solution.py:26
  26.1 3.2 %collective-permute-start.5 = (f32[128,256]{1,0:T(8,128)S(1)}, f32[128,256]{1,0:T(8,128)S(1)}, u32[]{:S(2)}, u32[]{:S(2)}) collective-permute-start(f32[128,256]{1,0:T(8,128)S(1)} %add.117), channel_id=1, source_target_pairs={{0,6},{1,7},{2,4},{3,5},{4,2},{5,3},{6,0},{7,1},{8,14},{9,15},{10,... | collective-permute-start | bytes 393224 | tf_op jit(solution)/shard_map/ppermute | solution.py:26
  29.2 3.6 %collective-permute-done.5 = f32[128,256]{1,0:T(8,128)S(1)} collective-permute-done((f32[128,256]{1,0:T(8,128)S(1)}, f32[128,256]{1,0:T(8,128)S(1)}, u32[]{:S(2)}, u32[]{:S(2)}) %collective-permute-start.5) | collective-permute-done | bytes 131104 | tf_op jit(solution)/shard_map/ppermute | solution.py:26
  33.5 4.9 %near_gram.1 = (f32[256,256]{1,0:T(8,128)}, bf16[4,256,384]{2,1,0:T(8,128)(2,1)}, bf16[4,256,384]{2,1,0:T(8,128)(2,1)}, bf16[256,384]{1,0:T(8,128)(2,1)}) custom-call(s32[2]{0:T(128)} %pad_add_fusion.place.refs_0_, bf16[256,8192]{1,0:T(8,128)(2,1)} %bitcast.26, bf16[256,2048]{1,0:T(8,128)(2,1)} %collective-permute-done.6.p1.refs_18_), custom_call_target="tpu_custom_call" | custom-call | flops 268435456 | bytes 2097152 | tf_op jit(solution)/shard_map/near_gram/pallas_call | solution.py:199
  38.5 14.3 %collective-permute-done.1.p3.refs_20_ = bf16[256,2048]{1,0:T(8,128)(2,1)} collective-permute-done((bf16[256,2048]{1,0:T(8,128)(2,1)}, bf16[256,2048]{1,0:T(8,128)(2,1)}, u32[]{:S(2)}, u32[]{:S(2)}) %collective-permute-start.1) | collective-permute-done | bytes 1048608 | tf_op jit(solution)/shard_map/ppermute | solution.py:26
  52.7 3.9 %collective-permute-done.p2.refs_19_ = bf16[256,2048]{1,0:T(8,128)(2,1)} collective-permute-done((bf16[256,2048]{1,0:T(8,128)(2,1)}, bf16[256,2048]{1,0:T(8,128)(2,1)}, u32[]{:S(2)}, u32[]{:S(2)}) %collective-permute-start) | collective-permute-done | bytes 1048608 | tf_op jit(solution)/shard_map/ppermute | solution.py:26
  56.6 3.8 %far_gram.1 = (f32[4,64,256]{2,1,0:T(8,128)}, f32[4,64,256]{2,1,0:T(8,128)}, bf16[4,256,384]{2,1,0:T(8,128)(2,1)}) custom-call(s32[2]{0:T(128)} %pad_add_fusion.place.refs_0_, f32[256,256]{1,0:T(8,128)} %get-tuple-element.51.near, bf16[256,2048]{1,0:T(8,128)(2,1)} %collective-permute-done.p2.refs_19_, ...), custom_call_target="tpu_custom_call", output_to_operand_aliasing={{2}: (4, {})} | custom-call | flops 268435456 | bytes 2097152 | tf_op jit(solution)/shard_map/far_gram/pallas_call | solution.py:241
  67.5 2.2 %collective-permute-done.16 = f32[64,256]{1,0:T(8,128)S(1)} collective-permute-done((f32[64,256]{1,0:T(8,128)S(1)}, f32[64,256]{1,0:T(8,128)S(1)}, u32[]{:S(2)}, u32[]{:S(2)}) %collective-permute-start.16) | collective-permute-done | bytes 65568 | tf_op jit(solution)/shard_map/ppermute | solution.py:26
  72.0 2.6 %collective-permute-start.19 = (f32[64,256]{1,0:T(8,128)S(1)}, f32[64,256]{1,0:T(8,128)S(1)}, u32[]{:S(2)}, u32[]{:S(2)}) collective-permute-start(f32[64,256]{1,0:T(8,128)S(1)} %add_add_fusion.4), channel_id=1, source_target_pairs={{0,4},{1,5},{2,6},{3,7},{4,0},{5,1},{6,2},{7,3},{8,12},{9,13},{10,... | collective-permute-start | bytes 196616 | tf_op jit(solution)/shard_map/ppermute | solution.py:26
  78.6 2.1 collective-permute-done.20
  86.6 3.6 %collective-permute-done.23.refs_12_ = f32[64,256]{1,0:T(8,128)S(1)} collective-permute-done((f32[64,256]{1,0:T(8,128)S(1)}, f32[64,256]{1,0:T(8,128)S(1)}, u32[]{:S(2)}, u32[]{:S(2)}) %collective-permute-start.23) | collective-permute-done | bytes 65568 | tf_op jit(solution)/shard_map/ppermute | solution.py:26
  92.7 11.2 %first.1 = (bf16[512,2048]{1,0:T(8,128)(2,1)}, bf16[512,384]{1,0:T(8,128)(2,1)}, bf16[512,256]{1,0:T(8,128)(2,1)}, bf16[2,256,512]{2,1,0:T(8,128)(2,1)}, f32[4,72,256]{2,1,0:T(8,128)}, /*index=5*/f32[4,72,256]{2,1,0:T(8,128)}) custom-call(s32[2]{0:T(128)} %pad_add_fusion.place.refs_0_, f32[128,256]{1,0:T(8,128)} %add_add_fusion.refs_1_, ...), custom_call_target="tpu_custom_call" | custom-call | flops 4563402752 | bytes 6291456 | tf_op jit(solution)/shard_map/first/pallas_call | solution.py:350
  112.0 2.2 %collective-permute-done.31 = f32[72,256]{1,0:T(8,128)S(1)} collective-permute-done((f32[72,256]{1,0:T(8,128)S(1)}, f32[72,256]{1,0:T(8,128)S(1)}, u32[]{:S(2)}, u32[]{:S(2)}) %collective-permute-start.31) | collective-permute-done | bytes 73760 | tf_op jit(solution)/shard_map/ppermute | solution.py:26
  114.3 3.5 %collective-permute-start.33 = (f32[72,256]{1,0:T(8,128)S(1)}, f32[72,256]{1,0:T(8,128)S(1)}, u32[]{:S(2)}, u32[]{:S(2)}) collective-permute-start(f32[72,256]{1,0:T(8,128)S(1)} %add_add_fusion.2), channel_id=1, source_target_pairs={{0,4},{1,5},{2,6},{3,7},{4,0},{5,1},{6,2},{7,3},{8,12},{9,13},{10,... | collective-permute-start | bytes 221192 | tf_op jit(solution)/shard_map/ppermute | solution.py:26
  125.6 1.9 collective-permute-done.50.d
  129.0 16.2 %collective-permute-done.35.refs_2_ = f32[72,256]{1,0:T(8,128)S(1)} collective-permute-done((f32[72,256]{1,0:T(8,128)S(1)}, f32[72,256]{1,0:T(8,128)S(1)}, u32[]{:S(2)}, u32[]{:S(2)}) %collective-permute-start.35) | collective-permute-done | bytes 73760 | tf_op jit(solution)/shard_map/ppermute | solution.py:26
  145.2 2.2 %collective-permute-start.37 = (f32[72,256]{1,0:T(8,128)S(1)}, f32[72,256]{1,0:T(8,128)S(1)}, u32[]{:S(2)}, u32[]{:S(2)}) collective-permute-start(f32[72,256]{1,0:T(8,128)S(1)} %add_add_fusion.1.refs_1_), channel_id=1, source_target_pairs={{0,24},{8,16},{16,8},{24,0},{1,25},{9,17},{17,9},{25,1},{2,26},{10... | collective-permute-start | bytes 221192 | tf_op jit(solution)/shard_map/ppermute | solution.py:26
  147.5 5.3 %collective-permute-done.37.refs_4_ = f32[72,256]{1,0:T(8,128)S(1)} collective-permute-done((f32[72,256]{1,0:T(8,128)S(1)}, f32[72,256]{1,0:T(8,128)S(1)}, u32[]{:S(2)}, u32[]{:S(2)}) %collective-permute-start.37) | collective-permute-done | bytes 73760 | tf_op jit(solution)/shard_map/ppermute | solution.py:26
  158.8 6.5 %second.1 = (bf16[256,512]{1,0:T(8,128)(2,1)}, bf16[256,512]{1,0:T(8,128)(2,1)}, bf16[1,256,512]{2,1,0:T(8,128)(2,1)}) custom-call(s32[2]{0:T(128)} %pad_add_fusion.place.refs_0_, f32[72,256]{1,0:T(8,128)} %copy-done.9, f32[72,256]{1,0:T(8,128)} %copy-done.18, f32[72,256]{1,0:T(8,128)} %copy-done.19, f32[72,256]{1,0:T(8,128)} %copy-done.20, ...), custom_call_target="tpu_custom_call" | custom-call | flops 1610612736 | bytes 3145728 | tf_op jit(solution)/shard_map/second/pallas_call | solution.py:409
  168.6 5.9 %collective-permute-done.56.refs_5_ = bf16[512,256]{1,0:T(8,128)(2,1)S(1)} collective-permute-done((bf16[512,256]{1,0:T(8,128)(2,1)S(1)}, bf16[512,256]{1,0:T(8,128)(2,1)S(1)}, u32[]{:S(2)}, u32[]{:S(2)}) %collective-permute-start.56) | collective-permute-done | bytes 262176 | tf_op jit(solution)/shard_map/ppermute | solution.py:26
  175.7 4.5 %collective-permute-done.42.refs_0_ = bf16[256,512]{1,0:T(8,128)(2,1)} collective-permute-done((bf16[256,512]{1,0:T(8,128)(2,1)}, bf16[256,512]{1,0:T(8,128)(2,1)}, u32[]{:S(2)}, u32[]{:S(2)}) %collective-permute-start.42) | collective-permute-done | bytes 262176 | tf_op jit(solution)/shard_map/ppermute | solution.py:26
  181.5 15.0 %collective-permute-done.44.refs_1_ = bf16[256,512]{1,0:T(8,128)(2,1)} collective-permute-done((bf16[256,512]{1,0:T(8,128)(2,1)}, bf16[256,512]{1,0:T(8,128)(2,1)}, u32[]{:S(2)}, u32[]{:S(2)}) %collective-permute-start.44) | collective-permute-done | bytes 262176 | tf_op jit(solution)/shard_map/ppermute | solution.py:26
  198.5 5.1 %late.1._ = bf16[256,8192]{1,0:T(8,128)(2,1)} custom-call(s32[2]{0:T(128)} %pad_add_fusion.place.refs_0_, bf16[1,256,512]{2,1,0:T(8,128)(2,1)} %get-tuple-element.79.w.w1, bf16[256,512]{1,0:T(8,128)(2,1)} %get-tuple-element.76.a, bf16[256,512]{1,0:T(8,128)(2,1)} %get-tuple-element.77.b, bf16[512,2048]{1,0:T(8,128)(2,1)} %get-tuple-element.75.refs_9_.m, ...), custom_call_target="tpu_custom_call" | custom-call | flops 1073741824 | bytes 6291456 | tf_op jit(solution)/shard_map/late/pallas_call | solution.py:506
  204.5 5.2 %raw_merge.1.refs_4_ = bf16[256,8192]{1,0:T(8,128)(2,1)} custom-call(s32[2]{0:T(128)} %pad_add_fusion.place.refs_0_, bf16[2,256,512]{2,1,0:T(8,128)(2,1)} %get-tuple-element.78.w0, bf16[1,256,512]{2,1,0:T(8,128)(2,1)} %get-tuple-element.79.w.w1, bf16[256,8192]{1,0:T(8,128)(2,1)} %bitcast.28, ...), custom_call_target="tpu_custom_call", output_to_operand_aliasing={{}: (7, {})} | custom-call | flops 905969664 | bytes 2949120 | tf_op jit(solution)/shard_map/raw_merge/pallas_call | solution.py:458
  209.7 2.6 %put.2.refs_2_ = bf16[256,8192]{1,0:T(8,128)(2,1)} custom-call(s32[2]{0:T(128)} %pad_add_fusion.place.refs_0_, bf16[256,512]{1,0:T(8,128)(2,1)} %collective-permute-done.42.refs_0_, bf16[256,512]{1,0:T(8,128)(2,1)} %collective-permute-done.44.refs_1_, bf16[256,512]{1,0:T(8,128)(2,1)} %collective-permute-done.46.refs_2_, ...), custom_call_target="tpu_custom_call", output_to_operand_aliasing={{}: (5, {})} | custom-call | bytes 2097152 | tf_op jit(solution)/shard_map/put/pallas_call | solution.py:541
  212.4 2.4 %put.3 = bf16[256,8192]{1,0:T(8,128)(2,1)} custom-call(s32[2]{0:T(128)} %pad_add_fusion.place.refs_0_, bf16[256,512]{1,0:T(8,128)(2,1)} %collective-permute-done.43.refs_0_, bf16[256,512]{1,0:T(8,128)(2,1)} %collective-permute-done.45.refs_1_, bf16[256,8192]{1,0:T(8,128)(2,1)} %put.2.refs_2_), custom_call_target="tpu_custom_call", output_to_operand_aliasing={{}: (3, {})} | custom-call | bytes 1048576 | tf_op jit(solution)/shard_map/put/pallas_call | solution.py:541
  (164 shorter events, 59.2 us)
Async XLA Ops:
  2.7 30.8 %collective-permute-start.6 = (bf16[256,2048]{1,0:T(8,128)(2,1)S(1)}, bf16[256,2048]{1,0:T(8,128)(2,1)}, u32[]{:S(2)}, u32[]{:S(2)}) collective-permute-start(bf16[256,2048]{1,0:T(8,128)(2,1)S(1)} %get-tuple-element.49), channel_id=1, source_target_pairs={{0,8},{8,0},{16,24},{24,16},{1,9},{9,1},{17,25},{25,17},{2,10},{10... | collective-permute-start | bytes 3145736 | tf_op jit(solution)/shard_map/ppermute | solution.py:26
  8.0 44.7 %collective-permute-start.1 = (bf16[256,2048]{1,0:T(8,128)(2,1)}, bf16[256,2048]{1,0:T(8,128)(2,1)}, u32[]{:S(2)}, u32[]{:S(2)}) collective-permute-start(bf16[256,2048]{1,0:T(8,128)(2,1)} %constant_dynamic-slice_fusion), channel_id=1, source_target_pairs={{0,24},{8,16},{16,8},{24,0},{1,25},{9,17},{17,9},{25,1},{2,26},{10... | collective-permute-start | bytes 3145736 | tf_op jit(solution)/shard_map/ppermute | solution.py:26
  9.5 47.1 %collective-permute-start = (bf16[256,2048]{1,0:T(8,128)(2,1)}, bf16[256,2048]{1,0:T(8,128)(2,1)}, u32[]{:S(2)}, u32[]{:S(2)}) collective-permute-start(bf16[256,2048]{1,0:T(8,128)(2,1)} %get-tuple-element.45), channel_id=1, source_target_pairs={{0,16},{8,24},{16,0},{24,8},{1,17},{9,25},{17,1},{25,9},{2,18},{10... | collective-permute-start | bytes 3145736 | tf_op jit(solution)/shard_map/ppermute | solution.py:26
  18.0 8.1 %collective-permute-start.3 = (f32[128,256]{1,0:T(8,128)S(1)}, f32[128,256]{1,0:T(8,128)S(1)}, u32[]{:S(2)}, u32[]{:S(2)}) collective-permute-start(f32[128,256]{1,0:T(8,128)S(1)} %add.117), channel_id=1, source_target_pairs={{0,2},{1,3},{2,0},{3,1},{4,6},{5,7},{6,4},{7,5},{8,10},{9,11},{10,... | collective-permute-start | bytes 393224 | tf_op jit(solution)/shard_map/ppermute | solution.py:26
  20.1 9.2 %collective-permute-start.4 = (f32[128,256]{1,0:T(8,128)S(1)}, f32[128,256]{1,0:T(8,128)S(1)}, u32[]{:S(2)}, u32[]{:S(2)}) collective-permute-start(f32[128,256]{1,0:T(8,128)S(1)} %add.117), channel_id=1, source_target_pairs={{0,4},{1,5},{2,6},{3,7},{4,0},{5,1},{6,2},{7,3},{8,12},{9,13},{10,... | collective-permute-start | bytes 393224 | tf_op jit(solution)/shard_map/ppermute | solution.py:26
  26.1 6.8 %collective-permute-start.5 = (f32[128,256]{1,0:T(8,128)S(1)}, f32[128,256]{1,0:T(8,128)S(1)}, u32[]{:S(2)}, u32[]{:S(2)}) collective-permute-start(f32[128,256]{1,0:T(8,128)S(1)} %add.117), channel_id=1, source_target_pairs={{0,6},{1,7},{2,4},{3,5},{4,2},{5,3},{6,0},{7,1},{8,14},{9,15},{10,... | collective-permute-start | bytes 393224 | tf_op jit(solution)/shard_map/ppermute | solution.py:26
  70.4 6.5 %collective-permute-start.18 = (f32[64,256]{1,0:T(8,128)S(1)}, f32[64,256]{1,0:T(8,128)S(1)}, u32[]{:S(2)}, u32[]{:S(2)}) collective-permute-start(f32[64,256]{1,0:T(8,128)S(1)} %add_add_fusion.4), channel_id=1, source_target_pairs={{0,2},{1,3},{2,0},{3,1},{4,6},{5,7},{6,4},{7,5},{8,10},{9,11},{10,... | collective-permute-start | bytes 196616 | tf_op jit(solution)/shard_map/ppermute | solution.py:26
  72.0 6.6 %collective-permute-start.19 = (f32[64,256]{1,0:T(8,128)S(1)}, f32[64,256]{1,0:T(8,128)S(1)}, u32[]{:S(2)}, u32[]{:S(2)}) collective-permute-start(f32[64,256]{1,0:T(8,128)S(1)} %add_add_fusion.4), channel_id=1, source_target_pairs={{0,4},{1,5},{2,6},{3,7},{4,0},{5,1},{6,2},{7,3},{8,12},{9,13},{10,... | collective-permute-start | bytes 196616 | tf_op jit(solution)/shard_map/ppermute | solution.py:26
  75.3 7.5 %collective-permute-start.9 = (f32[128,256]{1,0:T(8,128)}, f32[128,256]{1,0:T(8,128)S(1)}, u32[]{:S(2)}, u32[]{:S(2)}) collective-permute-start(f32[128,256]{1,0:T(8,128)} %add_add_fusion.refs_1_), channel_id=1, source_target_pairs={{0,16},{8,24},{16,0},{24,8},{1,17},{9,25},{17,1},{25,9},{2,18},{10... | collective-permute-start | bytes 393224 | tf_op jit(solution)/shard_map/ppermute | solution.py:26
  82.8 8.0 %collective-permute-start.12 = (f32[128,256]{1,0:T(8,128)S(1)}, f32[128,256]{1,0:T(8,128)S(1)}, u32[]{:S(2)}, u32[]{:S(2)}) collective-permute-start(f32[128,256]{1,0:T(8,128)S(1)} %collective-permute-done.8.refs_2_), channel_id=1, source_target_pairs={{0,1},{1,0},{2,3},{3,2},{4,5},{5,4},{6,7},{7,6},{8,9},{9,8},{10,11... | collective-permute-start | bytes 393224 | tf_op jit(solution)/shard_map/ppermute | solution.py:26
  83.2 7.7 %collective-permute-start.13 = (f32[128,256]{1,0:T(8,128)S(1)}, f32[128,256]{1,0:T(8,128)S(1)}, u32[]{:S(2)}, u32[]{:S(2)}) collective-permute-start(f32[128,256]{1,0:T(8,128)S(1)} %collective-permute-done.9.refs_3_), channel_id=1, source_target_pairs={{0,1},{1,0},{2,3},{3,2},{4,5},{5,4},{6,7},{7,6},{8,9},{9,8},{10,11... | collective-permute-start | bytes 393224 | tf_op jit(solution)/shard_map/ppermute | solution.py:26
  83.4 7.5 %collective-permute-start.14 = (f32[128,256]{1,0:T(8,128)S(1)}, f32[128,256]{1,0:T(8,128)S(1)}, u32[]{:S(2)}, u32[]{:S(2)}) collective-permute-start(f32[128,256]{1,0:T(8,128)S(1)} %collective-permute-done.10.refs_4_), channel_id=1, source_target_pairs={{0,1},{1,0},{2,3},{3,2},{4,5},{5,4},{6,7},{7,6},{8,9},{9,8},{10,11... | collective-permute-start | bytes 393224 | tf_op jit(solution)/shard_map/ppermute | solution.py:26
  114.2 6.6 %collective-permute-start.32 = (f32[72,256]{1,0:T(8,128)S(1)}, f32[72,256]{1,0:T(8,128)S(1)}, u32[]{:S(2)}, u32[]{:S(2)}) collective-permute-start(f32[72,256]{1,0:T(8,128)S(1)} %add_add_fusion.2), channel_id=1, source_target_pairs={{0,2},{1,3},{2,0},{3,1},{4,6},{5,7},{6,4},{7,5},{8,10},{9,11},{10,... | collective-permute-start | bytes 221192 | tf_op jit(solution)/shard_map/ppermute | solution.py:26
  114.3 7.9 %collective-permute-start.33 = (f32[72,256]{1,0:T(8,128)S(1)}, f32[72,256]{1,0:T(8,128)S(1)}, u32[]{:S(2)}, u32[]{:S(2)}) collective-permute-start(f32[72,256]{1,0:T(8,128)S(1)} %add_add_fusion.2), channel_id=1, source_target_pairs={{0,4},{1,5},{2,6},{3,7},{4,0},{5,1},{6,2},{7,3},{8,12},{9,13},{10,... | collective-permute-start | bytes 221192 | tf_op jit(solution)/shard_map/ppermute | solution.py:26
  118.7 8.9 %collective-permute-start.50 = (bf16[256,384]{1,0:T(8,128)(2,1)}, bf16[256,384]{1,0:T(8,128)(2,1)S(1)}, u32[]{:S(2)}, u32[]{:S(2)}) collective-permute-start(bf16[256,384]{1,0:T(8,128)(2,1)} %get-tuple-element.82), channel_id=1, source_target_pairs={{0,24},{8,16},{16,8},{24,0},{1,25},{9,17},{17,9},{25,1},{2,26},{10... | collective-permute-start | bytes 589832 | tf_op jit(solution)/shard_map/ppermute | solution.py:26
  120.3 46.3 %collective-permute-start.48 = (bf16[4,256,384]{2,1,0:T(8,128)(2,1)}, bf16[4,256,384]{2,1,0:T(8,128)(2,1)S(1)}, u32[]{:S(2)}, u32[]{:S(2)}) collective-permute-start(bf16[4,256,384]{2,1,0:T(8,128)(2,1)} %get-tuple-element.80), channel_id=1, source_target_pairs={{0,8},{8,0},{16,24},{24,16},{1,9},{9,1},{17,25},{25,17},{2,10},{10... | collective-permute-start | bytes 2359304 | tf_op jit(solution)/shard_map/ppermute | solution.py:26
  120.8 32.5 %collective-permute-start.55 = (bf16[512,256]{1,0:T(8,128)(2,1)}, bf16[512,256]{1,0:T(8,128)(2,1)S(1)}, u32[]{:S(2)}, u32[]{:S(2)}) collective-permute-start(bf16[512,256]{1,0:T(8,128)(2,1)} %get-tuple-element.84), channel_id=1, source_target_pairs={{0,16},{8,24},{16,0},{24,8},{1,17},{9,25},{17,1},{25,9},{2,18},{10... | collective-permute-start | bytes 786440 | tf_op jit(solution)/shard_map/ppermute | solution.py:26
  124.0 21.3 %collective-permute-start.35 = (f32[72,256]{1,0:T(8,128)S(1)}, f32[72,256]{1,0:T(8,128)S(1)}, u32[]{:S(2)}, u32[]{:S(2)}) collective-permute-start(f32[72,256]{1,0:T(8,128)S(1)} %add_add_fusion.1.refs_1_), channel_id=1, source_target_pairs={{0,8},{8,0},{16,24},{24,16},{1,9},{9,1},{17,25},{25,17},{2,10},{10... | collective-permute-start | bytes 221192 | tf_op jit(solution)/shard_map/ppermute | solution.py:26
  124.6 22.9 %collective-permute-start.36 = (f32[72,256]{1,0:T(8,128)S(1)}, f32[72,256]{1,0:T(8,128)S(1)}, u32[]{:S(2)}, u32[]{:S(2)}) collective-permute-start(f32[72,256]{1,0:T(8,128)S(1)} %add_add_fusion.1.refs_1_), channel_id=1, source_target_pairs={{0,16},{8,24},{16,0},{24,8},{1,17},{9,25},{17,1},{25,9},{2,18},{10... | collective-permute-start | bytes 221192 | tf_op jit(solution)/shard_map/ppermute | solution.py:26
  127.5 30.4 %collective-permute-start.51 = (bf16[512,384]{1,0:T(8,128)(2,1)}, bf16[512,384]{1,0:T(8,128)(2,1)S(1)}, u32[]{:S(2)}, u32[]{:S(2)}) collective-permute-start(bf16[512,384]{1,0:T(8,128)(2,1)} %get-tuple-element.83), channel_id=1, source_target_pairs={{0,8},{8,0},{16,24},{24,16},{1,9},{9,1},{17,25},{25,17},{2,10},{10... | collective-permute-start | bytes 1179656 | tf_op jit(solution)/shard_map/ppermute | solution.py:26
  145.2 7.5 %collective-permute-start.37 = (f32[72,256]{1,0:T(8,128)S(1)}, f32[72,256]{1,0:T(8,128)S(1)}, u32[]{:S(2)}, u32[]{:S(2)}) collective-permute-start(f32[72,256]{1,0:T(8,128)S(1)} %add_add_fusion.1.refs_1_), channel_id=1, source_target_pairs={{0,24},{8,16},{16,8},{24,0},{1,25},{9,17},{17,9},{25,1},{2,26},{10... | collective-permute-start | bytes 221192 | tf_op jit(solution)/shard_map/ppermute | solution.py:26
  153.3 14.1 %collective-permute-start.52 = (bf16[512,384]{1,0:T(8,128)(2,1)}, bf16[512,384]{1,0:T(8,128)(2,1)S(1)}, u32[]{:S(2)}, u32[]{:S(2)}) collective-permute-start(bf16[512,384]{1,0:T(8,128)(2,1)} %get-tuple-element.83), channel_id=1, source_target_pairs={{0,16},{8,24},{16,0},{24,8},{1,17},{9,25},{17,1},{25,9},{2,18},{10... | collective-permute-start | bytes 1179656 | tf_op jit(solution)/shard_map/ppermute | solution.py:26
  154.1 49.6 %collective-permute-start.49 = (bf16[4,256,384]{2,1,0:T(8,128)(2,1)}, bf16[4,256,384]{2,1,0:T(8,128)(2,1)S(1)}, u32[]{:S(2)}, u32[]{:S(2)}) collective-permute-start(bf16[4,256,384]{2,1,0:T(8,128)(2,1)} %get-tuple-element.81), channel_id=1, source_target_pairs={{0,16},{8,24},{16,0},{24,8},{1,17},{9,25},{17,1},{25,9},{2,18},{10... | collective-permute-start | bytes 2359304 | tf_op jit(solution)/shard_map/ppermute | solution.py:26
  156.6 8.6 %collective-permute-start.54 = (bf16[512,256]{1,0:T(8,128)(2,1)}, bf16[512,256]{1,0:T(8,128)(2,1)S(1)}, u32[]{:S(2)}, u32[]{:S(2)}) collective-permute-start(bf16[512,256]{1,0:T(8,128)(2,1)} %get-tuple-element.84), channel_id=1, source_target_pairs={{0,8},{8,0},{16,24},{24,16},{1,9},{9,1},{17,25},{25,17},{2,10},{10... | collective-permute-start | bytes 786440 | tf_op jit(solution)/shard_map/ppermute | solution.py:26
  158.0 39.2 %collective-permute-start.53 = (bf16[512,384]{1,0:T(8,128)(2,1)S(1)}, bf16[512,384]{1,0:T(8,128)(2,1)S(1)}, u32[]{:S(2)}, u32[]{:S(2)}) collective-permute-start(bf16[512,384]{1,0:T(8,128)(2,1)S(1)} %collective-permute-done.51.refs_0_), channel_id=1, source_target_pairs={{0,16},{8,24},{16,0},{24,8},{1,17},{9,25},{17,1},{25,9},{2,18},{10... | collective-permute-start | bytes 1179656 | tf_op jit(solution)/shard_map/ppermute | solution.py:26
  165.3 9.2 %collective-permute-start.56 = (bf16[512,256]{1,0:T(8,128)(2,1)S(1)}, bf16[512,256]{1,0:T(8,128)(2,1)S(1)}, u32[]{:S(2)}, u32[]{:S(2)}) collective-permute-start(bf16[512,256]{1,0:T(8,128)(2,1)S(1)} %collective-permute-done.55.refs_4_), channel_id=1, source_target_pairs={{0,8},{8,0},{16,24},{24,16},{1,9},{9,1},{17,25},{25,17},{2,10},{10... | collective-permute-start | bytes 786440 | tf_op jit(solution)/shard_map/ppermute | solution.py:26
  166.5 13.7 %collective-permute-start.42 = (bf16[256,512]{1,0:T(8,128)(2,1)}, bf16[256,512]{1,0:T(8,128)(2,1)}, u32[]{:S(2)}, u32[]{:S(2)}) collective-permute-start(bf16[256,512]{1,0:T(8,128)(2,1)} %get-tuple-element.76.a), channel_id=1, source_target_pairs={{0,8},{8,0},{16,24},{24,16},{1,9},{9,1},{17,25},{25,17},{2,10},{10... | collective-permute-start | bytes 786440 | tf_op jit(solution)/shard_map/ppermute | solution.py:26
  167.4 29.1 %collective-permute-start.44 = (bf16[256,512]{1,0:T(8,128)(2,1)}, bf16[256,512]{1,0:T(8,128)(2,1)}, u32[]{:S(2)}, u32[]{:S(2)}) collective-permute-start(bf16[256,512]{1,0:T(8,128)(2,1)} %get-tuple-element.77.b), channel_id=1, source_target_pairs={{0,16},{8,24},{16,0},{24,8},{1,17},{9,25},{17,1},{25,9},{2,18},{10... | collective-permute-start | bytes 786440 | tf_op jit(solution)/shard_map/ppermute | solution.py:26
  174.5 35.2 %collective-permute-start.46 = (bf16[256,512]{1,0:T(8,128)(2,1)}, bf16[256,512]{1,0:T(8,128)(2,1)}, u32[]{:S(2)}, u32[]{:S(2)}) collective-permute-start(bf16[256,512]{1,0:T(8,128)(2,1)} %get-tuple-element.77.b), channel_id=1, source_target_pairs={{0,8},{8,0},{16,24},{24,16},{1,9},{9,1},{17,25},{25,17},{2,10},{10... | collective-permute-start | bytes 786440 | tf_op jit(solution)/shard_map/ppermute | solution.py:26
  180.2 29.5 %collective-permute-start.47 = (bf16[256,512]{1,0:T(8,128)(2,1)}, bf16[256,512]{1,0:T(8,128)(2,1)}, u32[]{:S(2)}, u32[]{:S(2)}) collective-permute-start(bf16[256,512]{1,0:T(8,128)(2,1)} %get-tuple-element.76.a), channel_id=1, source_target_pairs={{0,16},{8,24},{16,0},{24,8},{1,17},{9,25},{17,1},{25,9},{2,18},{10... | collective-permute-start | bytes 786440 | tf_op jit(solution)/shard_map/ppermute | solution.py:26
  196.5 15.9 %collective-permute-start.43 = (bf16[256,512]{1,0:T(8,128)(2,1)}, bf16[256,512]{1,0:T(8,128)(2,1)}, u32[]{:S(2)}, u32[]{:S(2)}) collective-permute-start(bf16[256,512]{1,0:T(8,128)(2,1)} %collective-permute-done.42.refs_0_), channel_id=1, source_target_pairs={{0,16},{8,24},{16,0},{24,8},{1,17},{9,25},{17,1},{25,9},{2,18},{10... | collective-permute-start | bytes 786440 | tf_op jit(solution)/shard_map/ppermute | solution.py:26
  197.2 15.2 %collective-permute-start.45 = (bf16[256,512]{1,0:T(8,128)(2,1)}, bf16[256,512]{1,0:T(8,128)(2,1)}, u32[]{:S(2)}, u32[]{:S(2)}) collective-permute-start(bf16[256,512]{1,0:T(8,128)(2,1)} %collective-permute-done.44.refs_1_), channel_id=1, source_target_pairs={{0,8},{8,0},{16,24},{24,16},{1,9},{9,1},{17,25},{25,17},{2,10},{10... | collective-permute-start | bytes 786440 | tf_op jit(solution)/shard_map/ppermute | solution.py:26
  (56 other events, 464.8 us)

commit v8 on v6

--- a/solution.py
+++ b/solution.py
@@ -64,29 +64,41 @@
     mask = eye_mask(n)
     eye = jnp.where(mask, 1.0, 0.0)
     parts = [halves(k) for k in kernels]
+    spreads = []
     for j, k in enumerate(kernels):
         diag = jnp.where(mask, k, 0.0)
         row = 1.0 / jnp.sum(diag, axis=0, keepdims=True)
         col = 1.0 / jnp.sum(diag, axis=1, keepdims=True)
         scaled = jnp.where(mask, 0.0, k) * row
-        spread = jnp.sum(scaled * (jnp.where(mask, 0.0, k) * col))
-        bound = jnp.minimum(jnp.max(jnp.sum(jnp.abs(k), axis=0, keepdims=True)), limit)
-        near = jnp.where(mask, row, -scaled * col)
-        far = eye * (2.0 / (1.0 + bound))
-        x_ref[j] = jnp.where(spread < 0.9, near, far)
-
-    def step():
+        spreads.append(jnp.sum(scaled * (jnp.where(mask, 0.0, k) * col)))
+        x_ref[j] = jnp.where(mask, row, -scaled * col)
+
+    def step(update=lambda xs, rest: dot(xs[0], rest.astype(BF16))):
         worst = jnp.float32(0.0)
         for j, part in enumerate(parts):
             x = x_ref[j]
             xs = halves(x)
             rest = eye - product(part, xs)
             worst = jnp.maximum(worst, jnp.sum(rest * rest))
-            x_ref[j] = x + dot(xs[0], rest.astype(BF16))
+            x_ref[j] = x + update(xs, rest)
         return worst
 
     step()
-    lax.while_loop(lambda s: (s[0] < 24) & (s[1] > 1e-6), lambda s: (s[0] + 1, step()), (jnp.int32(2), step()))
+    worst = step()
+    wide = functools.reduce(jnp.maximum, spreads) >= 0.9
+
+    def more(state):
+        count, _ = state
+        for j, k in enumerate(kernels):
+
+            @pl.when((count == 0) & (spreads[j] >= 0.9))
+            def _():
+                bound = jnp.minimum(jnp.max(jnp.sum(jnp.abs(k), axis=0, keepdims=True)), limit)
+                x_ref[j] = eye * (2.0 / (1.0 + bound))
+
+        return count + 1, step(lambda xs, rest: product(xs, halves(rest)))
+
+    lax.while_loop(lambda s: (s[0] < 24) & ((s[1] > 1e-6) | ((s[0] == 0) & wide)), more, (jnp.int32(0), worst))
 
 
 def resolvent(grams, x_ref, out_ref):
@@ -95,8 +107,8 @@
     eye = jnp.where(mask, 1.0, 0.0)
     scaled = []
     for a, b, d in grams:
-        average = jnp.sum(jnp.where(mask, a + d, 0.0)) / (2 * n)
-        scaled.append((eye + a / average, b / average, eye + d / average))
+        scale = (2 * n) / jnp.sum(jnp.where(mask, a + d, 0.0))
+        scaled.append((eye + a * scale, b * scale, eye + d * scale))
     limit = 1.0 + 2 * n
     invert([d for _, _, d in scaled], x_ref, limit)
     ties, schurs = [], []

time: 215 us -> 215 us (level)
  transfers between devices with their start and end apart: 57 -> 57, of which waited for: 30 -> 31; matrix products, arithmetic and copies ran while one was open for 2% -> 2% of each run, Pallas kernels for 14% -> 14%
where the time goes in v8:
time: 215 us; the launch traced here: 214 us
  waiting for transfers between devices  98.8 us (46%)
  starting transfers between devices  58 us (27%)
  Pallas kernels  45.6 us (21%)
  local copies, waits for them, and re-layouts  6.81 us (3%)
  other arithmetic  4.34 us (2%)
    ppermute x57, waiting for transfers between devices, send(): return lax.ppermute(block, axis, [(i, i ^ shift) for i in range(count)])  98.8 us
    ppermute x57, starting transfers between devices, send(): return lax.ppermute(block, axis, [(i, i ^ shift) for i in range(count)])  58 us
    pallas_call x1, Pallas kernels, first(): pl.pallas_call(functools.partial(first_kernel, raw, tile), out_shape=tupl...  10.1 us
    pallas_call x1, Pallas kernels, second(): pl.pallas_call(second_kernel, out_shape=(shape(rows, half, dtype=BF16),)...  6.05 us
    pallas_call x1, Pallas kernels, own_gram(): pl.pallas_call(own_gram_kernel, out_shape=(half, half), grid_spec=pltpu.P...  5.39 us
    pallas_call x1, Pallas kernels, raw_merge(): pl.pallas_call(functools.partial(raw_merge_kernel, share), out_shape=shap...  5.16 us
    pallas_call x1, Pallas kernels, late(): pl.pallas_call(functools.partial(late_kernel, share, raw), out_shape=shap...  5.11 us
    pallas_call x2, Pallas kernels, put(): pl.pallas_call(functools.partial(put_kernel, spots, share), out_shape=sha...  5.08 us
  transfers between devices with their start and end apart: 57, of which 31 were waited for; matrix products, arithmetic and copies ran while one was open for 2% of the time, Pallas kernels for 14%

profile of v8, /device:TPU:0, one launch (start us, length us, event | category | flops | bytes accessed | tf_op | source)
XLA Modules:
  0.0 214.1 jit_solution(11802546122835246195)
XLA Ops:
  0.0 2.7 %dynamic-slice_bitcast_fusion = (bf16[256,2048]{1,0:T(8,128)(2,1)}, bf16[256,2048]{1,0:T(8,128)(2,1)S(1)}) fusion(bf16[1,256,8192]{2,1,0:T(8,128)(2,1)} %param.1, s32[]{:T(128)S(6)} %select_n.23, s32[]{:T(128)S(6)} %select_n.22), kind=kLoop, calls=%fused_computation | loop fusion | bytes 4194312 | tf_op jit(solution)/shard_map/dynamic_slice | solution.py:579
  2.7 3.0 %collective-permute-start.6 = (bf16[256,2048]{1,0:T(8,128)(2,1)S(1)}, bf16[256,2048]{1,0:T(8,128)(2,1)}, u32[]{:S(2)}, u32[]{:S(2)}) collective-permute-start(bf16[256,2048]{1,0:T(8,128)(2,1)S(1)} %get-tuple-element.49), channel_id=1, source_target_pairs={{0,8},{8,0},{16,24},{24,16},{1,9},{9,1},{17,25},{25,17},{2,10},{10... | collective-permute-start | bytes 3145736 | tf_op jit(solution)/shard_map/ppermute | solution.py:26
  5.7 2.3 %constant_dynamic-slice_fusion = bf16[256,2048]{1,0:T(8,128)(2,1)} fusion(bf16[256,8192]{1,0:T(8,128)(2,1)} %bitcast.24, s32[]{:T(128)S(6)} %select_n.24), kind=kLoop, calls=%fused_computation.23 | loop fusion | bytes 2097156 | tf_op jit(solution)/shard_map/dynamic_slice | solution.py:579
  10.2 5.4 %own_gram.1 = (f32[128,256]{1,0:T(8,128)}, f32[128,256]{1,0:T(8,128)}) custom-call(s32[2]{0:T(128)} %pad_add_fusion.place.refs_0_, bf16[256,8192]{1,0:T(8,128)(2,1)} %bitcast.25), custom_call_target="tpu_custom_call" | custom-call | flops 1073741824 | bytes 4194304 | tf_op jit(solution)/shard_map/own_gram/pallas_call | solution.py:148
  18.0 2.1 collective-permute-start.3
  20.2 2.6 %collective-permute-start.4 = (f32[128,256]{1,0:T(8,128)S(1)}, f32[128,256]{1,0:T(8,128)S(1)}, u32[]{:S(2)}, u32[]{:S(2)}) collective-permute-start(f32[128,256]{1,0:T(8,128)S(1)} %add.117), channel_id=1, source_target_pairs={{0,4},{1,5},{2,6},{3,7},{4,0},{5,1},{6,2},{7,3},{8,12},{9,13},{10,... | collective-permute-start | bytes 393224 | tf_op jit(solution)/shard_map/ppermute | solution.py:26
  22.7 3.4 %collective-permute-done.3 = f32[128,256]{1,0:T(8,128)S(1)} collective-permute-done((f32[128,256]{1,0:T(8,128)S(1)}, f32[128,256]{1,0:T(8,128)S(1)}, u32[]{:S(2)}, u32[]{:S(2)}) %collective-permute-start.3) | collective-permute-done | bytes 131104 | tf_op jit(solution)/shard_map/ppermute | solution.py:26
  26.1 3.2 %collective-permute-start.5 = (f32[128,256]{1,0:T(8,128)S(1)}, f32[128,256]{1,0:T(8,128)S(1)}, u32[]{:S(2)}, u32[]{:S(2)}) collective-permute-start(f32[128,256]{1,0:T(8,128)S(1)} %add.117), channel_id=1, source_target_pairs={{0,6},{1,7},{2,4},{3,5},{4,2},{5,3},{6,0},{7,1},{8,14},{9,15},{10,... | collective-permute-start | bytes 393224 | tf_op jit(solution)/shard_map/ppermute | solution.py:26
  29.3 3.6 %collective-permute-done.5 = f32[128,256]{1,0:T(8,128)S(1)} collective-permute-done((f32[128,256]{1,0:T(8,128)S(1)}, f32[128,256]{1,0:T(8,128)S(1)}, u32[]{:S(2)}, u32[]{:S(2)}) %collective-permute-start.5) | collective-permute-done | bytes 131104 | tf_op jit(solution)/shard_map/ppermute | solution.py:26
  33.6 4.9 %near_gram.1 = (f32[256,256]{1,0:T(8,128)}, bf16[4,256,384]{2,1,0:T(8,128)(2,1)}, bf16[4,256,384]{2,1,0:T(8,128)(2,1)}, bf16[256,384]{1,0:T(8,128)(2,1)}) custom-call(s32[2]{0:T(128)} %pad_add_fusion.place.refs_0_, bf16[256,8192]{1,0:T(8,128)(2,1)} %bitcast.26, bf16[256,2048]{1,0:T(8,128)(2,1)} %collective-permute-done.6.p1.refs_18_), custom_call_target="tpu_custom_call" | custom-call | flops 268435456 | bytes 2097152 | tf_op jit(solution)/shard_map/near_gram/pallas_call | solution.py:213
  38.5 14.2 %collective-permute-done.1.p3.refs_20_ = bf16[256,2048]{1,0:T(8,128)(2,1)} collective-permute-done((bf16[256,2048]{1,0:T(8,128)(2,1)}, bf16[256,2048]{1,0:T(8,128)(2,1)}, u32[]{:S(2)}, u32[]{:S(2)}) %collective-permute-start.1) | collective-permute-done | bytes 1048608 | tf_op jit(solution)/shard_map/ppermute | solution.py:26
  52.7 3.9 %collective-permute-done.p2.refs_19_ = bf16[256,2048]{1,0:T(8,128)(2,1)} collective-permute-done((bf16[256,2048]{1,0:T(8,128)(2,1)}, bf16[256,2048]{1,0:T(8,128)(2,1)}, u32[]{:S(2)}, u32[]{:S(2)}) %collective-permute-start) | collective-permute-done | bytes 1048608 | tf_op jit(solution)/shard_map/ppermute | solution.py:26
  56.6 3.8 %far_gram.1 = (f32[4,64,256]{2,1,0:T(8,128)}, f32[4,64,256]{2,1,0:T(8,128)}, bf16[4,256,384]{2,1,0:T(8,128)(2,1)}) custom-call(s32[2]{0:T(128)} %pad_add_fusion.place.refs_0_, f32[256,256]{1,0:T(8,128)} %get-tuple-element.51.near, bf16[256,2048]{1,0:T(8,128)(2,1)} %collective-permute-done.p2.refs_19_, ...), custom_call_target="tpu_custom_call", output_to_operand_aliasing={{2}: (4, {})} | custom-call | flops 268435456 | bytes 2097152 | tf_op jit(solution)/shard_map/far_gram/pallas_call | solution.py:255
  67.5 2.2 %collective-permute-done.16 = f32[64,256]{1,0:T(8,128)S(1)} collective-permute-done((f32[64,256]{1,0:T(8,128)S(1)}, f32[64,256]{1,0:T(8,128)S(1)}, u32[]{:S(2)}, u32[]{:S(2)}) %collective-permute-start.16) | collective-permute-done | bytes 65568 | tf_op jit(solution)/shard_map/ppermute | solution.py:26
  72.0 2.6 %collective-permute-start.19 = (f32[64,256]{1,0:T(8,128)S(1)}, f32[64,256]{1,0:T(8,128)S(1)}, u32[]{:S(2)}, u32[]{:S(2)}) collective-permute-start(f32[64,256]{1,0:T(8,128)S(1)} %add_add_fusion.4), channel_id=1, source_target_pairs={{0,4},{1,5},{2,6},{3,7},{4,0},{5,1},{6,2},{7,3},{8,12},{9,13},{10,... | collective-permute-start | bytes 196616 | tf_op jit(solution)/shard_map/ppermute | solution.py:26
  78.6 2.1 collective-permute-done.20
  86.6 3.7 %collective-permute-done.23.refs_12_ = f32[64,256]{1,0:T(8,128)S(1)} collective-permute-done((f32[64,256]{1,0:T(8,128)S(1)}, f32[64,256]{1,0:T(8,128)S(1)}, u32[]{:S(2)}, u32[]{:S(2)}) %collective-permute-start.23) | collective-permute-done | bytes 65568 | tf_op jit(solution)/shard_map/ppermute | solution.py:26
  92.9 10.1 %first.1 = (bf16[512,2048]{1,0:T(8,128)(2,1)}, bf16[512,384]{1,0:T(8,128)(2,1)}, bf16[512,256]{1,0:T(8,128)(2,1)}, bf16[2,256,512]{2,1,0:T(8,128)(2,1)}, f32[4,72,256]{2,1,0:T(8,128)}, /*index=5*/f32[4,72,256]{2,1,0:T(8,128)}) custom-call(s32[2]{0:T(128)} %pad_add_fusion.place.refs_0_, f32[128,256]{1,0:T(8,128)} %add_add_fusion.refs_1_, ...), custom_call_target="tpu_custom_call" | custom-call | flops 4563402752 | bytes 6291456 | tf_op jit(solution)/shard_map/first/pallas_call | solution.py:355
  111.1 2.2 %collective-permute-done.31 = f32[72,256]{1,0:T(8,128)S(1)} collective-permute-done((f32[72,256]{1,0:T(8,128)S(1)}, f32[72,256]{1,0:T(8,128)S(1)}, u32[]{:S(2)}, u32[]{:S(2)}) %collective-permute-start.31) | collective-permute-done | bytes 73760 | tf_op jit(solution)/shard_map/ppermute | solution.py:26
  113.4 3.5 %collective-permute-start.33 = (f32[72,256]{1,0:T(8,128)S(1)}, f32[72,256]{1,0:T(8,128)S(1)}, u32[]{:S(2)}, u32[]{:S(2)}) collective-permute-start(f32[72,256]{1,0:T(8,128)S(1)} %add_add_fusion.2), channel_id=1, source_target_pairs={{0,4},{1,5},{2,6},{3,7},{4,0},{5,1},{6,2},{7,3},{8,12},{9,13},{10,... | collective-permute-start | bytes 221192 | tf_op jit(solution)/shard_map/ppermute | solution.py:26
  121.3 1.8 collective-permute-done.34
  127.9 16.2 %collective-permute-done.35.refs_2_ = f32[72,256]{1,0:T(8,128)S(1)} collective-permute-done((f32[72,256]{1,0:T(8,128)S(1)}, f32[72,256]{1,0:T(8,128)S(1)}, u32[]{:S(2)}, u32[]{:S(2)}) %collective-permute-start.35) | collective-permute-done | bytes 73760 | tf_op jit(solution)/shard_map/ppermute | solution.py:26
  144.1 2.2 %collective-permute-start.37 = (f32[72,256]{1,0:T(8,128)S(1)}, f32[72,256]{1,0:T(8,128)S(1)}, u32[]{:S(2)}, u32[]{:S(2)}) collective-permute-start(f32[72,256]{1,0:T(8,128)S(1)} %add_add_fusion.1.refs_1_), channel_id=1, source_target_pairs={{0,24},{8,16},{16,8},{24,0},{1,25},{9,17},{17,9},{25,1},{2,26},{10... | collective-permute-start | bytes 221192 | tf_op jit(solution)/shard_map/ppermute | solution.py:26
  146.4 5.5 %collective-permute-done.37.refs_4_ = f32[72,256]{1,0:T(8,128)S(1)} collective-permute-done((f32[72,256]{1,0:T(8,128)S(1)}, f32[72,256]{1,0:T(8,128)S(1)}, u32[]{:S(2)}, u32[]{:S(2)}) %collective-permute-start.37) | collective-permute-done | bytes 73760 | tf_op jit(solution)/shard_map/ppermute | solution.py:26
  158.0 6.1 %second.1 = (bf16[256,512]{1,0:T(8,128)(2,1)}, bf16[256,512]{1,0:T(8,128)(2,1)}, bf16[1,256,512]{2,1,0:T(8,128)(2,1)}) custom-call(s32[2]{0:T(128)} %pad_add_fusion.place.refs_0_, f32[72,256]{1,0:T(8,128)} %copy-done.9, f32[72,256]{1,0:T(8,128)} %copy-done.19, f32[72,256]{1,0:T(8,128)} %copy-done.20, f32[72,256]{1,0:T(8,128)} %copy-done.21, ...), custom_call_target="tpu_custom_call" | custom-call | flops 1610612736 | bytes 3145728 | tf_op jit(solution)/shard_map/second/pallas_call | solution.py:413
  167.4 6.4 %collective-permute-done.56.refs_5_ = bf16[512,256]{1,0:T(8,128)(2,1)S(1)} collective-permute-done((bf16[512,256]{1,0:T(8,128)(2,1)}, bf16[512,256]{1,0:T(8,128)(2,1)S(1)}, u32[]{:S(2)}, u32[]{:S(2)}) %collective-permute-start.56) | collective-permute-done | bytes 262176 | tf_op jit(solution)/shard_map/ppermute | solution.py:26
  175.1 4.4 %collective-permute-done.42.refs_0_ = bf16[256,512]{1,0:T(8,128)(2,1)} collective-permute-done((bf16[256,512]{1,0:T(8,128)(2,1)}, bf16[256,512]{1,0:T(8,128)(2,1)}, u32[]{:S(2)}, u32[]{:S(2)}) %collective-permute-start.42) | collective-permute-done | bytes 262176 | tf_op jit(solution)/shard_map/ppermute | solution.py:26
  180.4 15.1 %collective-permute-done.44.refs_1_ = bf16[256,512]{1,0:T(8,128)(2,1)} collective-permute-done((bf16[256,512]{1,0:T(8,128)(2,1)}, bf16[256,512]{1,0:T(8,128)(2,1)}, u32[]{:S(2)}, u32[]{:S(2)}) %collective-permute-start.44) | collective-permute-done | bytes 262176 | tf_op jit(solution)/shard_map/ppermute | solution.py:26
  197.6 5.1 %late.1._ = bf16[256,8192]{1,0:T(8,128)(2,1)} custom-call(s32[2]{0:T(128)} %pad_add_fusion.place.refs_0_, bf16[1,256,512]{2,1,0:T(8,128)(2,1)} %get-tuple-element.79.w.w1, bf16[256,512]{1,0:T(8,128)(2,1)} %get-tuple-element.76.a, bf16[256,512]{1,0:T(8,128)(2,1)} %get-tuple-element.77.b, bf16[512,2048]{1,0:T(8,128)(2,1)} %get-tuple-element.75.refs_9_.m, ...), custom_call_target="tpu_custom_call" | custom-call | flops 1073741824 | bytes 6291456 | tf_op jit(solution)/shard_map/late/pallas_call | solution.py:510
  203.7 5.2 %raw_merge.1.refs_4_ = bf16[256,8192]{1,0:T(8,128)(2,1)} custom-call(s32[2]{0:T(128)} %pad_add_fusion.place.refs_0_, bf16[2,256,512]{2,1,0:T(8,128)(2,1)} %get-tuple-element.78.w0, bf16[1,256,512]{2,1,0:T(8,128)(2,1)} %get-tuple-element.79.w.w1, bf16[256,8192]{1,0:T(8,128)(2,1)} %bitcast.28, ...), custom_call_target="tpu_custom_call", output_to_operand_aliasing={{}: (7, {})} | custom-call | flops 905969664 | bytes 2949120 | tf_op jit(solution)/shard_map/raw_merge/pallas_call | solution.py:462
  208.9 2.6 %put.2.refs_2_ = bf16[256,8192]{1,0:T(8,128)(2,1)} custom-call(s32[2]{0:T(128)} %pad_add_fusion.place.refs_0_, bf16[256,512]{1,0:T(8,128)(2,1)} %collective-permute-done.42.refs_0_, bf16[256,512]{1,0:T(8,128)(2,1)} %collective-permute-done.44.refs_1_, bf16[256,512]{1,0:T(8,128)(2,1)} %collective-permute-done.46.refs_2_, ...), custom_call_target="tpu_custom_call", output_to_operand_aliasing={{}: (5, {})} | custom-call | bytes 2097152 | tf_op jit(solution)/shard_map/put/pallas_call | solution.py:545
  211.5 2.4 %put.3 = bf16[256,8192]{1,0:T(8,128)(2,1)} custom-call(s32[2]{0:T(128)} %pad_add_fusion.place.refs_0_, bf16[256,512]{1,0:T(8,128)(2,1)} %collective-permute-done.43.refs_0_, bf16[256,512]{1,0:T(8,128)(2,1)} %collective-permute-done.45.refs_1_, bf16[256,8192]{1,0:T(8,128)(2,1)} %put.2.refs_2_), custom_call_target="tpu_custom_call", output_to_operand_aliasing={{}: (3, {})} | custom-call | bytes 1048576 | tf_op jit(solution)/shard_map/put/pallas_call | solution.py:545
  (166 shorter events, 59.2 us)
Async XLA Ops:
  2.7 30.9 %collective-permute-start.6 = (bf16[256,2048]{1,0:T(8,128)(2,1)S(1)}, bf16[256,2048]{1,0:T(8,128)(2,1)}, u32[]{:S(2)}, u32[]{:S(2)}) collective-permute-start(bf16[256,2048]{1,0:T(8,128)(2,1)S(1)} %get-tuple-element.49), channel_id=1, source_target_pairs={{0,8},{8,0},{16,24},{24,16},{1,9},{9,1},{17,25},{25,17},{2,10},{10... | collective-permute-start | bytes 3145736 | tf_op jit(solution)/shard_map/ppermute | solution.py:26
  8.0 44.7 %collective-permute-start.1 = (bf16[256,2048]{1,0:T(8,128)(2,1)}, bf16[256,2048]{1,0:T(8,128)(2,1)}, u32[]{:S(2)}, u32[]{:S(2)}) collective-permute-start(bf16[256,2048]{1,0:T(8,128)(2,1)} %constant_dynamic-slice_fusion), channel_id=1, source_target_pairs={{0,24},{8,16},{16,8},{24,0},{1,25},{9,17},{17,9},{25,1},{2,26},{10... | collective-permute-start | bytes 3145736 | tf_op jit(solution)/shard_map/ppermute | solution.py:26
  9.5 47.1 %collective-permute-start = (bf16[256,2048]{1,0:T(8,128)(2,1)}, bf16[256,2048]{1,0:T(8,128)(2,1)}, u32[]{:S(2)}, u32[]{:S(2)}) collective-permute-start(bf16[256,2048]{1,0:T(8,128)(2,1)} %get-tuple-element.45), channel_id=1, source_target_pairs={{0,16},{8,24},{16,0},{24,8},{1,17},{9,25},{17,1},{25,9},{2,18},{10... | collective-permute-start | bytes 3145736 | tf_op jit(solution)/shard_map/ppermute | solution.py:26
  18.0 8.1 %collective-permute-start.3 = (f32[128,256]{1,0:T(8,128)S(1)}, f32[128,256]{1,0:T(8,128)S(1)}, u32[]{:S(2)}, u32[]{:S(2)}) collective-permute-start(f32[128,256]{1,0:T(8,128)S(1)} %add.117), channel_id=1, source_target_pairs={{0,2},{1,3},{2,0},{3,1},{4,6},{5,7},{6,4},{7,5},{8,10},{9,11},{10,... | collective-permute-start | bytes 393224 | tf_op jit(solution)/shard_map/ppermute | solution.py:26
  20.2 9.2 %collective-permute-start.4 = (f32[128,256]{1,0:T(8,128)S(1)}, f32[128,256]{1,0:T(8,128)S(1)}, u32[]{:S(2)}, u32[]{:S(2)}) collective-permute-start(f32[128,256]{1,0:T(8,128)S(1)} %add.117), channel_id=1, source_target_pairs={{0,4},{1,5},{2,6},{3,7},{4,0},{5,1},{6,2},{7,3},{8,12},{9,13},{10,... | collective-permute-start | bytes 393224 | tf_op jit(solution)/shard_map/ppermute | solution.py:26
  26.1 6.8 %collective-permute-start.5 = (f32[128,256]{1,0:T(8,128)S(1)}, f32[128,256]{1,0:T(8,128)S(1)}, u32[]{:S(2)}, u32[]{:S(2)}) collective-permute-start(f32[128,256]{1,0:T(8,128)S(1)} %add.117), channel_id=1, source_target_pairs={{0,6},{1,7},{2,4},{3,5},{4,2},{5,3},{6,0},{7,1},{8,14},{9,15},{10,... | collective-permute-start | bytes 393224 | tf_op jit(solution)/shard_map/ppermute | solution.py:26
  70.4 6.5 %collective-permute-start.18 = (f32[64,256]{1,0:T(8,128)S(1)}, f32[64,256]{1,0:T(8,128)S(1)}, u32[]{:S(2)}, u32[]{:S(2)}) collective-permute-start(f32[64,256]{1,0:T(8,128)S(1)} %add_add_fusion.4), channel_id=1, source_target_pairs={{0,2},{1,3},{2,0},{3,1},{4,6},{5,7},{6,4},{7,5},{8,10},{9,11},{10,... | collective-permute-start | bytes 196616 | tf_op jit(solution)/shard_map/ppermute | solution.py:26
  72.0 6.6 %collective-permute-start.19 = (f32[64,256]{1,0:T(8,128)S(1)}, f32[64,256]{1,0:T(8,128)S(1)}, u32[]{:S(2)}, u32[]{:S(2)}) collective-permute-start(f32[64,256]{1,0:T(8,128)S(1)} %add_add_fusion.4), channel_id=1, source_target_pairs={{0,4},{1,5},{2,6},{3,7},{4,0},{5,1},{6,2},{7,3},{8,12},{9,13},{10,... | collective-permute-start | bytes 196616 | tf_op jit(solution)/shard_map/ppermute | solution.py:26
  75.3 7.6 %collective-permute-start.9 = (f32[128,256]{1,0:T(8,128)}, f32[128,256]{1,0:T(8,128)S(1)}, u32[]{:S(2)}, u32[]{:S(2)}) collective-permute-start(f32[128,256]{1,0:T(8,128)} %add_add_fusion.refs_1_), channel_id=1, source_target_pairs={{0,16},{8,24},{16,0},{24,8},{1,17},{9,25},{17,1},{25,9},{2,18},{10... | collective-permute-start | bytes 393224 | tf_op jit(solution)/shard_map/ppermute | solution.py:26
  82.9 7.9 %collective-permute-start.12 = (f32[128,256]{1,0:T(8,128)S(1)}, f32[128,256]{1,0:T(8,128)S(1)}, u32[]{:S(2)}, u32[]{:S(2)}) collective-permute-start(f32[128,256]{1,0:T(8,128)S(1)} %collective-permute-done.8.refs_2_), channel_id=1, source_target_pairs={{0,1},{1,0},{2,3},{3,2},{4,5},{5,4},{6,7},{7,6},{8,9},{9,8},{10,11... | collective-permute-start | bytes 393224 | tf_op jit(solution)/shard_map/ppermute | solution.py:26
  83.2 7.7 %collective-permute-start.13 = (f32[128,256]{1,0:T(8,128)S(1)}, f32[128,256]{1,0:T(8,128)S(1)}, u32[]{:S(2)}, u32[]{:S(2)}) collective-permute-start(f32[128,256]{1,0:T(8,128)S(1)} %collective-permute-done.9.refs_3_), channel_id=1, source_target_pairs={{0,1},{1,0},{2,3},{3,2},{4,5},{5,4},{6,7},{7,6},{8,9},{9,8},{10,11... | collective-permute-start | bytes 393224 | tf_op jit(solution)/shard_map/ppermute | solution.py:26
  83.4 7.5 %collective-permute-start.14 = (f32[128,256]{1,0:T(8,128)S(1)}, f32[128,256]{1,0:T(8,128)S(1)}, u32[]{:S(2)}, u32[]{:S(2)}) collective-permute-start(f32[128,256]{1,0:T(8,128)S(1)} %collective-permute-done.10.refs_4_), channel_id=1, source_target_pairs={{0,1},{1,0},{2,3},{3,2},{4,5},{5,4},{6,7},{7,6},{8,9},{9,8},{10,11... | collective-permute-start | bytes 393224 | tf_op jit(solution)/shard_map/ppermute | solution.py:26
  113.3 6.6 %collective-permute-start.32 = (f32[72,256]{1,0:T(8,128)S(1)}, f32[72,256]{1,0:T(8,128)S(1)}, u32[]{:S(2)}, u32[]{:S(2)}) collective-permute-start(f32[72,256]{1,0:T(8,128)S(1)} %add_add_fusion.2), channel_id=1, source_target_pairs={{0,2},{1,3},{2,0},{3,1},{4,6},{5,7},{6,4},{7,5},{8,10},{9,11},{10,... | collective-permute-start | bytes 221192 | tf_op jit(solution)/shard_map/ppermute | solution.py:26
  113.4 7.9 %collective-permute-start.33 = (f32[72,256]{1,0:T(8,128)S(1)}, f32[72,256]{1,0:T(8,128)S(1)}, u32[]{:S(2)}, u32[]{:S(2)}) collective-permute-start(f32[72,256]{1,0:T(8,128)S(1)} %add_add_fusion.2), channel_id=1, source_target_pairs={{0,4},{1,5},{2,6},{3,7},{4,0},{5,1},{6,2},{7,3},{8,12},{9,13},{10,... | collective-permute-start | bytes 221192 | tf_op jit(solution)/shard_map/ppermute | solution.py:26
  117.8 8.7 %collective-permute-start.50 = (bf16[256,384]{1,0:T(8,128)(2,1)S(1)}, bf16[256,384]{1,0:T(8,128)(2,1)S(1)}, u32[]{:S(2)}, u32[]{:S(2)}) collective-permute-start(bf16[256,384]{1,0:T(8,128)(2,1)S(1)} %copy-done.11), channel_id=1, source_target_pairs={{0,24},{8,16},{16,8},{24,0},{1,25},{9,17},{17,9},{25,1},{2,26},{10... | collective-permute-start | bytes 589832 | tf_op jit(solution)/shard_map/ppermute | solution.py:26
  119.4 46.3 %collective-permute-start.48 = (bf16[4,256,384]{2,1,0:T(8,128)(2,1)S(1)}, bf16[4,256,384]{2,1,0:T(8,128)(2,1)S(1)}, u32[]{:S(2)}, u32[]{:S(2)}) collective-permute-start(bf16[4,256,384]{2,1,0:T(8,128)(2,1)S(1)} %copy-done.2), channel_id=1, source_target_pairs={{0,8},{8,0},{16,24},{24,16},{1,9},{9,1},{17,25},{25,17},{2,10},{10... | collective-permute-start | bytes 2359304 | tf_op jit(solution)/shard_map/ppermute | solution.py:26
  119.9 32.4 %collective-permute-start.55 = (bf16[512,256]{1,0:T(8,128)(2,1)}, bf16[512,256]{1,0:T(8,128)(2,1)S(1)}, u32[]{:S(2)}, u32[]{:S(2)}) collective-permute-start(bf16[512,256]{1,0:T(8,128)(2,1)} %get-tuple-element.84), channel_id=1, source_target_pairs={{0,16},{8,24},{16,0},{24,8},{1,17},{9,25},{17,1},{25,9},{2,18},{10... | collective-permute-start | bytes 786440 | tf_op jit(solution)/shard_map/ppermute | solution.py:26
  123.1 21.0 %collective-permute-start.35 = (f32[72,256]{1,0:T(8,128)S(1)}, f32[72,256]{1,0:T(8,128)S(1)}, u32[]{:S(2)}, u32[]{:S(2)}) collective-permute-start(f32[72,256]{1,0:T(8,128)S(1)} %add_add_fusion.1.refs_1_), channel_id=1, source_target_pairs={{0,8},{8,0},{16,24},{24,16},{1,9},{9,1},{17,25},{25,17},{2,10},{10... | collective-permute-start | bytes 221192 | tf_op jit(solution)/shard_map/ppermute | solution.py:26
  123.7 22.7 %collective-permute-start.36 = (f32[72,256]{1,0:T(8,128)S(1)}, f32[72,256]{1,0:T(8,128)S(1)}, u32[]{:S(2)}, u32[]{:S(2)}) collective-permute-start(f32[72,256]{1,0:T(8,128)S(1)} %add_add_fusion.1.refs_1_), channel_id=1, source_target_pairs={{0,16},{8,24},{16,0},{24,8},{1,17},{9,25},{17,1},{25,9},{2,18},{10... | collective-permute-start | bytes 221192 | tf_op jit(solution)/shard_map/ppermute | solution.py:26
  126.4 30.6 %collective-permute-start.51 = (bf16[512,384]{1,0:T(8,128)(2,1)}, bf16[512,384]{1,0:T(8,128)(2,1)S(1)}, u32[]{:S(2)}, u32[]{:S(2)}) collective-permute-start(bf16[512,384]{1,0:T(8,128)(2,1)} %get-tuple-element.83), channel_id=1, source_target_pairs={{0,8},{8,0},{16,24},{24,16},{1,9},{9,1},{17,25},{25,17},{2,10},{10... | collective-permute-start | bytes 1179656 | tf_op jit(solution)/shard_map/ppermute | solution.py:26
  144.1 7.7 %collective-permute-start.37 = (f32[72,256]{1,0:T(8,128)S(1)}, f32[72,256]{1,0:T(8,128)S(1)}, u32[]{:S(2)}, u32[]{:S(2)}) collective-permute-start(f32[72,256]{1,0:T(8,128)S(1)} %add_add_fusion.1.refs_1_), channel_id=1, source_target_pairs={{0,24},{8,16},{16,8},{24,0},{1,25},{9,17},{17,9},{25,1},{2,26},{10... | collective-permute-start | bytes 221192 | tf_op jit(solution)/shard_map/ppermute | solution.py:26
  152.4 14.0 %collective-permute-start.52 = (bf16[512,384]{1,0:T(8,128)(2,1)}, bf16[512,384]{1,0:T(8,128)(2,1)S(1)}, u32[]{:S(2)}, u32[]{:S(2)}) collective-permute-start(bf16[512,384]{1,0:T(8,128)(2,1)} %get-tuple-element.83), channel_id=1, source_target_pairs={{0,16},{8,24},{16,0},{24,8},{1,17},{9,25},{17,1},{25,9},{2,18},{10... | collective-permute-start | bytes 1179656 | tf_op jit(solution)/shard_map/ppermute | solution.py:26
  153.3 49.5 %collective-permute-start.49 = (bf16[4,256,384]{2,1,0:T(8,128)(2,1)}, bf16[4,256,384]{2,1,0:T(8,128)(2,1)S(1)}, u32[]{:S(2)}, u32[]{:S(2)}) collective-permute-start(bf16[4,256,384]{2,1,0:T(8,128)(2,1)} %get-tuple-element.81), channel_id=1, source_target_pairs={{0,16},{8,24},{16,0},{24,8},{1,17},{9,25},{17,1},{25,9},{2,18},{10... | collective-permute-start | bytes 2359304 | tf_op jit(solution)/shard_map/ppermute | solution.py:26
  155.7 8.7 %collective-permute-start.54 = (bf16[512,256]{1,0:T(8,128)(2,1)}, bf16[512,256]{1,0:T(8,128)(2,1)}, u32[]{:S(2)}, u32[]{:S(2)}) collective-permute-start(bf16[512,256]{1,0:T(8,128)(2,1)} %get-tuple-element.84), channel_id=1, source_target_pairs={{0,8},{8,0},{16,24},{24,16},{1,9},{9,1},{17,25},{25,17},{2,10},{10... | collective-permute-start | bytes 786440 | tf_op jit(solution)/shard_map/ppermute | solution.py:26
  157.1 39.2 %collective-permute-start.53 = (bf16[512,384]{1,0:T(8,128)(2,1)S(1)}, bf16[512,384]{1,0:T(8,128)(2,1)S(1)}, u32[]{:S(2)}, u32[]{:S(2)}) collective-permute-start(bf16[512,384]{1,0:T(8,128)(2,1)S(1)} %collective-permute-done.51.refs_0_), channel_id=1, source_target_pairs={{0,16},{8,24},{16,0},{24,8},{1,17},{9,25},{17,1},{25,9},{2,18},{10... | collective-permute-start | bytes 1179656 | tf_op jit(solution)/shard_map/ppermute | solution.py:26
  164.4 9.4 %collective-permute-start.56 = (bf16[512,256]{1,0:T(8,128)(2,1)}, bf16[512,256]{1,0:T(8,128)(2,1)S(1)}, u32[]{:S(2)}, u32[]{:S(2)}) collective-permute-start(bf16[512,256]{1,0:T(8,128)(2,1)} %copy-done.6), channel_id=1, source_target_pairs={{0,8},{8,0},{16,24},{24,16},{1,9},{9,1},{17,25},{25,17},{2,10},{10... | collective-permute-start | bytes 786440 | tf_op jit(solution)/shard_map/ppermute | solution.py:26
  165.7 13.8 %collective-permute-start.42 = (bf16[256,512]{1,0:T(8,128)(2,1)}, bf16[256,512]{1,0:T(8,128)(2,1)}, u32[]{:S(2)}, u32[]{:S(2)}) collective-permute-start(bf16[256,512]{1,0:T(8,128)(2,1)} %get-tuple-element.76.a), channel_id=1, source_target_pairs={{0,8},{8,0},{16,24},{24,16},{1,9},{9,1},{17,25},{25,17},{2,10},{10... | collective-permute-start | bytes 786440 | tf_op jit(solution)/shard_map/ppermute | solution.py:26
  166.4 29.2 %collective-permute-start.44 = (bf16[256,512]{1,0:T(8,128)(2,1)}, bf16[256,512]{1,0:T(8,128)(2,1)}, u32[]{:S(2)}, u32[]{:S(2)}) collective-permute-start(bf16[256,512]{1,0:T(8,128)(2,1)} %get-tuple-element.77.b), channel_id=1, source_target_pairs={{0,16},{8,24},{16,0},{24,8},{1,17},{9,25},{17,1},{25,9},{2,18},{10... | collective-permute-start | bytes 786440 | tf_op jit(solution)/shard_map/ppermute | solution.py:26
  173.8 35.1 %collective-permute-start.46 = (bf16[256,512]{1,0:T(8,128)(2,1)}, bf16[256,512]{1,0:T(8,128)(2,1)}, u32[]{:S(2)}, u32[]{:S(2)}) collective-permute-start(bf16[256,512]{1,0:T(8,128)(2,1)} %get-tuple-element.77.b), channel_id=1, source_target_pairs={{0,8},{8,0},{16,24},{24,16},{1,9},{9,1},{17,25},{25,17},{2,10},{10... | collective-permute-start | bytes 786440 | tf_op jit(solution)/shard_map/ppermute | solution.py:26
  179.5 29.4 %collective-permute-start.47 = (bf16[256,512]{1,0:T(8,128)(2,1)}, bf16[256,512]{1,0:T(8,128)(2,1)}, u32[]{:S(2)}, u32[]{:S(2)}) collective-permute-start(bf16[256,512]{1,0:T(8,128)(2,1)} %get-tuple-element.76.a), channel_id=1, source_target_pairs={{0,16},{8,24},{16,0},{24,8},{1,17},{9,25},{17,1},{25,9},{2,18},{10... | collective-permute-start | bytes 786440 | tf_op jit(solution)/shard_map/ppermute | solution.py:26
  195.6 15.9 %collective-permute-start.43 = (bf16[256,512]{1,0:T(8,128)(2,1)}, bf16[256,512]{1,0:T(8,128)(2,1)}, u32[]{:S(2)}, u32[]{:S(2)}) collective-permute-start(bf16[256,512]{1,0:T(8,128)(2,1)} %collective-permute-done.42.refs_0_), channel_id=1, source_target_pairs={{0,16},{8,24},{16,0},{24,8},{1,17},{9,25},{17,1},{25,9},{2,18},{10... | collective-permute-start | bytes 786440 | tf_op jit(solution)/shard_map/ppermute | solution.py:26
  196.3 15.3 %collective-permute-start.45 = (bf16[256,512]{1,0:T(8,128)(2,1)}, bf16[256,512]{1,0:T(8,128)(2,1)}, u32[]{:S(2)}, u32[]{:S(2)}) collective-permute-start(bf16[256,512]{1,0:T(8,128)(2,1)} %collective-permute-done.44.refs_1_), channel_id=1, source_target_pairs={{0,8},{8,0},{16,24},{24,16},{1,9},{9,1},{17,25},{25,17},{2,10},{10... | collective-permute-start | bytes 786440 | tf_op jit(solution)/shard_map/ppermute | solution.py:26
  (57 other events, 491.2 us)

commit v9 on v6

--- a/solution.py
+++ b/solution.py
@@ -59,21 +59,22 @@
     return lax.broadcasted_iota(jnp.int32, (n, n), 0) == lax.broadcasted_iota(jnp.int32, (n, n), 1)
 
 
-def invert(kernels, x_ref, limit):
-    n = kernels[0].shape[0]
-    mask = eye_mask(n)
-    eye = jnp.where(mask, 1.0, 0.0)
+def narrow(k):
+    mask = eye_mask(k.shape[0])
+    diag = jnp.where(mask, k, 0.0)
+    row = 1.0 / jnp.sum(diag, axis=0, keepdims=True)
+    col = 1.0 / jnp.sum(diag, axis=1, keepdims=True)
+    rest = jnp.where(mask, 0.0, k)
+    scaled = rest * row
+    return jnp.where(mask, row, -scaled * col), jnp.sum(scaled * (rest * col))
+
+
+def invert(kernels, x_ref, eye):
     parts = [halves(k) for k in kernels]
+    spread = jnp.float32(0.0)
     for j, k in enumerate(kernels):
-        diag = jnp.where(mask, k, 0.0)
-        row = 1.0 / jnp.sum(diag, axis=0, keepdims=True)
-        col = 1.0 / jnp.sum(diag, axis=1, keepdims=True)
-        scaled = jnp.where(mask, 0.0, k) * row
-        spread = jnp.sum(scaled * (jnp.where(mask, 0.0, k) * col))
-        bound = jnp.minimum(jnp.max(jnp.sum(jnp.abs(k), axis=0, keepdims=True)), limit)
-        near = jnp.where(mask, row, -scaled * col)
-        far = eye * (2.0 / (1.0 + bound))
-        x_ref[j] = jnp.where(spread < 0.9, near, far)
+        x_ref[j], norm = narrow(k)
+        spread = jnp.maximum(spread, norm)
 
     def step():
         worst = jnp.float32(0.0)
@@ -86,7 +87,28 @@
         return worst
 
     step()
-    lax.while_loop(lambda s: (s[0] < 24) & (s[1] > 1e-6), lambda s: (s[0] + 1, step()), (jnp.int32(2), step()))
+    lax.while_loop(lambda s: (s[0] < 24) & (s[1] > 1e-6) & (spread < WIDE), lambda s: (s[0] + 1, step()), (jnp.int32(2), step()))
+    return spread
+
+
+def full(a, b, dims=NN):
+    return lax.dot_general(a, b, dims, precision=lax.Precision.HIGHEST, preferred_element_type=F32)
+
+
+def invert_wide(k, x_ref, eye, limit):
+    bound = jnp.minimum(jnp.max(jnp.sum(jnp.abs(k), axis=0, keepdims=True)), limit)
+    x_ref[...] = eye * (2.0 / (1.0 + bound))
+
+    def step(state):
+        x = x_ref[...]
+        rest = eye - full(k, x)
+        x_ref[...] = x + full(x, rest)
+        return state[0] + 1, jnp.sum(rest * rest)
+
+    lax.while_loop(lambda s: (s[0] < 24) & (s[1] > 1e-6), step, (jnp.int32(0), jnp.float32(1.0)))
+
+
+WIDE = 0.9
 
 
 def resolvent(grams, x_ref, out_ref):
@@ -95,21 +117,30 @@
     eye = jnp.where(mask, 1.0, 0.0)
     scaled = []
     for a, b, d in grams:
-        average = jnp.sum(jnp.where(mask, a + d, 0.0)) / (2 * n)
-        scaled.append((eye + a / average, b / average, eye + d / average))
-    limit = 1.0 + 2 * n
-    invert([d for _, _, d in scaled], x_ref, limit)
+        scale = (2 * n) / jnp.sum(jnp.where(mask, a + d, 0.0))
+        scaled.append((eye + a * scale, b * scale, eye + d * scale))
+    spread = invert([d for _, _, d in scaled], x_ref, eye)
     ties, schurs = [], []
     for j, (a, b, d) in enumerate(scaled):
         bs = halves(b)
         tie = halves(product(bs, halves(x_ref[j])))
         ties.append(tie)
         schurs.append(a - product(tie, bs, NT))
-    invert(schurs, x_ref, limit)
+    spread = jnp.maximum(spread, invert(schurs, x_ref, eye))
     for j, tie in enumerate(ties):
         x = x_ref[j]
         out_ref[j, :, :n] = x.astype(BF16)
         out_ref[j, :, n:] = (-product(halves(x), tie)).astype(BF16)
+
+    @pl.when(jnp.logical_not(spread < WIDE))
+    def _():
+        for j, (a, b, d) in enumerate(scaled):
+            x = x_ref.at[j]
+            invert_wide(d, x, eye, 1.0 + 2 * n)
+            tie = full(b, x[...])
+            invert_wide(a - full(tie, b, NT), x, eye, 1.0 + 2 * n)
+            out_ref[j, :, :n] = x[...].astype(BF16)
+            out_ref[j, :, n:] = (-full(x[...], tie)).astype(BF16)
 
 
 def own_gram_kernel(place, x_ref, keep_ref, give_ref, acc):
@@ -466,11 +497,14 @@
     )(place, w0, w1, x, *messages, out)
 
 
-def late_kernel(share, raw, place, w, a, b, m, *refs):
-    early, (out, mine, own, buffer, load, save) = refs[:-6], refs[-6:]
+def late_kernel(share, raw, place, w_in, a, b, m, *refs):
+    early, (out, w, mine, own, ends, wide, thin, buffer, load, save) = refs[:-10], refs[-10:]
     me, size, half = place[0], mine.shape[1], a.shape[1]
-    copy = pltpu.make_async_copy(m.at[:, :size], mine, load)
-    copy.start()
+    boxes = [box.at[i] for box in (wide, thin) for i in range(len(PEERS))]
+    moves = [(w_in, w), *zip(early, boxes), (m.at[:, :size], mine), (a, ends.at[0]), (b, ends.at[1])]
+    loads = [pltpu.make_async_copy(source, target, load.at[i]) for i, (source, target) in enumerate(moves)]
+    for copy in loads:
+        copy.start()
     saves = []
 
     def put(source, owner, column):
@@ -478,36 +512,44 @@
         saves.append(pltpu.make_async_copy(source, target, save.at[len(saves)]))
         saves[-1].start()
 
-    put(a, me, size)
-    put(b, me, size + half)
-    work = [(pair, s, raw) for pair, s in zip(early, PEERS)]
-    work += [(pair, s, raw + early[0].shape[1]) for pair, s in zip(early[len(PEERS) :], PEERS)]
-    for pair, s, column in work:
-        spot = buffer.at[s - 1, :, column - raw : column - raw + pair.shape[1]]
-        spot[...] = merge_rows(pair[...], w[0])
-        put(spot, me ^ s, column)
-    copy.wait()
+    loads[0].wait()
+    for i, box in enumerate(boxes):
+        loads[1 + i].wait()
+        s, column = PEERS[i % len(PEERS)], 0 if i < len(PEERS) else wide.shape[2]
+        spot = buffer.at[s - 1, :, column : column + box.shape[1]]
+        spot[...] = merge_rows(box[...], w[0])
+        put(spot, me ^ s, raw + column)
+    loads[-3].wait()
     own[...] = merge_rows(mine[...], w[0])
     put(own, me, 0)
+    for i in range(2):
+        loads[i - 2].wait()
+        put(ends.at[i], me, size + i * half)
     for copy in saves:
         copy.wait()
 
 
 def late(place, w, a, b, m, pairs, raw, share):
-    rows, size = a.shape[0], share - 2 * a.shape[1]
+    rows, half = a.shape
+    size = share - 2 * half
+    boxes = [pltpu.VMEM((len(PEERS), *pairs[i].shape), BF16) for i in (0, len(PEERS))]
     return pl.pallas_call(
         functools.partial(late_kernel, share, raw),
         out_shape=shape(rows, GROUP * share, dtype=BF16),
-        in_specs=[SMEM] + [VMEM] * 3 + [HBM] + [VMEM] * len(pairs),
+        in_specs=[SMEM] + [HBM] * (4 + len(pairs)),
         out_specs=HBM,
         scratch_shapes=[
+            pltpu.VMEM(w.shape, BF16),
             pltpu.VMEM((2 * rows, size), BF16),
             pltpu.VMEM((rows, size), BF16),
+            pltpu.VMEM((2, rows, half), BF16),
+            *boxes,
             pltpu.VMEM((GROUP - 1, rows, size - raw), BF16),
-            pltpu.SemaphoreType.DMA,
+            pltpu.SemaphoreType.DMA((len(pairs) + 4,)),
             pltpu.SemaphoreType.DMA((len(pairs) + 3,)),
         ],
         cost_estimate=cost(4 * rows * rows * size * GROUP, 6 * rows * size * GROUP),
+        compiler_params=WHOLE,
         name="late",
     )(place, w, a, b, m, *pairs)
 

time: 215 us -> 214 us (level)
  transfers between devices with their start and end apart: 57 -> 57, of which waited for: 30 -> 31; matrix products, arithmetic and copies ran while one was open for 2% -> 2% of each run, Pallas kernels for 14% -> 14%
where the time goes in v9:
time: 214 us; the launch traced here: 213 us
  waiting for transfers between devices  98.5 us (46%)
  starting transfers between devices  58.3 us (27%)
  Pallas kernels  45.6 us (21%)
  local copies, waits for them, and re-layouts  5.91 us (3%)
  other arithmetic  4.34 us (2%)
    ppermute x57, waiting for transfers between devices, send(): return lax.ppermute(block, axis, [(i, i ^ shift) for i in range(count)])  98.5 us
    ppermute x57, starting transfers between devices, send(): return lax.ppermute(block, axis, [(i, i ^ shift) for i in range(count)])  58.3 us
    pallas_call x1, Pallas kernels, first(): pl.pallas_call(functools.partial(first_kernel, raw, tile), out_shape=tupl...  10 us
    pallas_call x1, Pallas kernels, second(): pl.pallas_call(second_kernel, out_shape=(shape(rows, half, dtype=BF16),)...  6.09 us
    pallas_call x1, Pallas kernels, own_gram(): pl.pallas_call(own_gram_kernel, out_shape=(half, half), grid_spec=pltpu.P...  5.39 us
    pallas_call x1, Pallas kernels, raw_merge(): pl.pallas_call(functools.partial(raw_merge_kernel, share), out_shape=shap...  5.16 us
    pallas_call x1, Pallas kernels, late(): pl.pallas_call(functools.partial(late_kernel, share, raw), out_shape=shap...  5.13 us
    pallas_call x2, Pallas kernels, put(): pl.pallas_call(functools.partial(put_kernel, spots, share), out_shape=sha...  5.08 us
  transfers between devices with their start and end apart: 57, of which 31 were waited for; matrix products, arithmetic and copies ran while one was open for 2% of the time, Pallas kernels for 14%

profile of v9, /device:TPU:0, one launch (start us, length us, event | category | flops | bytes accessed | tf_op | source)
XLA Modules:
  0.0 213.2 jit_solution(1637985875597855363)
XLA Ops:
  0.0 2.7 %dynamic-slice_bitcast_fusion = (bf16[256,2048]{1,0:T(8,128)(2,1)}, bf16[256,2048]{1,0:T(8,128)(2,1)S(1)}) fusion(bf16[1,256,8192]{2,1,0:T(8,128)(2,1)} %param.1, s32[]{:T(128)S(6)} %select_n.23, s32[]{:T(128)S(6)} %select_n.22), kind=kLoop, calls=%fused_computation | loop fusion | bytes 4194312 | tf_op jit(solution)/shard_map/dynamic_slice | solution.py:609
  2.7 3.0 %collective-permute-start.6 = (bf16[256,2048]{1,0:T(8,128)(2,1)S(1)}, bf16[256,2048]{1,0:T(8,128)(2,1)}, u32[]{:S(2)}, u32[]{:S(2)}) collective-permute-start(bf16[256,2048]{1,0:T(8,128)(2,1)S(1)} %get-tuple-element.49), channel_id=1, source_target_pairs={{0,8},{8,0},{16,24},{24,16},{1,9},{9,1},{17,25},{25,17},{2,10},{10... | collective-permute-start | bytes 3145736 | tf_op jit(solution)/shard_map/ppermute | solution.py:26
  5.7 2.3 %constant_dynamic-slice_fusion = bf16[256,2048]{1,0:T(8,128)(2,1)} fusion(bf16[256,8192]{1,0:T(8,128)(2,1)} %bitcast.24, s32[]{:T(128)S(6)} %select_n.24), kind=kLoop, calls=%fused_computation.23 | loop fusion | bytes 2097156 | tf_op jit(solution)/shard_map/dynamic_slice | solution.py:609
  10.2 5.4 %own_gram.1 = (f32[128,256]{1,0:T(8,128)}, f32[128,256]{1,0:T(8,128)}) custom-call(s32[2]{0:T(128)} %pad_add_fusion.place.refs_0_, bf16[256,8192]{1,0:T(8,128)(2,1)} %bitcast.25), custom_call_target="tpu_custom_call" | custom-call | flops 1073741824 | bytes 4194304 | tf_op jit(solution)/shard_map/own_gram/pallas_call | solution.py:167
  18.0 2.1 collective-permute-start.3
  20.2 2.6 %collective-permute-start.4 = (f32[128,256]{1,0:T(8,128)S(1)}, f32[128,256]{1,0:T(8,128)S(1)}, u32[]{:S(2)}, u32[]{:S(2)}) collective-permute-start(f32[128,256]{1,0:T(8,128)S(1)} %add.117), channel_id=1, source_target_pairs={{0,4},{1,5},{2,6},{3,7},{4,0},{5,1},{6,2},{7,3},{8,12},{9,13},{10,... | collective-permute-start | bytes 393224 | tf_op jit(solution)/shard_map/ppermute | solution.py:26
  22.7 3.4 %collective-permute-done.3 = f32[128,256]{1,0:T(8,128)S(1)} collective-permute-done((f32[128,256]{1,0:T(8,128)S(1)}, f32[128,256]{1,0:T(8,128)S(1)}, u32[]{:S(2)}, u32[]{:S(2)}) %collective-permute-start.3) | collective-permute-done | bytes 131104 | tf_op jit(solution)/shard_map/ppermute | solution.py:26
  26.1 3.2 %collective-permute-start.5 = (f32[128,256]{1,0:T(8,128)S(1)}, f32[128,256]{1,0:T(8,128)S(1)}, u32[]{:S(2)}, u32[]{:S(2)}) collective-permute-start(f32[128,256]{1,0:T(8,128)S(1)} %add.117), channel_id=1, source_target_pairs={{0,6},{1,7},{2,4},{3,5},{4,2},{5,3},{6,0},{7,1},{8,14},{9,15},{10,... | collective-permute-start | bytes 393224 | tf_op jit(solution)/shard_map/ppermute | solution.py:26
  29.3 3.6 %collective-permute-done.5 = f32[128,256]{1,0:T(8,128)S(1)} collective-permute-done((f32[128,256]{1,0:T(8,128)S(1)}, f32[128,256]{1,0:T(8,128)S(1)}, u32[]{:S(2)}, u32[]{:S(2)}) %collective-permute-start.5) | collective-permute-done | bytes 131104 | tf_op jit(solution)/shard_map/ppermute | solution.py:26
  33.6 4.9 %near_gram.1 = (f32[256,256]{1,0:T(8,128)}, bf16[4,256,384]{2,1,0:T(8,128)(2,1)}, bf16[4,256,384]{2,1,0:T(8,128)(2,1)}, bf16[256,384]{1,0:T(8,128)(2,1)}) custom-call(s32[2]{0:T(128)} %pad_add_fusion.place.refs_0_, bf16[256,8192]{1,0:T(8,128)(2,1)} %bitcast.26, bf16[256,2048]{1,0:T(8,128)(2,1)} %collective-permute-done.6.p1.refs_18_), custom_call_target="tpu_custom_call" | custom-call | flops 268435456 | bytes 2097152 | tf_op jit(solution)/shard_map/near_gram/pallas_call | solution.py:232
  38.5 14.2 %collective-permute-done.1.p3.refs_20_ = bf16[256,2048]{1,0:T(8,128)(2,1)} collective-permute-done((bf16[256,2048]{1,0:T(8,128)(2,1)}, bf16[256,2048]{1,0:T(8,128)(2,1)}, u32[]{:S(2)}, u32[]{:S(2)}) %collective-permute-start.1) | collective-permute-done | bytes 1048608 | tf_op jit(solution)/shard_map/ppermute | solution.py:26
  52.7 3.9 %collective-permute-done.p2.refs_19_ = bf16[256,2048]{1,0:T(8,128)(2,1)} collective-permute-done((bf16[256,2048]{1,0:T(8,128)(2,1)}, bf16[256,2048]{1,0:T(8,128)(2,1)}, u32[]{:S(2)}, u32[]{:S(2)}) %collective-permute-start) | collective-permute-done | bytes 1048608 | tf_op jit(solution)/shard_map/ppermute | solution.py:26
  56.6 3.8 %far_gram.1 = (f32[4,64,256]{2,1,0:T(8,128)}, f32[4,64,256]{2,1,0:T(8,128)}, bf16[4,256,384]{2,1,0:T(8,128)(2,1)}) custom-call(s32[2]{0:T(128)} %pad_add_fusion.place.refs_0_, f32[256,256]{1,0:T(8,128)} %get-tuple-element.51.near, bf16[256,2048]{1,0:T(8,128)(2,1)} %collective-permute-done.p2.refs_19_, ...), custom_call_target="tpu_custom_call", output_to_operand_aliasing={{2}: (4, {})} | custom-call | flops 268435456 | bytes 2097152 | tf_op jit(solution)/shard_map/far_gram/pallas_call | solution.py:274
  67.5 2.2 %collective-permute-done.16 = f32[64,256]{1,0:T(8,128)S(1)} collective-permute-done((f32[64,256]{1,0:T(8,128)S(1)}, f32[64,256]{1,0:T(8,128)S(1)}, u32[]{:S(2)}, u32[]{:S(2)}) %collective-permute-start.16) | collective-permute-done | bytes 65568 | tf_op jit(solution)/shard_map/ppermute | solution.py:26
  72.0 2.6 %collective-permute-start.19 = (f32[64,256]{1,0:T(8,128)S(1)}, f32[64,256]{1,0:T(8,128)S(1)}, u32[]{:S(2)}, u32[]{:S(2)}) collective-permute-start(f32[64,256]{1,0:T(8,128)S(1)} %add_add_fusion.4), channel_id=1, source_target_pairs={{0,4},{1,5},{2,6},{3,7},{4,0},{5,1},{6,2},{7,3},{8,12},{9,13},{10,... | collective-permute-start | bytes 196616 | tf_op jit(solution)/shard_map/ppermute | solution.py:26
  78.6 2.1 collective-permute-done.20
  86.6 3.7 %collective-permute-done.23.refs_12_ = f32[64,256]{1,0:T(8,128)S(1)} collective-permute-done((f32[64,256]{1,0:T(8,128)S(1)}, f32[64,256]{1,0:T(8,128)S(1)}, u32[]{:S(2)}, u32[]{:S(2)}) %collective-permute-start.23) | collective-permute-done | bytes 65568 | tf_op jit(solution)/shard_map/ppermute | solution.py:26
  92.9 10.0 %first.1 = (bf16[512,2048]{1,0:T(8,128)(2,1)}, bf16[512,384]{1,0:T(8,128)(2,1)}, bf16[512,256]{1,0:T(8,128)(2,1)}, bf16[2,256,512]{2,1,0:T(8,128)(2,1)}, f32[4,72,256]{2,1,0:T(8,128)}, /*index=5*/f32[4,72,256]{2,1,0:T(8,128)}) custom-call(s32[2]{0:T(128)} %pad_add_fusion.place.refs_0_, f32[128,256]{1,0:T(8,128)} %add_add_fusion.refs_1_, ...), custom_call_target="tpu_custom_call" | custom-call | flops 4563402752 | bytes 6291456 | tf_op jit(solution)/shard_map/first/pallas_call | solution.py:374
  111.0 2.2 %collective-permute-done.31 = f32[72,256]{1,0:T(8,128)S(1)} collective-permute-done((f32[72,256]{1,0:T(8,128)S(1)}, f32[72,256]{1,0:T(8,128)S(1)}, u32[]{:S(2)}, u32[]{:S(2)}) %collective-permute-start.31) | collective-permute-done | bytes 73760 | tf_op jit(solution)/shard_map/ppermute | solution.py:26
  113.4 3.5 %collective-permute-start.33 = (f32[72,256]{1,0:T(8,128)S(1)}, f32[72,256]{1,0:T(8,128)S(1)}, u32[]{:S(2)}, u32[]{:S(2)}) collective-permute-start(f32[72,256]{1,0:T(8,128)S(1)} %add_add_fusion.2), channel_id=1, source_target_pairs={{0,4},{1,5},{2,6},{3,7},{4,0},{5,1},{6,2},{7,3},{8,12},{9,13},{10,... | collective-permute-start | bytes 221192 | tf_op jit(solution)/shard_map/ppermute | solution.py:26
  121.2 1.8 collective-permute-done.34
  127.9 16.2 %collective-permute-done.35.refs_2_ = f32[72,256]{1,0:T(8,128)S(1)} collective-permute-done((f32[72,256]{1,0:T(8,128)S(1)}, f32[72,256]{1,0:T(8,128)S(1)}, u32[]{:S(2)}, u32[]{:S(2)}) %collective-permute-start.35) | collective-permute-done | bytes 73760 | tf_op jit(solution)/shard_map/ppermute | solution.py:26
  144.1 2.2 %collective-permute-start.37 = (f32[72,256]{1,0:T(8,128)S(1)}, f32[72,256]{1,0:T(8,128)S(1)}, u32[]{:S(2)}, u32[]{:S(2)}) collective-permute-start(f32[72,256]{1,0:T(8,128)S(1)} %add_add_fusion.1.refs_1_), channel_id=1, source_target_pairs={{0,24},{8,16},{16,8},{24,0},{1,25},{9,17},{17,9},{25,1},{2,26},{10... | collective-permute-start | bytes 221192 | tf_op jit(solution)/shard_map/ppermute | solution.py:26
  146.3 5.5 %collective-permute-done.37.refs_4_ = f32[72,256]{1,0:T(8,128)S(1)} collective-permute-done((f32[72,256]{1,0:T(8,128)S(1)}, f32[72,256]{1,0:T(8,128)S(1)}, u32[]{:S(2)}, u32[]{:S(2)}) %collective-permute-start.37) | collective-permute-done | bytes 73760 | tf_op jit(solution)/shard_map/ppermute | solution.py:26
  157.9 6.1 %second.1 = (bf16[256,512]{1,0:T(8,128)(2,1)}, bf16[256,512]{1,0:T(8,128)(2,1)}, bf16[1,256,512]{2,1,0:T(8,128)(2,1)}) custom-call(s32[2]{0:T(128)} %pad_add_fusion.place.refs_0_, f32[72,256]{1,0:T(8,128)} %copy-done.8, f32[72,256]{1,0:T(8,128)} %copy-done.18, f32[72,256]{1,0:T(8,128)} %copy-done.19, f32[72,256]{1,0:T(8,128)} %copy-done.20, ...), custom_call_target="tpu_custom_call" | custom-call | flops 1610612736 | bytes 3145728 | tf_op jit(solution)/shard_map/second/pallas_call | solution.py:432
  167.4 6.0 %collective-permute-done.56.refs_5_ = bf16[512,256]{1,0:T(8,128)(2,1)S(1)} collective-permute-done((bf16[512,256]{1,0:T(8,128)(2,1)S(1)}, bf16[512,256]{1,0:T(8,128)(2,1)S(1)}, u32[]{:S(2)}, u32[]{:S(2)}) %collective-permute-start.56) | collective-permute-done | bytes 262176 | tf_op jit(solution)/shard_map/ppermute | solution.py:26
  174.8 4.4 %collective-permute-done.42.refs_0_ = bf16[256,512]{1,0:T(8,128)(2,1)} collective-permute-done((bf16[256,512]{1,0:T(8,128)(2,1)}, bf16[256,512]{1,0:T(8,128)(2,1)}, u32[]{:S(2)}, u32[]{:S(2)}) %collective-permute-start.42) | collective-permute-done | bytes 262176 | tf_op jit(solution)/shard_map/ppermute | solution.py:26
  180.2 15.3 %collective-permute-done.44.refs_1_ = bf16[256,512]{1,0:T(8,128)(2,1)} collective-permute-done((bf16[256,512]{1,0:T(8,128)(2,1)}, bf16[256,512]{1,0:T(8,128)(2,1)}, u32[]{:S(2)}, u32[]{:S(2)}) %collective-permute-start.44) | collective-permute-done | bytes 262176 | tf_op jit(solution)/shard_map/ppermute | solution.py:26
  197.6 5.1 %late.1._ = bf16[256,8192]{1,0:T(8,128)(2,1)} custom-call(s32[2]{0:T(128)} %pad_add_fusion.place.refs_0_, bf16[1,256,512]{2,1,0:T(8,128)(2,1)} %get-tuple-element.79.w_in.w1, bf16[256,512]{1,0:T(8,128)(2,1)} %get-tuple-element.76.a, bf16[256,512]{1,0:T(8,128)(2,1)} %get-tuple-element.77.b, bf16[512,2048]{1,0:T(8,128)(2,1)} %get-tuple-element.75.refs_9_.m, ...), custom_call_target="tpu_custom_call" | custom-call | flops 1073741824 | bytes 6291456 | tf_op jit(solution)/shard_map/late/pallas_call | solution.py:536
  202.7 5.2 %raw_merge.1.refs_4_ = bf16[256,8192]{1,0:T(8,128)(2,1)} custom-call(s32[2]{0:T(128)} %pad_add_fusion.place.refs_0_, bf16[2,256,512]{2,1,0:T(8,128)(2,1)} %get-tuple-element.78.w0, bf16[1,256,512]{2,1,0:T(8,128)(2,1)} %get-tuple-element.79.w_in.w1, bf16[256,8192]{1,0:T(8,128)(2,1)} %bitcast.28, ...), custom_call_target="tpu_custom_call", output_to_operand_aliasing={{}: (7, {})} | custom-call | flops 905969664 | bytes 2949120 | tf_op jit(solution)/shard_map/raw_merge/pallas_call | solution.py:481
  207.9 2.6 %put.2.refs_2_ = bf16[256,8192]{1,0:T(8,128)(2,1)} custom-call(s32[2]{0:T(128)} %pad_add_fusion.place.refs_0_, bf16[256,512]{1,0:T(8,128)(2,1)} %collective-permute-done.42.refs_0_, bf16[256,512]{1,0:T(8,128)(2,1)} %collective-permute-done.44.refs_1_, bf16[256,512]{1,0:T(8,128)(2,1)} %collective-permute-done.46.refs_2_, ...), custom_call_target="tpu_custom_call", output_to_operand_aliasing={{}: (5, {})} | custom-call | bytes 2097152 | tf_op jit(solution)/shard_map/put/pallas_call | solution.py:575
  210.6 2.4 %put.3 = bf16[256,8192]{1,0:T(8,128)(2,1)} custom-call(s32[2]{0:T(128)} %pad_add_fusion.place.refs_0_, bf16[256,512]{1,0:T(8,128)(2,1)} %collective-permute-done.43.refs_0_, bf16[256,512]{1,0:T(8,128)(2,1)} %collective-permute-done.45.refs_1_, bf16[256,8192]{1,0:T(8,128)(2,1)} %put.2.refs_2_), custom_call_target="tpu_custom_call", output_to_operand_aliasing={{}: (3, {})} | custom-call | bytes 1048576 | tf_op jit(solution)/shard_map/put/pallas_call | solution.py:575
  (166 shorter events, 58.5 us)
Async XLA Ops:
  2.7 30.9 %collective-permute-start.6 = (bf16[256,2048]{1,0:T(8,128)(2,1)S(1)}, bf16[256,2048]{1,0:T(8,128)(2,1)}, u32[]{:S(2)}, u32[]{:S(2)}) collective-permute-start(bf16[256,2048]{1,0:T(8,128)(2,1)S(1)} %get-tuple-element.49), channel_id=1, source_target_pairs={{0,8},{8,0},{16,24},{24,16},{1,9},{9,1},{17,25},{25,17},{2,10},{10... | collective-permute-start | bytes 3145736 | tf_op jit(solution)/shard_map/ppermute | solution.py:26
  8.0 44.7 %collective-permute-start.1 = (bf16[256,2048]{1,0:T(8,128)(2,1)}, bf16[256,2048]{1,0:T(8,128)(2,1)}, u32[]{:S(2)}, u32[]{:S(2)}) collective-permute-start(bf16[256,2048]{1,0:T(8,128)(2,1)} %constant_dynamic-slice_fusion), channel_id=1, source_target_pairs={{0,24},{8,16},{16,8},{24,0},{1,25},{9,17},{17,9},{25,1},{2,26},{10... | collective-permute-start | bytes 3145736 | tf_op jit(solution)/shard_map/ppermute | solution.py:26
  9.5 47.1 %collective-permute-start = (bf16[256,2048]{1,0:T(8,128)(2,1)}, bf16[256,2048]{1,0:T(8,128)(2,1)}, u32[]{:S(2)}, u32[]{:S(2)}) collective-permute-start(bf16[256,2048]{1,0:T(8,128)(2,1)} %get-tuple-element.45), channel_id=1, source_target_pairs={{0,16},{8,24},{16,0},{24,8},{1,17},{9,25},{17,1},{25,9},{2,18},{10... | collective-permute-start | bytes 3145736 | tf_op jit(solution)/shard_map/ppermute | solution.py:26
  18.0 8.1 %collective-permute-start.3 = (f32[128,256]{1,0:T(8,128)S(1)}, f32[128,256]{1,0:T(8,128)S(1)}, u32[]{:S(2)}, u32[]{:S(2)}) collective-permute-start(f32[128,256]{1,0:T(8,128)S(1)} %add.117), channel_id=1, source_target_pairs={{0,2},{1,3},{2,0},{3,1},{4,6},{5,7},{6,4},{7,5},{8,10},{9,11},{10,... | collective-permute-start | bytes 393224 | tf_op jit(solution)/shard_map/ppermute | solution.py:26
  20.2 9.2 %collective-permute-start.4 = (f32[128,256]{1,0:T(8,128)S(1)}, f32[128,256]{1,0:T(8,128)S(1)}, u32[]{:S(2)}, u32[]{:S(2)}) collective-permute-start(f32[128,256]{1,0:T(8,128)S(1)} %add.117), channel_id=1, source_target_pairs={{0,4},{1,5},{2,6},{3,7},{4,0},{5,1},{6,2},{7,3},{8,12},{9,13},{10,... | collective-permute-start | bytes 393224 | tf_op jit(solution)/shard_map/ppermute | solution.py:26
  26.1 6.8 %collective-permute-start.5 = (f32[128,256]{1,0:T(8,128)S(1)}, f32[128,256]{1,0:T(8,128)S(1)}, u32[]{:S(2)}, u32[]{:S(2)}) collective-permute-start(f32[128,256]{1,0:T(8,128)S(1)} %add.117), channel_id=1, source_target_pairs={{0,6},{1,7},{2,4},{3,5},{4,2},{5,3},{6,0},{7,1},{8,14},{9,15},{10,... | collective-permute-start | bytes 393224 | tf_op jit(solution)/shard_map/ppermute | solution.py:26
  70.4 6.5 %collective-permute-start.18 = (f32[64,256]{1,0:T(8,128)S(1)}, f32[64,256]{1,0:T(8,128)S(1)}, u32[]{:S(2)}, u32[]{:S(2)}) collective-permute-start(f32[64,256]{1,0:T(8,128)S(1)} %add_add_fusion.4), channel_id=1, source_target_pairs={{0,2},{1,3},{2,0},{3,1},{4,6},{5,7},{6,4},{7,5},{8,10},{9,11},{10,... | collective-permute-start | bytes 196616 | tf_op jit(solution)/shard_map/ppermute | solution.py:26
  72.0 6.6 %collective-permute-start.19 = (f32[64,256]{1,0:T(8,128)S(1)}, f32[64,256]{1,0:T(8,128)S(1)}, u32[]{:S(2)}, u32[]{:S(2)}) collective-permute-start(f32[64,256]{1,0:T(8,128)S(1)} %add_add_fusion.4), channel_id=1, source_target_pairs={{0,4},{1,5},{2,6},{3,7},{4,0},{5,1},{6,2},{7,3},{8,12},{9,13},{10,... | collective-permute-start | bytes 196616 | tf_op jit(solution)/shard_map/ppermute | solution.py:26
  75.3 7.6 %collective-permute-start.9 = (f32[128,256]{1,0:T(8,128)}, f32[128,256]{1,0:T(8,128)S(1)}, u32[]{:S(2)}, u32[]{:S(2)}) collective-permute-start(f32[128,256]{1,0:T(8,128)} %add_add_fusion.refs_1_), channel_id=1, source_target_pairs={{0,16},{8,24},{16,0},{24,8},{1,17},{9,25},{17,1},{25,9},{2,18},{10... | collective-permute-start | bytes 393224 | tf_op jit(solution)/shard_map/ppermute | solution.py:26
  82.9 7.9 %collective-permute-start.12 = (f32[128,256]{1,0:T(8,128)S(1)}, f32[128,256]{1,0:T(8,128)S(1)}, u32[]{:S(2)}, u32[]{:S(2)}) collective-permute-start(f32[128,256]{1,0:T(8,128)S(1)} %collective-permute-done.8.refs_2_), channel_id=1, source_target_pairs={{0,1},{1,0},{2,3},{3,2},{4,5},{5,4},{6,7},{7,6},{8,9},{9,8},{10,11... | collective-permute-start | bytes 393224 | tf_op jit(solution)/shard_map/ppermute | solution.py:26
  83.2 7.7 %collective-permute-start.13 = (f32[128,256]{1,0:T(8,128)S(1)}, f32[128,256]{1,0:T(8,128)S(1)}, u32[]{:S(2)}, u32[]{:S(2)}) collective-permute-start(f32[128,256]{1,0:T(8,128)S(1)} %collective-permute-done.9.refs_3_), channel_id=1, source_target_pairs={{0,1},{1,0},{2,3},{3,2},{4,5},{5,4},{6,7},{7,6},{8,9},{9,8},{10,11... | collective-permute-start | bytes 393224 | tf_op jit(solution)/shard_map/ppermute | solution.py:26
  83.4 7.5 %collective-permute-start.14 = (f32[128,256]{1,0:T(8,128)S(1)}, f32[128,256]{1,0:T(8,128)S(1)}, u32[]{:S(2)}, u32[]{:S(2)}) collective-permute-start(f32[128,256]{1,0:T(8,128)S(1)} %collective-permute-done.10.refs_4_), channel_id=1, source_target_pairs={{0,1},{1,0},{2,3},{3,2},{4,5},{5,4},{6,7},{7,6},{8,9},{9,8},{10,11... | collective-permute-start | bytes 393224 | tf_op jit(solution)/shard_map/ppermute | solution.py:26
  113.3 6.6 %collective-permute-start.32 = (f32[72,256]{1,0:T(8,128)S(1)}, f32[72,256]{1,0:T(8,128)S(1)}, u32[]{:S(2)}, u32[]{:S(2)}) collective-permute-start(f32[72,256]{1,0:T(8,128)S(1)} %add_add_fusion.2), channel_id=1, source_target_pairs={{0,2},{1,3},{2,0},{3,1},{4,6},{5,7},{6,4},{7,5},{8,10},{9,11},{10,... | collective-permute-start | bytes 221192 | tf_op jit(solution)/shard_map/ppermute | solution.py:26
  113.4 7.9 %collective-permute-start.33 = (f32[72,256]{1,0:T(8,128)S(1)}, f32[72,256]{1,0:T(8,128)S(1)}, u32[]{:S(2)}, u32[]{:S(2)}) collective-permute-start(f32[72,256]{1,0:T(8,128)S(1)} %add_add_fusion.2), channel_id=1, source_target_pairs={{0,4},{1,5},{2,6},{3,7},{4,0},{5,1},{6,2},{7,3},{8,12},{9,13},{10,... | collective-permute-start | bytes 221192 | tf_op jit(solution)/shard_map/ppermute | solution.py:26
  117.7 8.7 %collective-permute-start.50 = (bf16[256,384]{1,0:T(8,128)(2,1)S(1)}, bf16[256,384]{1,0:T(8,128)(2,1)S(1)}, u32[]{:S(2)}, u32[]{:S(2)}) collective-permute-start(bf16[256,384]{1,0:T(8,128)(2,1)S(1)} %copy-done.10), channel_id=1, source_target_pairs={{0,24},{8,16},{16,8},{24,0},{1,25},{9,17},{17,9},{25,1},{2,26},{10... | collective-permute-start | bytes 589832 | tf_op jit(solution)/shard_map/ppermute | solution.py:26
  119.3 46.2 %collective-permute-start.48 = (bf16[4,256,384]{2,1,0:T(8,128)(2,1)S(1)}, bf16[4,256,384]{2,1,0:T(8,128)(2,1)}, u32[]{:S(2)}, u32[]{:S(2)}) collective-permute-start(bf16[4,256,384]{2,1,0:T(8,128)(2,1)S(1)} %copy-done), channel_id=1, source_target_pairs={{0,8},{8,0},{16,24},{24,16},{1,9},{9,1},{17,25},{25,17},{2,10},{10... | collective-permute-start | bytes 2359304 | tf_op jit(solution)/shard_map/ppermute | solution.py:26
  119.9 32.4 %collective-permute-start.55 = (bf16[512,256]{1,0:T(8,128)(2,1)}, bf16[512,256]{1,0:T(8,128)(2,1)S(1)}, u32[]{:S(2)}, u32[]{:S(2)}) collective-permute-start(bf16[512,256]{1,0:T(8,128)(2,1)} %get-tuple-element.84), channel_id=1, source_target_pairs={{0,16},{8,24},{16,0},{24,8},{1,17},{9,25},{17,1},{25,9},{2,18},{10... | collective-permute-start | bytes 786440 | tf_op jit(solution)/shard_map/ppermute | solution.py:26
  123.0 21.0 %collective-permute-start.35 = (f32[72,256]{1,0:T(8,128)S(1)}, f32[72,256]{1,0:T(8,128)S(1)}, u32[]{:S(2)}, u32[]{:S(2)}) collective-permute-start(f32[72,256]{1,0:T(8,128)S(1)} %add_add_fusion.1.refs_1_), channel_id=1, source_target_pairs={{0,8},{8,0},{16,24},{24,16},{1,9},{9,1},{17,25},{25,17},{2,10},{10... | collective-permute-start | bytes 221192 | tf_op jit(solution)/shard_map/ppermute | solution.py:26
  123.6 22.7 %collective-permute-start.36 = (f32[72,256]{1,0:T(8,128)S(1)}, f32[72,256]{1,0:T(8,128)S(1)}, u32[]{:S(2)}, u32[]{:S(2)}) collective-permute-start(f32[72,256]{1,0:T(8,128)S(1)} %add_add_fusion.1.refs_1_), channel_id=1, source_target_pairs={{0,16},{8,24},{16,0},{24,8},{1,17},{9,25},{17,1},{25,9},{2,18},{10... | collective-permute-start | bytes 221192 | tf_op jit(solution)/shard_map/ppermute | solution.py:26
  126.4 30.6 %collective-permute-start.51 = (bf16[512,384]{1,0:T(8,128)(2,1)}, bf16[512,384]{1,0:T(8,128)(2,1)S(1)}, u32[]{:S(2)}, u32[]{:S(2)}) collective-permute-start(bf16[512,384]{1,0:T(8,128)(2,1)} %get-tuple-element.83), channel_id=1, source_target_pairs={{0,8},{8,0},{16,24},{24,16},{1,9},{9,1},{17,25},{25,17},{2,10},{10... | collective-permute-start | bytes 1179656 | tf_op jit(solution)/shard_map/ppermute | solution.py:26
  144.1 7.7 %collective-permute-start.37 = (f32[72,256]{1,0:T(8,128)S(1)}, f32[72,256]{1,0:T(8,128)S(1)}, u32[]{:S(2)}, u32[]{:S(2)}) collective-permute-start(f32[72,256]{1,0:T(8,128)S(1)} %add_add_fusion.1.refs_1_), channel_id=1, source_target_pairs={{0,24},{8,16},{16,8},{24,0},{1,25},{9,17},{17,9},{25,1},{2,26},{10... | collective-permute-start | bytes 221192 | tf_op jit(solution)/shard_map/ppermute | solution.py:26
  152.3 13.9 %collective-permute-start.52 = (bf16[512,384]{1,0:T(8,128)(2,1)}, bf16[512,384]{1,0:T(8,128)(2,1)S(1)}, u32[]{:S(2)}, u32[]{:S(2)}) collective-permute-start(bf16[512,384]{1,0:T(8,128)(2,1)} %get-tuple-element.83), channel_id=1, source_target_pairs={{0,16},{8,24},{16,0},{24,8},{1,17},{9,25},{17,1},{25,9},{2,18},{10... | collective-permute-start | bytes 1179656 | tf_op jit(solution)/shard_map/ppermute | solution.py:26
  153.1 49.6 %collective-permute-start.49 = (bf16[4,256,384]{2,1,0:T(8,128)(2,1)}, bf16[4,256,384]{2,1,0:T(8,128)(2,1)}, u32[]{:S(2)}, u32[]{:S(2)}) collective-permute-start(bf16[4,256,384]{2,1,0:T(8,128)(2,1)} %get-tuple-element.81), channel_id=1, source_target_pairs={{0,16},{8,24},{16,0},{24,8},{1,17},{9,25},{17,1},{25,9},{2,18},{10... | collective-permute-start | bytes 2359304 | tf_op jit(solution)/shard_map/ppermute | solution.py:26
  155.6 8.6 %collective-permute-start.54 = (bf16[512,256]{1,0:T(8,128)(2,1)}, bf16[512,256]{1,0:T(8,128)(2,1)S(1)}, u32[]{:S(2)}, u32[]{:S(2)}) collective-permute-start(bf16[512,256]{1,0:T(8,128)(2,1)} %get-tuple-element.84), channel_id=1, source_target_pairs={{0,8},{8,0},{16,24},{24,16},{1,9},{9,1},{17,25},{25,17},{2,10},{10... | collective-permute-start | bytes 786440 | tf_op jit(solution)/shard_map/ppermute | solution.py:26
  157.0 39.2 %collective-permute-start.53 = (bf16[512,384]{1,0:T(8,128)(2,1)S(1)}, bf16[512,384]{1,0:T(8,128)(2,1)S(1)}, u32[]{:S(2)}, u32[]{:S(2)}) collective-permute-start(bf16[512,384]{1,0:T(8,128)(2,1)S(1)} %collective-permute-done.51.refs_0_), channel_id=1, source_target_pairs={{0,16},{8,24},{16,0},{24,8},{1,17},{9,25},{17,1},{25,9},{2,18},{10... | collective-permute-start | bytes 1179656 | tf_op jit(solution)/shard_map/ppermute | solution.py:26
  164.2 9.2 %collective-permute-start.56 = (bf16[512,256]{1,0:T(8,128)(2,1)S(1)}, bf16[512,256]{1,0:T(8,128)(2,1)S(1)}, u32[]{:S(2)}, u32[]{:S(2)}) collective-permute-start(bf16[512,256]{1,0:T(8,128)(2,1)S(1)} %collective-permute-done.55.refs_4_), channel_id=1, source_target_pairs={{0,8},{8,0},{16,24},{24,16},{1,9},{9,1},{17,25},{25,17},{2,10},{10... | collective-permute-start | bytes 786440 | tf_op jit(solution)/shard_map/ppermute | solution.py:26
  165.6 13.5 %collective-permute-start.42 = (bf16[256,512]{1,0:T(8,128)(2,1)}, bf16[256,512]{1,0:T(8,128)(2,1)}, u32[]{:S(2)}, u32[]{:S(2)}) collective-permute-start(bf16[256,512]{1,0:T(8,128)(2,1)} %get-tuple-element.76.a), channel_id=1, source_target_pairs={{0,8},{8,0},{16,24},{24,16},{1,9},{9,1},{17,25},{25,17},{2,10},{10... | collective-permute-start | bytes 786440 | tf_op jit(solution)/shard_map/ppermute | solution.py:26
  166.3 29.3 %collective-permute-start.44 = (bf16[256,512]{1,0:T(8,128)(2,1)}, bf16[256,512]{1,0:T(8,128)(2,1)}, u32[]{:S(2)}, u32[]{:S(2)}) collective-permute-start(bf16[256,512]{1,0:T(8,128)(2,1)} %get-tuple-element.77.b), channel_id=1, source_target_pairs={{0,16},{8,24},{16,0},{24,8},{1,17},{9,25},{17,1},{25,9},{2,18},{10... | collective-permute-start | bytes 786440 | tf_op jit(solution)/shard_map/ppermute | solution.py:26
  173.4 34.5 %collective-permute-start.46 = (bf16[256,512]{1,0:T(8,128)(2,1)}, bf16[256,512]{1,0:T(8,128)(2,1)}, u32[]{:S(2)}, u32[]{:S(2)}) collective-permute-start(bf16[256,512]{1,0:T(8,128)(2,1)} %get-tuple-element.77.b), channel_id=1, source_target_pairs={{0,8},{8,0},{16,24},{24,16},{1,9},{9,1},{17,25},{25,17},{2,10},{10... | collective-permute-start | bytes 786440 | tf_op jit(solution)/shard_map/ppermute | solution.py:26
  179.1 28.8 %collective-permute-start.47 = (bf16[256,512]{1,0:T(8,128)(2,1)}, bf16[256,512]{1,0:T(8,128)(2,1)}, u32[]{:S(2)}, u32[]{:S(2)}) collective-permute-start(bf16[256,512]{1,0:T(8,128)(2,1)} %get-tuple-element.76.a), channel_id=1, source_target_pairs={{0,16},{8,24},{16,0},{24,8},{1,17},{9,25},{17,1},{25,9},{2,18},{10... | collective-permute-start | bytes 786440 | tf_op jit(solution)/shard_map/ppermute | solution.py:26
  195.5 15.0 %collective-permute-start.43 = (bf16[256,512]{1,0:T(8,128)(2,1)}, bf16[256,512]{1,0:T(8,128)(2,1)}, u32[]{:S(2)}, u32[]{:S(2)}) collective-permute-start(bf16[256,512]{1,0:T(8,128)(2,1)} %collective-permute-done.42.refs_0_), channel_id=1, source_target_pairs={{0,16},{8,24},{16,0},{24,8},{1,17},{9,25},{17,1},{25,9},{2,18},{10... | collective-permute-start | bytes 786440 | tf_op jit(solution)/shard_map/ppermute | solution.py:26
  196.2 14.4 %collective-permute-start.45 = (bf16[256,512]{1,0:T(8,128)(2,1)}, bf16[256,512]{1,0:T(8,128)(2,1)}, u32[]{:S(2)}, u32[]{:S(2)}) collective-permute-start(bf16[256,512]{1,0:T(8,128)(2,1)} %collective-permute-done.44.refs_1_), channel_id=1, source_target_pairs={{0,8},{8,0},{16,24},{24,16},{1,9},{9,1},{17,25},{25,17},{2,10},{10... | collective-permute-start | bytes 786440 | tf_op jit(solution)/shard_map/ppermute | solution.py:26
  (57 other events, 498.3 us)

commit v10 on v9

--- a/solution.py
+++ b/solution.py
@@ -497,14 +497,11 @@
     )(place, w0, w1, x, *messages, out)
 
 
-def late_kernel(share, raw, place, w_in, a, b, m, *refs):
-    early, (out, w, mine, own, ends, wide, thin, buffer, load, save) = refs[:-10], refs[-10:]
+def late_kernel(share, raw, place, w, a, b, m, *refs):
+    early, (out, mine, own, buffer, load, save) = refs[:-6], refs[-6:]
     me, size, half = place[0], mine.shape[1], a.shape[1]
-    boxes = [box.at[i] for box in (wide, thin) for i in range(len(PEERS))]
-    moves = [(w_in, w), *zip(early, boxes), (m.at[:, :size], mine), (a, ends.at[0]), (b, ends.at[1])]
-    loads = [pltpu.make_async_copy(source, target, load.at[i]) for i, (source, target) in enumerate(moves)]
-    for copy in loads:
-        copy.start()
+    copy = pltpu.make_async_copy(m.at[:, :size], mine, load)
+    copy.start()
     saves = []
 
     def put(source, owner, column):
@@ -512,44 +509,36 @@
         saves.append(pltpu.make_async_copy(source, target, save.at[len(saves)]))
         saves[-1].start()
 
-    loads[0].wait()
-    for i, box in enumerate(boxes):
-        loads[1 + i].wait()
-        s, column = PEERS[i % len(PEERS)], 0 if i < len(PEERS) else wide.shape[2]
-        spot = buffer.at[s - 1, :, column : column + box.shape[1]]
-        spot[...] = merge_rows(box[...], w[0])
-        put(spot, me ^ s, raw + column)
-    loads[-3].wait()
+    put(a, me, size)
+    put(b, me, size + half)
+    work = [(pair, s, raw) for pair, s in zip(early, PEERS)]
+    work += [(pair, s, raw + early[0].shape[1]) for pair, s in zip(early[len(PEERS) :], PEERS)]
+    for pair, s, column in work:
+        spot = buffer.at[s - 1, :, column - raw : column - raw + pair.shape[1]]
+        spot[...] = merge_rows(pair[...], w[0])
+        put(spot, me ^ s, column)
+    copy.wait()
     own[...] = merge_rows(mine[...], w[0])
     put(own, me, 0)
-    for i in range(2):
-        loads[i - 2].wait()
-        put(ends.at[i], me, size + i * half)
     for copy in saves:
         copy.wait()
 
 
 def late(place, w, a, b, m, pairs, raw, share):
-    rows, half = a.shape
-    size = share - 2 * half
-    boxes = [pltpu.VMEM((len(PEERS), *pairs[i].shape), BF16) for i in (0, len(PEERS))]
+    rows, size = a.shape[0], share - 2 * a.shape[1]
     return pl.pallas_call(
         functools.partial(late_kernel, share, raw),
         out_shape=shape(rows, GROUP * share, dtype=BF16),
-        in_specs=[SMEM] + [HBM] * (4 + len(pairs)),
+        in_specs=[SMEM] + [VMEM] * 3 + [HBM] + [VMEM] * len(pairs),
         out_specs=HBM,
         scratch_shapes=[
-            pltpu.VMEM(w.shape, BF16),
             pltpu.VMEM((2 * rows, size), BF16),
             pltpu.VMEM((rows, size), BF16),
-            pltpu.VMEM((2, rows, half), BF16),
-            *boxes,
             pltpu.VMEM((GROUP - 1, rows, size - raw), BF16),
-            pltpu.SemaphoreType.DMA((len(pairs) + 4,)),
+            pltpu.SemaphoreType.DMA,
             pltpu.SemaphoreType.DMA((len(pairs) + 3,)),
         ],
         cost_estimate=cost(4 * rows * rows * size * GROUP, 6 * rows * size * GROUP),
-        compiler_params=WHOLE,
         name="late",
     )(place, w, a, b, m, *pairs)
 
@@ -599,7 +588,7 @@
     x = sketches[0]
     rows, columns = x.shape
     share = columns // GROUP
-    raw, ahead = 3 * share // 16, (3 * share // 16, share // 8)
+    raw, ahead = share // 4, (share // 8, share // 8)
     early = raw + sum(ahead)
     me = lax.axis_index("dp") % GROUP
     place = jnp.stack([me, lax.axis_index("feat") % CORES]).astype(jnp.int32)

time: 214 us -> 208 us (0.972)
  waiting for transfers between devices: 98.5 us -> 91.4 us
    ppermute x57, waiting for transfers between devices: 98.5 us -> 91.4 us  [send(): return lax.ppermute(block, axis, [(i, i ^ shift) for i in range(count)])]
where the time goes in v10:
time: 208 us; the launch traced here: 207 us
  waiting for transfers between devices  91.4 us (44%)
  starting transfers between devices  58.9 us (28%)
  Pallas kernels  45.2 us (22%)
  local copies, waits for them, and re-layouts  6.8 us (3%)
  other arithmetic  4.34 us (2%)
    ppermute x57, waiting for transfers between devices, send(): return lax.ppermute(block, axis, [(i, i ^ shift) for i in range(count)])  91.4 us
    ppermute x57, starting transfers between devices, send(): return lax.ppermute(block, axis, [(i, i ^ shift) for i in range(count)])  58.9 us
    pallas_call x1, Pallas kernels, first(): pl.pallas_call(functools.partial(first_kernel, raw, tile), out_shape=tupl...  9.98 us
    pallas_call x1, Pallas kernels, second(): pl.pallas_call(second_kernel, out_shape=(shape(rows, half, dtype=BF16),)...  6.07 us
    pallas_call x1, Pallas kernels, own_gram(): pl.pallas_call(own_gram_kernel, out_shape=(half, half), grid_spec=pltpu.P...  5.38 us
    pallas_call x1, Pallas kernels, near_gram(): pl.pallas_call(functools.partial(near_gram_kernel, chunk), out_shape=(sha...  5.13 us
    pallas_call x2, Pallas kernels, put(): pl.pallas_call(functools.partial(put_kernel, spots, share), out_shape=sha...  5.08 us
    pallas_call x1, Pallas kernels, raw_merge(): pl.pallas_call(functools.partial(raw_merge_kernel, share), out_shape=shap...  5.08 us
  transfers between devices with their start and end apart: 57, of which 31 were waited for; matrix products, arithmetic and copies ran while one was open for 2% of the time, Pallas kernels for 14%

profile of v10, /device:TPU:0, one launch (start us, length us, event | category | flops | bytes accessed | tf_op | source)
XLA Modules:
  0.0 207.2 jit_solution(12141863405015022800)
XLA Ops:
  0.0 2.7 %dynamic-slice_bitcast_fusion = (bf16[256,2048]{1,0:T(8,128)(2,1)}, bf16[256,2048]{1,0:T(8,128)(2,1)S(1)}) fusion(bf16[1,256,8192]{2,1,0:T(8,128)(2,1)} %param.1, s32[]{:T(128)S(6)} %select_n.23, s32[]{:T(128)S(6)} %select_n.22), kind=kLoop, calls=%fused_computation | loop fusion | bytes 4194312 | tf_op jit(solution)/shard_map/dynamic_slice | solution.py:598
  2.7 3.0 %collective-permute-start.6 = (bf16[256,2048]{1,0:T(8,128)(2,1)S(1)}, bf16[256,2048]{1,0:T(8,128)(2,1)}, u32[]{:S(2)}, u32[]{:S(2)}) collective-permute-start(bf16[256,2048]{1,0:T(8,128)(2,1)S(1)} %get-tuple-element.49), channel_id=1, source_target_pairs={{0,8},{8,0},{16,24},{24,16},{1,9},{9,1},{17,25},{25,17},{2,10},{10... | collective-permute-start | bytes 3145736 | tf_op jit(solution)/shard_map/ppermute | solution.py:26
  5.7 2.3 %constant_dynamic-slice_fusion = bf16[256,2048]{1,0:T(8,128)(2,1)} fusion(bf16[256,8192]{1,0:T(8,128)(2,1)} %bitcast.24, s32[]{:T(128)S(6)} %select_n.24), kind=kLoop, calls=%fused_computation.23 | loop fusion | bytes 2097156 | tf_op jit(solution)/shard_map/dynamic_slice | solution.py:598
  10.1 5.4 %own_gram.1 = (f32[128,256]{1,0:T(8,128)}, f32[128,256]{1,0:T(8,128)}) custom-call(s32[2]{0:T(128)} %pad_add_fusion.place.refs_0_, bf16[256,8192]{1,0:T(8,128)(2,1)} %bitcast.25), custom_call_target="tpu_custom_call" | custom-call | flops 1073741824 | bytes 4194304 | tf_op jit(solution)/shard_map/own_gram/pallas_call | solution.py:167
  18.0 2.1 %collective-permute-start.3 = (f32[128,256]{1,0:T(8,128)S(1)}, f32[128,256]{1,0:T(8,128)S(1)}, u32[]{:S(2)}, u32[]{:S(2)}) collective-permute-start(f32[128,256]{1,0:T(8,128)S(1)} %add.117), channel_id=1, source_target_pairs={{0,2},{1,3},{2,0},{3,1},{4,6},{5,7},{6,4},{7,5},{8,10},{9,11},{10,... | collective-permute-start | bytes 393224 | tf_op jit(solution)/shard_map/ppermute | solution.py:26
  20.1 2.6 %collective-permute-start.4 = (f32[128,256]{1,0:T(8,128)S(1)}, f32[128,256]{1,0:T(8,128)S(1)}, u32[]{:S(2)}, u32[]{:S(2)}) collective-permute-start(f32[128,256]{1,0:T(8,128)S(1)} %add.117), channel_id=1, source_target_pairs={{0,4},{1,5},{2,6},{3,7},{4,0},{5,1},{6,2},{7,3},{8,12},{9,13},{10,... | collective-permute-start | bytes 393224 | tf_op jit(solution)/shard_map/ppermute | solution.py:26
  22.7 3.4 %collective-permute-done.3 = f32[128,256]{1,0:T(8,128)S(1)} collective-permute-done((f32[128,256]{1,0:T(8,128)S(1)}, f32[128,256]{1,0:T(8,128)S(1)}, u32[]{:S(2)}, u32[]{:S(2)}) %collective-permute-start.3) | collective-permute-done | bytes 131104 | tf_op jit(solution)/shard_map/ppermute | solution.py:26
  26.1 3.2 %collective-permute-start.5 = (f32[128,256]{1,0:T(8,128)S(1)}, f32[128,256]{1,0:T(8,128)S(1)}, u32[]{:S(2)}, u32[]{:S(2)}) collective-permute-start(f32[128,256]{1,0:T(8,128)S(1)} %add.117), channel_id=1, source_target_pairs={{0,6},{1,7},{2,4},{3,5},{4,2},{5,3},{6,0},{7,1},{8,14},{9,15},{10,... | collective-permute-start | bytes 393224 | tf_op jit(solution)/shard_map/ppermute | solution.py:26
  29.3 3.6 %collective-permute-done.5 = f32[128,256]{1,0:T(8,128)S(1)} collective-permute-done((f32[128,256]{1,0:T(8,128)S(1)}, f32[128,256]{1,0:T(8,128)S(1)}, u32[]{:S(2)}, u32[]{:S(2)}) %collective-permute-start.5) | collective-permute-done | bytes 131104 | tf_op jit(solution)/shard_map/ppermute | solution.py:26
  33.6 5.1 %near_gram.1 = (f32[256,256]{1,0:T(8,128)}, bf16[4,256,512]{2,1,0:T(8,128)(2,1)}, bf16[4,256,512]{2,1,0:T(8,128)(2,1)}, bf16[256,512]{1,0:T(8,128)(2,1)}) custom-call(s32[2]{0:T(128)} %pad_add_fusion.place.refs_0_, bf16[256,8192]{1,0:T(8,128)(2,1)} %bitcast.26, bf16[256,2048]{1,0:T(8,128)(2,1)} %collective-permute-done.6.p1.refs_18_), custom_call_target="tpu_custom_call" | custom-call | flops 268435456 | bytes 2097152 | tf_op jit(solution)/shard_map/near_gram/pallas_call | solution.py:232
  38.7 14.0 %collective-permute-done.1.p3.refs_20_ = bf16[256,2048]{1,0:T(8,128)(2,1)} collective-permute-done((bf16[256,2048]{1,0:T(8,128)(2,1)}, bf16[256,2048]{1,0:T(8,128)(2,1)}, u32[]{:S(2)}, u32[]{:S(2)}) %collective-permute-start.1) | collective-permute-done | bytes 1048608 | tf_op jit(solution)/shard_map/ppermute | solution.py:26
  52.7 3.9 %collective-permute-done.p2.refs_19_ = bf16[256,2048]{1,0:T(8,128)(2,1)} collective-permute-done((bf16[256,2048]{1,0:T(8,128)(2,1)}, bf16[256,2048]{1,0:T(8,128)(2,1)}, u32[]{:S(2)}, u32[]{:S(2)}) %collective-permute-start) | collective-permute-done | bytes 1048608 | tf_op jit(solution)/shard_map/ppermute | solution.py:26
  56.6 3.8 %far_gram.1 = (f32[4,64,256]{2,1,0:T(8,128)}, f32[4,64,256]{2,1,0:T(8,128)}, bf16[4,256,512]{2,1,0:T(8,128)(2,1)}) custom-call(s32[2]{0:T(128)} %pad_add_fusion.place.refs_0_, f32[256,256]{1,0:T(8,128)} %get-tuple-element.51.near, bf16[256,2048]{1,0:T(8,128)(2,1)} %collective-permute-done.p2.refs_19_, ...), custom_call_target="tpu_custom_call", output_to_operand_aliasing={{2}: (4, {})} | custom-call | flops 268435456 | bytes 2097152 | tf_op jit(solution)/shard_map/far_gram/pallas_call | solution.py:274
  67.5 2.2 %collective-permute-done.16 = f32[64,256]{1,0:T(8,128)S(1)} collective-permute-done((f32[64,256]{1,0:T(8,128)S(1)}, f32[64,256]{1,0:T(8,128)S(1)}, u32[]{:S(2)}, u32[]{:S(2)}) %collective-permute-start.16) | collective-permute-done | bytes 65568 | tf_op jit(solution)/shard_map/ppermute | solution.py:26
  72.0 2.6 %collective-permute-start.19 = (f32[64,256]{1,0:T(8,128)S(1)}, f32[64,256]{1,0:T(8,128)S(1)}, u32[]{:S(2)}, u32[]{:S(2)}) collective-permute-start(f32[64,256]{1,0:T(8,128)S(1)} %add_add_fusion.4), channel_id=1, source_target_pairs={{0,4},{1,5},{2,6},{3,7},{4,0},{5,1},{6,2},{7,3},{8,12},{9,13},{10,... | collective-permute-start | bytes 196616 | tf_op jit(solution)/shard_map/ppermute | solution.py:26
  86.5 3.7 %collective-permute-done.23.refs_12_ = f32[64,256]{1,0:T(8,128)S(1)} collective-permute-done((f32[64,256]{1,0:T(8,128)S(1)}, f32[64,256]{1,0:T(8,128)S(1)}, u32[]{:S(2)}, u32[]{:S(2)}) %collective-permute-start.23) | collective-permute-done | bytes 65568 | tf_op jit(solution)/shard_map/ppermute | solution.py:26
  92.9 10.0 %first.1 = (bf16[512,2048]{1,0:T(8,128)(2,1)}, bf16[512,256]{1,0:T(8,128)(2,1)}, bf16[512,256]{1,0:T(8,128)(2,1)}, bf16[2,256,512]{2,1,0:T(8,128)(2,1)}, f32[4,72,256]{2,1,0:T(8,128)}, /*index=5*/f32[4,72,256]{2,1,0:T(8,128)}) custom-call(s32[2]{0:T(128)} %pad_add_fusion.place.refs_0_, f32[128,256]{1,0:T(8,128)} %add_add_fusion.refs_1_, ...), custom_call_target="tpu_custom_call" | custom-call | flops 4563402752 | bytes 6291456 | tf_op jit(solution)/shard_map/first/pallas_call | solution.py:374
  110.9 2.2 %collective-permute-done.31 = f32[72,256]{1,0:T(8,128)S(1)} collective-permute-done((f32[72,256]{1,0:T(8,128)S(1)}, f32[72,256]{1,0:T(8,128)S(1)}, u32[]{:S(2)}, u32[]{:S(2)}) %collective-permute-start.31) | collective-permute-done | bytes 73760 | tf_op jit(solution)/shard_map/ppermute | solution.py:26
  113.2 3.5 %collective-permute-start.33 = (f32[72,256]{1,0:T(8,128)S(1)}, f32[72,256]{1,0:T(8,128)S(1)}, u32[]{:S(2)}, u32[]{:S(2)}) collective-permute-start(f32[72,256]{1,0:T(8,128)S(1)} %add_add_fusion.2), channel_id=1, source_target_pairs={{0,4},{1,5},{2,6},{3,7},{4,0},{5,1},{6,2},{7,3},{8,12},{9,13},{10,... | collective-permute-start | bytes 221192 | tf_op jit(solution)/shard_map/ppermute | solution.py:26
  125.0 3.0 %collective-permute-done.50.d = bf16[256,512]{1,0:T(8,128)(2,1)} collective-permute-done((bf16[256,512]{1,0:T(8,128)(2,1)}, bf16[256,512]{1,0:T(8,128)(2,1)}, u32[]{:S(2)}, u32[]{:S(2)}) %collective-permute-start.50) | collective-permute-done | bytes 262176 | tf_op jit(solution)/shard_map/ppermute | solution.py:26
  128.7 22.2 %collective-permute-done.35.refs_2_ = f32[72,256]{1,0:T(8,128)S(1)} collective-permute-done((f32[72,256]{1,0:T(8,128)S(1)}, f32[72,256]{1,0:T(8,128)S(1)}, u32[]{:S(2)}, u32[]{:S(2)}) %collective-permute-start.35) | collective-permute-done | bytes 73760 | tf_op jit(solution)/shard_map/ppermute | solution.py:26
  152.3 3.0 %collective-permute-done.36.refs_3_ = f32[72,256]{1,0:T(8,128)S(1)} collective-permute-done((f32[72,256]{1,0:T(8,128)S(1)}, f32[72,256]{1,0:T(8,128)S(1)}, u32[]{:S(2)}, u32[]{:S(2)}) %collective-permute-start.36) | collective-permute-done | bytes 73760 | tf_op jit(solution)/shard_map/ppermute | solution.py:26
  155.3 2.2 %collective-permute-start.37 = (f32[72,256]{1,0:T(8,128)S(1)}, f32[72,256]{1,0:T(8,128)S(1)}, u32[]{:S(2)}, u32[]{:S(2)}) collective-permute-start(f32[72,256]{1,0:T(8,128)S(1)} %add_add_fusion.1.refs_1_), channel_id=1, source_target_pairs={{0,24},{8,16},{16,8},{24,0},{1,25},{9,17},{17,9},{25,1},{2,26},{10... | collective-permute-start | bytes 221192 | tf_op jit(solution)/shard_map/ppermute | solution.py:26
  157.5 3.1 %collective-permute-done.37.refs_4_ = f32[72,256]{1,0:T(8,128)S(1)} collective-permute-done((f32[72,256]{1,0:T(8,128)S(1)}, f32[72,256]{1,0:T(8,128)S(1)}, u32[]{:S(2)}, u32[]{:S(2)}) %collective-permute-start.37) | collective-permute-done | bytes 73760 | tf_op jit(solution)/shard_map/ppermute | solution.py:26
  166.5 6.1 %second.1 = (bf16[256,512]{1,0:T(8,128)(2,1)}, bf16[256,512]{1,0:T(8,128)(2,1)}, bf16[1,256,512]{2,1,0:T(8,128)(2,1)}) custom-call(s32[2]{0:T(128)} %pad_add_fusion.place.refs_0_, f32[72,256]{1,0:T(8,128)} %copy-done.6, f32[72,256]{1,0:T(8,128)} %copy-done.15, f32[72,256]{1,0:T(8,128)} %copy-done.16, f32[72,256]{1,0:T(8,128)} %copy-done.17, ...), custom_call_target="tpu_custom_call" | custom-call | flops 1610612736 | bytes 3145728 | tf_op jit(solution)/shard_map/second/pallas_call | solution.py:432
  174.7 2.7 %collective-permute-done.53.refs_2_ = bf16[512,256]{1,0:T(8,128)(2,1)} collective-permute-done((bf16[512,256]{1,0:T(8,128)(2,1)S(1)}, bf16[512,256]{1,0:T(8,128)(2,1)}, u32[]{:S(2)}, u32[]{:S(2)}) %collective-permute-start.53) | collective-permute-done | bytes 262176 | tf_op jit(solution)/shard_map/ppermute | solution.py:26
  178.8 3.3 %collective-permute-done.56.refs_5_ = bf16[512,256]{1,0:T(8,128)(2,1)S(1)} collective-permute-done((bf16[512,256]{1,0:T(8,128)(2,1)}, bf16[512,256]{1,0:T(8,128)(2,1)S(1)}, u32[]{:S(2)}, u32[]{:S(2)}) %collective-permute-start.56) | collective-permute-done | bytes 262176 | tf_op jit(solution)/shard_map/ppermute | solution.py:26
  183.3 4.5 %collective-permute-done.42.refs_0_ = bf16[256,512]{1,0:T(8,128)(2,1)} collective-permute-done((bf16[256,512]{1,0:T(8,128)(2,1)}, bf16[256,512]{1,0:T(8,128)(2,1)}, u32[]{:S(2)}, u32[]{:S(2)}) %collective-permute-start.42) | collective-permute-done | bytes 262176 | tf_op jit(solution)/shard_map/ppermute | solution.py:26
  191.1 4.7 %late.1._ = bf16[256,8192]{1,0:T(8,128)(2,1)} custom-call(s32[2]{0:T(128)} %pad_add_fusion.place.refs_0_, bf16[1,256,512]{2,1,0:T(8,128)(2,1)} %get-tuple-element.79.w.w1, bf16[256,512]{1,0:T(8,128)(2,1)} %get-tuple-element.76.a, bf16[256,512]{1,0:T(8,128)(2,1)} %get-tuple-element.77.b, bf16[512,2048]{1,0:T(8,128)(2,1)} %get-tuple-element.75.refs_9_.m, ...), custom_call_target="tpu_custom_call" | custom-call | flops 1073741824 | bytes 6291456 | tf_op jit(solution)/shard_map/late/pallas_call | solution.py:529
  196.8 5.1 %raw_merge.1.refs_4_ = bf16[256,8192]{1,0:T(8,128)(2,1)} custom-call(s32[2]{0:T(128)} %pad_add_fusion.place.refs_0_, bf16[2,256,512]{2,1,0:T(8,128)(2,1)} %get-tuple-element.78.w0, bf16[1,256,512]{2,1,0:T(8,128)(2,1)} %get-tuple-element.79.w.w1, bf16[256,8192]{1,0:T(8,128)(2,1)} %bitcast.28, ...), custom_call_target="tpu_custom_call", output_to_operand_aliasing={{}: (7, {})} | custom-call | flops 1207959552 | bytes 3932160 | tf_op jit(solution)/shard_map/raw_merge/pallas_call | solution.py:481
  201.9 2.6 %put.2.refs_2_ = bf16[256,8192]{1,0:T(8,128)(2,1)} custom-call(s32[2]{0:T(128)} %pad_add_fusion.place.refs_0_, bf16[256,512]{1,0:T(8,128)(2,1)} %collective-permute-done.42.refs_0_, bf16[256,512]{1,0:T(8,128)(2,1)} %collective-permute-done.44.refs_1_, bf16[256,512]{1,0:T(8,128)(2,1)} %collective-permute-done.46.refs_2_, ...), custom_call_target="tpu_custom_call", output_to_operand_aliasing={{}: (5, {})} | custom-call | bytes 2097152 | tf_op jit(solution)/shard_map/put/pallas_call | solution.py:564
  204.6 2.4 %put.3 = bf16[256,8192]{1,0:T(8,128)(2,1)} custom-call(s32[2]{0:T(128)} %pad_add_fusion.place.refs_0_, bf16[256,512]{1,0:T(8,128)(2,1)} %collective-permute-done.43.refs_0_, bf16[256,512]{1,0:T(8,128)(2,1)} %collective-permute-done.45.refs_1_, bf16[256,8192]{1,0:T(8,128)(2,1)} %put.2.refs_2_), custom_call_target="tpu_custom_call", output_to_operand_aliasing={{}: (3, {})} | custom-call | bytes 1048576 | tf_op jit(solution)/shard_map/put/pallas_call | solution.py:564
  (160 shorter events, 62.6 us)
Async XLA Ops:
  2.7 30.8 %collective-permute-start.6 = (bf16[256,2048]{1,0:T(8,128)(2,1)S(1)}, bf16[256,2048]{1,0:T(8,128)(2,1)}, u32[]{:S(2)}, u32[]{:S(2)}) collective-permute-start(bf16[256,2048]{1,0:T(8,128)(2,1)S(1)} %get-tuple-element.49), channel_id=1, source_target_pairs={{0,8},{8,0},{16,24},{24,16},{1,9},{9,1},{17,25},{25,17},{2,10},{10... | collective-permute-start | bytes 3145736 | tf_op jit(solution)/shard_map/ppermute | solution.py:26
  8.0 44.8 %collective-permute-start.1 = (bf16[256,2048]{1,0:T(8,128)(2,1)}, bf16[256,2048]{1,0:T(8,128)(2,1)}, u32[]{:S(2)}, u32[]{:S(2)}) collective-permute-start(bf16[256,2048]{1,0:T(8,128)(2,1)} %constant_dynamic-slice_fusion), channel_id=1, source_target_pairs={{0,24},{8,16},{16,8},{24,0},{1,25},{9,17},{17,9},{25,1},{2,26},{10... | collective-permute-start | bytes 3145736 | tf_op jit(solution)/shard_map/ppermute | solution.py:26
  9.5 47.1 %collective-permute-start = (bf16[256,2048]{1,0:T(8,128)(2,1)}, bf16[256,2048]{1,0:T(8,128)(2,1)}, u32[]{:S(2)}, u32[]{:S(2)}) collective-permute-start(bf16[256,2048]{1,0:T(8,128)(2,1)} %get-tuple-element.45), channel_id=1, source_target_pairs={{0,16},{8,24},{16,0},{24,8},{1,17},{9,25},{17,1},{25,9},{2,18},{10... | collective-permute-start | bytes 3145736 | tf_op jit(solution)/shard_map/ppermute | solution.py:26
  18.0 8.1 %collective-permute-start.3 = (f32[128,256]{1,0:T(8,128)S(1)}, f32[128,256]{1,0:T(8,128)S(1)}, u32[]{:S(2)}, u32[]{:S(2)}) collective-permute-start(f32[128,256]{1,0:T(8,128)S(1)} %add.117), channel_id=1, source_target_pairs={{0,2},{1,3},{2,0},{3,1},{4,6},{5,7},{6,4},{7,5},{8,10},{9,11},{10,... | collective-permute-start | bytes 393224 | tf_op jit(solution)/shard_map/ppermute | solution.py:26
  20.1 9.2 %collective-permute-start.4 = (f32[128,256]{1,0:T(8,128)S(1)}, f32[128,256]{1,0:T(8,128)S(1)}, u32[]{:S(2)}, u32[]{:S(2)}) collective-permute-start(f32[128,256]{1,0:T(8,128)S(1)} %add.117), channel_id=1, source_target_pairs={{0,4},{1,5},{2,6},{3,7},{4,0},{5,1},{6,2},{7,3},{8,12},{9,13},{10,... | collective-permute-start | bytes 393224 | tf_op jit(solution)/shard_map/ppermute | solution.py:26
  26.1 6.8 %collective-permute-start.5 = (f32[128,256]{1,0:T(8,128)S(1)}, f32[128,256]{1,0:T(8,128)S(1)}, u32[]{:S(2)}, u32[]{:S(2)}) collective-permute-start(f32[128,256]{1,0:T(8,128)S(1)} %add.117), channel_id=1, source_target_pairs={{0,6},{1,7},{2,4},{3,5},{4,2},{5,3},{6,0},{7,1},{8,14},{9,15},{10,... | collective-permute-start | bytes 393224 | tf_op jit(solution)/shard_map/ppermute | solution.py:26
  70.4 6.5 %collective-permute-start.18 = (f32[64,256]{1,0:T(8,128)S(1)}, f32[64,256]{1,0:T(8,128)S(1)}, u32[]{:S(2)}, u32[]{:S(2)}) collective-permute-start(f32[64,256]{1,0:T(8,128)S(1)} %add_add_fusion.4), channel_id=1, source_target_pairs={{0,2},{1,3},{2,0},{3,1},{4,6},{5,7},{6,4},{7,5},{8,10},{9,11},{10,... | collective-permute-start | bytes 196616 | tf_op jit(solution)/shard_map/ppermute | solution.py:26
  72.0 6.6 %collective-permute-start.19 = (f32[64,256]{1,0:T(8,128)S(1)}, f32[64,256]{1,0:T(8,128)S(1)}, u32[]{:S(2)}, u32[]{:S(2)}) collective-permute-start(f32[64,256]{1,0:T(8,128)S(1)} %add_add_fusion.4), channel_id=1, source_target_pairs={{0,4},{1,5},{2,6},{3,7},{4,0},{5,1},{6,2},{7,3},{8,12},{9,13},{10,... | collective-permute-start | bytes 196616 | tf_op jit(solution)/shard_map/ppermute | solution.py:26
  74.8 6.5 %collective-permute-start.8 = (f32[128,256]{1,0:T(8,128)}, f32[128,256]{1,0:T(8,128)S(1)}, u32[]{:S(2)}, u32[]{:S(2)}) collective-permute-start(f32[128,256]{1,0:T(8,128)} %add_add_fusion.refs_1_), channel_id=1, source_target_pairs={{0,8},{8,0},{16,24},{24,16},{1,9},{9,1},{17,25},{25,17},{2,10},{10... | collective-permute-start | bytes 393224 | tf_op jit(solution)/shard_map/ppermute | solution.py:26
  75.3 7.6 %collective-permute-start.9 = (f32[128,256]{1,0:T(8,128)}, f32[128,256]{1,0:T(8,128)S(1)}, u32[]{:S(2)}, u32[]{:S(2)}) collective-permute-start(f32[128,256]{1,0:T(8,128)} %add_add_fusion.refs_1_), channel_id=1, source_target_pairs={{0,16},{8,24},{16,0},{24,8},{1,17},{9,25},{17,1},{25,9},{2,18},{10... | collective-permute-start | bytes 393224 | tf_op jit(solution)/shard_map/ppermute | solution.py:26
  76.9 6.3 %collective-permute-start.10 = (f32[128,256]{1,0:T(8,128)}, f32[128,256]{1,0:T(8,128)S(1)}, u32[]{:S(2)}, u32[]{:S(2)}) collective-permute-start(f32[128,256]{1,0:T(8,128)} %add_add_fusion.refs_1_), channel_id=1, source_target_pairs={{0,24},{8,16},{16,8},{24,0},{1,25},{9,17},{17,9},{25,1},{2,26},{10... | collective-permute-start | bytes 393224 | tf_op jit(solution)/shard_map/ppermute | solution.py:26
  82.8 7.9 %collective-permute-start.12 = (f32[128,256]{1,0:T(8,128)S(1)}, f32[128,256]{1,0:T(8,128)S(1)}, u32[]{:S(2)}, u32[]{:S(2)}) collective-permute-start(f32[128,256]{1,0:T(8,128)S(1)} %collective-permute-done.8.refs_2_), channel_id=1, source_target_pairs={{0,1},{1,0},{2,3},{3,2},{4,5},{5,4},{6,7},{7,6},{8,9},{9,8},{10,11... | collective-permute-start | bytes 393224 | tf_op jit(solution)/shard_map/ppermute | solution.py:26
  83.2 7.6 %collective-permute-start.13 = (f32[128,256]{1,0:T(8,128)S(1)}, f32[128,256]{1,0:T(8,128)S(1)}, u32[]{:S(2)}, u32[]{:S(2)}) collective-permute-start(f32[128,256]{1,0:T(8,128)S(1)} %collective-permute-done.9.refs_3_), channel_id=1, source_target_pairs={{0,1},{1,0},{2,3},{3,2},{4,5},{5,4},{6,7},{7,6},{8,9},{9,8},{10,11... | collective-permute-start | bytes 393224 | tf_op jit(solution)/shard_map/ppermute | solution.py:26
  83.4 7.5 %collective-permute-start.14 = (f32[128,256]{1,0:T(8,128)S(1)}, f32[128,256]{1,0:T(8,128)S(1)}, u32[]{:S(2)}, u32[]{:S(2)}) collective-permute-start(f32[128,256]{1,0:T(8,128)S(1)} %collective-permute-done.10.refs_4_), channel_id=1, source_target_pairs={{0,1},{1,0},{2,3},{3,2},{4,5},{5,4},{6,7},{7,6},{8,9},{9,8},{10,11... | collective-permute-start | bytes 393224 | tf_op jit(solution)/shard_map/ppermute | solution.py:26
  113.1 6.6 %collective-permute-start.32 = (f32[72,256]{1,0:T(8,128)S(1)}, f32[72,256]{1,0:T(8,128)S(1)}, u32[]{:S(2)}, u32[]{:S(2)}) collective-permute-start(f32[72,256]{1,0:T(8,128)S(1)} %add_add_fusion.2), channel_id=1, source_target_pairs={{0,2},{1,3},{2,0},{3,1},{4,6},{5,7},{6,4},{7,5},{8,10},{9,11},{10,... | collective-permute-start | bytes 221192 | tf_op jit(solution)/shard_map/ppermute | solution.py:26
  113.2 7.9 %collective-permute-start.33 = (f32[72,256]{1,0:T(8,128)S(1)}, f32[72,256]{1,0:T(8,128)S(1)}, u32[]{:S(2)}, u32[]{:S(2)}) collective-permute-start(f32[72,256]{1,0:T(8,128)S(1)} %add_add_fusion.2), channel_id=1, source_target_pairs={{0,4},{1,5},{2,6},{3,7},{4,0},{5,1},{6,2},{7,3},{8,12},{9,13},{10,... | collective-permute-start | bytes 221192 | tf_op jit(solution)/shard_map/ppermute | solution.py:26
  117.6 10.4 %collective-permute-start.50 = (bf16[256,512]{1,0:T(8,128)(2,1)}, bf16[256,512]{1,0:T(8,128)(2,1)}, u32[]{:S(2)}, u32[]{:S(2)}) collective-permute-start(bf16[256,512]{1,0:T(8,128)(2,1)} %get-tuple-element.82), channel_id=1, source_target_pairs={{0,24},{8,16},{16,8},{24,0},{1,25},{9,17},{17,9},{25,1},{2,26},{10... | collective-permute-start | bytes 786440 | tf_op jit(solution)/shard_map/ppermute | solution.py:26
  119.2 70.6 %collective-permute-start.48 = (bf16[4,256,512]{2,1,0:T(8,128)(2,1)S(1)}, bf16[4,256,512]{2,1,0:T(8,128)(2,1)S(1)}, u32[]{:S(2)}, u32[]{:S(2)}) collective-permute-start(bf16[4,256,512]{2,1,0:T(8,128)(2,1)S(1)} %copy-done.2), channel_id=1, source_target_pairs={{0,8},{8,0},{16,24},{24,16},{1,9},{9,1},{17,25},{25,17},{2,10},{10... | collective-permute-start | bytes 3145736 | tf_op jit(solution)/shard_map/ppermute | solution.py:26
  119.8 76.1 %collective-permute-start.49 = (bf16[4,256,512]{2,1,0:T(8,128)(2,1)}, bf16[4,256,512]{2,1,0:T(8,128)(2,1)S(1)}, u32[]{:S(2)}, u32[]{:S(2)}) collective-permute-start(bf16[4,256,512]{2,1,0:T(8,128)(2,1)} %get-tuple-element.81), channel_id=1, source_target_pairs={{0,16},{8,24},{16,0},{24,8},{1,17},{9,25},{17,1},{25,9},{2,18},{10... | collective-permute-start | bytes 3145736 | tf_op jit(solution)/shard_map/ppermute | solution.py:26
  122.9 28.0 %collective-permute-start.35 = (f32[72,256]{1,0:T(8,128)S(1)}, f32[72,256]{1,0:T(8,128)S(1)}, u32[]{:S(2)}, u32[]{:S(2)}) collective-permute-start(f32[72,256]{1,0:T(8,128)S(1)} %add_add_fusion.1.refs_1_), channel_id=1, source_target_pairs={{0,8},{8,0},{16,24},{24,16},{1,9},{9,1},{17,25},{25,17},{2,10},{10... | collective-permute-start | bytes 221192 | tf_op jit(solution)/shard_map/ppermute | solution.py:26
  123.5 38.5 %collective-permute-start.51 = (bf16[512,256]{1,0:T(8,128)(2,1)}, bf16[512,256]{1,0:T(8,128)(2,1)S(1)}, u32[]{:S(2)}, u32[]{:S(2)}) collective-permute-start(bf16[512,256]{1,0:T(8,128)(2,1)} %get-tuple-element.83), channel_id=1, source_target_pairs={{0,8},{8,0},{16,24},{24,16},{1,9},{9,1},{17,25},{25,17},{2,10},{10... | collective-permute-start | bytes 786440 | tf_op jit(solution)/shard_map/ppermute | solution.py:26
  128.0 34.4 %collective-permute-start.55 = (bf16[512,256]{1,0:T(8,128)(2,1)}, bf16[512,256]{1,0:T(8,128)(2,1)S(1)}, u32[]{:S(2)}, u32[]{:S(2)}) collective-permute-start(bf16[512,256]{1,0:T(8,128)(2,1)} %get-tuple-element.84), channel_id=1, source_target_pairs={{0,16},{8,24},{16,0},{24,8},{1,17},{9,25},{17,1},{25,9},{2,18},{10... | collective-permute-start | bytes 786440 | tf_op jit(solution)/shard_map/ppermute | solution.py:26
  163.1 9.5 %collective-permute-start.52 = (bf16[512,256]{1,0:T(8,128)(2,1)}, bf16[512,256]{1,0:T(8,128)(2,1)}, u32[]{:S(2)}, u32[]{:S(2)}) collective-permute-start(bf16[512,256]{1,0:T(8,128)(2,1)} %get-tuple-element.83), channel_id=1, source_target_pairs={{0,16},{8,24},{16,0},{24,8},{1,17},{9,25},{17,1},{25,9},{2,18},{10... | collective-permute-start | bytes 786440 | tf_op jit(solution)/shard_map/ppermute | solution.py:26
  164.5 9.4 %collective-permute-start.54 = (bf16[512,256]{1,0:T(8,128)(2,1)}, bf16[512,256]{1,0:T(8,128)(2,1)}, u32[]{:S(2)}, u32[]{:S(2)}) collective-permute-start(bf16[512,256]{1,0:T(8,128)(2,1)} %get-tuple-element.84), channel_id=1, source_target_pairs={{0,8},{8,0},{16,24},{24,16},{1,9},{9,1},{17,25},{25,17},{2,10},{10... | collective-permute-start | bytes 786440 | tf_op jit(solution)/shard_map/ppermute | solution.py:26
  165.9 11.5 %collective-permute-start.53 = (bf16[512,256]{1,0:T(8,128)(2,1)S(1)}, bf16[512,256]{1,0:T(8,128)(2,1)}, u32[]{:S(2)}, u32[]{:S(2)}) collective-permute-start(bf16[512,256]{1,0:T(8,128)(2,1)S(1)} %collective-permute-done.51.refs_0_), channel_id=1, source_target_pairs={{0,16},{8,24},{16,0},{24,8},{1,17},{9,25},{17,1},{25,9},{2,18},{10... | collective-permute-start | bytes 786440 | tf_op jit(solution)/shard_map/ppermute | solution.py:26
  172.6 9.5 %collective-permute-start.56 = (bf16[512,256]{1,0:T(8,128)(2,1)}, bf16[512,256]{1,0:T(8,128)(2,1)S(1)}, u32[]{:S(2)}, u32[]{:S(2)}) collective-permute-start(bf16[512,256]{1,0:T(8,128)(2,1)} %copy-done.4), channel_id=1, source_target_pairs={{0,8},{8,0},{16,24},{24,16},{1,9},{9,1},{17,25},{25,17},{2,10},{10... | collective-permute-start | bytes 786440 | tf_op jit(solution)/shard_map/ppermute | solution.py:26
  173.9 13.9 %collective-permute-start.42 = (bf16[256,512]{1,0:T(8,128)(2,1)}, bf16[256,512]{1,0:T(8,128)(2,1)}, u32[]{:S(2)}, u32[]{:S(2)}) collective-permute-start(bf16[256,512]{1,0:T(8,128)(2,1)} %get-tuple-element.76.a), channel_id=1, source_target_pairs={{0,8},{8,0},{16,24},{24,16},{1,9},{9,1},{17,25},{25,17},{2,10},{10... | collective-permute-start | bytes 786440 | tf_op jit(solution)/shard_map/ppermute | solution.py:26
  177.4 11.9 %collective-permute-start.44 = (bf16[256,512]{1,0:T(8,128)(2,1)}, bf16[256,512]{1,0:T(8,128)(2,1)}, u32[]{:S(2)}, u32[]{:S(2)}) collective-permute-start(bf16[256,512]{1,0:T(8,128)(2,1)} %get-tuple-element.77.b), channel_id=1, source_target_pairs={{0,16},{8,24},{16,0},{24,8},{1,17},{9,25},{17,1},{25,9},{2,18},{10... | collective-permute-start | bytes 786440 | tf_op jit(solution)/shard_map/ppermute | solution.py:26
  182.1 19.8 %collective-permute-start.46 = (bf16[256,512]{1,0:T(8,128)(2,1)}, bf16[256,512]{1,0:T(8,128)(2,1)}, u32[]{:S(2)}, u32[]{:S(2)}) collective-permute-start(bf16[256,512]{1,0:T(8,128)(2,1)} %get-tuple-element.77.b), channel_id=1, source_target_pairs={{0,8},{8,0},{16,24},{24,16},{1,9},{9,1},{17,25},{25,17},{2,10},{10... | collective-permute-start | bytes 786440 | tf_op jit(solution)/shard_map/ppermute | solution.py:26
  187.8 14.1 %collective-permute-start.47 = (bf16[256,512]{1,0:T(8,128)(2,1)}, bf16[256,512]{1,0:T(8,128)(2,1)}, u32[]{:S(2)}, u32[]{:S(2)}) collective-permute-start(bf16[256,512]{1,0:T(8,128)(2,1)} %get-tuple-element.76.a), channel_id=1, source_target_pairs={{0,16},{8,24},{16,0},{24,8},{1,17},{9,25},{17,1},{25,9},{2,18},{10... | collective-permute-start | bytes 786440 | tf_op jit(solution)/shard_map/ppermute | solution.py:26
  189.3 15.3 %collective-permute-start.43 = (bf16[256,512]{1,0:T(8,128)(2,1)}, bf16[256,512]{1,0:T(8,128)(2,1)}, u32[]{:S(2)}, u32[]{:S(2)}) collective-permute-start(bf16[256,512]{1,0:T(8,128)(2,1)} %collective-permute-done.42.refs_0_), channel_id=1, source_target_pairs={{0,16},{8,24},{16,0},{24,8},{1,17},{9,25},{17,1},{25,9},{2,18},{10... | collective-permute-start | bytes 786440 | tf_op jit(solution)/shard_map/ppermute | solution.py:26
  189.8 14.8 %collective-permute-start.45 = (bf16[256,512]{1,0:T(8,128)(2,1)}, bf16[256,512]{1,0:T(8,128)(2,1)}, u32[]{:S(2)}, u32[]{:S(2)}) collective-permute-start(bf16[256,512]{1,0:T(8,128)(2,1)} %collective-permute-done.44.refs_1_), channel_id=1, source_target_pairs={{0,8},{8,0},{16,24},{24,16},{1,9},{9,1},{17,25},{25,17},{2,10},{10... | collective-permute-start | bytes 786440 | tf_op jit(solution)/shard_map/ppermute | solution.py:26
  (54 other events, 334.0 us)
